TPU v7x, 256 devices: a whole 4x4x8 slice. The times are simulated.
256 devices in a mesh: space: 32 (over x, z), rep: 8 (over y, core).
Axes of the slice: x: 4, y: 4, z: 8, core: 2. Of those that a mesh axis runs over, the one named last changes fastest.
Arguments:
- stem_input: bfloat16 [8, 128, 512, 256], P('rep', 'space'), may hold values from -6 to 6
- stem_preact: bfloat16 [8, 64, 256, 256], P('rep', 'space'), may hold values from -6 to 6
- deep_cotangent: bfloat16 [8, 64, 256, 1024], P('rep', None, 'space'), may hold values from -6 to 6
- tissue_tiles: int32 [8], P('rep'), may hold values from 1 to 64
- conv_weight: bfloat16 [3, 3, 256, 256], replicated, may hold values from -0.125 to 0.125
- expand_weight: bfloat16 [256, 1024], replicated, may hold values from -0.1875 to 0.1875
Outputs:
- grad_input: bfloat16 [8, 128, 512, 256], P('rep', 'space')
- grad_conv: float32 [3, 3, 256, 256], replicated
- grad_expand: float32 [256, 1024], replicated
All inputs are finite; a program needn't handle non-finite values.
Results may differ from a plain program's by a relative error of at most 0.001.
The roundings to bfloat16 on the way count: a program that leaves them out, or rounds other values in their place, can miss the bound.
Values may be sent and summed in bfloat16 or wider, within the bound.
No kernel may reach another device: no remote copies, remote signals or barrier semaphores. Data moves between devices by JAX's collectives and lax.ppermute only.
A program may use at most 128 MiB of HBM per device.

v0:
```python
import jax
import jax.numpy as jnp
from jax import lax
from jax.sharding import PartitionSpec as P

TILES = 64


def shifted(x, axis, by):
    length = lax.axis_size(axis)
    pairs = [(i, i + by) for i in range(length) if 0 <= i + by < length]
    return lax.ppermute(x, axis, pairs)


def weight_taps(above, strip_rows, cotangent):
    samples_here, half_rows, width_out, channels_out = cotangent.shape
    zero_row = jnp.zeros_like(strip_rows[:, :1])
    padded = jnp.concatenate([above, strip_rows, zero_row], axis=1)
    zero_col = jnp.zeros_like(padded[:, :, :1])
    padded = jnp.concatenate([zero_col, padded, zero_col], axis=2)
    padded = padded.reshape(samples_here, half_rows + 1, 2, width_out + 1, 2, strip_rows.shape[3])
    blocks = []
    for row_tap in range(3):
        for col_tap in range(3):
            window = padded[
                :,
                row_tap // 2 : row_tap // 2 + half_rows,
                row_tap % 2,
                col_tap // 2 : col_tap // 2 + width_out,
                col_tap % 2,
                :,
            ]
            blocks.append(
                lax.dot_general(
                    window,
                    cotangent,
                    (((0, 1, 2), (0, 1, 2)), ((), ())),
                    preferred_element_type=jnp.float32,
                )
            )
    return jnp.stack(blocks, axis=1)


def input_grad(extended, conv_weight):
    samples_here, ext_rows, width_out, channels_out = extended.shape
    half_rows = ext_rows - 1
    tap_terms = lax.dot_general(
        extended, conv_weight, (((3,), (3,)), ((), ())), preferred_element_type=jnp.float32
    )
    accumulated = jnp.zeros(
        (samples_here, half_rows + 1, 2, width_out + 1, 2, conv_weight.shape[2]), jnp.float32
    )
    for row_tap in range(3):
        if row_tap < 2:
            row_target, row_source, row_parity = (
                slice(0, half_rows + 1),
                slice(0, half_rows + 1),
                row_tap,
            )
        else:
            row_target, row_source, row_parity = (slice(1, half_rows + 1), slice(0, half_rows), 0)
        for col_tap in range(3):
            if col_tap < 2:
                col_target, col_source, col_parity = (
                    slice(0, width_out),
                    slice(0, width_out),
                    col_tap,
                )
            else:
                col_target, col_source, col_parity = (
                    slice(1, width_out + 1),
                    slice(0, width_out),
                    0,
                )
            accumulated = accumulated.at[:, row_target, row_parity, col_target, col_parity, :].add(
                tap_terms[:, row_source, col_source, row_tap, col_tap, :]
            )
    accumulated = accumulated.reshape(
        samples_here, 2 * half_rows + 2, 2 * width_out + 2, conv_weight.shape[2]
    )
    return accumulated[:, 1 : 2 * half_rows + 1, 1 : 2 * width_out + 1, :].astype(jnp.bfloat16)


def body(stem_input, stem_preact, deep_cotangent, tissue_tiles, conv_weight, expand_weight):
    tile_share = tissue_tiles.astype(jnp.float32) / TILES
    weighted = (deep_cotangent.astype(jnp.float32) * tile_share[:, None, None, None]).astype(
        jnp.bfloat16
    )
    active = jnp.maximum(stem_preact, jnp.zeros_like(stem_preact))
    active_deep = lax.all_to_all(active, "space", split_axis=2, concat_axis=1, tiled=True)
    part_expand = lax.dot_general(
        active_deep,
        weighted,
        (((0, 1, 2), (0, 1, 2)), ((), ())),
        preferred_element_type=jnp.float32,
    )
    hidden_deep = lax.dot_general(
        weighted, expand_weight, (((3,), (1,)), ((), ())), preferred_element_type=jnp.float32
    ).astype(jnp.bfloat16)
    grad_hidden = lax.all_to_all(hidden_deep, "space", split_axis=1, concat_axis=2, tiled=True)
    grad_pre = jnp.where(stem_preact > 0, grad_hidden, jnp.zeros_like(grad_hidden))
    above = shifted(stem_input[:, -1:], "space", 1)
    below = shifted(grad_pre[:, :1], "space", -1)
    part_conv = weight_taps(above, stem_input, grad_pre)
    grad_input = input_grad(jnp.concatenate([grad_pre, below], axis=1), conv_weight)
    samples_all = stem_input.shape[0] * lax.axis_size("rep")
    rows_all = stem_preact.shape[1] * lax.axis_size("space")
    grad_scale = float(samples_all * rows_all * stem_preact.shape[2]) ** (-0.5)
    channels = conv_weight.shape[2]
    partial_sum = (
        jnp.concatenate([part_conv.reshape(channels, 9 * channels), part_expand], axis=1)
        * grad_scale
    )
    summed = lax.psum(partial_sum, ("space", "rep"))
    grad_conv = summed[:, : 9 * channels].reshape(channels, 3, 3, channels).transpose(1, 2, 0, 3)
    grad_expand = summed[:, 9 * channels :]
    return (grad_input, grad_conv, grad_expand)


def solution(mesh):
    return jax.shard_map(
        body,
        mesh=mesh,
        in_specs=(
            P("rep", "space", None, None),
            P("rep", "space", None, None),
            P("rep", None, "space", None),
            P("rep"),
            P(),
            P(),
        ),
        out_specs=(P("rep", "space", None, None), P(), P()),
        check_vma=False,
    )
```

profile of v0, /device:TPU:2, one launch (start us, length us, event | category | flops | bytes accessed | tf_op | source)
XLA Modules:
  0.0 429.4 jit_solution(16519835688769396188)
XLA Ops:
  8.3 4.0 collective-permute-start.1
  16.5 10.7 %all-to-all-start = ((bf16[1,64,8,256]{3,2,0,1:T(8,128)(2,1)}), bf16[1,64,8,256]{3,2,0,1:T(8,128)(2,1)S(1)}, u32[]{:S(2)}, u32[]{:S(2)}) async-start(bf16[1,64,8,256]{3,2,0,1:T(8,128)(2,1)} %fusion.11), calls=%async_computation | async-start | bytes 524288 | tf_op jit(solution)/shard_map/all_to_all | solution.py:100
  29.1 2.8 reshape.527
  31.9 4.5 %fusion.34 = (bf16[1,2,1,256,1,256]{5,4,3,2,1,0:T(2,128)(2,1)S(1)}, bf16[1,2,1,256,1,256]{5,4,3,2,1,0:T(2,128)(2,1)}, bf16[1,2,1,256,1,256]{5,4,3,2,1,0:T(2,128)...) fusion(bf16[1,3,2,257,2,256]{5,4,3,2,1,0:T(2,128)(2,1)S(1)} %re, ...), kind=kLoop, calls=%fused_computation.71 | loop fusion | bytes 4718592 | tf_op jit(solution)/shard_map/slice | solution.py:25
  39.1 3.0 collective-permute-start
  43.1 7.7 %all-to-all-start.1 = ((bf16[1,2,256,256]{3,1,0,2:T(2,128)(2,1)}), bf16[1,2,256,256]{3,1,0,2:T(2,128)(2,1)S(1)}, u32[]{:S(2)}, u32[]{:S(2)}) async-start(bf16[1,2,256,256]{3,1,0,2:T(2,128)(2,1)} %copy.120), calls=%async_computation.1 | async-start | bytes 524288 | tf_op jit(solution)/shard_map/all_to_all | solution.py:90
  52.0 2.1 fusion.9
  56.1 2.0 fusion.7
  60.2 2.0 fusion.5
  65.2 3.9 fusion
  69.1 11.5 %copy.170 = f32[3,256,3,3,256]{4,2,3,1,0:T(4,128)} copy(f32[3,256,3,3,256]{4,1,3,2,0:T(8,128)} %fusion) | data formatting | bytes 14155776 | tf_op jit(solution)/shard_map/dot_general | solution.py:47
  80.7 3.9 slice_bitcast_fusion.4
  84.6 2.6 scatter-add.30
  87.2 16.7 %scatter-add.31 = f32[1,3,2,257,2,256]{5,4,3,2,1,0:T(2,128)} dynamic-update-slice(f32[1,3,2,257,2,256]{5,4,3,2,1,0:T(2,128)} %scatter-add.30, f32[1,3,1,256,1,256]{5,4,3,2,1,0:T(1,128)S(1)} %get-tuple-element.120, s32[]{:T(128)} %constant.309.clone.1, s32[]{:T(128)} %constant.309.clone.1, s32[]{:T(128)} %constant.309.clone.1, s32[]{:T(128)} %constant.309.clone.1, s32[]{:T(128)} %constant.310.clone.1, ...) | dynamic-update-slice | bytes 1572868 | tf_op jit(solution)/shard_map/scatter-add | solution.py:75
  103.9 3.2 fusion.17
  107.1 16.7 %scatter-add.34 = f32[1,3,2,257,2,256]{5,4,3,2,1,0:T(2,128)} dynamic-update-slice(f32[1,3,2,257,2,256]{5,4,3,2,1,0:T(2,128)} %scatter-add.31, f32[1,3,1,256,1,256]{5,4,3,2,1,0:T(1,128)S(1)} %fusion.17, s32[]{:T(128)} %constant.309.clone.1, s32[]{:T(128)} %constant.309.clone.1, s32[]{:T(128)} %constant.309.clone.1, s32[]{:T(128)} %constant.310.clone.1, s32[]{:T(128)} %constant.309.clone.1, ...) | dynamic-update-slice | bytes 1572868 | tf_op jit(solution)/shard_map/scatter-add | solution.py:75
  123.8 3.7 fusion.16
  127.5 16.7 %scatter-add.35 = f32[1,3,2,257,2,256]{5,4,3,2,1,0:T(2,128)} dynamic-update-slice(f32[1,3,2,257,2,256]{5,4,3,2,1,0:T(2,128)} %scatter-add.34, f32[1,3,1,256,1,256]{5,4,3,2,1,0:T(1,128)S(1)} %fusion.16, s32[]{:T(128)} %constant.309.clone.1, s32[]{:T(128)} %constant.309.clone.1, s32[]{:T(128)} %constant.310.clone.1, s32[]{:T(128)} %constant.309.clone.1, s32[]{:T(128)} %constant.309.clone.1, ...) | dynamic-update-slice | bytes 1572868 | tf_op jit(solution)/shard_map/scatter-add | solution.py:75
  145.8 3.7 maximum_multiply_fusion
  149.5 3.8 fusion.15
  153.3 16.7 %scatter-add.36 = f32[1,3,2,257,2,256]{5,4,3,2,1,0:T(2,128)} dynamic-update-slice(f32[1,3,2,257,2,256]{5,4,3,2,1,0:T(2,128)} %scatter-add.35, f32[1,3,1,256,1,256]{5,4,3,2,1,0:T(1,128)S(1)} %fusion.15, s32[]{:T(128)} %constant.309.clone.1, s32[]{:T(128)} %constant.309.clone.1, s32[]{:T(128)} %constant.310.clone.1, s32[]{:T(128)} %constant.309.clone.1, s32[]{:T(128)} %constant.310.clone.1, ...) | dynamic-update-slice | bytes 1572868 | tf_op jit(solution)/shard_map/scatter-add | solution.py:75
  170.0 3.6 fusion.14
  173.6 16.7 %scatter-add.39 = f32[1,3,2,257,2,256]{5,4,3,2,1,0:T(2,128)} dynamic-update-slice(f32[1,3,2,257,2,256]{5,4,3,2,1,0:T(2,128)} %scatter-add.36, f32[1,3,1,256,1,256]{5,4,3,2,1,0:T(1,128)S(1)} %fusion.14, s32[]{:T(128)} %constant.309.clone.1, s32[]{:T(128)} %constant.309.clone.1, s32[]{:T(128)} %constant.310.clone.1, s32[]{:T(128)} %constant.310.clone.1, s32[]{:T(128)} %constant.309.clone.1, ...) | dynamic-update-slice | bytes 1572868 | tf_op jit(solution)/shard_map/scatter-add | solution.py:75
  190.4 2.7 fusion.20
  193.1 11.6 %scatter-add.40 = f32[1,3,2,257,2,256]{5,4,3,2,1,0:T(2,128)} dynamic-update-slice(f32[1,3,2,257,2,256]{5,4,3,2,1,0:T(2,128)} %scatter-add.39, f32[1,2,1,256,1,256]{5,4,3,2,1,0:T(1,128)S(1)} %fusion.20, s32[]{:T(128)} %constant.309.clone.1, s32[]{:T(128)} %constant.310.clone.1, s32[]{:T(128)} %constant.309.clone.1, s32[]{:T(128)} %constant.309.clone.1, s32[]{:T(128)} %constant.309.clone.1, ...) | dynamic-update-slice | bytes 1048580 | tf_op jit(solution)/shard_map/scatter-add | solution.py:75
  204.6 2.8 fusion.19
  207.5 11.5 %scatter-add.41 = f32[1,3,2,257,2,256]{5,4,3,2,1,0:T(2,128)} dynamic-update-slice(f32[1,3,2,257,2,256]{5,4,3,2,1,0:T(2,128)} %scatter-add.40, f32[1,2,1,256,1,256]{5,4,3,2,1,0:T(1,128)S(1)} %fusion.19, s32[]{:T(128)} %constant.309.clone.1, s32[]{:T(128)} %constant.310.clone.1, s32[]{:T(128)} %constant.309.clone.1, s32[]{:T(128)} %constant.309.clone.1, s32[]{:T(128)} %constant.310.clone.1, ...) | dynamic-update-slice | bytes 1048580 | tf_op jit(solution)/shard_map/scatter-add | solution.py:75
  219.0 2.7 fusion.18
  221.7 11.5 %scatter-add.44 = f32[1,3,2,257,2,256]{5,4,3,2,1,0:T(2,128)} dynamic-update-slice(f32[1,3,2,257,2,256]{5,4,3,2,1,0:T(2,128)} %scatter-add.41, f32[1,2,1,256,1,256]{5,4,3,2,1,0:T(1,128)S(1)} %fusion.18, s32[]{:T(128)} %constant.309.clone.1, s32[]{:T(128)} %constant.310.clone.1, s32[]{:T(128)} %constant.309.clone.1, s32[]{:T(128)} %constant.310.clone.1, s32[]{:T(128)} %constant.309.clone.1, ...) | dynamic-update-slice | bytes 1048580 | tf_op jit(solution)/shard_map/scatter-add | solution.py:75
  233.3 3.0 convert.4
  238.2 2.5 slice.538
  240.7 175.7 %all-reduce.3.cloned.1.call-done = f32[256,3328]{0,1:T(8,128)} async-done(((f32[256,3328]{0,1:T(8,128)}), f32[256,3328]{0,1:T(8,128)}) %all-reduce.3.cloned.1.call-update) | async-done | bytes 3407888 | tf_op jit(solution)/shard_map/psum | solution.py:114
  (48 shorter events, 28.1 us)
Async XLA Ops:
  7.2 58.0 %copy-start = (bf16[3,3,256,256]{3,2,1,0:T(8,128)(2,1)S(1)}, bf16[3,3,256,256]{3,2,1,0:T(8,128)(2,1)}, u32[]{:S(2)}) copy-start(bf16[3,3,256,256]{3,2,1,0:T(8,128)(2,1)} %param.28) | copy-start | bytes 3538948
  7.2 8.2 %copy-start.7 = (bf16[256,1024]{1,0:T(8,128)(2,1)S(1)}, bf16[256,1024]{1,0:T(8,128)(2,1)}, u32[]{:S(2)}) copy-start(bf16[256,1024]{1,0:T(8,128)(2,1)} %param.29) | copy-start | bytes 1572868
  8.3 19.0 %copy-start.3 = (bf16[1,4,512,256]{3,2,1,0:T(8,128)(2,1)S(1)}, bf16[1,4,512,256]{3,2,1,0:T(8,128)(2,1)}, u32[]{:S(2)}) copy-start(bf16[1,4,512,256]{3,2,1,0:T(8,128)(2,1)} %param.24) | copy-start | bytes 3145732
  8.3 19.0 %collective-permute-start.1 = (bf16[1,1,512,256]{3,2,1,0:T(8,128)(2,1)S(1)}, bf16[1,1,512,256]{3,2,1,0:T(8,128)(2,1)S(1)}, u32[]{:S(2)}, u32[]{:S(2)}) collective-permute-start(bf16[1,1,512,256]{3,2,1,0:T(8,128)(2,1)S(1)} %slice.509), channel_id=1, source_target_pairs={{0,8},{8,16},{16,24},{24,32},{32,40},{40,48},{48,56},{56,64},{64,7... | collective-permute-start | bytes 786440 | tf_op jit(solution)/shard_map/ppermute | solution.py:12
  14.4 1.0 copy-start.1
  16.5 21.6 %all-to-all-start = ((bf16[1,64,8,256]{3,2,0,1:T(8,128)(2,1)}), bf16[1,64,8,256]{3,2,0,1:T(8,128)(2,1)S(1)}, u32[]{:S(2)}, u32[]{:S(2)}) async-start(bf16[1,64,8,256]{3,2,0,1:T(8,128)(2,1)} %fusion.11), calls=%async_computation | async-start | bytes 524288 | tf_op jit(solution)/shard_map/all_to_all | solution.py:100
  36.4 14.6 %copy-start.6 = (bf16[1,2,1,256,1,256]{5,4,3,2,1,0:T(2,128)(2,1)S(1)}, bf16[1,2,1,256,1,256]{5,4,3,2,1,0:T(2,128)(2,1)}, u32[]{:S(2)}) copy-start(bf16[1,2,1,256,1,256]{5,4,3,2,1,0:T(2,128)(2,1)} %get-tuple-element.130) | copy-start | bytes 786436
  39.1 26.0 %collective-permute-start = (bf16[1,1,256,256]{3,2,1,0:T(8,128)(2,1)S(1)}, bf16[1,1,256,256]{3,2,1,0:T(8,128)(2,1)S(1)}, u32[]{:S(2)}, u32[]{:S(2)}) collective-permute-start(bf16[1,1,256,256]{3,2,1,0:T(8,128)(2,1)S(1)} %slice.521), channel_id=1, source_target_pairs={{8,0},{16,8},{24,16},{32,24},{40,32},{48,40},{56,48},{64,56},{72,6... | collective-permute-start | bytes 393224 | tf_op jit(solution)/shard_map/ppermute | solution.py:12
  43.1 101.1 %all-to-all-start.1 = ((bf16[1,2,256,256]{3,1,0,2:T(2,128)(2,1)}), bf16[1,2,256,256]{3,1,0,2:T(2,128)(2,1)S(1)}, u32[]{:S(2)}, u32[]{:S(2)}) async-start(bf16[1,2,256,256]{3,1,0,2:T(2,128)(2,1)} %copy.120), calls=%async_computation.1 | async-start | bytes 524288 | tf_op jit(solution)/shard_map/all_to_all | solution.py:90
  50.8 365.6 %all-reduce.3.cloned.1.call-start = ((), (), s32[]{:S(2)}) async-start(), calls=%async_computation.2 | async-start | bytes 6815744 | tf_op jit(solution)/shard_map/psum | solution.py:114
  51.0 11.2 %copy-start.5 = (bf16[1,2,1,256,1,256]{5,4,3,2,1,0:T(2,128)(2,1)S(1)}, bf16[1,2,1,256,1,256]{5,4,3,2,1,0:T(2,128)(2,1)}, u32[]{:S(2)}) copy-start(bf16[1,2,1,256,1,256]{5,4,3,2,1,0:T(2,128)(2,1)} %get-tuple-element.124) | copy-start | bytes 786436
  52.0 11.2 %copy-start.4 = (bf16[1,2,1,256,1,256]{5,4,3,2,1,0:T(2,128)(2,1)S(1)}, bf16[1,2,1,256,1,256]{5,4,3,2,1,0:T(2,128)(2,1)}, u32[]{:S(2)}) copy-start(bf16[1,2,1,256,1,256]{5,4,3,2,1,0:T(2,128)(2,1)} %get-tuple-element.123) | copy-start | bytes 786436
  123.8 20.7 %copy-start.2 = (bf16[64,8,1024]{2,1,0:T(8,128)(2,1)S(1)}, bf16[64,8,1024]{2,1,0:T(8,128)(2,1)}, u32[]{:S(2)}) copy-start(bf16[64,8,1024]{2,1,0:T(8,128)(2,1)} %copy-done.1) | copy-start | bytes 3145732
  416.4 1.7 slice-start
  420.0 1.2 slice-start.1
Sparse Core Ops, SparseCore 0:
  149.6 266.7 all-reduce.2
where the time goes:
time: 438 us; the launch traced here: 429 us
  waiting for transfers between devices  177 us (40%)
  local copies, waits for them, and re-layouts  158 us (36%)
  other arithmetic  33.4 us (8%)
  starting transfers between devices  25.6 us (6%)
  matrix products  20.5 us (5%)
  between operations  14.9 us (3%)
    psum x1, waiting for transfers between devices, body(): summed = lax.psum(partial_sum, ('space', 'rep'))  176 us
    scatter-add x9, local copies, waits for them, and re-layouts, input_grad(): accumulated.at[:, row_target, row_parity, col_target, col_parity, :]  121 us
    add x7, other arithmetic, input_grad(): accumulated.at[:, row_target, row_parity, col_target, col_parity, :]  22.5 us
    dot_general x9, matrix products, weight_taps(): lax.dot_general(window, cotangent, (((0, 1, 2), (0, 1, 2)), ((), ())), pr...  14.1 us
    dot_general x1, local copies, waits for them, and re-layouts, input_grad(): lax.dot_general(extended, conv_weight, (((3,), (3,)), ((), ())), preferre...  11.5 us
    all_to_all x1, starting transfers between devices, body(): lax.all_to_all(hidden_deep, 'space', split_axis=1, concat_axis=2, tiled=T...  10.7 us
  transfers between devices with their start and end apart: 5, of which 2 were waited for; matrix products, arithmetic and copies ran while one was open for 46% of the time, Pallas kernels for 0%

commit v1 on v0

v1 whole, which is shorter than its diff:
```python
import functools

import jax
import jax.numpy as jnp
from jax import lax
from jax.experimental import pallas as pl
from jax.experimental.pallas import tpu as pltpu
from jax.sharding import Mesh
from jax.sharding import PartitionSpec as P

TILES = 64
LANES = 128
SIZES = {"x": 4, "z": 8, "y": 4, "core": 2}
SPACE = ("x", "z")
REP = ("y", "core")
VMEM_BYTES = 48 * 1024 * 1024


def whole(*_):
    return pl.BlockSpec(memory_space=pltpu.VMEM)


def shifted(x, by):
    length = SIZES["x"] * SIZES["z"]
    pairs = [(i, i + by) for i in range(length) if 0 <= i + by < length]
    return lax.ppermute(x, SPACE, pairs)


def prepare_kernel(above_ref, x_ref, out_ref, wide):
    half = out_ref.shape[2]
    first = lax.broadcasted_iota(jnp.int32, (LANES, half), 1) == 0
    for row in range(5):
        source = above_ref[0] if row == 0 else x_ref[row - 1]
        for part in range(source.shape[1] // LANES):
            lanes = slice(part * LANES, (part + 1) * LANES)
            wide[...] = source[:, lanes].astype(jnp.float32)
            even = wide[pl.ds(0, half, stride=2), :].T
            odd = wide[pl.ds(1, half, stride=2), :].T
            late = jnp.where(first, 0.0, pltpu.roll(odd, 1, 1))
            out_ref[3 * row, lanes, :] = late.astype(jnp.bfloat16)
            out_ref[3 * row + 1, lanes, :] = even.astype(jnp.bfloat16)
            out_ref[3 * row + 2, lanes, :] = odd.astype(jnp.bfloat16)


def prepare(above, x):
    rows, cols, channels = x.shape
    return pl.pallas_call(
        prepare_kernel,
        out_shape=jax.ShapeDtypeStruct((15, channels, cols // 2), jnp.bfloat16),
        in_specs=[whole()] * 2,
        out_specs=whole(),
        scratch_shapes=[pltpu.VMEM((cols, LANES), jnp.float32)],
        compiler_params=pltpu.CompilerParams(vmem_limit_bytes=VMEM_BYTES),
        cost_estimate=pl.CostEstimate(flops=10**7, bytes_accessed=3 * 10**6, transcendentals=0),
        name="prepare",
    )(above, x)


def taps_kernel(blocks_ref, grad_ref, out_ref):
    for row_tap in range(3):
        for col_tap in range(3):
            total = None
            for i in range(2):
                term = jnp.dot(
                    blocks_ref[3 * (2 * i + row_tap) + col_tap],
                    grad_ref[i],
                    preferred_element_type=jnp.float32,
                )
                total = term if total is None else total + term
            out_ref[3 * row_tap + col_tap] = total


def taps(blocks, grad):
    channels = blocks.shape[1]
    return pl.pallas_call(
        taps_kernel,
        out_shape=jax.ShapeDtypeStruct((9, channels, grad.shape[2]), jnp.float32),
        in_specs=[whole()] * 2,
        out_specs=whole(),
        compiler_params=pltpu.CompilerParams(vmem_limit_bytes=VMEM_BYTES),
        cost_estimate=pl.CostEstimate(flops=604 * 10**6, bytes_accessed=5 * 10**6, transcendentals=0),
        name="taps",
    )(blocks, grad)


def input_kernel(grad_ref, below_ref, weight_ref, out_ref, wide):
    half = grad_ref.shape[1]
    last = lax.broadcasted_iota(jnp.int32, grad_ref.shape[1:], 0) == half - 1

    def early(g):
        moved = pltpu.roll(g.astype(jnp.float32), half - 1, 0)
        return jnp.where(last, 0.0, moved).astype(jnp.bfloat16)

    grads = [grad_ref[0], grad_ref[1], below_ref[0]]
    moved = [early(g) for g in grads]

    def times(g, row_tap, col_tap):
        return lax.dot_general(
            g,
            weight_ref[row_tap, col_tap],
            (((1,), (1,)), ((), ())),
            preferred_element_type=jnp.float32,
        )

    for row in range(4):
        i = row // 2
        terms = [(i, 1)] if row % 2 == 0 else [(i, 2), (i + 1, 0)]
        even = sum(times(grads[n], p, 1) for n, p in terms)
        odd = sum(times(grads[n], p, 2) + times(moved[n], p, 0) for n, p in terms)
        for part in range(even.shape[1] // LANES):
            lanes = slice(part * LANES, (part + 1) * LANES)
            wide[pl.ds(0, half, stride=2), :] = even[:, lanes]
            wide[pl.ds(1, half, stride=2), :] = odd[:, lanes]
            out_ref[row, :, lanes] = wide[...].astype(jnp.bfloat16)


def input_grad(grad, below, weight):
    rows, half, channels = grad.shape
    return pl.pallas_call(
        input_kernel,
        out_shape=jax.ShapeDtypeStruct((2 * rows, 2 * half, weight.shape[2]), jnp.bfloat16),
        in_specs=[whole()] * 3,
        out_specs=whole(),
        scratch_shapes=[pltpu.VMEM((2 * half, LANES), jnp.float32)],
        compiler_params=pltpu.CompilerParams(vmem_limit_bytes=VMEM_BYTES),
        cost_estimate=pl.CostEstimate(flops=604 * 10**6, bytes_accessed=3 * 10**6, transcendentals=0),
        name="input_grad",
    )(grad, below, weight)


def exchange(x, axis):
    return lax.all_to_all(x, axis, split_axis=0, concat_axis=0, tiled=True)


def place(axis, by=0):
    return (lax.axis_index(axis).astype(jnp.uint32) + jnp.uint32(by % SIZES[axis])) & jnp.uint32(SIZES[axis] - 1)


def pick(parts, index):
    zero = jnp.uint32(0)
    return lax.dynamic_slice(parts, (index, zero, zero), (1,) + parts.shape[1:])[0]


def put(parts, piece, index):
    zero = jnp.uint32(0)
    return lax.dynamic_update_slice(parts, piece[None], (index, zero, zero))


def rotated(x, axis, by):
    size = SIZES[axis]
    return lax.ppermute(x, axis, [(i, (i + by) % size) for i in range(size)])


def scatter_sum(x, axis):
    size = SIZES[axis]
    parts = exchange(x.reshape(size, x.shape[0] // size, x.shape[1]), axis)
    return jnp.sum(parts, axis=0)


def gather(x, axis):
    size = SIZES[axis]
    parts = exchange(jnp.broadcast_to(x[None], (size,) + x.shape), axis)
    return parts.reshape(size * x.shape[0], x.shape[1])


def scatter_sum_by_permutes(x, axis):
    size = SIZES[axis]
    parts = x.reshape(size, x.shape[0] // size, x.shape[1])
    arrived = [rotated(pick(parts, place(axis, by)), axis, by) for by in range(1, size)]
    return sum(arrived, pick(parts, place(axis)))


def gather_by_permutes(x, axis):
    size = SIZES[axis]
    out = jnp.zeros((size,) + x.shape, x.dtype)
    for by in range(size):
        piece = x if by == 0 else rotated(x, axis, by)
        out = put(out, piece, place(axis, -by))
    return out.reshape(size * x.shape[0], x.shape[1])


def core_sum(x):
    return scatter_sum_by_permutes(x, "core")


def core_gather(x):
    first = lax.axis_index("core") == 0
    got = lax.ppermute(x, "core", [(0, 1), (1, 0)])
    return jnp.where(first, x, got), jnp.where(first, got, x)


def total_sums(groups, orders, scale):
    parts = []
    for x, order in zip(groups, orders):
        x = core_sum(x)
        for axis in order:
            x = scatter_sum_by_permutes(x, axis)
        parts.append(x)
    lengths = [p.shape[0] for p in parts]
    rows = sum(lengths)
    padded = -(-rows // 64) * 64
    joined = jnp.concatenate(parts + [jnp.zeros((padded - rows, parts[0].shape[1]), jnp.float32)])
    joined = gather(scatter_sum(joined, "z") * scale, "z")
    out, start = [], 0
    for length, order in zip(lengths, orders):
        x = joined[start : start + length]
        start += length
        for axis in reversed(order):
            x = gather_by_permutes(x, axis)
        out.append(core_gather(x))
    return out


def body(stem_input, stem_preact, deep_cotangent, tissue_tiles, conv_weight, expand_weight):
    _, out_rows, out_cols, channels = stem_preact.shape
    _, all_rows, band, deep = deep_cotangent.shape
    devices = SIZES["x"] * SIZES["z"]
    preact = stem_preact[0]
    x = stem_input[0]
    tile_share = tissue_tiles.astype(jnp.float32) / TILES
    weighted = (deep_cotangent[0].astype(jnp.float32) * tile_share[:, None, None]).astype(jnp.bfloat16)
    weighted = weighted.reshape(all_rows * band, deep)
    hidden = lax.dot_general(
        weighted, expand_weight, (((1,), (1,)), ((), ())), preferred_element_type=jnp.float32
    ).astype(jnp.bfloat16)
    hidden = exchange(hidden.reshape(devices, out_rows * band, channels), SPACE)
    hidden = hidden.reshape(devices, out_rows, band, channels).transpose(1, 0, 2, 3)
    hidden = hidden.reshape(out_rows, out_cols, channels)
    grad = jnp.where(preact > 0, hidden, jnp.zeros_like(hidden))
    active = jnp.maximum(preact, jnp.zeros_like(preact))
    active = active.reshape(out_rows, devices, band, channels).transpose(1, 0, 2, 3)
    active = exchange(active.reshape(devices, out_rows * band, channels), SPACE)
    active = active.reshape(all_rows * band, channels)
    part_expand = lax.dot_general(
        active, weighted, (((0,), (0,)), ((), ())), preferred_element_type=jnp.float32
    )
    above = shifted(x[-1:], 1)
    below = shifted(grad[:1], -1)
    part_conv = taps(prepare(above, x), grad)
    grad_input = input_grad(grad, below, conv_weight)

    samples_all = stem_input.shape[0] * SIZES["y"] * SIZES["core"]
    scale = float(samples_all * all_rows * out_cols) ** (-0.5)
    columns = deep // channels
    expand_rows = jnp.concatenate(
        [part_expand[:, n * channels : (n + 1) * channels] for n in range(columns)]
    )
    first = part_conv[:6].reshape(6 * channels, channels)
    second = jnp.concatenate([part_conv[6:].reshape(3 * channels, channels), expand_rows])
    (first, second) = total_sums([first, second], [("y", "x"), ("x", "y")], scale)
    first, second = jnp.concatenate(first), jnp.concatenate(second)
    grad_conv = jnp.concatenate([first, second[: 3 * channels]]).reshape(3, 3, channels, channels)
    pieces = second[3 * channels :].reshape(columns, channels, channels)
    grad_expand = jnp.concatenate([pieces[n] for n in range(columns)], axis=1)
    return (grad_input[None], grad_conv, grad_expand)


def solution(mesh):
    fine = Mesh(
        mesh.devices.reshape(SIZES["x"], SIZES["z"], SIZES["y"], SIZES["core"]),
        ("x", "z", "y", "core"),
    )
    return jax.shard_map(
        body,
        mesh=fine,
        in_specs=(
            P(REP, SPACE, None, None),
            P(REP, SPACE, None, None),
            P(REP, None, SPACE, None),
            P(REP),
            P(),
            P(),
        ),
        out_specs=(P(REP, SPACE, None, None), P(), P()),
        check_vma=False,
    )
```

time: 438 us -> 158 us (0.36)
  the two profiles are of different devices: /device:TPU:2 before, /device:TPU:1 now
where the time goes in v1:
time: 158 us
  starting transfers between devices  76.7 us (49%)
  waiting for transfers between devices  28.2 us (18%)
  blocking collectives  21.1 us (13%)
  local copies, waits for them, and re-layouts  11.9 us (8%)
  other arithmetic  10.2 us (6%)
  matrix products  4.24 us (3%)
  Pallas kernels  3.45 us (2%)
  between operations  1.87 us (1%)
    ppermute x26, starting transfers between devices, rotated(): return lax.ppermute(x, axis, [(i, (i + by) % size) for i in range(size)])  37.9 us
    all_to_all x2, starting transfers between devices, exchange(): return lax.all_to_all(x, axis, split_axis=0, concat_axis=0, tiled=True)  22.4 us
    all_to_all x2, blocking collectives, exchange(): return lax.all_to_all(x, axis, split_axis=0, concat_axis=0, tiled=True)  21.1 us
    ppermute x2, waiting for transfers between devices, shifted(): return lax.ppermute(x, SPACE, pairs)  12.8 us
    ppermute x2, starting transfers between devices, core_gather(): got = lax.ppermute(x, 'core', [(0, 1), (1, 0)])  12.1 us
    ppermute x26, waiting for transfers between devices, rotated(): return lax.ppermute(x, axis, [(i, (i + by) % size) for i in range(size)])  12 us
    unnamed x24, local copies, waits for them, and re-layouts  5.43 us
    ppermute x2, starting transfers between devices, shifted(): return lax.ppermute(x, SPACE, pairs)  4.37 us
  transfers between devices with their start and end apart: 32, of which 13 were waited for; matrix products, arithmetic and copies ran while one was open for 10% of the time, Pallas kernels for 2%

profile of v1, /device:TPU:1, one launch (start us, length us, event | category | flops | bytes accessed | tf_op | source)
XLA Modules:
  0.0 157.7 jit_solution(7633833736262681859)
XLA Ops:
  1.7 2.4 %convolution_convert_fusion = bf16[512,256]{1,0:T(8,128)(2,1)} fusion(bf16[256,1024]{1,0:T(8,128)(2,1)S(1)} %copy-done, bf16[1,64,8,1024]{3,2,1,0:T(8,128)(2,1)} %param.8, f32[]{:T(128)} %bitcast.1), kind=kOutput, calls=%fused_computation.2 | convolution fusion | flops 270139392 | bytes 1835012 | tf_op jit(solution)/shard_map/dot_general | solution.py:223
  4.1 12.0 %all-to-all-start = ((bf16[32,16,256]{2,1,0:T(8,128)(2,1)}), bf16[32,16,256]{2,1,0:T(8,128)(2,1)}, u32[]{:S(2)}, u32[]{:S(2)}) async-start(bf16[32,16,256]{2,1,0:T(8,128)(2,1)} %bitcast.3), calls=%async_computation | async-start | bytes 524288 | tf_op jit(solution)/shard_map/all_to_all | solution.py:132
  16.1 3.1 %collective-permute-start.1 = (bf16[1,512,256]{2,1,0:T(8,128)(2,1)S(1)}, bf16[1,512,256]{2,1,0:T(8,128)(2,1)S(1)}, u32[]{:S(2)}, u32[]{:S(2)}) collective-permute-start(bf16[1,512,256]{2,1,0:T(8,128)(2,1)S(1)} %slice_bitcast_fusion), channel_id=1, source_target_pairs={{0,8},{8,16},{16,24},{24,32},{32,40},{40,48},{48,56},{56,64},{64,7... | collective-permute-start | bytes 786440 | tf_op jit(solution)/shard_map/ppermute | solution.py:26
  20.0 7.1 %collective-permute-done.1.above_ref = bf16[1,512,256]{2,1,0:T(8,128)(2,1)S(1)} collective-permute-done((bf16[1,512,256]{2,1,0:T(8,128)(2,1)S(1)}, bf16[1,512,256]{2,1,0:T(8,128)(2,1)S(1)}, u32[]{:S(2)}, u32[]{:S(2)}) %collective-permute-start.1) | collective-permute-done | bytes 262176 | tf_op jit(solution)/shard_map/ppermute | solution.py:26
  29.5 10.4 %all-to-all-start.1 = ((bf16[32,16,256]{2,1,0:T(8,128)(2,1)}), bf16[32,16,256]{2,1,0:T(8,128)(2,1)S(1)}, u32[]{:S(2)}, u32[]{:S(2)}) async-start(bf16[32,16,256]{2,1,0:T(8,128)(2,1)} %copy_bitcast_fusion), calls=%async_computation.1 | async-start | bytes 524288 | tf_op jit(solution)/shard_map/all_to_all | solution.py:132
  46.3 3.3 %all-to-all-done.1 = bf16[32,16,256]{2,1,0:T(8,128)(2,1)S(1)} async-done(((bf16[32,16,256]{2,1,0:T(8,128)(2,1)}), bf16[32,16,256]{2,1,0:T(8,128)(2,1)S(1)}, u32[]{:S(2)}, u32[]{:S(2)}) %all-to-all-start.1) | async-done | bytes 262176 | tf_op jit(solution)/shard_map/all_to_all | solution.py:132
  49.7 1.8 %fusion.4 = f32[256,1024]{1,0:T(8,128)S(1)} fusion(bf16[512,256]{1,0:T(8,128)(2,1)S(1)} %bitcast.151, bf16[1,64,8,1024]{3,2,1,0:T(8,128)(2,1)} %param.8, f32[]{:T(128)} %bitcast.1), kind=kOutput, calls=%fused_computation.8 | convolution fusion | flops 270008320 | bytes 2359300 | tf_op jit(solution)/shard_map/dot_general | solution.py:234
  53.8 3.6 %collective-permute-start.9 = (f32[896,256]{1,0:T(8,128)}, f32[896,256]{1,0:T(8,128)}, u32[]{:S(2)}, u32[]{:S(2)}) collective-permute-start(f32[896,256]{1,0:T(8,128)} %dynamic-slice_bitcast_fusion), channel_id=1, source_target_pairs={{0,1},{1,0},{2,3},{3,2},{4,5},{5,4},{6,7},{7,6},{8,9},{9,8},{10,11... | collective-permute-start | bytes 2752520 | tf_op jit(solution)/shard_map/ppermute | solution.py:151
  57.5 1.4 bitcast_add_fusion.1
  58.9 1.4 collective-permute-start.3
  60.3 2.6 %collective-permute-start.4 = (f32[192,256]{1,0:T(8,128)S(1)}, f32[192,256]{1,0:T(8,128)S(1)}, u32[]{:S(2)}, u32[]{:S(2)}) collective-permute-start(f32[192,256]{1,0:T(8,128)S(1)} %get-tuple-element.15), channel_id=1, source_target_pairs={{0,4},{2,6},{4,0},{6,2},{1,5},{3,7},{5,1},{7,3},{8,12},{10,14},{12... | collective-permute-start | bytes 589832 | tf_op jit(solution)/shard_map/ppermute | solution.py:151
  65.8 1.8 %collective-permute-start.11 = (f32[224,256]{1,0:T(8,128)S(1)}, f32[224,256]{1,0:T(8,128)S(1)}, u32[]{:S(2)}, u32[]{:S(2)}) collective-permute-start(f32[224,256]{1,0:T(8,128)S(1)} %get-tuple-element.12), channel_id=1, source_target_pairs={{0,128},{64,192},{128,0},{192,64},{1,129},{65,193},{129,1},{193,65... | collective-permute-start | bytes 688136 | tf_op jit(solution)/shard_map/ppermute | solution.py:151
  68.7 3.5 %collective-permute-done.4 = f32[192,256]{1,0:T(8,128)S(1)} collective-permute-done((f32[192,256]{1,0:T(8,128)S(1)}, f32[192,256]{1,0:T(8,128)S(1)}, u32[]{:S(2)}, u32[]{:S(2)}) %collective-permute-start.4) | collective-permute-done | bytes 196640 | tf_op jit(solution)/shard_map/ppermute | solution.py:151
  72.7 1.8 %collective-permute-start.7 = (f32[48,256]{1,0:T(8,128)S(1)}, f32[48,256]{1,0:T(8,128)S(1)}, u32[]{:S(2)}, u32[]{:S(2)}) collective-permute-start(f32[48,256]{1,0:T(8,128)S(1)} %get-tuple-element.21), channel_id=1, source_target_pairs={{0,128},{64,192},{128,0},{192,64},{1,129},{65,193},{129,1},{193,65... | collective-permute-start | bytes 147464 | tf_op jit(solution)/shard_map/ppermute | solution.py:151
  75.7 1.7 %collective-permute-done.11 = f32[224,256]{1,0:T(8,128)S(1)} collective-permute-done((f32[224,256]{1,0:T(8,128)S(1)}, f32[224,256]{1,0:T(8,128)S(1)}, u32[]{:S(2)}, u32[]{:S(2)}) %collective-permute-start.11) | collective-permute-done | bytes 229408 | tf_op jit(solution)/shard_map/ppermute | solution.py:151
  77.3 1.7 %collective-permute-done.12 = f32[224,256]{1,0:T(8,128)S(1)} collective-permute-done((f32[224,256]{1,0:T(8,128)S(1)}, f32[224,256]{1,0:T(8,128)S(1)}, u32[]{:S(2)}, u32[]{:S(2)}) %collective-permute-start.12) | collective-permute-done | bytes 229408 | tf_op jit(solution)/shard_map/ppermute | solution.py:151
  80.9 1.4 collective-permute-start.15
  84.9 10.8 %all_to_all.20 = f32[8,16,256]{2,1,0:T(8,128)S(1)} all-to-all(f32[8,16,256]{2,1,0:T(8,128)S(1)} %bitcast.167), channel_id=1, replica_groups=mesh['x'=4,'z'=8,'y'=4,'core'=2] {'z'}, dimensions={0} | all-to-all | bytes 262144 | tf_op jit(solution)/shard_map/all_to_all | solution.py:132
  95.8 10.3 %all_to_all.21 = f32[8,16,256]{2,1,0:T(8,128)S(1)} all-to-all(f32[8,16,256]{2,1,0:T(8,128)S(1)} %broadcast_in_dim.71), channel_id=1, replica_groups=mesh['x'=4,'z'=8,'y'=4,'core'=2] {'z'}, dimensions={0} | all-to-all | bytes 262144 | tf_op jit(solution)/shard_map/all_to_all | solution.py:132
  107.1 2.5 %collective-permute-start.24 = (f32[56,256]{1,0:T(8,128)S(1)}, f32[56,256]{1,0:T(8,128)S(1)}, u32[]{:S(2)}, u32[]{:S(2)}) collective-permute-start(f32[56,256]{1,0:T(8,128)S(1)} %slice.88), channel_id=1, source_target_pairs={{0,4},{2,6},{4,0},{6,2},{1,5},{3,7},{5,1},{7,3},{8,12},{10,14},{12... | collective-permute-start | bytes 172040 | tf_op jit(solution)/shard_map/ppermute | solution.py:151
  109.6 1.8 %collective-permute-start.16 = (f32[48,256]{1,0:T(8,128)S(1)}, f32[48,256]{1,0:T(8,128)S(1)}, u32[]{:S(2)}, u32[]{:S(2)}) collective-permute-start(f32[48,256]{1,0:T(8,128)S(1)} %bitcast.168), channel_id=1, source_target_pairs={{0,64},{64,128},{128,192},{192,0},{1,65},{65,129},{129,193},{193,1... | collective-permute-start | bytes 147464 | tf_op jit(solution)/shard_map/ppermute | solution.py:151
  111.4 3.5 %collective-permute-start.17 = (f32[48,256]{1,0:T(8,128)S(1)}, f32[48,256]{1,0:T(8,128)S(1)}, u32[]{:S(2)}, u32[]{:S(2)}) collective-permute-start(f32[48,256]{1,0:T(8,128)S(1)} %bitcast.169), channel_id=1, source_target_pairs={{0,128},{64,192},{128,0},{192,64},{1,129},{65,193},{129,1},{193,65... | collective-permute-start | bytes 147464 | tf_op jit(solution)/shard_map/ppermute | solution.py:151
  115.2 1.5 collective-permute-start.18
  116.9 1.5 collective-permute-done.18
  120.2 2.0 %collective-permute-start.21 = (f32[192,256]{1,0:T(8,128)S(1)}, f32[192,256]{1,0:T(8,128)S(1)}, u32[]{:S(2)}, u32[]{:S(2)}) collective-permute-start(f32[192,256]{1,0:T(8,128)S(1)} %bitcast.164), channel_id=1, source_target_pairs={{0,6},{2,0},{4,2},{6,4},{1,7},{3,1},{5,3},{7,5},{8,14},{10,8},{12,... | collective-permute-start | bytes 589832 | tf_op jit(solution)/shard_map/ppermute | solution.py:151
  122.4 3.5 %collective-permute-start.27 = (f32[224,256]{1,0:T(8,128)S(1)}, f32[224,256]{1,0:T(8,128)S(1)}, u32[]{:S(2)}, u32[]{:S(2)}) collective-permute-start(f32[224,256]{1,0:T(8,128)S(1)} %bitcast.154), channel_id=1, source_target_pairs={{0,128},{64,192},{128,0},{192,64},{1,129},{65,193},{129,1},{193,65... | collective-permute-start | bytes 688136 | tf_op jit(solution)/shard_map/ppermute | solution.py:151
  128.9 7.6 %collective-permute-start.22 = (f32[768,256]{1,0:T(8,128)S(1)}, f32[768,256]{1,0:T(8,128)}, u32[]{:S(2)}, u32[]{:S(2)}) collective-permute-start(f32[768,256]{1,0:T(8,128)S(1)} %bitcast.149), channel_id=1, source_target_pairs={{0,1},{1,0},{2,3},{3,2},{4,5},{5,4},{6,7},{7,6},{8,9},{9,8},{10,11... | collective-permute-start | bytes 2359304 | tf_op jit(solution)/shard_map/ppermute | solution.py:188
  138.7 4.4 %collective-permute-start.29 = (f32[896,256]{1,0:T(8,128)}, f32[896,256]{1,0:T(8,128)}, u32[]{:S(2)}, u32[]{:S(2)}) collective-permute-start(f32[896,256]{1,0:T(8,128)} %bitcast.63), channel_id=1, source_target_pairs={{0,1},{1,0},{2,3},{3,2},{4,5},{5,4},{6,7},{7,6},{8,9},{9,8},{10,11... | collective-permute-start | bytes 2752520 | tf_op jit(solution)/shard_map/ppermute | solution.py:188
  144.4 5.7 %collective-permute-done.below_ref = bf16[1,256,256]{2,1,0:T(8,128)(2,1)S(1)} collective-permute-done((bf16[1,256,256]{2,1,0:T(8,128)(2,1)S(1)}, bf16[1,256,256]{2,1,0:T(8,128)(2,1)S(1)}, u32[]{:S(2)}, u32[]{:S(2)}) %collective-permute-start) | collective-permute-done | bytes 131104 | tf_op jit(solution)/shard_map/ppermute | solution.py:26
  150.1 1.9 %input_grad.1 = bf16[4,512,256]{2,1,0:T(8,128)(2,1)} custom-call(bf16[2,256,256]{2,1,0:T(8,128)(2,1)S(1)} %bitcast_select_fusion.grad_ref, bf16[1,256,256]{2,1,0:T(8,128)(2,1)S(1)} %collective-permute-done.below_ref, bf16[3,3,256,256]{3,2,1,0:T(8,128)(2,1)S(1)} %copy-done.3), custom_call_target="tpu_custom_call" | custom-call | flops 604000000 | bytes 3000000 | tf_op jit(solution)/shard_map/input_grad/pallas_call | solution.py:119
  153.3 1.6 %broadcast_select_fusion = (f32[896,256]{1,0:T(8,128)S(1)}, f32[896,256]{1,0:T(8,128)S(1)}) fusion(f32[896,256]{1,0:T(8,128)} %collective-permute-done.29, pred[]{:T(512)S(6)} %eq.4, f32[4,224,256]{2,1,0:T(8,128)} %bitcast_dynamic-update-slice_fusion), kind=kLoop, calls=%fused_computation.14 | loop fusion | flops 458752 | bytes 3670017 | tf_op jit(solution)/shard_map/jit(_where)/select_n | solution.py:189
  156.1 1.6 pad_maximum_fusion
  (117 shorter events, 34.6 us)
Async XLA Ops:
  4.1 25.4 %all-to-all-start = ((bf16[32,16,256]{2,1,0:T(8,128)(2,1)}), bf16[32,16,256]{2,1,0:T(8,128)(2,1)}, u32[]{:S(2)}, u32[]{:S(2)}) async-start(bf16[32,16,256]{2,1,0:T(8,128)(2,1)} %bitcast.3), calls=%async_computation | async-start | bytes 524288 | tf_op jit(solution)/shard_map/all_to_all | solution.py:132
  16.1 11.0 %collective-permute-start.1 = (bf16[1,512,256]{2,1,0:T(8,128)(2,1)S(1)}, bf16[1,512,256]{2,1,0:T(8,128)(2,1)S(1)}, u32[]{:S(2)}, u32[]{:S(2)}) collective-permute-start(bf16[1,512,256]{2,1,0:T(8,128)(2,1)S(1)} %slice_bitcast_fusion), channel_id=1, source_target_pairs={{0,8},{8,16},{16,24},{24,32},{32,40},{40,48},{48,56},{56,64},{64,7... | collective-permute-start | bytes 786440 | tf_op jit(solution)/shard_map/ppermute | solution.py:26
  29.5 20.1 %all-to-all-start.1 = ((bf16[32,16,256]{2,1,0:T(8,128)(2,1)}), bf16[32,16,256]{2,1,0:T(8,128)(2,1)S(1)}, u32[]{:S(2)}, u32[]{:S(2)}) async-start(bf16[32,16,256]{2,1,0:T(8,128)(2,1)} %copy_bitcast_fusion), calls=%async_computation.1 | async-start | bytes 524288 | tf_op jit(solution)/shard_map/all_to_all | solution.py:132
  44.2 13.3 %collective-permute-start.2 = (f32[768,256]{1,0:T(8,128)}, f32[768,256]{1,0:T(8,128)}, u32[]{:S(2)}, u32[]{:S(2)}) collective-permute-start(f32[768,256]{1,0:T(8,128)} %dynamic-slice_bitcast_fusion.1), channel_id=1, source_target_pairs={{0,1},{1,0},{2,3},{3,2},{4,5},{5,4},{6,7},{7,6},{8,9},{9,8},{10,11... | collective-permute-start | bytes 2359304 | tf_op jit(solution)/shard_map/ppermute | solution.py:151
  53.8 10.2 %collective-permute-start.9 = (f32[896,256]{1,0:T(8,128)}, f32[896,256]{1,0:T(8,128)}, u32[]{:S(2)}, u32[]{:S(2)}) collective-permute-start(f32[896,256]{1,0:T(8,128)} %dynamic-slice_bitcast_fusion), channel_id=1, source_target_pairs={{0,1},{1,0},{2,3},{3,2},{4,5},{5,4},{6,7},{7,6},{8,9},{9,8},{10,11... | collective-permute-start | bytes 2752520 | tf_op jit(solution)/shard_map/ppermute | solution.py:151
  58.9 8.6 %collective-permute-start.3 = (f32[192,256]{1,0:T(8,128)S(1)}, f32[192,256]{1,0:T(8,128)S(1)}, u32[]{:S(2)}, u32[]{:S(2)}) collective-permute-start(f32[192,256]{1,0:T(8,128)S(1)} %get-tuple-element.13), channel_id=1, source_target_pairs={{0,2},{2,4},{4,6},{6,0},{1,3},{3,5},{5,7},{7,1},{8,10},{10,12},{12... | collective-permute-start | bytes 589832 | tf_op jit(solution)/shard_map/ppermute | solution.py:151
  60.3 11.9 %collective-permute-start.4 = (f32[192,256]{1,0:T(8,128)S(1)}, f32[192,256]{1,0:T(8,128)S(1)}, u32[]{:S(2)}, u32[]{:S(2)}) collective-permute-start(f32[192,256]{1,0:T(8,128)S(1)} %get-tuple-element.15), channel_id=1, source_target_pairs={{0,4},{2,6},{4,0},{6,2},{1,5},{3,7},{5,1},{7,3},{8,12},{10,14},{12... | collective-permute-start | bytes 589832 | tf_op jit(solution)/shard_map/ppermute | solution.py:151
  62.9 9.3 %collective-permute-start.5 = (f32[192,256]{1,0:T(8,128)S(1)}, f32[192,256]{1,0:T(8,128)S(1)}, u32[]{:S(2)}, u32[]{:S(2)}) collective-permute-start(f32[192,256]{1,0:T(8,128)S(1)} %get-tuple-element.14), channel_id=1, source_target_pairs={{0,6},{2,0},{4,2},{6,4},{1,7},{3,1},{5,3},{7,5},{8,14},{10,8},{12,... | collective-permute-start | bytes 589832 | tf_op jit(solution)/shard_map/ppermute | solution.py:151
  65.4 9.1 %collective-permute-start.10 = (f32[224,256]{1,0:T(8,128)S(1)}, f32[224,256]{1,0:T(8,128)S(1)}, u32[]{:S(2)}, u32[]{:S(2)}) collective-permute-start(f32[224,256]{1,0:T(8,128)S(1)} %get-tuple-element.10), channel_id=1, source_target_pairs={{0,64},{64,128},{128,192},{192,0},{1,65},{65,129},{129,193},{193,1... | collective-permute-start | bytes 688136 | tf_op jit(solution)/shard_map/ppermute | solution.py:151
  65.8 11.5 %collective-permute-start.11 = (f32[224,256]{1,0:T(8,128)S(1)}, f32[224,256]{1,0:T(8,128)S(1)}, u32[]{:S(2)}, u32[]{:S(2)}) collective-permute-start(f32[224,256]{1,0:T(8,128)S(1)} %get-tuple-element.12), channel_id=1, source_target_pairs={{0,128},{64,192},{128,0},{192,64},{1,129},{65,193},{129,1},{193,65... | collective-permute-start | bytes 688136 | tf_op jit(solution)/shard_map/ppermute | solution.py:151
  67.6 11.5 %collective-permute-start.12 = (f32[224,256]{1,0:T(8,128)S(1)}, f32[224,256]{1,0:T(8,128)S(1)}, u32[]{:S(2)}, u32[]{:S(2)}) collective-permute-start(f32[224,256]{1,0:T(8,128)S(1)} %get-tuple-element.11), channel_id=1, source_target_pairs={{0,192},{64,0},{128,64},{192,128},{1,193},{65,1},{129,65},{193,129... | collective-permute-start | bytes 688136 | tf_op jit(solution)/shard_map/ppermute | solution.py:151
  72.3 8.6 %collective-permute-start.6 = (f32[48,256]{1,0:T(8,128)S(1)}, f32[48,256]{1,0:T(8,128)S(1)}, u32[]{:S(2)}, u32[]{:S(2)}) collective-permute-start(f32[48,256]{1,0:T(8,128)S(1)} %get-tuple-element.19), channel_id=1, source_target_pairs={{0,64},{64,128},{128,192},{192,0},{1,65},{65,129},{129,193},{193,1... | collective-permute-start | bytes 147464 | tf_op jit(solution)/shard_map/ppermute | solution.py:151
  72.7 9.6 %collective-permute-start.7 = (f32[48,256]{1,0:T(8,128)S(1)}, f32[48,256]{1,0:T(8,128)S(1)}, u32[]{:S(2)}, u32[]{:S(2)}) collective-permute-start(f32[48,256]{1,0:T(8,128)S(1)} %get-tuple-element.21), channel_id=1, source_target_pairs={{0,128},{64,192},{128,0},{192,64},{1,129},{65,193},{129,1},{193,65... | collective-permute-start | bytes 147464 | tf_op jit(solution)/shard_map/ppermute | solution.py:151
  74.5 7.8 %collective-permute-start.8 = (f32[48,256]{1,0:T(8,128)S(1)}, f32[48,256]{1,0:T(8,128)S(1)}, u32[]{:S(2)}, u32[]{:S(2)}) collective-permute-start(f32[48,256]{1,0:T(8,128)S(1)} %get-tuple-element.20), channel_id=1, source_target_pairs={{0,192},{64,0},{128,64},{192,128},{1,193},{65,1},{129,65},{193,129... | collective-permute-start | bytes 147464 | tf_op jit(solution)/shard_map/ppermute | solution.py:151
  79.1 4.5 %collective-permute-start.13 = (f32[56,256]{1,0:T(8,128)S(1)}, f32[56,256]{1,0:T(8,128)S(1)}, u32[]{:S(2)}, u32[]{:S(2)}) collective-permute-start(f32[56,256]{1,0:T(8,128)S(1)} %get-tuple-element.16), channel_id=1, source_target_pairs={{0,2},{2,4},{4,6},{6,0},{1,3},{3,5},{5,7},{7,1},{8,10},{10,12},{12... | collective-permute-start | bytes 172040 | tf_op jit(solution)/shard_map/ppermute | solution.py:151
  79.8 5.0 %collective-permute-start.14 = (f32[56,256]{1,0:T(8,128)S(1)}, f32[56,256]{1,0:T(8,128)S(1)}, u32[]{:S(2)}, u32[]{:S(2)}) collective-permute-start(f32[56,256]{1,0:T(8,128)S(1)} %get-tuple-element.18), channel_id=1, source_target_pairs={{0,4},{2,6},{4,0},{6,2},{1,5},{3,7},{5,1},{7,3},{8,12},{10,14},{12... | collective-permute-start | bytes 172040 | tf_op jit(solution)/shard_map/ppermute | solution.py:151
  80.9 3.9 %collective-permute-start.15 = (f32[56,256]{1,0:T(8,128)S(1)}, f32[56,256]{1,0:T(8,128)S(1)}, u32[]{:S(2)}, u32[]{:S(2)}) collective-permute-start(f32[56,256]{1,0:T(8,128)S(1)} %get-tuple-element.17), channel_id=1, source_target_pairs={{0,6},{2,0},{4,2},{6,4},{1,7},{3,1},{5,3},{7,5},{8,14},{10,8},{12,... | collective-permute-start | bytes 172040 | tf_op jit(solution)/shard_map/ppermute | solution.py:151
  106.1 14.1 %collective-permute-start.23 = (f32[56,256]{1,0:T(8,128)S(1)}, f32[56,256]{1,0:T(8,128)S(1)}, u32[]{:S(2)}, u32[]{:S(2)}) collective-permute-start(f32[56,256]{1,0:T(8,128)S(1)} %slice.88), channel_id=1, source_target_pairs={{0,2},{2,4},{4,6},{6,0},{1,3},{3,5},{5,7},{7,1},{8,10},{10,12},{12... | collective-permute-start | bytes 172040 | tf_op jit(solution)/shard_map/ppermute | solution.py:151
  107.1 15.2 %collective-permute-start.24 = (f32[56,256]{1,0:T(8,128)S(1)}, f32[56,256]{1,0:T(8,128)S(1)}, u32[]{:S(2)}, u32[]{:S(2)}) collective-permute-start(f32[56,256]{1,0:T(8,128)S(1)} %slice.88), channel_id=1, source_target_pairs={{0,4},{2,6},{4,0},{6,2},{1,5},{3,7},{5,1},{7,3},{8,12},{10,14},{12... | collective-permute-start | bytes 172040 | tf_op jit(solution)/shard_map/ppermute | solution.py:151
  109.6 12.6 %collective-permute-start.25 = (f32[56,256]{1,0:T(8,128)S(1)}, f32[56,256]{1,0:T(8,128)S(1)}, u32[]{:S(2)}, u32[]{:S(2)}) collective-permute-start(f32[56,256]{1,0:T(8,128)S(1)} %slice.88), channel_id=1, source_target_pairs={{0,6},{2,0},{4,2},{6,4},{1,7},{3,1},{5,3},{7,5},{8,14},{10,8},{12,... | collective-permute-start | bytes 172040 | tf_op jit(solution)/shard_map/ppermute | solution.py:151
  109.6 5.6 %collective-permute-start.16 = (f32[48,256]{1,0:T(8,128)S(1)}, f32[48,256]{1,0:T(8,128)S(1)}, u32[]{:S(2)}, u32[]{:S(2)}) collective-permute-start(f32[48,256]{1,0:T(8,128)S(1)} %bitcast.168), channel_id=1, source_target_pairs={{0,64},{64,128},{128,192},{192,0},{1,65},{65,129},{129,193},{193,1... | collective-permute-start | bytes 147464 | tf_op jit(solution)/shard_map/ppermute | solution.py:151
  111.4 5.5 %collective-permute-start.17 = (f32[48,256]{1,0:T(8,128)S(1)}, f32[48,256]{1,0:T(8,128)S(1)}, u32[]{:S(2)}, u32[]{:S(2)}) collective-permute-start(f32[48,256]{1,0:T(8,128)S(1)} %bitcast.169), channel_id=1, source_target_pairs={{0,128},{64,192},{128,0},{192,64},{1,129},{65,193},{129,1},{193,65... | collective-permute-start | bytes 147464 | tf_op jit(solution)/shard_map/ppermute | solution.py:151
  115.2 3.2 %collective-permute-start.18 = (f32[48,256]{1,0:T(8,128)S(1)}, f32[48,256]{1,0:T(8,128)S(1)}, u32[]{:S(2)}, u32[]{:S(2)}) collective-permute-start(f32[48,256]{1,0:T(8,128)S(1)} %bitcast.171), channel_id=1, source_target_pairs={{0,192},{64,0},{128,64},{192,128},{1,193},{65,1},{129,65},{193,129... | collective-permute-start | bytes 147464 | tf_op jit(solution)/shard_map/ppermute | solution.py:151
  118.5 9.2 %collective-permute-start.19 = (f32[192,256]{1,0:T(8,128)S(1)}, f32[192,256]{1,0:T(8,128)S(1)}, u32[]{:S(2)}, u32[]{:S(2)}) collective-permute-start(f32[192,256]{1,0:T(8,128)S(1)} %bitcast.161), channel_id=1, source_target_pairs={{0,2},{2,4},{4,6},{6,0},{1,3},{3,5},{5,7},{7,1},{8,10},{10,12},{12... | collective-permute-start | bytes 589832 | tf_op jit(solution)/shard_map/ppermute | solution.py:151
  119.6 9.3 %collective-permute-start.20 = (f32[192,256]{1,0:T(8,128)S(1)}, f32[192,256]{1,0:T(8,128)S(1)}, u32[]{:S(2)}, u32[]{:S(2)}) collective-permute-start(f32[192,256]{1,0:T(8,128)S(1)} %bitcast.162), channel_id=1, source_target_pairs={{0,4},{2,6},{4,0},{6,2},{1,5},{3,7},{5,1},{7,3},{8,12},{10,14},{12... | collective-permute-start | bytes 589832 | tf_op jit(solution)/shard_map/ppermute | solution.py:151
  120.2 8.7 %collective-permute-start.21 = (f32[192,256]{1,0:T(8,128)S(1)}, f32[192,256]{1,0:T(8,128)S(1)}, u32[]{:S(2)}, u32[]{:S(2)}) collective-permute-start(f32[192,256]{1,0:T(8,128)S(1)} %bitcast.164), channel_id=1, source_target_pairs={{0,6},{2,0},{4,2},{6,4},{1,7},{3,1},{5,3},{7,5},{8,14},{10,8},{12,... | collective-permute-start | bytes 589832 | tf_op jit(solution)/shard_map/ppermute | solution.py:151
  122.3 14.3 %collective-permute-start.26 = (f32[224,256]{1,0:T(8,128)S(1)}, f32[224,256]{1,0:T(8,128)S(1)}, u32[]{:S(2)}, u32[]{:S(2)}) collective-permute-start(f32[224,256]{1,0:T(8,128)S(1)} %bitcast.153), channel_id=1, source_target_pairs={{0,64},{64,128},{128,192},{192,0},{1,65},{65,129},{129,193},{193,1... | collective-permute-start | bytes 688136 | tf_op jit(solution)/shard_map/ppermute | solution.py:151
  122.4 14.9 %collective-permute-start.27 = (f32[224,256]{1,0:T(8,128)S(1)}, f32[224,256]{1,0:T(8,128)S(1)}, u32[]{:S(2)}, u32[]{:S(2)}) collective-permute-start(f32[224,256]{1,0:T(8,128)S(1)} %bitcast.154), channel_id=1, source_target_pairs={{0,128},{64,192},{128,0},{192,64},{1,129},{65,193},{129,1},{193,65... | collective-permute-start | bytes 688136 | tf_op jit(solution)/shard_map/ppermute | solution.py:151
  127.6 10.3 %collective-permute-start.28 = (f32[224,256]{1,0:T(8,128)S(1)}, f32[224,256]{1,0:T(8,128)S(1)}, u32[]{:S(2)}, u32[]{:S(2)}) collective-permute-start(f32[224,256]{1,0:T(8,128)S(1)} %bitcast.156), channel_id=1, source_target_pairs={{0,192},{64,0},{128,64},{192,128},{1,193},{65,1},{129,65},{193,129... | collective-permute-start | bytes 688136 | tf_op jit(solution)/shard_map/ppermute | solution.py:151
  128.9 23.1 %collective-permute-start.22 = (f32[768,256]{1,0:T(8,128)S(1)}, f32[768,256]{1,0:T(8,128)}, u32[]{:S(2)}, u32[]{:S(2)}) collective-permute-start(f32[768,256]{1,0:T(8,128)S(1)} %bitcast.149), channel_id=1, source_target_pairs={{0,1},{1,0},{2,3},{3,2},{4,5},{5,4},{6,7},{7,6},{8,9},{9,8},{10,11... | collective-permute-start | bytes 2359304 | tf_op jit(solution)/shard_map/ppermute | solution.py:188
  138.7 14.6 %collective-permute-start.29 = (f32[896,256]{1,0:T(8,128)}, f32[896,256]{1,0:T(8,128)}, u32[]{:S(2)}, u32[]{:S(2)}) collective-permute-start(f32[896,256]{1,0:T(8,128)} %bitcast.63), channel_id=1, source_target_pairs={{0,1},{1,0},{2,3},{3,2},{4,5},{5,4},{6,7},{7,6},{8,9},{9,8},{10,11... | collective-permute-start | bytes 2752520 | tf_op jit(solution)/shard_map/ppermute | solution.py:188
  143.1 7.0 %collective-permute-start = (bf16[1,256,256]{2,1,0:T(8,128)(2,1)S(1)}, bf16[1,256,256]{2,1,0:T(8,128)(2,1)S(1)}, u32[]{:S(2)}, u32[]{:S(2)}) collective-permute-start(bf16[1,256,256]{2,1,0:T(8,128)(2,1)S(1)} %slice.80), channel_id=1, source_target_pairs={{8,0},{16,8},{24,16},{32,24},{40,32},{48,40},{56,48},{64,56},{72,6... | collective-permute-start | bytes 393224 | tf_op jit(solution)/shard_map/ppermute | solution.py:26
  (11 other events, 73.1 us)

commit v2 on v1

v2 whole, which is shorter than its diff:
```python
import functools

import jax
import jax.numpy as jnp
from jax import lax
from jax.experimental import pallas as pl
from jax.experimental.pallas import tpu as pltpu
from jax.sharding import Mesh
from jax.sharding import PartitionSpec as P

TILES = 64
LANES = 128
SIZES = {"x": 4, "z": 8, "y": 4, "core": 2}
SPACE = ("x", "z")
REP = ("y", "core")
VMEM_BYTES = 48 * 1024 * 1024


def whole(*_):
    return pl.BlockSpec(memory_space=pltpu.VMEM)


def scalars():
    return pl.BlockSpec(memory_space=pltpu.SMEM)


def params():
    return pltpu.CompilerParams(vmem_limit_bytes=VMEM_BYTES)


def shifted(x, by):
    length = SIZES["x"] * SIZES["z"]
    pairs = [(i, i + by) for i in range(length) if 0 <= i + by < length]
    return lax.ppermute(x, SPACE, pairs)


def prepare_kernel(share_ref, x_ref, cotangent_ref, out_ref, weighted_ref, wide):
    half = out_ref.shape[2]
    first = lax.broadcasted_iota(jnp.int32, (LANES, half), 1) == 0
    for row in range(x_ref.shape[0]):
        for part in range(x_ref.shape[2] // LANES):
            lanes = slice(part * LANES, (part + 1) * LANES)
            wide[...] = x_ref[row, :, lanes].astype(jnp.float32)
            even = wide[pl.ds(0, half, stride=2), :].T
            odd = wide[pl.ds(1, half, stride=2), :].T
            late = jnp.where(first, 0.0, pltpu.roll(odd, 1, 1))
            out_ref[3 * row, lanes, :] = late.astype(jnp.bfloat16)
            out_ref[3 * row + 1, lanes, :] = even.astype(jnp.bfloat16)
            out_ref[3 * row + 2, lanes, :] = odd.astype(jnp.bfloat16)
    weighted_ref[...] = (cotangent_ref[...].astype(jnp.float32) * share_ref[0]).astype(jnp.bfloat16)


def prepare(share, x, cotangent):
    rows, cols, channels = x.shape
    return pl.pallas_call(
        prepare_kernel,
        out_shape=(
            jax.ShapeDtypeStruct((3 * rows, channels, cols // 2), jnp.bfloat16),
            jax.ShapeDtypeStruct(cotangent.shape, jnp.bfloat16),
        ),
        in_specs=[scalars(), whole(), whole()],
        out_specs=(whole(), whole()),
        scratch_shapes=[pltpu.VMEM((cols, LANES), jnp.float32)],
        compiler_params=params(),
        cost_estimate=pl.CostEstimate(flops=10**7, bytes_accessed=5 * 10**6, transcendentals=0),
        name="prepare",
    )(share, x, cotangent)


def half_taps(blocks_ref, grads, row_tap, col_tap, start):
    total = None
    for i, grad in enumerate(grads):
        row = 2 * i + row_tap - 1
        if 0 <= row < blocks_ref.shape[0] // 3:
            term = jnp.dot(
                blocks_ref[3 * row + col_tap, pl.ds(start, LANES), :],
                grad,
                preferred_element_type=jnp.float32,
            )
            total = term if total is None else total + term
    return total


def inner_kernel(core_ref, blocks_ref, grad_ref, own_ref, other_ref):
    grads = [grad_ref[0], grad_ref[1]]
    for out_ref, owner in ((other_ref, 1 - core_ref[0]), (own_ref, core_ref[0])):
        start = pl.multiple_of(owner * LANES, LANES)
        for row_tap in (1, 2):
            for col_tap in range(3):
                at = (3 * (row_tap - 1) + col_tap) * LANES
                out_ref[at : at + LANES, :] = half_taps(blocks_ref, grads, row_tap, col_tap, start)


def outer_kernel(core_ref, blocks_ref, grad_ref, below_ref, active_ref, weighted_ref, own_ref, other_ref, turned):
    channels = grad_ref.shape[2]
    grads = [grad_ref[0], grad_ref[1], below_ref[0]]
    turned[...] = active_ref[...].T
    for out_ref, owner in ((other_ref, 1 - core_ref[0]), (own_ref, core_ref[0])):
        start = pl.multiple_of(owner * LANES, LANES)
        for col_tap in range(3):
            at = col_tap * LANES
            out_ref[at : at + LANES, :] = half_taps(blocks_ref, grads, 0, col_tap, start)
        for n in range(weighted_ref.shape[1] // channels):
            at = (3 + n) * LANES
            out_ref[at : at + LANES, :] = jnp.dot(
                turned[pl.ds(start, LANES), :],
                weighted_ref[:, n * channels : (n + 1) * channels],
                preferred_element_type=jnp.float32,
            )


def halves(kernel, rows, core, *arrays, scratch=()):
    shape = jax.ShapeDtypeStruct((rows, 2 * LANES), jnp.float32)
    return pl.pallas_call(
        kernel,
        out_shape=(shape, shape),
        in_specs=[scalars()] + [whole()] * len(arrays),
        out_specs=(whole(), whole()),
        scratch_shapes=scratch,
        compiler_params=params(),
        cost_estimate=pl.CostEstimate(flops=400 * 10**6, bytes_accessed=4 * 10**6, transcendentals=0),
        name="halves",
    )(core, *arrays)


def input_kernel(grad_ref, below_ref, weight_ref, out_ref, wide):
    half = grad_ref.shape[1]
    last = lax.broadcasted_iota(jnp.int32, grad_ref.shape[1:], 0) == half - 1

    def early(g):
        moved = pltpu.roll(g.astype(jnp.float32), half - 1, 0)
        return jnp.where(last, 0.0, moved).astype(jnp.bfloat16)

    grads = [grad_ref[0], grad_ref[1], below_ref[0]]
    moved = [early(g) for g in grads]

    def times(g, row_tap, col_tap):
        return lax.dot_general(
            g,
            weight_ref[row_tap, col_tap],
            (((1,), (1,)), ((), ())),
            preferred_element_type=jnp.float32,
        )

    for row in range(4):
        i = row // 2
        terms = [(i, 1)] if row % 2 == 0 else [(i, 2), (i + 1, 0)]
        even = sum(times(grads[n], p, 1) for n, p in terms)
        odd = sum(times(grads[n], p, 2) + times(moved[n], p, 0) for n, p in terms)
        for part in range(even.shape[1] // LANES):
            lanes = slice(part * LANES, (part + 1) * LANES)
            wide[pl.ds(0, half, stride=2), :] = even[:, lanes]
            wide[pl.ds(1, half, stride=2), :] = odd[:, lanes]
            out_ref[row, :, lanes] = wide[...].astype(jnp.bfloat16)


def input_grad(grad, below, weight):
    rows, half, channels = grad.shape
    return pl.pallas_call(
        input_kernel,
        out_shape=jax.ShapeDtypeStruct((2 * rows, 2 * half, weight.shape[2]), jnp.bfloat16),
        in_specs=[whole()] * 3,
        out_specs=whole(),
        scratch_shapes=[pltpu.VMEM((2 * half, LANES), jnp.float32)],
        compiler_params=params(),
        cost_estimate=pl.CostEstimate(flops=604 * 10**6, bytes_accessed=3 * 10**6, transcendentals=0),
        name="input_grad",
    )(grad, below, weight)


def exchange(x, axis):
    return lax.all_to_all(x, axis, split_axis=0, concat_axis=0, tiled=True)


def place(axis, by=0):
    return (lax.axis_index(axis).astype(jnp.uint32) + jnp.uint32(by % SIZES[axis])) & jnp.uint32(SIZES[axis] - 1)


def pick(parts, index):
    zero = jnp.uint32(0)
    return lax.dynamic_slice(parts, (index, zero, zero), (1,) + parts.shape[1:])[0]


def put(parts, piece, index):
    zero = jnp.uint32(0)
    return lax.dynamic_update_slice(parts, piece[None], (index, zero, zero))


def rotated(x, axis, by):
    size = SIZES[axis]
    return lax.ppermute(x, axis, [(i, (i + by) % size) for i in range(size)])


def scatter_sum(x, axis):
    size = SIZES[axis]
    parts = x.reshape(size, x.shape[0] // size, x.shape[1])
    arrived = [rotated(pick(parts, place(axis, by)), axis, by) for by in range(1, size)]
    return sum(arrived, pick(parts, place(axis)))


def gather_pieces(x, axis):
    return [x] + [rotated(x, axis, by) for by in range(1, SIZES[axis])]


def gather(x, axis):
    out = jnp.zeros((SIZES[axis],) + x.shape, x.dtype)
    for by, piece in enumerate(gather_pieces(x, axis)):
        out = put(out, piece, place(axis, -by))
    return out.reshape(-1, x.shape[1])


def swapped(x, axis, bit):
    return lax.ppermute(x, axis, [(i, i ^ bit) for i in range(SIZES[axis])])


def sum_along_z(pair, scale):
    rows = max(p.shape[0] for p in pair)
    both = jnp.stack([jnp.pad(p, ((0, rows - p.shape[0]), (0, 0))) for p in pair])
    bit = place("z") & jnp.uint32(1)
    part = pick(both, bit) + swapped(pick(both, jnp.uint32(1) - bit), "z", 1)
    part = part + swapped(part, "z", 2)
    part = (part + swapped(part, "z", 4)) * scale
    got = swapped(part, "z", 1)
    even = bit == 0
    out = (jnp.where(even, part, got), jnp.where(even, got, part))
    return [o[: p.shape[0]] for o, p in zip(out, pair)]


def assemble_kernel(where_ref, *refs):
    groups, (conv_ref, expand_ref), scratch = (refs[:8], refs[8:16]), refs[16:18], refs[18:]
    channels = conv_ref.shape[2]
    core = where_ref[0]
    for n, (pieces, whole_ref) in enumerate(zip(groups, scratch)):
        for by in range(4):
            rows = pieces[by].shape[0]
            at = pl.multiple_of(((where_ref[1 + n] + 4 - by) & 3) * rows, 8)
            whole_ref[core, pl.ds(at, rows), :] = pieces[by][...]
            whole_ref[1 - core, pl.ds(at, rows), :] = pieces[4 + by][...]
    for half in range(2):
        lanes = slice(half * LANES, (half + 1) * LANES)
        for tap in range(6):
            conv_ref[3 + tap, lanes, :] = scratch[0][half, tap * LANES : (tap + 1) * LANES, :]
        for tap in range(3):
            conv_ref[tap, lanes, :] = scratch[1][half, tap * LANES : (tap + 1) * LANES, :]
        for n in range(expand_ref.shape[1] // channels):
            at = (3 + n) * LANES
            expand_ref[lanes, n * channels : (n + 1) * channels] = scratch[1][half, at : at + LANES, :]


def assemble(where, groups, channels, deep):
    refs = [piece for group in groups for piece in group]
    return pl.pallas_call(
        assemble_kernel,
        out_shape=(
            jax.ShapeDtypeStruct((9, channels, channels), jnp.float32),
            jax.ShapeDtypeStruct((channels, deep), jnp.float32),
        ),
        in_specs=[scalars()] + [whole()] * len(refs),
        out_specs=(whole(), whole()),
        scratch_shapes=[pltpu.VMEM((2, 4 * group[0].shape[0], channels), jnp.float32) for group in groups],
        compiler_params=params(),
        cost_estimate=pl.CostEstimate(flops=0, bytes_accessed=7 * 10**6, transcendentals=0),
        name="assemble",
    )(where, *refs)


def body(stem_input, stem_preact, deep_cotangent, tissue_tiles, conv_weight, expand_weight):
    _, out_rows, out_cols, channels = stem_preact.shape
    _, all_rows, band, deep = deep_cotangent.shape
    devices = SIZES["x"] * SIZES["z"]
    preact = stem_preact[0]
    cotangent = deep_cotangent[0].reshape(all_rows * band, deep)
    share = tissue_tiles.astype(jnp.float32) / TILES
    core = lax.axis_index("core").astype(jnp.int32)
    where = jnp.stack([core, lax.axis_index("y"), lax.axis_index("x")]).astype(jnp.int32)

    hidden = lax.dot_general(
        (cotangent.astype(jnp.float32) * share[:, None]).astype(jnp.bfloat16),
        expand_weight,
        (((1,), (1,)), ((), ())),
        preferred_element_type=jnp.float32,
    ).astype(jnp.bfloat16)
    active = jnp.maximum(preact, jnp.zeros_like(preact))
    active = active.reshape(out_rows, devices, band, channels).transpose(1, 0, 2, 3)
    chunk = out_rows * band
    sent = jnp.concatenate(
        [hidden.reshape(devices, chunk, channels), active.reshape(devices, chunk, channels)], axis=1
    )
    blocks, weighted = prepare(share, stem_input[0], cotangent)
    arrived = exchange(sent, SPACE)
    hidden = arrived[:, :chunk].reshape(devices, out_rows, band, channels).transpose(1, 0, 2, 3)
    hidden = hidden.reshape(out_rows, out_cols, channels)
    active = arrived[:, chunk:].reshape(all_rows * band, channels)
    grad = jnp.where(preact > 0, hidden, jnp.zeros_like(hidden))
    below = shifted(grad[:1], -1)

    own_inner, other_inner = halves(inner_kernel, 6 * LANES, where[:1], blocks, grad)
    own_outer, other_outer = halves(
        outer_kernel,
        3 * LANES + deep // 2,
        where[:1],
        blocks,
        grad,
        below,
        active,
        weighted,
        scratch=[pltpu.VMEM((channels, all_rows * band), jnp.bfloat16)],
    )
    grad_input = input_grad(grad, below, conv_weight)

    samples_all = stem_input.shape[0] * SIZES["y"] * SIZES["core"]
    scale = float(samples_all * all_rows * out_cols) ** (-0.5)
    inner = own_inner + swapped(other_inner, "core", 1)
    outer = own_outer + swapped(other_outer, "core", 1)
    inner = scatter_sum(scatter_sum(inner, "y"), "x")
    outer = scatter_sum(scatter_sum(outer, "x"), "y")
    inner, outer = sum_along_z([inner, outer], scale)
    inner = gather_pieces(gather(inner, "x"), "y")
    outer = gather_pieces(gather(outer, "y"), "x")
    groups = [pieces + [swapped(piece, "core", 1) for piece in pieces] for pieces in (inner, outer)]
    grad_conv, grad_expand = assemble(where, groups, channels, deep)
    return (grad_input[None], grad_conv.reshape(3, 3, channels, channels), grad_expand)


def solution(mesh):
    fine = Mesh(
        mesh.devices.reshape(SIZES["x"], SIZES["z"], SIZES["y"], SIZES["core"]),
        ("x", "z", "y", "core"),
    )
    return jax.shard_map(
        body,
        mesh=fine,
        in_specs=(
            P(REP, SPACE, None, None),
            P(REP, SPACE, None, None),
            P(REP, None, SPACE, None),
            P(REP),
            P(),
            P(),
        ),
        out_specs=(P(REP, SPACE, None, None), P(), P()),
        check_vma=False,
    )
```

time: 158 us -> 152 us (0.962)
  waiting for transfers between devices: 28.2 us -> 55.9 us
  blocking collectives: 21.1 us -> 0 us
  local copies, waits for them, and re-layouts: 11.9 us -> 4.3 us
  Pallas kernels: 3.45 us -> 8.28 us
  starting transfers between devices: 76.7 us -> 73.1 us
  other arithmetic: 10.2 us -> 7.05 us
  matrix products: 4.24 us -> 1.79 us
    all_to_all x2 -> x0, blocking collectives: 21.1 us -> none  [exchange(): return lax.all_to_all(x, axis, split_axis=0, concat_axis=0, tiled=True)]
    ppermute x26 -> x24, waiting for transfers between devices: 12 us -> 28.8 us  [rotated(): return lax.ppermute(x, axis, [(i, (i + by) % size) for i in range(size)])]
    ppermute x2 -> x14, starting transfers between devices: 12.1 us -> 28.5 us  [swapped(): return lax.ppermute(x, axis, [(i, i ^ bit) for i in range(SIZES[axis])])]
    all_to_all x2 -> x1, starting transfers between devices: 22.4 us -> 12.1 us  [exchange(): return lax.all_to_all(x, axis, split_axis=0, concat_axis=0, tiled=True)]
    ppermute x2 -> x14, waiting for transfers between devices: 0.01 us -> 9.28 us  [swapped(): return lax.ppermute(x, axis, [(i, i ^ bit) for i in range(SIZES[axis])])]
    all_to_all x2 -> x1, waiting for transfers between devices: 3.31 us -> 11.1 us  [exchange(): return lax.all_to_all(x, axis, split_axis=0, concat_axis=0, tiled=True)]
    ppermute x26 -> x24, starting transfers between devices: 37.9 us -> 31.1 us  [rotated(): return lax.ppermute(x, axis, [(i, (i + by) % size) for i in range(size)])]
    ppermute x2 -> x1, waiting for transfers between devices: 12.8 us -> 6.73 us  [shifted(): return lax.ppermute(x, SPACE, pairs)]
  transfers between devices with their start and end apart: 32 -> 40, of which waited for: 13 -> 18; matrix products, arithmetic and copies ran while one was open for 10% -> 3% of each run, Pallas kernels for 2% -> 3%
where the time goes in v2:
time: 152 us
  starting transfers between devices  73.1 us (48%)
  waiting for transfers between devices  55.9 us (37%)
  Pallas kernels  8.28 us (5%)
  other arithmetic  7.05 us (5%)
  local copies, waits for them, and re-layouts  4.3 us (3%)
  matrix products  1.79 us (1%)
  between operations  1.63 us (1%)
    ppermute x24, starting transfers between devices, rotated(): return lax.ppermute(x, axis, [(i, (i + by) % size) for i in range(size)])  31.1 us
    ppermute x24, waiting for transfers between devices, rotated(): return lax.ppermute(x, axis, [(i, (i + by) % size) for i in range(size)])  28.8 us
    ppermute x14, starting transfers between devices, swapped(): return lax.ppermute(x, axis, [(i, i ^ bit) for i in range(SIZES[axis])])  28.5 us
    all_to_all x1, starting transfers between devices, exchange(): return lax.all_to_all(x, axis, split_axis=0, concat_axis=0, tiled=True)  12.1 us
    all_to_all x1, waiting for transfers between devices, exchange(): return lax.all_to_all(x, axis, split_axis=0, concat_axis=0, tiled=True)  11.1 us
    ppermute x14, waiting for transfers between devices, swapped(): return lax.ppermute(x, axis, [(i, i ^ bit) for i in range(SIZES[axis])])  9.28 us
    ppermute x1, waiting for transfers between devices, shifted(): return lax.ppermute(x, SPACE, pairs)  6.73 us
  transfers between devices with their start and end apart: 40, of which 18 were waited for; matrix products, arithmetic and copies ran while one was open for 3% of the time, Pallas kernels for 3%

profile of v2, /device:TPU:1, one launch (start us, length us, event | category | flops | bytes accessed | tf_op | source)
XLA Modules:
  0.0 152.0 jit_solution(3826986585381316899)
XLA Ops:
  2.4 1.8 %convolution_convert_fusion = bf16[512,256]{1,0:T(8,128)(2,1)S(1)} fusion(bf16[256,1024]{1,0:T(8,128)(2,1)S(1)} %copy-done, f32[]{:T(128)} %bitcast.2, bf16[1,64,8,1024]{3,2,1,0:T(8,128)(2,1)} %param.8), kind=kOutput, calls=%fused_computation.1 | convolution fusion | flops 270139392 | bytes 1835012 | tf_op jit(solution)/shard_map/dot_general | solution.py:277
  5.0 12.1 %all-to-all-start = ((bf16[32,32,256]{2,1,0:T(8,128)(2,1)}), bf16[32,32,256]{2,1,0:T(8,128)(2,1)}, u32[]{:S(2)}, u32[]{:S(2)}) async-start(bf16[32,32,256]{2,1,0:T(8,128)(2,1)} %pad_maximum_fusion), calls=%async_computation | async-start | bytes 1048576 | tf_op jit(solution)/shard_map/all_to_all | solution.py:172
  20.4 11.1 %all-to-all-done = bf16[32,32,256]{2,1,0:T(8,128)(2,1)} async-done(((bf16[32,32,256]{2,1,0:T(8,128)(2,1)}), bf16[32,32,256]{2,1,0:T(8,128)(2,1)}, u32[]{:S(2)}, u32[]{:S(2)}) %all-to-all-start) | async-done | bytes 524320 | tf_op jit(solution)/shard_map/all_to_all | solution.py:172
  34.0 3.5 %collective-permute-start.1 = (f32[768,256]{1,0:T(8,128)}, f32[768,256]{1,0:T(8,128)}, u32[]{:S(2)}, u32[]{:S(2)}) collective-permute-start(f32[768,256]{1,0:T(8,128)} %get-tuple-element.13), channel_id=1, source_target_pairs={{0,1},{1,0},{2,3},{3,2},{4,5},{5,4},{6,7},{7,6},{8,9},{9,8},{10,11... | collective-permute-start | bytes 2359304 | tf_op jit(solution)/shard_map/ppermute | solution.py:213
  38.8 6.7 %collective-permute-done.below_ref = bf16[1,256,256]{2,1,0:T(8,128)(2,1)S(1)} collective-permute-done((bf16[1,256,256]{2,1,0:T(8,128)(2,1)S(1)}, bf16[1,256,256]{2,1,0:T(8,128)(2,1)S(1)}, u32[]{:S(2)}, u32[]{:S(2)}) %collective-permute-start) | collective-permute-done | bytes 131104 | tf_op jit(solution)/shard_map/ppermute | solution.py:34
  51.0 2.6 %collective-permute-start.3 = (f32[192,256]{1,0:T(8,128)S(1)}, f32[192,256]{1,0:T(8,128)}, u32[]{:S(2)}, u32[]{:S(2)}) collective-permute-start(f32[192,256]{1,0:T(8,128)S(1)} %get-tuple-element.28), channel_id=1, source_target_pairs={{0,4},{2,6},{4,0},{6,2},{1,5},{3,7},{5,1},{7,3},{8,12},{10,14},{12... | collective-permute-start | bytes 589832 | tf_op jit(solution)/shard_map/ppermute | solution.py:191
  54.7 3.1 %collective-permute-done.2 = f32[192,256]{1,0:T(8,128)S(1)} collective-permute-done((f32[192,256]{1,0:T(8,128)}, f32[192,256]{1,0:T(8,128)S(1)}, u32[]{:S(2)}, u32[]{:S(2)}) %collective-permute-start.2) | collective-permute-done | bytes 196640 | tf_op jit(solution)/shard_map/ppermute | solution.py:191
  57.8 5.4 %collective-permute-done.3 = f32[192,256]{1,0:T(8,128)} collective-permute-done((f32[192,256]{1,0:T(8,128)S(1)}, f32[192,256]{1,0:T(8,128)}, u32[]{:S(2)}, u32[]{:S(2)}) %collective-permute-start.3) | collective-permute-done | bytes 196640 | tf_op jit(solution)/shard_map/ppermute | solution.py:191
  64.7 1.8 %collective-permute-start.6 = (f32[48,256]{1,0:T(8,128)S(1)}, f32[48,256]{1,0:T(8,128)S(1)}, u32[]{:S(2)}, u32[]{:S(2)}) collective-permute-start(f32[48,256]{1,0:T(8,128)S(1)} %get-tuple-element.36), channel_id=1, source_target_pairs={{0,128},{64,192},{128,0},{192,64},{1,129},{65,193},{129,1},{193,65... | collective-permute-start | bytes 147464 | tf_op jit(solution)/shard_map/ppermute | solution.py:191
  69.0 2.0 %collective-permute-start.10 = (f32[224,256]{1,0:T(8,128)S(1)}, f32[224,256]{1,0:T(8,128)S(1)}, u32[]{:S(2)}, u32[]{:S(2)}) collective-permute-start(f32[224,256]{1,0:T(8,128)S(1)} %get-tuple-element.25), channel_id=1, source_target_pairs={{0,128},{64,192},{128,0},{192,64},{1,129},{65,193},{129,1},{193,65... | collective-permute-start | bytes 688136 | tf_op jit(solution)/shard_map/ppermute | solution.py:191
  72.4 3.6 %collective-permute-done.10 = f32[224,256]{1,0:T(8,128)S(1)} collective-permute-done((f32[224,256]{1,0:T(8,128)S(1)}, f32[224,256]{1,0:T(8,128)S(1)}, u32[]{:S(2)}, u32[]{:S(2)}) %collective-permute-start.10) | collective-permute-done | bytes 229408 | tf_op jit(solution)/shard_map/ppermute | solution.py:191
  76.0 3.7 %collective-permute-done.11 = f32[224,256]{1,0:T(8,128)S(1)} collective-permute-done((f32[224,256]{1,0:T(8,128)S(1)}, f32[224,256]{1,0:T(8,128)S(1)}, u32[]{:S(2)}, u32[]{:S(2)}) %collective-permute-start.11) | collective-permute-done | bytes 229408 | tf_op jit(solution)/shard_map/ppermute | solution.py:191
  79.7 2.2 %collective-permute-done.9 = f32[224,256]{1,0:T(8,128)} collective-permute-done((f32[224,256]{1,0:T(8,128)S(1)}, f32[224,256]{1,0:T(8,128)}, u32[]{:S(2)}, u32[]{:S(2)}) %collective-permute-start.9) | collective-permute-done | bytes 229408 | tf_op jit(solution)/shard_map/ppermute | solution.py:191
  83.2 3.3 %collective-permute-start.13 = (f32[56,256]{1,0:T(8,128)S(1)}, f32[56,256]{1,0:T(8,128)S(1)}, u32[]{:S(2)}, u32[]{:S(2)}) collective-permute-start(f32[56,256]{1,0:T(8,128)S(1)} %get-tuple-element.33), channel_id=1, source_target_pairs={{0,4},{2,6},{4,0},{6,2},{1,5},{3,7},{5,1},{7,3},{8,12},{10,14},{12... | collective-permute-start | bytes 172040 | tf_op jit(solution)/shard_map/ppermute | solution.py:191
  89.9 1.5 %collective-permute-start.15 = (f32[56,256]{1,0:T(8,128)S(1)}, f32[56,256]{1,0:T(8,128)S(1)}, u32[]{:S(2)}, u32[]{:S(2)}) collective-permute-start(f32[56,256]{1,0:T(8,128)S(1)} %fusion.6), channel_id=1, source_target_pairs={{0,8},{8,0},{16,24},{24,16},{32,40},{40,32},{48,56},{56,48},{1,9},... | collective-permute-start | bytes 172040 | tf_op jit(solution)/shard_map/ppermute | solution.py:213
  91.4 1.6 %collective-permute-done.15 = f32[56,256]{1,0:T(8,128)S(1)} collective-permute-done((f32[56,256]{1,0:T(8,128)S(1)}, f32[56,256]{1,0:T(8,128)S(1)}, u32[]{:S(2)}, u32[]{:S(2)}) %collective-permute-start.15) | collective-permute-done | bytes 57376 | tf_op jit(solution)/shard_map/ppermute | solution.py:213
  93.0 2.2 %collective-permute-start.16 = (f32[56,256]{1,0:T(8,128)S(1)}, f32[56,256]{1,0:T(8,128)S(1)}, u32[]{:S(2)}, u32[]{:S(2)}) collective-permute-start(f32[56,256]{1,0:T(8,128)S(1)} %fusion.9), channel_id=1, source_target_pairs={{0,16},{8,24},{16,0},{24,8},{32,48},{40,56},{48,32},{56,40},{1,17}... | collective-permute-start | bytes 172040 | tf_op jit(solution)/shard_map/ppermute | solution.py:213
  95.2 1.8 %collective-permute-done.16 = f32[56,256]{1,0:T(8,128)S(1)} collective-permute-done((f32[56,256]{1,0:T(8,128)S(1)}, f32[56,256]{1,0:T(8,128)S(1)}, u32[]{:S(2)}, u32[]{:S(2)}) %collective-permute-start.16) | collective-permute-done | bytes 57376 | tf_op jit(solution)/shard_map/ppermute | solution.py:213
  97.0 3.8 %collective-permute-start.17 = (f32[56,256]{1,0:T(8,128)S(1)}, f32[56,256]{1,0:T(8,128)S(1)}, u32[]{:S(2)}, u32[]{:S(2)}) collective-permute-start(f32[56,256]{1,0:T(8,128)S(1)} %add.104), channel_id=1, source_target_pairs={{0,32},{8,40},{16,48},{24,56},{32,0},{40,8},{48,16},{56,24},{1,33}... | collective-permute-start | bytes 172040 | tf_op jit(solution)/shard_map/ppermute | solution.py:213
  100.9 3.7 %collective-permute-done.17 = f32[56,256]{1,0:T(8,128)S(1)} collective-permute-done((f32[56,256]{1,0:T(8,128)S(1)}, f32[56,256]{1,0:T(8,128)S(1)}, u32[]{:S(2)}, u32[]{:S(2)}) %collective-permute-start.17) | collective-permute-done | bytes 57376 | tf_op jit(solution)/shard_map/ppermute | solution.py:213
  105.8 2.2 %collective-permute-done.18 = f32[56,256]{1,0:T(8,128)S(1)} collective-permute-done((f32[56,256]{1,0:T(8,128)S(1)}, f32[56,256]{1,0:T(8,128)S(1)}, u32[]{:S(2)}, u32[]{:S(2)}) %collective-permute-start.18) | collective-permute-done | bytes 57376 | tf_op jit(solution)/shard_map/ppermute | solution.py:213
  108.8 1.8 %collective-permute-start.30 = (f32[56,256]{1,0:T(8,128)S(1)}, f32[56,256]{1,0:T(8,128)S(1)}, u32[]{:S(2)}, u32[]{:S(2)}) collective-permute-start(f32[56,256]{1,0:T(8,128)S(1)} %get-tuple-element.20), channel_id=1, source_target_pairs={{0,4},{2,6},{4,0},{6,2},{1,5},{3,7},{5,1},{7,3},{8,12},{10,14},{12... | collective-permute-start | bytes 172040 | tf_op jit(solution)/shard_map/ppermute | solution.py:191
  111.9 1.9 %collective-permute-start.20 = (f32[48,256]{1,0:T(8,128)S(1)}, f32[48,256]{1,0:T(8,128)S(1)}, u32[]{:S(2)}, u32[]{:S(2)}) collective-permute-start(f32[48,256]{1,0:T(8,128)S(1)} %get-tuple-element.22), channel_id=1, source_target_pairs={{0,128},{64,192},{128,0},{192,64},{1,129},{65,193},{129,1},{193,65... | collective-permute-start | bytes 147464 | tf_op jit(solution)/shard_map/ppermute | solution.py:191
  113.8 2.1 %collective-permute-start.21 = (f32[48,256]{1,0:T(8,128)S(1)}, f32[48,256]{1,0:T(8,128)S(1)}, u32[]{:S(2)}, u32[]{:S(2)}) collective-permute-start(f32[48,256]{1,0:T(8,128)S(1)} %get-tuple-element.22), channel_id=1, source_target_pairs={{0,192},{64,0},{128,64},{192,128},{1,193},{65,1},{129,65},{193,129... | collective-permute-start | bytes 147464 | tf_op jit(solution)/shard_map/ppermute | solution.py:191
  119.3 2.0 %collective-permute-start.24 = (f32[192,256]{1,0:T(8,128)S(1)}, f32[192,256]{1,0:T(8,128)S(1)}, u32[]{:S(2)}, u32[]{:S(2)}) collective-permute-start(f32[192,256]{1,0:T(8,128)S(1)} %bitcast.122), channel_id=1, source_target_pairs={{0,6},{2,0},{4,2},{6,4},{1,7},{3,1},{5,3},{7,5},{8,14},{10,8},{12,... | collective-permute-start | bytes 589832 | tf_op jit(solution)/shard_map/ppermute | solution.py:191
  121.3 10.6 %collective-permute-start.25 = (f32[192,256]{1,0:T(8,128)S(1)}, f32[192,256]{1,0:T(8,128)S(1)}, u32[]{:S(2)}, u32[]{:S(2)}) collective-permute-start(f32[192,256]{1,0:T(8,128)S(1)} %bitcast.123), channel_id=1, source_target_pairs={{0,1},{1,0},{2,3},{3,2},{4,5},{5,4},{6,7},{7,6},{8,9},{9,8},{10,11... | collective-permute-start | bytes 589832 | tf_op jit(solution)/shard_map/ppermute | solution.py:213
  132.8 2.4 %collective-permute-start.33 = (f32[224,256]{1,0:T(8,128)S(1)}, f32[224,256]{1,0:T(8,128)S(1)}, u32[]{:S(2)}, u32[]{:S(2)}) collective-permute-start(f32[224,256]{1,0:T(8,128)S(1)} %bitcast.116), channel_id=1, source_target_pairs={{0,128},{64,192},{128,0},{192,64},{1,129},{65,193},{129,1},{193,65... | collective-permute-start | bytes 688136 | tf_op jit(solution)/shard_map/ppermute | solution.py:191
  135.7 2.7 %collective-permute-start.35 = (f32[224,256]{1,0:T(8,128)S(1)}, f32[224,256]{1,0:T(8,128)S(1)}, u32[]{:S(2)}, u32[]{:S(2)}) collective-permute-start(f32[224,256]{1,0:T(8,128)S(1)} %bitcast.118), channel_id=1, source_target_pairs={{0,1},{1,0},{2,3},{3,2},{4,5},{5,4},{6,7},{7,6},{8,9},{9,8},{10,11... | collective-permute-start | bytes 688136 | tf_op jit(solution)/shard_map/ppermute | solution.py:213
  138.5 1.9 %collective-permute-done.32.refs_9_ = f32[224,256]{1,0:T(8,128)S(1)} collective-permute-done((f32[224,256]{1,0:T(8,128)S(1)}, f32[224,256]{1,0:T(8,128)S(1)}, u32[]{:S(2)}, u32[]{:S(2)}) %collective-permute-start.32) | collective-permute-done | bytes 229408 | tf_op jit(solution)/shard_map/ppermute | solution.py:191
  141.2 4.6 %collective-permute-done.33.refs_10_ = f32[224,256]{1,0:T(8,128)S(1)} collective-permute-done((f32[224,256]{1,0:T(8,128)S(1)}, f32[224,256]{1,0:T(8,128)S(1)}, u32[]{:S(2)}, u32[]{:S(2)}) %collective-permute-start.33) | collective-permute-done | bytes 229408 | tf_op jit(solution)/shard_map/ppermute | solution.py:191
  147.4 1.9 %input_grad.1 = bf16[4,512,256]{2,1,0:T(8,128)(2,1)} custom-call(bf16[2,256,256]{2,1,0:T(8,128)(2,1)S(1)} %bitcast_select_fusion.grad_ref, bf16[1,256,256]{2,1,0:T(8,128)(2,1)S(1)} %collective-permute-done.below_ref, bf16[3,3,256,256]{3,2,1,0:T(8,128)(2,1)S(1)} %copy-done.1), custom_call_target="tpu_custom_call" | custom-call | flops 604000000 | bytes 3000000 | tf_op jit(solution)/shard_map/input_grad/pallas_call | solution.py:159
  149.3 2.7 %assemble.1 = (f32[9,256,256]{2,1,0:T(8,128)}, f32[256,1024]{1,0:T(8,128)}) custom-call(s32[3]{0:T(128)S(1)} %pad_add_fusion.where_ref, f32[192,256]{1,0:T(8,128)S(1)} %bitcast.124, f32[192,256]{1,0:T(8,128)S(1)} %collective-permute-done.22.refs_1_, f32[192,256]{1,0:T(8,128)S(1)} %collective-permute-done.23.refs_2_, ...), custom_call_target="tpu_custom_call" | custom-call | bytes 7000000 | tf_op jit(solution)/shard_map/assemble/pallas_call | solution.py:252
  (103 shorter events, 36.0 us)
Async XLA Ops:
  5.0 26.4 %all-to-all-start = ((bf16[32,32,256]{2,1,0:T(8,128)(2,1)}), bf16[32,32,256]{2,1,0:T(8,128)(2,1)}, u32[]{:S(2)}, u32[]{:S(2)}) async-start(bf16[32,32,256]{2,1,0:T(8,128)(2,1)} %pad_maximum_fusion), calls=%async_computation | async-start | bytes 1048576 | tf_op jit(solution)/shard_map/all_to_all | solution.py:172
  34.0 13.5 %collective-permute-start.1 = (f32[768,256]{1,0:T(8,128)}, f32[768,256]{1,0:T(8,128)}, u32[]{:S(2)}, u32[]{:S(2)}) collective-permute-start(f32[768,256]{1,0:T(8,128)} %get-tuple-element.13), channel_id=1, source_target_pairs={{0,1},{1,0},{2,3},{3,2},{4,5},{5,4},{6,7},{7,6},{8,9},{9,8},{10,11... | collective-permute-start | bytes 2359304 | tf_op jit(solution)/shard_map/ppermute | solution.py:213
  37.5 8.0 %collective-permute-start = (bf16[1,256,256]{2,1,0:T(8,128)(2,1)S(1)}, bf16[1,256,256]{2,1,0:T(8,128)(2,1)S(1)}, u32[]{:S(2)}, u32[]{:S(2)}) collective-permute-start(bf16[1,256,256]{2,1,0:T(8,128)(2,1)S(1)} %slice.17), channel_id=1, source_target_pairs={{8,0},{16,8},{24,16},{32,24},{40,32},{48,40},{56,48},{64,56},{72,6... | collective-permute-start | bytes 393224 | tf_op jit(solution)/shard_map/ppermute | solution.py:34
  46.9 20.7 %collective-permute-start.8 = (f32[896,256]{1,0:T(8,128)}, f32[896,256]{1,0:T(8,128)}, u32[]{:S(2)}, u32[]{:S(2)}) collective-permute-start(f32[896,256]{1,0:T(8,128)} %get-tuple-element.16), channel_id=1, source_target_pairs={{0,1},{1,0},{2,3},{3,2},{4,5},{5,4},{6,7},{7,6},{8,9},{9,8},{10,11... | collective-permute-start | bytes 2752520 | tf_op jit(solution)/shard_map/ppermute | solution.py:213
  49.7 8.1 %collective-permute-start.2 = (f32[192,256]{1,0:T(8,128)}, f32[192,256]{1,0:T(8,128)S(1)}, u32[]{:S(2)}, u32[]{:S(2)}) collective-permute-start(f32[192,256]{1,0:T(8,128)} %get-tuple-element.26), channel_id=1, source_target_pairs={{0,2},{2,4},{4,6},{6,0},{1,3},{3,5},{5,7},{7,1},{8,10},{10,12},{12... | collective-permute-start | bytes 589832 | tf_op jit(solution)/shard_map/ppermute | solution.py:191
  51.0 12.2 %collective-permute-start.3 = (f32[192,256]{1,0:T(8,128)S(1)}, f32[192,256]{1,0:T(8,128)}, u32[]{:S(2)}, u32[]{:S(2)}) collective-permute-start(f32[192,256]{1,0:T(8,128)S(1)} %get-tuple-element.28), channel_id=1, source_target_pairs={{0,4},{2,6},{4,0},{6,2},{1,5},{3,7},{5,1},{7,3},{8,12},{10,14},{12... | collective-permute-start | bytes 589832 | tf_op jit(solution)/shard_map/ppermute | solution.py:191
  53.6 9.6 %collective-permute-start.4 = (f32[192,256]{1,0:T(8,128)S(1)}, f32[192,256]{1,0:T(8,128)}, u32[]{:S(2)}, u32[]{:S(2)}) collective-permute-start(f32[192,256]{1,0:T(8,128)S(1)} %get-tuple-element.27), channel_id=1, source_target_pairs={{0,6},{2,0},{4,2},{6,4},{1,7},{3,1},{5,3},{7,5},{8,14},{10,8},{12,... | collective-permute-start | bytes 589832 | tf_op jit(solution)/shard_map/ppermute | solution.py:191
  64.3 7.5 %collective-permute-start.5 = (f32[48,256]{1,0:T(8,128)S(1)}, f32[48,256]{1,0:T(8,128)S(1)}, u32[]{:S(2)}, u32[]{:S(2)}) collective-permute-start(f32[48,256]{1,0:T(8,128)S(1)} %get-tuple-element.34), channel_id=1, source_target_pairs={{0,64},{64,128},{128,192},{192,0},{1,65},{65,129},{129,193},{193,1... | collective-permute-start | bytes 147464 | tf_op jit(solution)/shard_map/ppermute | solution.py:191
  64.7 7.7 %collective-permute-start.6 = (f32[48,256]{1,0:T(8,128)S(1)}, f32[48,256]{1,0:T(8,128)S(1)}, u32[]{:S(2)}, u32[]{:S(2)}) collective-permute-start(f32[48,256]{1,0:T(8,128)S(1)} %get-tuple-element.36), channel_id=1, source_target_pairs={{0,128},{64,192},{128,0},{192,64},{1,129},{65,193},{129,1},{193,65... | collective-permute-start | bytes 147464 | tf_op jit(solution)/shard_map/ppermute | solution.py:191
  66.5 5.9 %collective-permute-start.7 = (f32[48,256]{1,0:T(8,128)S(1)}, f32[48,256]{1,0:T(8,128)S(1)}, u32[]{:S(2)}, u32[]{:S(2)}) collective-permute-start(f32[48,256]{1,0:T(8,128)S(1)} %get-tuple-element.35), channel_id=1, source_target_pairs={{0,192},{64,0},{128,64},{192,128},{1,193},{65,1},{129,65},{193,129... | collective-permute-start | bytes 147464 | tf_op jit(solution)/shard_map/ppermute | solution.py:191
  69.0 7.1 %collective-permute-start.10 = (f32[224,256]{1,0:T(8,128)S(1)}, f32[224,256]{1,0:T(8,128)S(1)}, u32[]{:S(2)}, u32[]{:S(2)}) collective-permute-start(f32[224,256]{1,0:T(8,128)S(1)} %get-tuple-element.25), channel_id=1, source_target_pairs={{0,128},{64,192},{128,0},{192,64},{1,129},{65,193},{129,1},{193,65... | collective-permute-start | bytes 688136 | tf_op jit(solution)/shard_map/ppermute | solution.py:191
  70.9 8.8 %collective-permute-start.11 = (f32[224,256]{1,0:T(8,128)S(1)}, f32[224,256]{1,0:T(8,128)S(1)}, u32[]{:S(2)}, u32[]{:S(2)}) collective-permute-start(f32[224,256]{1,0:T(8,128)S(1)} %get-tuple-element.24), channel_id=1, source_target_pairs={{0,192},{64,0},{128,64},{192,128},{1,193},{65,1},{129,65},{193,129... | collective-permute-start | bytes 688136 | tf_op jit(solution)/shard_map/ppermute | solution.py:191
  71.8 10.1 %collective-permute-start.9 = (f32[224,256]{1,0:T(8,128)S(1)}, f32[224,256]{1,0:T(8,128)}, u32[]{:S(2)}, u32[]{:S(2)}) collective-permute-start(f32[224,256]{1,0:T(8,128)S(1)} %get-tuple-element.23), channel_id=1, source_target_pairs={{0,64},{64,128},{128,192},{192,0},{1,65},{65,129},{129,193},{193,1... | collective-permute-start | bytes 688136 | tf_op jit(solution)/shard_map/ppermute | solution.py:191
  83.1 4.3 %collective-permute-start.12 = (f32[56,256]{1,0:T(8,128)S(1)}, f32[56,256]{1,0:T(8,128)S(1)}, u32[]{:S(2)}, u32[]{:S(2)}) collective-permute-start(f32[56,256]{1,0:T(8,128)S(1)} %get-tuple-element.31), channel_id=1, source_target_pairs={{0,2},{2,4},{4,6},{6,0},{1,3},{3,5},{5,7},{7,1},{8,10},{10,12},{12... | collective-permute-start | bytes 172040 | tf_op jit(solution)/shard_map/ppermute | solution.py:191
  83.2 5.5 %collective-permute-start.13 = (f32[56,256]{1,0:T(8,128)S(1)}, f32[56,256]{1,0:T(8,128)S(1)}, u32[]{:S(2)}, u32[]{:S(2)}) collective-permute-start(f32[56,256]{1,0:T(8,128)S(1)} %get-tuple-element.33), channel_id=1, source_target_pairs={{0,4},{2,6},{4,0},{6,2},{1,5},{3,7},{5,1},{7,3},{8,12},{10,14},{12... | collective-permute-start | bytes 172040 | tf_op jit(solution)/shard_map/ppermute | solution.py:191
  93.0 4.0 %collective-permute-start.16 = (f32[56,256]{1,0:T(8,128)S(1)}, f32[56,256]{1,0:T(8,128)S(1)}, u32[]{:S(2)}, u32[]{:S(2)}) collective-permute-start(f32[56,256]{1,0:T(8,128)S(1)} %fusion.9), channel_id=1, source_target_pairs={{0,16},{8,24},{16,0},{24,8},{32,48},{40,56},{48,32},{56,40},{1,17}... | collective-permute-start | bytes 172040 | tf_op jit(solution)/shard_map/ppermute | solution.py:213
  97.0 7.5 %collective-permute-start.17 = (f32[56,256]{1,0:T(8,128)S(1)}, f32[56,256]{1,0:T(8,128)S(1)}, u32[]{:S(2)}, u32[]{:S(2)}) collective-permute-start(f32[56,256]{1,0:T(8,128)S(1)} %add.104), channel_id=1, source_target_pairs={{0,32},{8,40},{16,48},{24,56},{32,0},{40,8},{48,16},{56,24},{1,33}... | collective-permute-start | bytes 172040 | tf_op jit(solution)/shard_map/ppermute | solution.py:213
  108.0 5.8 %collective-permute-start.19 = (f32[48,256]{1,0:T(8,128)S(1)}, f32[48,256]{1,0:T(8,128)S(1)}, u32[]{:S(2)}, u32[]{:S(2)}) collective-permute-start(f32[48,256]{1,0:T(8,128)S(1)} %get-tuple-element.22), channel_id=1, source_target_pairs={{0,64},{64,128},{128,192},{192,0},{1,65},{65,129},{129,193},{193,1... | collective-permute-start | bytes 147464 | tf_op jit(solution)/shard_map/ppermute | solution.py:191
  108.5 10.8 %collective-permute-start.29 = (f32[56,256]{1,0:T(8,128)S(1)}, f32[56,256]{1,0:T(8,128)S(1)}, u32[]{:S(2)}, u32[]{:S(2)}) collective-permute-start(f32[56,256]{1,0:T(8,128)S(1)} %get-tuple-element.20), channel_id=1, source_target_pairs={{0,2},{2,4},{4,6},{6,0},{1,3},{3,5},{5,7},{7,1},{8,10},{10,12},{12... | collective-permute-start | bytes 172040 | tf_op jit(solution)/shard_map/ppermute | solution.py:191
  108.8 12.5 %collective-permute-start.30 = (f32[56,256]{1,0:T(8,128)S(1)}, f32[56,256]{1,0:T(8,128)S(1)}, u32[]{:S(2)}, u32[]{:S(2)}) collective-permute-start(f32[56,256]{1,0:T(8,128)S(1)} %get-tuple-element.20), channel_id=1, source_target_pairs={{0,4},{2,6},{4,0},{6,2},{1,5},{3,7},{5,1},{7,3},{8,12},{10,14},{12... | collective-permute-start | bytes 172040 | tf_op jit(solution)/shard_map/ppermute | solution.py:191
  110.6 21.3 %collective-permute-start.31 = (f32[56,256]{1,0:T(8,128)S(1)}, f32[56,256]{1,0:T(8,128)S(1)}, u32[]{:S(2)}, u32[]{:S(2)}) collective-permute-start(f32[56,256]{1,0:T(8,128)S(1)} %get-tuple-element.20), channel_id=1, source_target_pairs={{0,6},{2,0},{4,2},{6,4},{1,7},{3,1},{5,3},{7,5},{8,14},{10,8},{12,... | collective-permute-start | bytes 172040 | tf_op jit(solution)/shard_map/ppermute | solution.py:191
  111.9 4.4 %collective-permute-start.20 = (f32[48,256]{1,0:T(8,128)S(1)}, f32[48,256]{1,0:T(8,128)S(1)}, u32[]{:S(2)}, u32[]{:S(2)}) collective-permute-start(f32[48,256]{1,0:T(8,128)S(1)} %get-tuple-element.22), channel_id=1, source_target_pairs={{0,128},{64,192},{128,0},{192,64},{1,129},{65,193},{129,1},{193,65... | collective-permute-start | bytes 147464 | tf_op jit(solution)/shard_map/ppermute | solution.py:191
  117.1 15.7 %collective-permute-start.22 = (f32[192,256]{1,0:T(8,128)S(1)}, f32[192,256]{1,0:T(8,128)S(1)}, u32[]{:S(2)}, u32[]{:S(2)}) collective-permute-start(f32[192,256]{1,0:T(8,128)S(1)} %bitcast.120), channel_id=1, source_target_pairs={{0,2},{2,4},{4,6},{6,0},{1,3},{3,5},{5,7},{7,1},{8,10},{10,12},{12... | collective-permute-start | bytes 589832 | tf_op jit(solution)/shard_map/ppermute | solution.py:191
  118.0 17.3 %collective-permute-start.23 = (f32[192,256]{1,0:T(8,128)S(1)}, f32[192,256]{1,0:T(8,128)S(1)}, u32[]{:S(2)}, u32[]{:S(2)}) collective-permute-start(f32[192,256]{1,0:T(8,128)S(1)} %bitcast.121), channel_id=1, source_target_pairs={{0,4},{2,6},{4,0},{6,2},{1,5},{3,7},{5,1},{7,3},{8,12},{10,14},{12... | collective-permute-start | bytes 589832 | tf_op jit(solution)/shard_map/ppermute | solution.py:191
  119.3 16.4 %collective-permute-start.24 = (f32[192,256]{1,0:T(8,128)S(1)}, f32[192,256]{1,0:T(8,128)S(1)}, u32[]{:S(2)}, u32[]{:S(2)}) collective-permute-start(f32[192,256]{1,0:T(8,128)S(1)} %bitcast.122), channel_id=1, source_target_pairs={{0,6},{2,0},{4,2},{6,4},{1,7},{3,1},{5,3},{7,5},{8,14},{10,8},{12,... | collective-permute-start | bytes 589832 | tf_op jit(solution)/shard_map/ppermute | solution.py:191
  121.3 17.1 %collective-permute-start.25 = (f32[192,256]{1,0:T(8,128)S(1)}, f32[192,256]{1,0:T(8,128)S(1)}, u32[]{:S(2)}, u32[]{:S(2)}) collective-permute-start(f32[192,256]{1,0:T(8,128)S(1)} %bitcast.123), channel_id=1, source_target_pairs={{0,1},{1,0},{2,3},{3,2},{4,5},{5,4},{6,7},{7,6},{8,9},{9,8},{10,11... | collective-permute-start | bytes 589832 | tf_op jit(solution)/shard_map/ppermute | solution.py:213
  131.9 8.5 %collective-permute-start.32 = (f32[224,256]{1,0:T(8,128)S(1)}, f32[224,256]{1,0:T(8,128)S(1)}, u32[]{:S(2)}, u32[]{:S(2)}) collective-permute-start(f32[224,256]{1,0:T(8,128)S(1)} %bitcast.115), channel_id=1, source_target_pairs={{0,64},{64,128},{128,192},{192,0},{1,65},{65,129},{129,193},{193,1... | collective-permute-start | bytes 688136 | tf_op jit(solution)/shard_map/ppermute | solution.py:191
  132.8 13.1 %collective-permute-start.33 = (f32[224,256]{1,0:T(8,128)S(1)}, f32[224,256]{1,0:T(8,128)S(1)}, u32[]{:S(2)}, u32[]{:S(2)}) collective-permute-start(f32[224,256]{1,0:T(8,128)S(1)} %bitcast.116), channel_id=1, source_target_pairs={{0,128},{64,192},{128,0},{192,64},{1,129},{65,193},{129,1},{193,65... | collective-permute-start | bytes 688136 | tf_op jit(solution)/shard_map/ppermute | solution.py:191
  135.2 11.5 %collective-permute-start.34 = (f32[224,256]{1,0:T(8,128)S(1)}, f32[224,256]{1,0:T(8,128)S(1)}, u32[]{:S(2)}, u32[]{:S(2)}) collective-permute-start(f32[224,256]{1,0:T(8,128)S(1)} %bitcast.117), channel_id=1, source_target_pairs={{0,192},{64,0},{128,64},{192,128},{1,193},{65,1},{129,65},{193,129... | collective-permute-start | bytes 688136 | tf_op jit(solution)/shard_map/ppermute | solution.py:191
  135.7 11.0 %collective-permute-start.35 = (f32[224,256]{1,0:T(8,128)S(1)}, f32[224,256]{1,0:T(8,128)S(1)}, u32[]{:S(2)}, u32[]{:S(2)}) collective-permute-start(f32[224,256]{1,0:T(8,128)S(1)} %bitcast.118), channel_id=1, source_target_pairs={{0,1},{1,0},{2,3},{3,2},{4,5},{5,4},{6,7},{7,6},{8,9},{9,8},{10,11... | collective-permute-start | bytes 688136 | tf_op jit(solution)/shard_map/ppermute | solution.py:213
  138.4 8.8 %collective-permute-start.26 = (f32[192,256]{1,0:T(8,128)S(1)}, f32[192,256]{1,0:T(8,128)S(1)}, u32[]{:S(2)}, u32[]{:S(2)}) collective-permute-start(f32[192,256]{1,0:T(8,128)S(1)} %collective-permute-done.22.refs_1_), channel_id=1, source_target_pairs={{0,1},{1,0},{2,3},{3,2},{4,5},{5,4},{6,7},{7,6},{8,9},{9,8},{10,11... | collective-permute-start | bytes 589832 | tf_op jit(solution)/shard_map/ppermute | solution.py:213
  140.4 8.9 %collective-permute-start.36 = (f32[224,256]{1,0:T(8,128)S(1)}, f32[224,256]{1,0:T(8,128)S(1)}, u32[]{:S(2)}, u32[]{:S(2)}) collective-permute-start(f32[224,256]{1,0:T(8,128)S(1)} %collective-permute-done.32.refs_9_), channel_id=1, source_target_pairs={{0,1},{1,0},{2,3},{3,2},{4,5},{5,4},{6,7},{7,6},{8,9},{9,8},{10,11... | collective-permute-start | bytes 688136 | tf_op jit(solution)/shard_map/ppermute | solution.py:213
  (17 other events, 175.6 us)

commit v3 on v2

--- a/solution.py
+++ b/solution.py
@@ -34,13 +34,14 @@
     return lax.ppermute(x, SPACE, pairs)
 
 
-def prepare_kernel(share_ref, x_ref, cotangent_ref, out_ref, weighted_ref, wide):
+def prepare_kernel(share_ref, above_ref, x_ref, cotangent_ref, out_ref, weighted_ref, wide):
     half = out_ref.shape[2]
     first = lax.broadcasted_iota(jnp.int32, (LANES, half), 1) == 0
-    for row in range(x_ref.shape[0]):
+    for row in range(x_ref.shape[0] + 1):
+        source = above_ref.at[0] if row == 0 else x_ref.at[row - 1]
         for part in range(x_ref.shape[2] // LANES):
             lanes = slice(part * LANES, (part + 1) * LANES)
-            wide[...] = x_ref[row, :, lanes].astype(jnp.float32)
+            wide[...] = source[:, lanes].astype(jnp.float32)
             even = wide[pl.ds(0, half, stride=2), :].T
             odd = wide[pl.ds(1, half, stride=2), :].T
             late = jnp.where(first, 0.0, pltpu.roll(odd, 1, 1))
@@ -50,56 +51,52 @@
     weighted_ref[...] = (cotangent_ref[...].astype(jnp.float32) * share_ref[0]).astype(jnp.bfloat16)
 
 
-def prepare(share, x, cotangent):
+def prepare(share, above, x, cotangent):
     rows, cols, channels = x.shape
     return pl.pallas_call(
         prepare_kernel,
         out_shape=(
-            jax.ShapeDtypeStruct((3 * rows, channels, cols // 2), jnp.bfloat16),
+            jax.ShapeDtypeStruct((3 * rows + 3, channels, cols // 2), jnp.bfloat16),
             jax.ShapeDtypeStruct(cotangent.shape, jnp.bfloat16),
         ),
-        in_specs=[scalars(), whole(), whole()],
+        in_specs=[scalars(), whole(), whole(), whole()],
         out_specs=(whole(), whole()),
         scratch_shapes=[pltpu.VMEM((cols, LANES), jnp.float32)],
         compiler_params=params(),
         cost_estimate=pl.CostEstimate(flops=10**7, bytes_accessed=5 * 10**6, transcendentals=0),
         name="prepare",
-    )(share, x, cotangent)
-
-
-def half_taps(blocks_ref, grads, row_tap, col_tap, start):
+    )(share, above, x, cotangent)
+
+
+def half_taps(blocks_ref, grad_ref, row_tap, col_tap, start):
     total = None
-    for i, grad in enumerate(grads):
-        row = 2 * i + row_tap - 1
-        if 0 <= row < blocks_ref.shape[0] // 3:
-            term = jnp.dot(
-                blocks_ref[3 * row + col_tap, pl.ds(start, LANES), :],
-                grad,
-                preferred_element_type=jnp.float32,
-            )
-            total = term if total is None else total + term
+    for i in range(2):
+        term = jnp.dot(
+            blocks_ref[3 * (2 * i + row_tap) + col_tap, pl.ds(start, LANES), :],
+            grad_ref[i],
+            preferred_element_type=jnp.float32,
+        )
+        total = term if total is None else total + term
     return total
 
 
 def inner_kernel(core_ref, blocks_ref, grad_ref, own_ref, other_ref):
-    grads = [grad_ref[0], grad_ref[1]]
     for out_ref, owner in ((other_ref, 1 - core_ref[0]), (own_ref, core_ref[0])):
         start = pl.multiple_of(owner * LANES, LANES)
         for row_tap in (1, 2):
             for col_tap in range(3):
                 at = (3 * (row_tap - 1) + col_tap) * LANES
-                out_ref[at : at + LANES, :] = half_taps(blocks_ref, grads, row_tap, col_tap, start)
-
-
-def outer_kernel(core_ref, blocks_ref, grad_ref, below_ref, active_ref, weighted_ref, own_ref, other_ref, turned):
+                out_ref[at : at + LANES, :] = half_taps(blocks_ref, grad_ref, row_tap, col_tap, start)
+
+
+def outer_kernel(core_ref, blocks_ref, grad_ref, active_ref, weighted_ref, own_ref, other_ref, turned):
     channels = grad_ref.shape[2]
-    grads = [grad_ref[0], grad_ref[1], below_ref[0]]
     turned[...] = active_ref[...].T
     for out_ref, owner in ((other_ref, 1 - core_ref[0]), (own_ref, core_ref[0])):
         start = pl.multiple_of(owner * LANES, LANES)
         for col_tap in range(3):
             at = col_tap * LANES
-            out_ref[at : at + LANES, :] = half_taps(blocks_ref, grads, 0, col_tap, start)
+            out_ref[at : at + LANES, :] = half_taps(blocks_ref, grad_ref, 0, col_tap, start)
         for n in range(weighted_ref.shape[1] // channels):
             at = (3 + n) * LANES
             out_ref[at : at + LANES, :] = jnp.dot(
@@ -191,60 +188,88 @@
     return lax.ppermute(x, axis, [(i, (i + by) % size) for i in range(size)])
 
 
-def scatter_sum(x, axis):
-    size = SIZES[axis]
-    parts = x.reshape(size, x.shape[0] // size, x.shape[1])
-    arrived = [rotated(pick(parts, place(axis, by)), axis, by) for by in range(1, size)]
-    return sum(arrived, pick(parts, place(axis)))
-
-
-def gather_pieces(x, axis):
-    return [x] + [rotated(x, axis, by) for by in range(1, SIZES[axis])]
-
-
-def gather(x, axis):
-    out = jnp.zeros((SIZES[axis],) + x.shape, x.dtype)
-    for by, piece in enumerate(gather_pieces(x, axis)):
-        out = put(out, piece, place(axis, -by))
-    return out.reshape(-1, x.shape[1])
+def split(x):
+    return x.reshape(4, x.shape[0] // 4, x.shape[1])
 
 
 def swapped(x, axis, bit):
     return lax.ppermute(x, axis, [(i, i ^ bit) for i in range(SIZES[axis])])
 
 
-def sum_along_z(pair, scale):
-    rows = max(p.shape[0] for p in pair)
-    both = jnp.stack([jnp.pad(p, ((0, rows - p.shape[0]), (0, 0))) for p in pair])
+def turned(x, by):
+    pairs = []
+    for i in range(SIZES["x"]):
+        for k in range(SIZES["z"]):
+            for j in range(SIZES["y"]):
+                to = (i, (j + by) % 4) if k % 2 else ((i + by) % 4, j)
+                pairs.append(((i * SIZES["z"] + k) * 4 + j, (to[0] * SIZES["z"] + k) * 4 + to[1]))
+    return lax.ppermute(x, ("x", "z", "y"), pairs)
+
+
+def turned_place(by=0):
+    odd = (place("z") & jnp.uint32(1)) == 1
+    return jnp.where(odd, place("y", by), place("x", by))
+
+
+barrier = lax.optimization_barrier
+STEPS = (1, 2, 3)
+
+
+def total_sums(inner, outer, scale, beside):
+    inner, outer = split(inner), split(outer)
+    inner, parts = barrier((inner, [pick(outer, place("x", by)) for by in STEPS]))
+    inner = exchange(inner, "y")
+    moved = [rotated(p, "x", by) for p, by in zip(parts, STEPS)]
+    inner, moved, beside = barrier((inner, moved, beside))
+    inner = jnp.sum(inner, axis=0)
+    outer = sum(moved, pick(outer, place("x")))
+
+    rows = outer.shape[0] - inner.shape[0]
+    both = jnp.stack([jnp.pad(inner, ((0, rows), (0, 0))), outer])
     bit = place("z") & jnp.uint32(1)
     part = pick(both, bit) + swapped(pick(both, jnp.uint32(1) - bit), "z", 1)
-    part = part + swapped(part, "z", 2)
-    part = (part + swapped(part, "z", 4)) * scale
+
+    parts = split(part)
+    moved = barrier([pick(parts, turned_place(by)) for by in STEPS])
+    moved = [turned(p, by) for p, by in zip(moved, STEPS)]
+    part = sum(moved, pick(parts, turned_place()))
+
+    two, four, six = [rotated(part, "z", by) for by in (2, 4, 6)]
+    part = ((part + four) + (two + six)) * scale
+
+    whole_part = jnp.zeros((4,) + part.shape, part.dtype)
+    for by in range(4):
+        whole_part = put(whole_part, turned(part, by) if by else part, turned_place(-by))
+    part = whole_part.reshape(-1, part.shape[1])
     got = swapped(part, "z", 1)
-    even = bit == 0
-    out = (jnp.where(even, part, got), jnp.where(even, got, part))
-    return [o[: p.shape[0]] for o, p in zip(out, pair)]
+    inner = jnp.where(bit == 0, part, got)[: part.shape[0] - rows]
+    outer = jnp.where(bit == 0, got, part)
+    inner, outer = barrier((inner, outer))
+    copies = barrier(jnp.broadcast_to(inner, (4,) + inner.shape))
+    copies, moved = barrier((exchange(copies, "y"), [rotated(outer, "x", by) for by in STEPS]))
+    return [copies.reshape(-1, part.shape[1])], [outer] + moved, beside
 
 
 def assemble_kernel(where_ref, *refs):
-    groups, (conv_ref, expand_ref), scratch = (refs[:8], refs[8:16]), refs[16:18], refs[18:]
+    inner, pieces, (conv_ref, expand_ref, joined) = refs[:2], refs[2:10], refs[10:]
     channels = conv_ref.shape[2]
     core = where_ref[0]
-    for n, (pieces, whole_ref) in enumerate(zip(groups, scratch)):
-        for by in range(4):
-            rows = pieces[by].shape[0]
-            at = pl.multiple_of(((where_ref[1 + n] + 4 - by) & 3) * rows, 8)
-            whole_ref[core, pl.ds(at, rows), :] = pieces[by][...]
-            whole_ref[1 - core, pl.ds(at, rows), :] = pieces[4 + by][...]
+    for by in range(4):
+        rows = pieces[by].shape[0]
+        at = pl.multiple_of(((where_ref[1] + 4 - by) & 3) * rows, 8)
+        joined[core, pl.ds(at, rows), :] = pieces[by][...]
+        joined[1 - core, pl.ds(at, rows), :] = pieces[4 + by][...]
+    for tap in range(6):
+        rows = slice(tap * LANES, (tap + 1) * LANES)
+        conv_ref[3 + tap, pl.ds(pl.multiple_of(core * LANES, LANES), LANES), :] = inner[0][rows, :]
+        conv_ref[3 + tap, pl.ds(pl.multiple_of((1 - core) * LANES, LANES), LANES), :] = inner[1][rows, :]
     for half in range(2):
         lanes = slice(half * LANES, (half + 1) * LANES)
-        for tap in range(6):
-            conv_ref[3 + tap, lanes, :] = scratch[0][half, tap * LANES : (tap + 1) * LANES, :]
         for tap in range(3):
-            conv_ref[tap, lanes, :] = scratch[1][half, tap * LANES : (tap + 1) * LANES, :]
+            conv_ref[tap, lanes, :] = joined[half, tap * LANES : (tap + 1) * LANES, :]
         for n in range(expand_ref.shape[1] // channels):
             at = (3 + n) * LANES
-            expand_ref[lanes, n * channels : (n + 1) * channels] = scratch[1][half, at : at + LANES, :]
+            expand_ref[lanes, n * channels : (n + 1) * channels] = joined[half, at : at + LANES, :]
 
 
 def assemble(where, groups, channels, deep):
@@ -257,7 +282,7 @@
         ),
         in_specs=[scalars()] + [whole()] * len(refs),
         out_specs=(whole(), whole()),
-        scratch_shapes=[pltpu.VMEM((2, 4 * group[0].shape[0], channels), jnp.float32) for group in groups],
+        scratch_shapes=[pltpu.VMEM((2, 4 * groups[1][0].shape[0], channels), jnp.float32)],
         compiler_params=params(),
         cost_estimate=pl.CostEstimate(flops=0, bytes_accessed=7 * 10**6, transcendentals=0),
         name="assemble",
@@ -272,7 +297,7 @@
     cotangent = deep_cotangent[0].reshape(all_rows * band, deep)
     share = tissue_tiles.astype(jnp.float32) / TILES
     core = lax.axis_index("core").astype(jnp.int32)
-    where = jnp.stack([core, lax.axis_index("y"), lax.axis_index("x")]).astype(jnp.int32)
+    where = jnp.stack([core, lax.axis_index("x")]).astype(jnp.int32)
 
     hidden = lax.dot_general(
         (cotangent.astype(jnp.float32) * share[:, None]).astype(jnp.bfloat16),
@@ -286,7 +311,8 @@
     sent = jnp.concatenate(
         [hidden.reshape(devices, chunk, channels), active.reshape(devices, chunk, channels)], axis=1
     )
-    blocks, weighted = prepare(share, stem_input[0], cotangent)
+    above = shifted(stem_input[0, -1:], 1)
+    blocks, weighted = prepare(share, above, stem_input[0], cotangent)
     arrived = exchange(sent, SPACE)
     hidden = arrived[:, :chunk].reshape(devices, out_rows, band, channels).transpose(1, 0, 2, 3)
     hidden = hidden.reshape(out_rows, out_cols, channels)
@@ -301,7 +327,6 @@
         where[:1],
         blocks,
         grad,
-        below,
         active,
         weighted,
         scratch=[pltpu.VMEM((channels, all_rows * band), jnp.bfloat16)],
@@ -312,11 +337,7 @@
     scale = float(samples_all * all_rows * out_cols) ** (-0.5)
     inner = own_inner + swapped(other_inner, "core", 1)
     outer = own_outer + swapped(other_outer, "core", 1)
-    inner = scatter_sum(scatter_sum(inner, "y"), "x")
-    outer = scatter_sum(scatter_sum(outer, "x"), "y")
-    inner, outer = sum_along_z([inner, outer], scale)
-    inner = gather_pieces(gather(inner, "x"), "y")
-    outer = gather_pieces(gather(outer, "y"), "x")
+    inner, outer, grad_input = total_sums(inner, outer, scale, grad_input)
     groups = [pieces + [swapped(piece, "core", 1) for piece in pieces] for pieces in (inner, outer)]
     grad_conv, grad_expand = assemble(where, groups, channels, deep)
     return (grad_input[None], grad_conv.reshape(3, 3, channels, channels), grad_expand)

time: 152 us -> 142 us (0.934)
  starting transfers between devices: 73.1 us -> 61 us
  local copies, waits for them, and re-layouts: 4.3 us -> 9.15 us
  waiting for transfers between devices: 55.9 us -> 52.4 us
    ppermute x14 -> x9, starting transfers between devices: 28.5 us -> 12.1 us  [swapped(): return lax.ppermute(x, axis, [(i, i ^ bit) for i in range(SIZES[axis])])]
    ppermute x24 -> x9, starting transfers between devices: 31.1 us -> 15.9 us  [rotated(): return lax.ppermute(x, axis, [(i, (i + by) % size) for i in range(size)])]
    ppermute x24 -> x9, waiting for transfers between devices: 28.8 us -> 14.1 us  [rotated(): return lax.ppermute(x, axis, [(i, (i + by) % size) for i in range(size)])]
    all_to_all x1 -> x3, waiting for transfers between devices: 11.1 us -> 0.01 us  [exchange(): return lax.all_to_all(x, axis, split_axis=0, concat_axis=0, tiled=True)]
    ppermute x1 -> x2, waiting for transfers between devices: 6.73 us -> 17.6 us  [shifted(): return lax.ppermute(x, SPACE, pairs)]
    all_to_all x1 -> x3, starting transfers between devices: 12.1 us -> 21.1 us  [exchange(): return lax.all_to_all(x, axis, split_axis=0, concat_axis=0, tiled=True)]
    ppermute x0 -> x6, starting transfers between devices: none -> 7.54 us  [turned(): return lax.ppermute(x, ('x', 'z', 'y'), pairs)]
    ppermute x0 -> x6, waiting for transfers between devices: none -> 6.64 us  [turned(): return lax.ppermute(x, ('x', 'z', 'y'), pairs)]
  transfers between devices with their start and end apart: 40 -> 29, of which waited for: 18 -> 20; matrix products, arithmetic and copies ran while one was open for 3% -> 1% of each run, Pallas kernels for 3% -> 3%
where the time goes in v3:
time: 142 us
  starting transfers between devices  61 us (43%)
  waiting for transfers between devices  52.4 us (37%)
  local copies, waits for them, and re-layouts  9.15 us (6%)
  Pallas kernels  8.23 us (6%)
  other arithmetic  7.5 us (5%)
  matrix products  1.79 us (1%)
  between operations  1.59 us (1%)
    all_to_all x3, starting transfers between devices, exchange(): return lax.all_to_all(x, axis, split_axis=0, concat_axis=0, tiled=True)  21.1 us
    ppermute x2, waiting for transfers between devices, shifted(): return lax.ppermute(x, SPACE, pairs)  17.6 us
    ppermute x9, starting transfers between devices, rotated(): return lax.ppermute(x, axis, [(i, (i + by) % size) for i in range(size)])  15.9 us
    ppermute x9, waiting for transfers between devices, rotated(): return lax.ppermute(x, axis, [(i, (i + by) % size) for i in range(size)])  14.1 us
    ppermute x9, waiting for transfers between devices, swapped(): return lax.ppermute(x, axis, [(i, i ^ bit) for i in range(SIZES[axis])])  14.1 us
    ppermute x9, starting transfers between devices, swapped(): return lax.ppermute(x, axis, [(i, i ^ bit) for i in range(SIZES[axis])])  12.1 us
    ppermute x6, starting transfers between devices, turned(): return lax.ppermute(x, ('x', 'z', 'y'), pairs)  7.54 us
    ppermute x6, waiting for transfers between devices, turned(): return lax.ppermute(x, ('x', 'z', 'y'), pairs)  6.64 us
  transfers between devices with their start and end apart: 29, of which 20 were waited for; matrix products, arithmetic and copies ran while one was open for 1% of the time, Pallas kernels for 3%

profile of v3, /device:TPU:1, one launch (start us, length us, event | category | flops | bytes accessed | tf_op | source)
XLA Modules:
  0.0 141.7 jit_solution(16292326885518762386)
XLA Ops:
  2.4 1.8 %convolution_convert_fusion = bf16[512,256]{1,0:T(8,128)(2,1)S(1)} fusion(bf16[256,1024]{1,0:T(8,128)(2,1)S(1)} %copy-done, f32[]{:T(128)} %bitcast.5, bf16[1,64,8,1024]{3,2,1,0:T(8,128)(2,1)} %param.8), kind=kOutput, calls=%fused_computation.1 | convolution fusion | flops 270139392 | bytes 1835012 | tf_op jit(solution)/shard_map/dot_general | solution.py:302
  5.0 12.0 %all-to-all-start = ((bf16[32,32,256]{2,1,0:T(8,128)(2,1)}), bf16[32,32,256]{2,1,0:T(8,128)(2,1)}, u32[]{:S(2)}, u32[]{:S(2)}) async-start(bf16[32,32,256]{2,1,0:T(8,128)(2,1)} %pad_maximum_fusion), calls=%async_computation | async-start | bytes 1048576 | tf_op jit(solution)/shard_map/all_to_all | solution.py:169
  17.1 3.1 %collective-permute-start = (bf16[1,512,256]{2,1,0:T(8,128)(2,1)S(1)}, bf16[1,512,256]{2,1,0:T(8,128)(2,1)S(1)}, u32[]{:S(2)}, u32[]{:S(2)}) collective-permute-start(bf16[1,512,256]{2,1,0:T(8,128)(2,1)S(1)} %slice_bitcast_fusion.1), channel_id=1, source_target_pairs={{0,8},{8,16},{16,24},{24,32},{32,40},{40,48},{48,56},{56,64},{64,7... | collective-permute-start | bytes 786440 | tf_op jit(solution)/shard_map/ppermute | solution.py:34
  20.2 12.8 %collective-permute-done.above_ref = bf16[1,512,256]{2,1,0:T(8,128)(2,1)S(1)} collective-permute-done((bf16[1,512,256]{2,1,0:T(8,128)(2,1)S(1)}, bf16[1,512,256]{2,1,0:T(8,128)(2,1)S(1)}, u32[]{:S(2)}, u32[]{:S(2)}) %collective-permute-start) | collective-permute-done | bytes 262176 | tf_op jit(solution)/shard_map/ppermute | solution.py:34
  42.4 1.7 %collective-permute-start.2 = (f32[896,256]{1,0:T(8,128)}, f32[896,256]{1,0:T(8,128)}, u32[]{:S(2)}, u32[]{:S(2)}) collective-permute-start(f32[896,256]{1,0:T(8,128)} %get-tuple-element.34), channel_id=1, source_target_pairs={{0,1},{1,0},{2,3},{3,2},{4,5},{5,4},{6,7},{7,6},{8,9},{9,8},{10,11... | collective-permute-start | bytes 2752520 | tf_op jit(solution)/shard_map/ppermute | solution.py:196
  45.3 2.5 %collective-permute-done.1 = f32[768,256]{1,0:T(8,128)S(1)} collective-permute-done((f32[768,256]{1,0:T(8,128)}, f32[768,256]{1,0:T(8,128)S(1)}, u32[]{:S(2)}, u32[]{:S(2)}) %collective-permute-start.1) | collective-permute-done | bytes 786464 | tf_op jit(solution)/shard_map/ppermute | solution.py:196
  48.8 2.2 %add.66 = f32[896,256]{1,0:T(8,128)} add(f32[896,256]{1,0:T(8,128)S(1)} %copy-done.7, f32[896,256]{1,0:T(8,128)} %collective-permute-done.2) | non-fusion elementwise | flops 229376 | bytes 2752512 | tf_op jit(solution)/shard_map/add | solution.py:339
  51.0 2.2 %dynamic-slice_bitcast_fusion = (f32[224,256]{1,0:T(8,128)}, f32[224,256]{1,0:T(8,128)}, f32[224,256]{1,0:T(8,128)}) fusion(f32[4,224,256]{2,1,0:T(8,128)} %bitcast.15, u32[]{:T(128)S(6)} %and.26, u32[]{:T(128)S(6)} %and.25, u32[]{:T(128)S(6)} %and.24), kind=kLoop, calls=%fused_computation.23 | loop fusion | bytes 1376268 | tf_op jit(solution)/shard_map/squeeze | solution.py:178
  53.2 4.2 %all-to-all-start.1 = ((f32[4,192,256]{2,1,0:T(8,128)}), f32[4,192,256]{2,1,0:T(8,128)S(1)}, u32[]{:S(2)}, u32[]{:S(2)}) async-start(f32[4,192,256]{2,1,0:T(8,128)} %bitcast.13), calls=%async_computation.1 | async-start | bytes 1572864 | tf_op jit(solution)/shard_map/all_to_all | solution.py:169
  57.4 4.5 %collective-permute-start.3 = (f32[224,256]{1,0:T(8,128)}, f32[224,256]{1,0:T(8,128)S(1)}, u32[]{:S(2)}, u32[]{:S(2)}) collective-permute-start(f32[224,256]{1,0:T(8,128)} %get-tuple-element.36), channel_id=1, source_target_pairs={{0,64},{64,128},{128,192},{192,0},{1,65},{65,129},{129,193},{193,1... | collective-permute-start | bytes 688136 | tf_op jit(solution)/shard_map/ppermute | solution.py:188
  61.8 2.7 %collective-permute-start.4 = (f32[224,256]{1,0:T(8,128)}, f32[224,256]{1,0:T(8,128)S(1)}, u32[]{:S(2)}, u32[]{:S(2)}) collective-permute-start(f32[224,256]{1,0:T(8,128)} %get-tuple-element.37), channel_id=1, source_target_pairs={{0,128},{64,192},{128,0},{192,64},{1,129},{65,193},{129,1},{193,65... | collective-permute-start | bytes 688136 | tf_op jit(solution)/shard_map/ppermute | solution.py:188
  66.7 4.8 %collective-permute-done.6.below_ref = bf16[1,256,256]{2,1,0:T(8,128)(2,1)S(1)} collective-permute-done((bf16[1,256,256]{2,1,0:T(8,128)(2,1)S(1)}, bf16[1,256,256]{2,1,0:T(8,128)(2,1)S(1)}, u32[]{:S(2)}, u32[]{:S(2)}) %collective-permute-start.6) | collective-permute-done | bytes 131104 | tf_op jit(solution)/shard_map/ppermute | solution.py:34
  71.6 1.9 %input_grad.1 = bf16[4,512,256]{2,1,0:T(8,128)(2,1)} custom-call(bf16[2,256,256]{2,1,0:T(8,128)(2,1)S(1)} %bitcast_select_fusion.grad_ref, bf16[1,256,256]{2,1,0:T(8,128)(2,1)S(1)} %collective-permute-done.6.below_ref, bf16[3,3,256,256]{3,2,1,0:T(8,128)(2,1)S(1)} %copy-done.2), custom_call_target="tpu_custom_call" | custom-call | flops 604000000 | bytes 3000000 | tf_op jit(solution)/shard_map/input_grad/pallas_call | solution.py:156
  73.5 1.5 %collective-permute-done.4 = f32[224,256]{1,0:T(8,128)S(1)} collective-permute-done((f32[224,256]{1,0:T(8,128)}, f32[224,256]{1,0:T(8,128)S(1)}, u32[]{:S(2)}, u32[]{:S(2)}) %collective-permute-start.4) | collective-permute-done | bytes 229408 | tf_op jit(solution)/shard_map/ppermute | solution.py:188
  76.4 5.8 %collective-permute-done.7 = f32[224,256]{1,0:T(8,128)S(1)} collective-permute-done((f32[224,256]{1,0:T(8,128)S(1)}, f32[224,256]{1,0:T(8,128)S(1)}, u32[]{:S(2)}, u32[]{:S(2)}) %collective-permute-start.7) | collective-permute-done | bytes 229408 | tf_op jit(solution)/shard_map/ppermute | solution.py:196
  82.2 1.4 collective-permute-start.8
  83.6 3.4 %collective-permute-start.9 = (f32[56,256]{1,0:T(8,128)S(1)}, f32[56,256]{1,0:T(8,128)S(1)}, u32[]{:S(2)}, u32[]{:S(2)}) collective-permute-start(f32[56,256]{1,0:T(8,128)S(1)} %get-tuple-element.45), channel_id=1, source_target_pairs={{0,128},{2,130},{4,132},{6,134},{8,12},{10,14},{12,8},{14,10},{16,... | collective-permute-start | bytes 172040 | tf_op jit(solution)/shard_map/ppermute | solution.py:206
  87.4 1.9 %collective-permute-done.9 = f32[56,256]{1,0:T(8,128)S(1)} collective-permute-done((f32[56,256]{1,0:T(8,128)S(1)}, f32[56,256]{1,0:T(8,128)S(1)}, u32[]{:S(2)}, u32[]{:S(2)}) %collective-permute-start.9) | collective-permute-done | bytes 57376 | tf_op jit(solution)/shard_map/ppermute | solution.py:206
  89.3 1.7 %collective-permute-done.10 = f32[56,256]{1,0:T(8,128)S(1)} collective-permute-done((f32[56,256]{1,0:T(8,128)S(1)}, f32[56,256]{1,0:T(8,128)S(1)}, u32[]{:S(2)}, u32[]{:S(2)}) %collective-permute-start.10) | collective-permute-done | bytes 57376 | tf_op jit(solution)/shard_map/ppermute | solution.py:206
  91.0 1.5 %collective-permute-start.13 = (f32[56,256]{1,0:T(8,128)S(1)}, f32[56,256]{1,0:T(8,128)S(1)}, u32[]{:S(2)}, u32[]{:S(2)}) collective-permute-start(f32[56,256]{1,0:T(8,128)S(1)} %fusion.10), channel_id=1, source_target_pairs={{0,48},{8,56},{16,0},{24,8},{32,16},{40,24},{48,32},{56,40},{1,49}... | collective-permute-start | bytes 172040 | tf_op jit(solution)/shard_map/ppermute | solution.py:188
  93.4 2.8 %collective-permute-start.11 = (f32[56,256]{1,0:T(8,128)S(1)}, f32[56,256]{1,0:T(8,128)S(1)}, u32[]{:S(2)}, u32[]{:S(2)}) collective-permute-start(f32[56,256]{1,0:T(8,128)S(1)} %fusion.10), channel_id=1, source_target_pairs={{0,32},{8,40},{16,48},{24,56},{32,0},{40,8},{48,16},{56,24},{1,33}... | collective-permute-start | bytes 172040 | tf_op jit(solution)/shard_map/ppermute | solution.py:188
  96.2 1.4 %collective-permute-done.12 = f32[56,256]{1,0:T(8,128)S(1)} collective-permute-done((f32[56,256]{1,0:T(8,128)S(1)}, f32[56,256]{1,0:T(8,128)S(1)}, u32[]{:S(2)}, u32[]{:S(2)}) %collective-permute-start.12) | collective-permute-done | bytes 57376 | tf_op jit(solution)/shard_map/ppermute | solution.py:188
  97.6 3.1 %collective-permute-done.11 = f32[56,256]{1,0:T(8,128)S(1)} collective-permute-done((f32[56,256]{1,0:T(8,128)S(1)}, f32[56,256]{1,0:T(8,128)S(1)}, u32[]{:S(2)}, u32[]{:S(2)}) %collective-permute-start.11) | collective-permute-done | bytes 57376 | tf_op jit(solution)/shard_map/ppermute | solution.py:188
  100.8 2.4 %collective-permute-start.15 = (f32[56,256]{1,0:T(8,128)S(1)}, f32[56,256]{1,0:T(8,128)S(1)}, u32[]{:S(2)}, u32[]{:S(2)}) collective-permute-start(f32[56,256]{1,0:T(8,128)S(1)} %get-tuple-element.56), channel_id=1, source_target_pairs={{0,128},{2,130},{4,132},{6,134},{8,12},{10,14},{12,8},{14,10},{16,... | collective-permute-start | bytes 172040 | tf_op jit(solution)/shard_map/ppermute | solution.py:206
  103.5 2.2 %collective-permute-done.14 = f32[56,256]{1,0:T(8,128)S(1)} collective-permute-done((f32[56,256]{1,0:T(8,128)S(1)}, f32[56,256]{1,0:T(8,128)S(1)}, u32[]{:S(2)}, u32[]{:S(2)}) %collective-permute-start.14) | collective-permute-done | bytes 57376 | tf_op jit(solution)/shard_map/ppermute | solution.py:206
  107.5 3.6 %collective-permute-done.17 = f32[224,256]{1,0:T(8,128)S(1)} collective-permute-done((f32[224,256]{1,0:T(8,128)S(1)}, f32[224,256]{1,0:T(8,128)S(1)}, u32[]{:S(2)}, u32[]{:S(2)}) %collective-permute-start.17) | collective-permute-done | bytes 229408 | tf_op jit(solution)/shard_map/ppermute | solution.py:196
  112.1 5.0 %all-to-all-start.2 = ((f32[4,192,256]{2,1,0:T(8,128)}), f32[4,192,256]{2,1,0:T(8,128)S(1)}, u32[]{:S(2)}, u32[]{:S(2)}) async-start(f32[4,192,256]{2,1,0:T(8,128)} %broadcast_in_dim.28), calls=%async_computation.2 | async-start | bytes 1572864 | tf_op jit(solution)/shard_map/all_to_all | solution.py:169
  117.1 1.8 %collective-permute-start.20 = (f32[224,256]{1,0:T(8,128)S(1)}, f32[224,256]{1,0:T(8,128)S(1)}, u32[]{:S(2)}, u32[]{:S(2)}) collective-permute-start(f32[224,256]{1,0:T(8,128)S(1)} %broadcast_select_fusion.refs_2_), channel_id=1, source_target_pairs={{0,192},{64,0},{128,64},{192,128},{1,193},{65,1},{129,65},{193,129... | collective-permute-start | bytes 688136 | tf_op jit(solution)/shard_map/ppermute | solution.py:188
  119.7 4.6 %collective-permute-done.20.refs_5_ = f32[224,256]{1,0:T(8,128)S(1)} collective-permute-done((f32[224,256]{1,0:T(8,128)S(1)}, f32[224,256]{1,0:T(8,128)S(1)}, u32[]{:S(2)}, u32[]{:S(2)}) %collective-permute-start.20) | collective-permute-done | bytes 229408 | tf_op jit(solution)/shard_map/ppermute | solution.py:188
  125.4 2.4 %collective-permute-done.18.refs_3_ = f32[224,256]{1,0:T(8,128)S(1)} collective-permute-done((f32[224,256]{1,0:T(8,128)S(1)}, f32[224,256]{1,0:T(8,128)S(1)}, u32[]{:S(2)}, u32[]{:S(2)}) %collective-permute-start.18) | collective-permute-done | bytes 229408 | tf_op jit(solution)/shard_map/ppermute | solution.py:188
  127.8 8.0 %collective-permute-start.21 = (f32[768,256]{1,0:T(8,128)S(1)}, f32[768,256]{1,0:T(8,128)S(1)}, u32[]{:S(2)}, u32[]{:S(2)}) collective-permute-start(f32[768,256]{1,0:T(8,128)S(1)} %bitcast.81), channel_id=1, source_target_pairs={{0,1},{1,0},{2,3},{3,2},{4,5},{5,4},{6,7},{7,6},{8,9},{9,8},{10,11... | collective-permute-start | bytes 2359304 | tf_op jit(solution)/shard_map/ppermute | solution.py:196
  139.1 2.6 %assemble.1 = (f32[9,256,256]{2,1,0:T(8,128)}, f32[256,1024]{1,0:T(8,128)}) custom-call(s32[2]{0:T(128)S(1)} %pad_add_fusion.where_ref, f32[768,256]{1,0:T(8,128)S(1)} %bitcast.82, f32[768,256]{1,0:T(8,128)S(1)} %collective-permute-done.21.refs_1_, f32[224,256]{1,0:T(8,128)S(1)} %broadcast_select_fusion.refs_2_, ...), custom_call_target="tpu_custom_call" | custom-call | bytes 7000000 | tf_op jit(solution)/shard_map/assemble/pallas_call | solution.py:277
  (76 shorter events, 26.7 us)
Async XLA Ops:
  2.4 14.7 %copy-start.1 = (bf16[1,4,512,256]{3,2,1,0:T(8,128)(2,1)S(1)}, bf16[1,4,512,256]{3,2,1,0:T(8,128)(2,1)}, u32[]{:S(2)}) copy-start(bf16[1,4,512,256]{3,2,1,0:T(8,128)(2,1)} %param.6) | copy-start | bytes 3145732
  5.0 32.8 %all-to-all-start = ((bf16[32,32,256]{2,1,0:T(8,128)(2,1)}), bf16[32,32,256]{2,1,0:T(8,128)(2,1)}, u32[]{:S(2)}, u32[]{:S(2)}) async-start(bf16[32,32,256]{2,1,0:T(8,128)(2,1)} %pad_maximum_fusion), calls=%async_computation | async-start | bytes 1048576 | tf_op jit(solution)/shard_map/all_to_all | solution.py:169
  17.1 15.9 %collective-permute-start = (bf16[1,512,256]{2,1,0:T(8,128)(2,1)S(1)}, bf16[1,512,256]{2,1,0:T(8,128)(2,1)S(1)}, u32[]{:S(2)}, u32[]{:S(2)}) collective-permute-start(bf16[1,512,256]{2,1,0:T(8,128)(2,1)S(1)} %slice_bitcast_fusion.1), channel_id=1, source_target_pairs={{0,8},{8,16},{16,24},{24,32},{32,40},{40,48},{48,56},{56,64},{64,7... | collective-permute-start | bytes 786440 | tf_op jit(solution)/shard_map/ppermute | solution.py:34
  42.4 6.4 %collective-permute-start.2 = (f32[896,256]{1,0:T(8,128)}, f32[896,256]{1,0:T(8,128)}, u32[]{:S(2)}, u32[]{:S(2)}) collective-permute-start(f32[896,256]{1,0:T(8,128)} %get-tuple-element.34), channel_id=1, source_target_pairs={{0,1},{1,0},{2,3},{3,2},{4,5},{5,4},{6,7},{7,6},{8,9},{9,8},{10,11... | collective-permute-start | bytes 2752520 | tf_op jit(solution)/shard_map/ppermute | solution.py:196
  45.3 3.5 %copy-start.7 = (f32[896,256]{1,0:T(8,128)S(1)}, f32[896,256]{1,0:T(8,128)}, u32[]{:S(2)}) copy-start(f32[896,256]{1,0:T(8,128)} %copy-done.6) | copy-start | bytes 2752516
  45.3 2.5 %collective-permute-start.1 = (f32[768,256]{1,0:T(8,128)}, f32[768,256]{1,0:T(8,128)S(1)}, u32[]{:S(2)}, u32[]{:S(2)}) collective-permute-start(f32[768,256]{1,0:T(8,128)} %get-tuple-element.31), channel_id=1, source_target_pairs={{0,1},{1,0},{2,3},{3,2},{4,5},{5,4},{6,7},{7,6},{8,9},{9,8},{10,11... | collective-permute-start | bytes 2359304 | tf_op jit(solution)/shard_map/ppermute | solution.py:196
  51.0 20.6 %copy-start.2 = (bf16[3,3,256,256]{3,2,1,0:T(8,128)(2,1)S(1)}, bf16[3,3,256,256]{3,2,1,0:T(8,128)(2,1)}, u32[]{:S(2)}) copy-start(bf16[3,3,256,256]{3,2,1,0:T(8,128)(2,1)} %weight_ref.1) | copy-start | bytes 3538948
  53.2 21.8 %all-to-all-start.1 = ((f32[4,192,256]{2,1,0:T(8,128)}), f32[4,192,256]{2,1,0:T(8,128)S(1)}, u32[]{:S(2)}, u32[]{:S(2)}) async-start(f32[4,192,256]{2,1,0:T(8,128)} %bitcast.13), calls=%async_computation.1 | async-start | bytes 1572864 | tf_op jit(solution)/shard_map/all_to_all | solution.py:169
  57.4 16.1 %collective-permute-start.3 = (f32[224,256]{1,0:T(8,128)}, f32[224,256]{1,0:T(8,128)S(1)}, u32[]{:S(2)}, u32[]{:S(2)}) collective-permute-start(f32[224,256]{1,0:T(8,128)} %get-tuple-element.36), channel_id=1, source_target_pairs={{0,64},{64,128},{128,192},{192,0},{1,65},{65,129},{129,193},{193,1... | collective-permute-start | bytes 688136 | tf_op jit(solution)/shard_map/ppermute | solution.py:188
  61.8 13.1 %collective-permute-start.4 = (f32[224,256]{1,0:T(8,128)}, f32[224,256]{1,0:T(8,128)S(1)}, u32[]{:S(2)}, u32[]{:S(2)}) collective-permute-start(f32[224,256]{1,0:T(8,128)} %get-tuple-element.37), channel_id=1, source_target_pairs={{0,128},{64,192},{128,0},{192,64},{1,129},{65,193},{129,1},{193,65... | collective-permute-start | bytes 688136 | tf_op jit(solution)/shard_map/ppermute | solution.py:188
  64.6 10.4 %collective-permute-start.5 = (f32[224,256]{1,0:T(8,128)}, f32[224,256]{1,0:T(8,128)}, u32[]{:S(2)}, u32[]{:S(2)}) collective-permute-start(f32[224,256]{1,0:T(8,128)} %get-tuple-element.38), channel_id=1, source_target_pairs={{0,192},{64,0},{128,64},{192,128},{1,193},{65,1},{129,65},{193,129... | collective-permute-start | bytes 688136 | tf_op jit(solution)/shard_map/ppermute | solution.py:188
  65.4 6.1 %collective-permute-start.6 = (bf16[1,256,256]{2,1,0:T(8,128)(2,1)S(1)}, bf16[1,256,256]{2,1,0:T(8,128)(2,1)S(1)}, u32[]{:S(2)}, u32[]{:S(2)}) collective-permute-start(bf16[1,256,256]{2,1,0:T(8,128)(2,1)S(1)} %slice.22), channel_id=1, source_target_pairs={{8,0},{16,8},{24,16},{32,24},{40,32},{48,40},{56,48},{64,56},{72,6... | collective-permute-start | bytes 393224 | tf_op jit(solution)/shard_map/ppermute | solution.py:34
  76.2 5.9 %collective-permute-start.7 = (f32[224,256]{1,0:T(8,128)S(1)}, f32[224,256]{1,0:T(8,128)S(1)}, u32[]{:S(2)}, u32[]{:S(2)}) collective-permute-start(f32[224,256]{1,0:T(8,128)S(1)} %fusion.2), channel_id=1, source_target_pairs={{0,8},{8,0},{16,24},{24,16},{32,40},{40,32},{48,56},{56,48},{1,9},... | collective-permute-start | bytes 688136 | tf_op jit(solution)/shard_map/ppermute | solution.py:196
  82.2 5.2 %collective-permute-start.8 = (f32[56,256]{1,0:T(8,128)S(1)}, f32[56,256]{1,0:T(8,128)S(1)}, u32[]{:S(2)}, u32[]{:S(2)}) collective-permute-start(f32[56,256]{1,0:T(8,128)S(1)} %get-tuple-element.44), channel_id=1, source_target_pairs={{0,64},{2,66},{4,68},{6,70},{8,10},{10,12},{12,14},{14,8},{16,80},... | collective-permute-start | bytes 172040 | tf_op jit(solution)/shard_map/ppermute | solution.py:206
  83.6 5.6 %collective-permute-start.9 = (f32[56,256]{1,0:T(8,128)S(1)}, f32[56,256]{1,0:T(8,128)S(1)}, u32[]{:S(2)}, u32[]{:S(2)}) collective-permute-start(f32[56,256]{1,0:T(8,128)S(1)} %get-tuple-element.45), channel_id=1, source_target_pairs={{0,128},{2,130},{4,132},{6,134},{8,12},{10,14},{12,8},{14,10},{16,... | collective-permute-start | bytes 172040 | tf_op jit(solution)/shard_map/ppermute | solution.py:206
  87.0 3.9 %collective-permute-start.10 = (f32[56,256]{1,0:T(8,128)S(1)}, f32[56,256]{1,0:T(8,128)S(1)}, u32[]{:S(2)}, u32[]{:S(2)}) collective-permute-start(f32[56,256]{1,0:T(8,128)S(1)} %get-tuple-element.46), channel_id=1, source_target_pairs={{0,192},{2,194},{4,196},{6,198},{8,14},{10,8},{12,10},{14,12},{16,... | collective-permute-start | bytes 172040 | tf_op jit(solution)/shard_map/ppermute | solution.py:206
  91.0 5.2 %collective-permute-start.13 = (f32[56,256]{1,0:T(8,128)S(1)}, f32[56,256]{1,0:T(8,128)S(1)}, u32[]{:S(2)}, u32[]{:S(2)}) collective-permute-start(f32[56,256]{1,0:T(8,128)S(1)} %fusion.10), channel_id=1, source_target_pairs={{0,48},{8,56},{16,0},{24,8},{32,16},{40,24},{48,32},{56,40},{1,49}... | collective-permute-start | bytes 172040 | tf_op jit(solution)/shard_map/ppermute | solution.py:188
  92.5 5.1 %collective-permute-start.12 = (f32[56,256]{1,0:T(8,128)S(1)}, f32[56,256]{1,0:T(8,128)S(1)}, u32[]{:S(2)}, u32[]{:S(2)}) collective-permute-start(f32[56,256]{1,0:T(8,128)S(1)} %fusion.10), channel_id=1, source_target_pairs={{0,16},{8,24},{16,32},{24,40},{32,48},{40,56},{48,0},{56,8},{1,17}... | collective-permute-start | bytes 172040 | tf_op jit(solution)/shard_map/ppermute | solution.py:188
  93.4 7.3 %collective-permute-start.11 = (f32[56,256]{1,0:T(8,128)S(1)}, f32[56,256]{1,0:T(8,128)S(1)}, u32[]{:S(2)}, u32[]{:S(2)}) collective-permute-start(f32[56,256]{1,0:T(8,128)S(1)} %fusion.10), channel_id=1, source_target_pairs={{0,32},{8,40},{16,48},{24,56},{32,0},{40,8},{48,16},{56,24},{1,33}... | collective-permute-start | bytes 172040 | tf_op jit(solution)/shard_map/ppermute | solution.py:188
  100.8 4.9 %collective-permute-start.14 = (f32[56,256]{1,0:T(8,128)S(1)}, f32[56,256]{1,0:T(8,128)S(1)}, u32[]{:S(2)}, u32[]{:S(2)}) collective-permute-start(f32[56,256]{1,0:T(8,128)S(1)} %get-tuple-element.56), channel_id=1, source_target_pairs={{0,64},{2,66},{4,68},{6,70},{8,10},{10,12},{12,14},{14,8},{16,80},... | collective-permute-start | bytes 172040 | tf_op jit(solution)/shard_map/ppermute | solution.py:206
  100.8 4.8 %collective-permute-start.15 = (f32[56,256]{1,0:T(8,128)S(1)}, f32[56,256]{1,0:T(8,128)S(1)}, u32[]{:S(2)}, u32[]{:S(2)}) collective-permute-start(f32[56,256]{1,0:T(8,128)S(1)} %get-tuple-element.56), channel_id=1, source_target_pairs={{0,128},{2,130},{4,132},{6,134},{8,12},{10,14},{12,8},{14,10},{16,... | collective-permute-start | bytes 172040 | tf_op jit(solution)/shard_map/ppermute | solution.py:206
  103.2 3.0 %collective-permute-start.16 = (f32[56,256]{1,0:T(8,128)S(1)}, f32[56,256]{1,0:T(8,128)S(1)}, u32[]{:S(2)}, u32[]{:S(2)}) collective-permute-start(f32[56,256]{1,0:T(8,128)S(1)} %get-tuple-element.56), channel_id=1, source_target_pairs={{0,192},{2,194},{4,196},{6,198},{8,14},{10,8},{12,10},{14,12},{16,... | collective-permute-start | bytes 172040 | tf_op jit(solution)/shard_map/ppermute | solution.py:206
  106.3 4.9 %collective-permute-start.17 = (f32[224,256]{1,0:T(8,128)S(1)}, f32[224,256]{1,0:T(8,128)S(1)}, u32[]{:S(2)}, u32[]{:S(2)}) collective-permute-start(f32[224,256]{1,0:T(8,128)S(1)} %bitcast.86), channel_id=1, source_target_pairs={{0,8},{8,0},{16,24},{24,16},{32,40},{40,32},{48,56},{56,48},{1,9},... | collective-permute-start | bytes 688136 | tf_op jit(solution)/shard_map/ppermute | solution.py:196
  112.1 15.6 %all-to-all-start.2 = ((f32[4,192,256]{2,1,0:T(8,128)}), f32[4,192,256]{2,1,0:T(8,128)S(1)}, u32[]{:S(2)}, u32[]{:S(2)}) async-start(f32[4,192,256]{2,1,0:T(8,128)} %broadcast_in_dim.28), calls=%async_computation.2 | async-start | bytes 1572864 | tf_op jit(solution)/shard_map/all_to_all | solution.py:169
  117.1 7.3 %collective-permute-start.20 = (f32[224,256]{1,0:T(8,128)S(1)}, f32[224,256]{1,0:T(8,128)S(1)}, u32[]{:S(2)}, u32[]{:S(2)}) collective-permute-start(f32[224,256]{1,0:T(8,128)S(1)} %broadcast_select_fusion.refs_2_), channel_id=1, source_target_pairs={{0,192},{64,0},{128,64},{192,128},{1,193},{65,1},{129,65},{193,129... | collective-permute-start | bytes 688136 | tf_op jit(solution)/shard_map/ppermute | solution.py:188
  118.9 6.5 %collective-permute-start.19 = (f32[224,256]{1,0:T(8,128)S(1)}, f32[224,256]{1,0:T(8,128)S(1)}, u32[]{:S(2)}, u32[]{:S(2)}) collective-permute-start(f32[224,256]{1,0:T(8,128)S(1)} %broadcast_select_fusion.refs_2_), channel_id=1, source_target_pairs={{0,128},{64,192},{128,0},{192,64},{1,129},{65,193},{129,1},{193,65... | collective-permute-start | bytes 688136 | tf_op jit(solution)/shard_map/ppermute | solution.py:188
  119.7 8.0 %collective-permute-start.18 = (f32[224,256]{1,0:T(8,128)S(1)}, f32[224,256]{1,0:T(8,128)S(1)}, u32[]{:S(2)}, u32[]{:S(2)}) collective-permute-start(f32[224,256]{1,0:T(8,128)S(1)} %broadcast_select_fusion.refs_2_), channel_id=1, source_target_pairs={{0,64},{64,128},{128,192},{192,0},{1,65},{65,129},{129,193},{193,1... | collective-permute-start | bytes 688136 | tf_op jit(solution)/shard_map/ppermute | solution.py:188
  127.8 11.3 %collective-permute-start.21 = (f32[768,256]{1,0:T(8,128)S(1)}, f32[768,256]{1,0:T(8,128)S(1)}, u32[]{:S(2)}, u32[]{:S(2)}) collective-permute-start(f32[768,256]{1,0:T(8,128)S(1)} %bitcast.81), channel_id=1, source_target_pairs={{0,1},{1,0},{2,3},{3,2},{4,5},{5,4},{6,7},{7,6},{8,9},{9,8},{10,11... | collective-permute-start | bytes 2359304 | tf_op jit(solution)/shard_map/ppermute | solution.py:196
  135.8 2.2 %collective-permute-start.22 = (f32[224,256]{1,0:T(8,128)S(1)}, f32[224,256]{1,0:T(8,128)S(1)}, u32[]{:S(2)}, u32[]{:S(2)}) collective-permute-start(f32[224,256]{1,0:T(8,128)S(1)} %broadcast_select_fusion.refs_2_), channel_id=1, source_target_pairs={{0,1},{1,0},{2,3},{3,2},{4,5},{5,4},{6,7},{7,6},{8,9},{9,8},{10,11... | collective-permute-start | bytes 688136 | tf_op jit(solution)/shard_map/ppermute | solution.py:196
  135.8 2.6 %collective-permute-start.23 = (f32[224,256]{1,0:T(8,128)S(1)}, f32[224,256]{1,0:T(8,128)S(1)}, u32[]{:S(2)}, u32[]{:S(2)}) collective-permute-start(f32[224,256]{1,0:T(8,128)S(1)} %collective-permute-done.18.refs_3_), channel_id=1, source_target_pairs={{0,1},{1,0},{2,3},{3,2},{4,5},{5,4},{6,7},{7,6},{8,9},{9,8},{10,11... | collective-permute-start | bytes 688136 | tf_op jit(solution)/shard_map/ppermute | solution.py:196
  136.3 2.4 %collective-permute-start.24 = (f32[224,256]{1,0:T(8,128)S(1)}, f32[224,256]{1,0:T(8,128)S(1)}, u32[]{:S(2)}, u32[]{:S(2)}) collective-permute-start(f32[224,256]{1,0:T(8,128)S(1)} %collective-permute-done.19.refs_4_), channel_id=1, source_target_pairs={{0,1},{1,0},{2,3},{3,2},{4,5},{5,4},{6,7},{7,6},{8,9},{9,8},{10,11... | collective-permute-start | bytes 688136 | tf_op jit(solution)/shard_map/ppermute | solution.py:196
  136.3 2.7 %collective-permute-start.25 = (f32[224,256]{1,0:T(8,128)S(1)}, f32[224,256]{1,0:T(8,128)S(1)}, u32[]{:S(2)}, u32[]{:S(2)}) collective-permute-start(f32[224,256]{1,0:T(8,128)S(1)} %collective-permute-done.20.refs_5_), channel_id=1, source_target_pairs={{0,1},{1,0},{2,3},{3,2},{4,5},{5,4},{6,7},{7,6},{8,9},{9,8},{10,11... | collective-permute-start | bytes 688136 | tf_op jit(solution)/shard_map/ppermute | solution.py:196
  (7 other events, 8.7 us)

commit v4 on v3

--- a/solution.py
+++ b/solution.py
@@ -13,19 +13,26 @@
 SIZES = {"x": 4, "z": 8, "y": 4, "core": 2}
 SPACE = ("x", "z")
 REP = ("y", "core")
-VMEM_BYTES = 48 * 1024 * 1024
-
-
-def whole(*_):
+
+
+def whole():
     return pl.BlockSpec(memory_space=pltpu.VMEM)
+
+
+def far():
+    return pl.BlockSpec(memory_space=pl.ANY)
+
+
+def room(x):
+    return pltpu.VMEM(x.shape, x.dtype)
 
 
 def scalars():
     return pl.BlockSpec(memory_space=pltpu.SMEM)
 
 
-def params():
-    return pltpu.CompilerParams(vmem_limit_bytes=VMEM_BYTES)
+def params(mib=24):
+    return pltpu.CompilerParams(vmem_limit_bytes=mib * 1024 * 1024)
 
 
 def shifted(x, by):
@@ -34,90 +41,212 @@
     return lax.ppermute(x, SPACE, pairs)
 
 
-def prepare_kernel(share_ref, above_ref, x_ref, cotangent_ref, out_ref, weighted_ref, wide):
+def send_kernel(
+    share_ref, cotangent_hbm, weight_hbm, preact_hbm, sent_hbm, weighted_hbm,
+    cotangent_ref, weight_ref, preact_ref, weighted_ref, sent_ref, sems,
+):
+    pairs = ((preact_hbm, preact_ref), (weight_hbm, weight_ref), (cotangent_hbm, cotangent_ref))
+    copies = [pltpu.make_async_copy(a, b, sems.at[n]) for n, (a, b) in enumerate(pairs)]
+    for copy in copies:
+        copy.start()
+    devices, chunk, channels = sent_ref.shape
+    chunk = chunk // 2
+    rows, cols = preact_ref.shape[:2]
+    band = cols // devices
+    copies[0].wait()
+    for i in range(rows):
+        active = jnp.maximum(preact_ref[i].astype(jnp.float32), 0.0).reshape(devices, band, channels)
+        sent_ref[:, chunk + i * band : chunk + (i + 1) * band, :] = active.astype(jnp.bfloat16)
+    copies[1].wait()
+    copies[2].wait()
+    weighted = (cotangent_ref[...].astype(jnp.float32) * share_ref[0]).astype(jnp.bfloat16)
+    weighted_ref[...] = weighted
+    back = pltpu.make_async_copy(weighted_ref, weighted_hbm, sems.at[3])
+    back.start()
+    hidden = lax.dot_general(
+        weighted, weight_ref[...], (((1,), (1,)), ((), ())), preferred_element_type=jnp.float32
+    )
+    sent_ref[:, :chunk, :] = hidden.reshape(devices, chunk, channels).astype(jnp.bfloat16)
+    out = pltpu.make_async_copy(sent_ref, sent_hbm, sems.at[4])
+    out.start()
+    back.wait()
+    out.wait()
+
+
+def build_sent(share, cotangent, weight, preact, devices):
+    rows, cols, channels = preact.shape
+    sent = jax.ShapeDtypeStruct((devices, 2 * rows * cols // devices, channels), jnp.bfloat16)
+    return pl.pallas_call(
+        send_kernel,
+        out_shape=(
+            sent,
+            jax.ShapeDtypeStruct(cotangent.shape, jnp.bfloat16),
+        ),
+        in_specs=[scalars()] + [far()] * 3,
+        out_specs=(far(), far()),
+        scratch_shapes=[room(x) for x in (cotangent, weight, preact, cotangent, sent)]
+        + [pltpu.SemaphoreType.DMA((5,))],
+        compiler_params=params(60),
+        cost_estimate=pl.CostEstimate(flops=268 * 10**6, bytes_accessed=4 * 10**6, transcendentals=0),
+        name="build_sent",
+    )(share, cotangent, weight, preact)
+
+
+def prepare_kernel(x_ref, out_ref, wide):
     half = out_ref.shape[2]
     first = lax.broadcasted_iota(jnp.int32, (LANES, half), 1) == 0
-    for row in range(x_ref.shape[0] + 1):
-        source = above_ref.at[0] if row == 0 else x_ref.at[row - 1]
+    for row in range(x_ref.shape[0]):
         for part in range(x_ref.shape[2] // LANES):
             lanes = slice(part * LANES, (part + 1) * LANES)
-            wide[...] = source[:, lanes].astype(jnp.float32)
+            wide[...] = x_ref[row, :, lanes].astype(jnp.float32)
             even = wide[pl.ds(0, half, stride=2), :].T
             odd = wide[pl.ds(1, half, stride=2), :].T
             late = jnp.where(first, 0.0, pltpu.roll(odd, 1, 1))
             out_ref[3 * row, lanes, :] = late.astype(jnp.bfloat16)
             out_ref[3 * row + 1, lanes, :] = even.astype(jnp.bfloat16)
             out_ref[3 * row + 2, lanes, :] = odd.astype(jnp.bfloat16)
-    weighted_ref[...] = (cotangent_ref[...].astype(jnp.float32) * share_ref[0]).astype(jnp.bfloat16)
-
-
-def prepare(share, above, x, cotangent):
+
+
+def prepare(x):
     rows, cols, channels = x.shape
     return pl.pallas_call(
         prepare_kernel,
-        out_shape=(
-            jax.ShapeDtypeStruct((3 * rows + 3, channels, cols // 2), jnp.bfloat16),
-            jax.ShapeDtypeStruct(cotangent.shape, jnp.bfloat16),
-        ),
-        in_specs=[scalars(), whole(), whole(), whole()],
-        out_specs=(whole(), whole()),
+        out_shape=jax.ShapeDtypeStruct((3 * rows, channels, cols // 2), jnp.bfloat16),
+        in_specs=[whole()],
+        out_specs=whole(),
         scratch_shapes=[pltpu.VMEM((cols, LANES), jnp.float32)],
         compiler_params=params(),
-        cost_estimate=pl.CostEstimate(flops=10**7, bytes_accessed=5 * 10**6, transcendentals=0),
+        cost_estimate=pl.CostEstimate(flops=10**7, bytes_accessed=3 * 10**6, transcendentals=0),
         name="prepare",
-    )(share, above, x, cotangent)
-
-
-def half_taps(blocks_ref, grad_ref, row_tap, col_tap, start):
-    total = None
-    for i in range(2):
-        term = jnp.dot(
-            blocks_ref[3 * (2 * i + row_tap) + col_tap, pl.ds(start, LANES), :],
-            grad_ref[i],
-            preferred_element_type=jnp.float32,
-        )
-        total = term if total is None else total + term
-    return total
-
-
-def inner_kernel(core_ref, blocks_ref, grad_ref, own_ref, other_ref):
-    for out_ref, owner in ((other_ref, 1 - core_ref[0]), (own_ref, core_ref[0])):
-        start = pl.multiple_of(owner * LANES, LANES)
-        for row_tap in (1, 2):
-            for col_tap in range(3):
-                at = (3 * (row_tap - 1) + col_tap) * LANES
-                out_ref[at : at + LANES, :] = half_taps(blocks_ref, grad_ref, row_tap, col_tap, start)
-
-
-def outer_kernel(core_ref, blocks_ref, grad_ref, active_ref, weighted_ref, own_ref, other_ref, turned):
-    channels = grad_ref.shape[2]
-    turned[...] = active_ref[...].T
-    for out_ref, owner in ((other_ref, 1 - core_ref[0]), (own_ref, core_ref[0])):
+    )(x)
+
+
+def terms_kernel(
+    core_ref, arrived_hbm, preact_hbm, above_hbm, blocks_hbm, weighted_hbm,
+    own_inner, other_inner, own_outer, other_outer, grad_hbm,
+    arrived_ref, preact_ref, above_ref, blocks_ref, weighted_ref,
+    grad_ref, turned, inner_ref, outer_ref, sems,
+):
+    pairs = (
+        (arrived_hbm, arrived_ref),
+        (preact_hbm, preact_ref),
+        (blocks_hbm, blocks_ref),
+        (above_hbm, above_ref),
+        (weighted_hbm, weighted_ref),
+    )
+    copies = [pltpu.make_async_copy(a, b, sems.at[n]) for n, (a, b) in enumerate(pairs)]
+    for copy in copies:
+        copy.start()
+    devices, chunk, channels = arrived_ref.shape
+    rows, cols = preact_ref.shape[:2]
+    chunk, band = chunk // 2, cols // devices
+    copies[0].wait()
+    copies[1].wait()
+    for i in range(rows):
+        hidden = arrived_ref[:, i * band : (i + 1) * band, :].astype(jnp.float32).reshape(cols, channels)
+        kept = jnp.where(preact_ref[i].astype(jnp.float32) > 0.0, hidden, 0.0)
+        grad_ref[i] = kept.astype(jnp.bfloat16)
+    back = [pltpu.make_async_copy(grad_ref, grad_hbm, sems.at[5])]
+    back[0].start()
+    active = arrived_ref[:, chunk:, :].astype(jnp.float32).reshape(devices * chunk, channels)
+    turned[...] = active.T.astype(jnp.bfloat16)
+
+    def half_taps(row_tap, col_tap, start):
+        total = None
+        for i in range(rows):
+            row = 2 * i + row_tap - 1
+            source, at = (above_ref, col_tap) if row < 0 else (blocks_ref, 3 * row + col_tap)
+            term = jnp.dot(
+                source[at, pl.ds(start, LANES), :], grad_ref[i], preferred_element_type=jnp.float32
+            )
+            total = term if total is None else total + term
+        return total
+
+    for copy in copies[2:]:
+        copy.wait()
+    for n, (inner_hbm, outer_hbm) in enumerate(((other_inner, other_outer), (own_inner, own_outer))):
+        owner = core_ref[0] if n else 1 - core_ref[0]
         start = pl.multiple_of(owner * LANES, LANES)
         for col_tap in range(3):
+            for row_tap in (1, 2):
+                at = (3 * (row_tap - 1) + col_tap) * LANES
+                inner_ref[n, at : at + LANES, :] = half_taps(row_tap, col_tap, start)
+        back.append(pltpu.make_async_copy(inner_ref.at[n], inner_hbm, sems.at[6 + 2 * n]))
+        back[-1].start()
+        for col_tap in range(3):
             at = col_tap * LANES
-            out_ref[at : at + LANES, :] = half_taps(blocks_ref, grad_ref, 0, col_tap, start)
-        for n in range(weighted_ref.shape[1] // channels):
-            at = (3 + n) * LANES
-            out_ref[at : at + LANES, :] = jnp.dot(
+            outer_ref[n, at : at + LANES, :] = half_taps(0, col_tap, start)
+        for k in range(weighted_ref.shape[1] // channels):
+            at = (3 + k) * LANES
+            outer_ref[n, at : at + LANES, :] = jnp.dot(
                 turned[pl.ds(start, LANES), :],
-                weighted_ref[:, n * channels : (n + 1) * channels],
+                weighted_ref[:, k * channels : (k + 1) * channels],
                 preferred_element_type=jnp.float32,
             )
-
-
-def halves(kernel, rows, core, *arrays, scratch=()):
-    shape = jax.ShapeDtypeStruct((rows, 2 * LANES), jnp.float32)
-    return pl.pallas_call(
-        kernel,
-        out_shape=(shape, shape),
-        in_specs=[scalars()] + [whole()] * len(arrays),
-        out_specs=(whole(), whole()),
-        scratch_shapes=scratch,
-        compiler_params=params(),
-        cost_estimate=pl.CostEstimate(flops=400 * 10**6, bytes_accessed=4 * 10**6, transcendentals=0),
-        name="halves",
-    )(core, *arrays)
+        back.append(pltpu.make_async_copy(outer_ref.at[n], outer_hbm, sems.at[7 + 2 * n]))
+        back[-1].start()
+    for copy in back:
+        copy.wait()
+
+
+def terms(core, arrived, preact, above, blocks, weighted):
+    rows, cols, channels = preact.shape
+    inner = jax.ShapeDtypeStruct((6 * LANES, channels), jnp.float32)
+    outer = jax.ShapeDtypeStruct((3 * LANES + weighted.shape[1] // 2, channels), jnp.float32)
+    return pl.pallas_call(
+        terms_kernel,
+        out_shape=(inner, inner, outer, outer, jax.ShapeDtypeStruct(preact.shape, jnp.bfloat16)),
+        in_specs=[scalars()] + [far()] * 5,
+        out_specs=(far(),) * 5,
+        scratch_shapes=[room(x) for x in (arrived, preact, above, blocks, weighted, preact)]
+        + [
+            pltpu.VMEM((channels, weighted.shape[0]), jnp.bfloat16),
+            pltpu.VMEM((2,) + inner.shape, jnp.float32),
+            pltpu.VMEM((2,) + outer.shape, jnp.float32),
+            pltpu.SemaphoreType.DMA((10,)),
+        ],
+        compiler_params=params(54),
+        cost_estimate=pl.CostEstimate(flops=870 * 10**6, bytes_accessed=8 * 10**6, transcendentals=0),
+        name="terms",
+    )(core, arrived, preact, above, blocks, weighted)
+
+
+def combine_kernel(where_ref, *refs):
+    hbm, (inner_hbm, *outer_hbm), room_refs, sems = refs[:4], refs[4:9], refs[9:13], refs[13]
+    copies = [pltpu.make_async_copy(a, b, sems.at[n]) for n, (a, b) in enumerate(zip(hbm, room_refs))]
+    for copy in copies:
+        copy.start()
+    own_inner, got_inner, own_outer, got_outer = room_refs
+    rows = own_outer.shape[0] // 4
+    copies[0].wait()
+    copies[1].wait()
+    own_inner[...] += got_inner[...]
+    back = [pltpu.make_async_copy(own_inner, inner_hbm, sems.at[4])]
+    back[0].start()
+    copies[2].wait()
+    copies[3].wait()
+    own_outer[...] += got_outer[...]
+    for by, out in enumerate(outer_hbm):
+        at = pl.ds(pl.multiple_of(((where_ref[1] + by) & 3) * rows, 8), rows)
+        back.append(pltpu.make_async_copy(own_outer.at[at, :], out, sems.at[5 + by]))
+        back[-1].start()
+    for copy in back:
+        copy.wait()
+
+
+def combine(where, *arrays):
+    inner, outer = arrays[0], arrays[2]
+    chunk = jax.ShapeDtypeStruct((outer.shape[0] // 4, outer.shape[1]), jnp.float32)
+    return pl.pallas_call(
+        combine_kernel,
+        out_shape=(jax.ShapeDtypeStruct(inner.shape, jnp.float32),) + (chunk,) * 4,
+        in_specs=[scalars()] + [far()] * 4,
+        out_specs=(far(),) * 5,
+        scratch_shapes=[room(x) for x in arrays] + [pltpu.SemaphoreType.DMA((9,))],
+        compiler_params=params(24),
+        cost_estimate=pl.CostEstimate(flops=10**6, bytes_accessed=5 * 10**6, transcendentals=0),
+        name="combine",
+    )(where, *arrays)
 
 
 def input_kernel(grad_ref, below_ref, weight_ref, out_ref, wide):
@@ -215,14 +344,13 @@
 STEPS = (1, 2, 3)
 
 
-def total_sums(inner, outer, scale, beside):
-    inner, outer = split(inner), split(outer)
-    inner, parts = barrier((inner, [pick(outer, place("x", by)) for by in STEPS]))
+def total_sums(inner, outer, parts, scale, below, beside):
+    inner, parts, below = barrier((split(inner), parts, below))
     inner = exchange(inner, "y")
     moved = [rotated(p, "x", by) for p, by in zip(parts, STEPS)]
-    inner, moved, beside = barrier((inner, moved, beside))
+    inner, moved = barrier((inner, moved))
     inner = jnp.sum(inner, axis=0)
-    outer = sum(moved, pick(outer, place("x")))
+    outer = sum(moved, outer)
 
     rows = outer.shape[0] - inner.shape[0]
     both = jnp.stack([jnp.pad(inner, ((0, rows), (0, 0))), outer])
@@ -234,7 +362,8 @@
     moved = [turned(p, by) for p, by in zip(moved, STEPS)]
     part = sum(moved, pick(parts, turned_place()))
 
-    two, four, six = [rotated(part, "z", by) for by in (2, 4, 6)]
+    moved = [rotated(part, "z", by) for by in (2, 4, 6)]
+    (two, four, six), beside = barrier((moved, beside(below)))
     part = ((part + four) + (two + six)) * scale
 
     whole_part = jnp.zeros((4,) + part.shape, part.dtype)
@@ -299,45 +428,22 @@
     core = lax.axis_index("core").astype(jnp.int32)
     where = jnp.stack([core, lax.axis_index("x")]).astype(jnp.int32)
 
-    hidden = lax.dot_general(
-        (cotangent.astype(jnp.float32) * share[:, None]).astype(jnp.bfloat16),
-        expand_weight,
-        (((1,), (1,)), ((), ())),
-        preferred_element_type=jnp.float32,
-    ).astype(jnp.bfloat16)
-    active = jnp.maximum(preact, jnp.zeros_like(preact))
-    active = active.reshape(out_rows, devices, band, channels).transpose(1, 0, 2, 3)
-    chunk = out_rows * band
-    sent = jnp.concatenate(
-        [hidden.reshape(devices, chunk, channels), active.reshape(devices, chunk, channels)], axis=1
-    )
-    above = shifted(stem_input[0, -1:], 1)
-    blocks, weighted = prepare(share, above, stem_input[0], cotangent)
+    sent, weighted = build_sent(share, cotangent, expand_weight, preact, devices)
+    blocks = prepare(stem_input[0])
+    above = prepare(shifted(stem_input[0, -1:], 1))
     arrived = exchange(sent, SPACE)
-    hidden = arrived[:, :chunk].reshape(devices, out_rows, band, channels).transpose(1, 0, 2, 3)
-    hidden = hidden.reshape(out_rows, out_cols, channels)
-    active = arrived[:, chunk:].reshape(all_rows * band, channels)
-    grad = jnp.where(preact > 0, hidden, jnp.zeros_like(hidden))
+    own_inner, other_inner, own_outer, other_outer, grad = terms(
+        where[:1], arrived, preact, above, blocks, weighted
+    )
     below = shifted(grad[:1], -1)
-
-    own_inner, other_inner = halves(inner_kernel, 6 * LANES, where[:1], blocks, grad)
-    own_outer, other_outer = halves(
-        outer_kernel,
-        3 * LANES + deep // 2,
-        where[:1],
-        blocks,
-        grad,
-        active,
-        weighted,
-        scratch=[pltpu.VMEM((channels, all_rows * band), jnp.bfloat16)],
-    )
-    grad_input = input_grad(grad, below, conv_weight)
 
     samples_all = stem_input.shape[0] * SIZES["y"] * SIZES["core"]
     scale = float(samples_all * all_rows * out_cols) ** (-0.5)
-    inner = own_inner + swapped(other_inner, "core", 1)
-    outer = own_outer + swapped(other_outer, "core", 1)
-    inner, outer, grad_input = total_sums(inner, outer, scale, grad_input)
+    got_inner, got_outer = swapped(other_inner, "core", 1), swapped(other_outer, "core", 1)
+    inner, outer, *parts = combine(where, own_inner, got_inner, own_outer, got_outer)
+    inner, outer, grad_input = total_sums(
+        inner, outer, parts, scale, below, lambda b: input_grad(grad, b, conv_weight)
+    )
     groups = [pieces + [swapped(piece, "core", 1) for piece in pieces] for pieces in (inner, outer)]
     grad_conv, grad_expand = assemble(where, groups, channels, deep)
     return (grad_input[None], grad_conv.reshape(3, 3, channels, channels), grad_expand)

time: 142 us -> 136 us (0.958)
  other arithmetic: 7.5 us -> 0.4 us
  Pallas kernels: 8.23 us -> 15.1 us
  local copies, waits for them, and re-layouts: 9.15 us -> 6.94 us
  waiting for transfers between devices: 52.4 us -> 50.3 us
  matrix products: 1.79 us -> 0 us
    pallas_call x3 -> x5, Pallas kernels: 3.7 us -> 10.6 us  [the longest x1 4.3 us: terms(): pl.pallas_call(terms_kernel, out_shape=(inner, inner, outer, outer, jax.S...]
    ppermute x2, waiting for transfers between devices: 17.6 us -> 11.1 us  [shifted(): return lax.ppermute(x, SPACE, pairs)]
    ppermute x9, waiting for transfers between devices: 14.1 us -> 19.5 us  [rotated(): return lax.ppermute(x, axis, [(i, (i + by) % size) for i in range(size)])]
    add x2 -> x0, other arithmetic: 3.2 us -> none  [the longest x1 2.22 us: body(): outer = own_outer + swapped(other_outer, 'core', 1)]
    squeeze x2 -> x1, local copies, waits for them, and re-layouts: 2.2 us -> 0.02 us  [pick(): lax.dynamic_slice(parts, (index, zero, zero), (1,) + parts.shape[1:])[0]]
    dot_general x1 -> x0, matrix products: 1.79 us -> none  [body(): lax.dot_general((cotangent.astype(jnp.float32) * share[:, None]).astype(j...]
    all_to_all x3, starting transfers between devices: 21.1 us -> 19.6 us  [exchange(): return lax.all_to_all(x, axis, split_axis=0, concat_axis=0, tiled=True)]
    unnamed x20 -> x16, local copies, waits for them, and re-layouts: 4.79 us -> 5.01 us
  transfers between devices with their start and end apart: 29 -> 29, of which waited for: 20 -> 19; matrix products, arithmetic and copies ran while one was open for 1% -> 1% of each run, Pallas kernels for 3% -> 4%
where the time goes in v4:
time: 136 us; the launch traced here: 135 us
  starting transfers between devices  60.6 us (45%)
  waiting for transfers between devices  50.3 us (37%)
  Pallas kernels  15.1 us (11%)
  local copies, waits for them, and re-layouts  6.94 us (5%)
  between operations  1.63 us (1%)
    all_to_all x3, starting transfers between devices, exchange(): return lax.all_to_all(x, axis, split_axis=0, concat_axis=0, tiled=True)  19.6 us
    ppermute x9, waiting for transfers between devices, rotated(): return lax.ppermute(x, axis, [(i, (i + by) % size) for i in range(size)])  19.5 us
    ppermute x9, starting transfers between devices, rotated(): return lax.ppermute(x, axis, [(i, (i + by) % size) for i in range(size)])  15.6 us
    ppermute x9, waiting for transfers between devices, swapped(): return lax.ppermute(x, axis, [(i, i ^ bit) for i in range(SIZES[axis])])  13 us
    ppermute x9, starting transfers between devices, swapped(): return lax.ppermute(x, axis, [(i, i ^ bit) for i in range(SIZES[axis])])  12.6 us
    ppermute x2, waiting for transfers between devices, shifted(): return lax.ppermute(x, SPACE, pairs)  11.1 us
    ppermute x6, starting transfers between devices, turned(): return lax.ppermute(x, ('x', 'z', 'y'), pairs)  8.52 us
    ppermute x6, waiting for transfers between devices, turned(): return lax.ppermute(x, ('x', 'z', 'y'), pairs)  6.56 us
  transfers between devices with their start and end apart: 29, of which 19 were waited for; matrix products, arithmetic and copies ran while one was open for 1% of the time, Pallas kernels for 4%

profile of v4, /device:TPU:1, one launch (start us, length us, event | category | flops | bytes accessed | tf_op | source)
XLA Modules:
  0.0 135.0 jit_solution(17161232524526347843)
XLA Ops:
  1.4 2.9 %build_sent.1 = (bf16[32,32,256]{2,1,0:T(8,128)(2,1)}, bf16[512,1024]{1,0:T(8,128)(2,1)}) custom-call(f32[1]{0:T(128)S(6)} %div.3.share_ref, bf16[512,1024]{1,0:T(8,128)(2,1)} %bitcast.49, bf16[256,1024]{1,0:T(8,128)(2,1)} %weight_hbm.1, bf16[2,256,256]{2,1,0:T(8,128)(2,1)} %bitcast.51), custom_call_target="tpu_custom_call" | custom-call | flops 268000000 | bytes 4000000 | tf_op jit(solution)/shard_map/build_sent/pallas_call | solution.py:79
  4.3 11.9 %all-to-all-start = ((bf16[32,32,256]{2,1,0:T(8,128)(2,1)}), bf16[32,32,256]{2,1,0:T(8,128)(2,1)S(1)}, u32[]{:S(2)}, u32[]{:S(2)}) async-start(bf16[32,32,256]{2,1,0:T(8,128)(2,1)} %get-tuple-element.39), calls=%async_computation | async-start | bytes 1048576 | tf_op jit(solution)/shard_map/all_to_all | solution.py:298
  16.3 3.1 %collective-permute-start = (bf16[1,512,256]{2,1,0:T(8,128)(2,1)S(1)}, bf16[1,512,256]{2,1,0:T(8,128)(2,1)S(1)}, u32[]{:S(2)}, u32[]{:S(2)}) collective-permute-start(bf16[1,512,256]{2,1,0:T(8,128)(2,1)S(1)} %slice_bitcast_fusion), channel_id=1, source_target_pairs={{0,8},{8,16},{16,24},{24,32},{32,40},{40,48},{48,56},{56,64},{64,7... | collective-permute-start | bytes 786440 | tf_op jit(solution)/shard_map/ppermute | solution.py:41
  21.1 11.1 %collective-permute-done.x_ref = bf16[1,512,256]{2,1,0:T(8,128)(2,1)S(1)} collective-permute-done((bf16[1,512,256]{2,1,0:T(8,128)(2,1)S(1)}, bf16[1,512,256]{2,1,0:T(8,128)(2,1)S(1)}, u32[]{:S(2)}, u32[]{:S(2)}) %collective-permute-start) | collective-permute-done | bytes 262176 | tf_op jit(solution)/shard_map/ppermute | solution.py:41
  34.1 4.3 %terms.1 = (f32[768,256]{1,0:T(8,128)}, f32[768,256]{1,0:T(8,128)}, f32[896,256]{1,0:T(8,128)}, f32[896,256]{1,0:T(8,128)}, bf16[2,256,256]{2,1,0:T(8,128)(2,1)}) custom-call(s32[1]{0:T(128)} %bitcast.core_ref, bf16[32,32,256]{2,1,0:T(8,128)(2,1)} %copy-done.7, bf16[2,256,256]{2,1,0:T(8,128)(2,1)} %bitcast.52, bf16[3,256,256]{2,1,0:T(8,128)(2,1)} %copy-done.2, ...), custom_call_target="tpu_custom_call" | custom-call | flops 870000000 | bytes 8000000 | tf_op jit(solution)/shard_map/terms/pallas_call | solution.py:196
  38.4 2.9 %collective-permute-start.2 = (f32[896,256]{1,0:T(8,128)}, f32[896,256]{1,0:T(8,128)S(1)}, u32[]{:S(2)}, u32[]{:S(2)}) collective-permute-start(f32[896,256]{1,0:T(8,128)} %get-tuple-element.44), channel_id=1, source_target_pairs={{0,1},{1,0},{2,3},{3,2},{4,5},{5,4},{6,7},{7,6},{8,9},{9,8},{10,11... | collective-permute-start | bytes 2752520 | tf_op jit(solution)/shard_map/ppermute | solution.py:325
  42.3 1.3 collective-permute-start.3
  47.0 2.6 %combine.1 = (f32[768,256]{1,0:T(8,128)}, f32[224,256]{1,0:T(8,128)S(1)}, f32[224,256]{1,0:T(8,128)S(1)}, f32[224,256]{1,0:T(8,128)S(1)}, f32[224,256]{1,0:T(8,128)S(1)}) custom-call(s32[2]{0:T(128)S(1)} %pad_add_fusion.where_ref, f32[768,256]{1,0:T(8,128)S(1)} %copy-done.5, f32[768,256]{1,0:T(8,128)S(1)} %collective-permute-done.1.refs_1_, ...), custom_call_target="tpu_custom_call" | custom-call | flops 1000000 | bytes 5000000 | tf_op jit(solution)/shard_map/combine/pallas_call | solution.py:240
  49.6 4.2 %all-to-all-start.1 = ((f32[4,192,256]{2,1,0:T(8,128)}), f32[4,192,256]{2,1,0:T(8,128)S(1)}, u32[]{:S(2)}, u32[]{:S(2)}) async-start(f32[4,192,256]{2,1,0:T(8,128)} %bitcast.6), calls=%async_computation.1 | async-start | bytes 1572864 | tf_op jit(solution)/shard_map/all_to_all | solution.py:298
  53.8 4.1 %collective-permute-start.4 = (f32[224,256]{1,0:T(8,128)S(1)}, f32[224,256]{1,0:T(8,128)S(1)}, u32[]{:S(2)}, u32[]{:S(2)}) collective-permute-start(f32[224,256]{1,0:T(8,128)S(1)} %get-tuple-element.51), channel_id=1, source_target_pairs={{0,64},{64,128},{128,192},{192,0},{1,65},{65,129},{129,193},{193,1... | collective-permute-start | bytes 688136 | tf_op jit(solution)/shard_map/ppermute | solution.py:317
  57.9 2.7 %collective-permute-start.5 = (f32[224,256]{1,0:T(8,128)S(1)}, f32[224,256]{1,0:T(8,128)S(1)}, u32[]{:S(2)}, u32[]{:S(2)}) collective-permute-start(f32[224,256]{1,0:T(8,128)S(1)} %get-tuple-element.52), channel_id=1, source_target_pairs={{0,128},{64,192},{128,0},{192,64},{1,129},{65,193},{129,1},{193,65... | collective-permute-start | bytes 688136 | tf_op jit(solution)/shard_map/ppermute | solution.py:317
  61.5 3.0 %collective-permute-done.4 = f32[224,256]{1,0:T(8,128)S(1)} collective-permute-done((f32[224,256]{1,0:T(8,128)S(1)}, f32[224,256]{1,0:T(8,128)S(1)}, u32[]{:S(2)}, u32[]{:S(2)}) %collective-permute-start.4) | collective-permute-done | bytes 229408 | tf_op jit(solution)/shard_map/ppermute | solution.py:317
  64.4 5.8 %collective-permute-done.5 = f32[224,256]{1,0:T(8,128)S(1)} collective-permute-done((f32[224,256]{1,0:T(8,128)S(1)}, f32[224,256]{1,0:T(8,128)S(1)}, u32[]{:S(2)}, u32[]{:S(2)}) %collective-permute-start.5) | collective-permute-done | bytes 229408 | tf_op jit(solution)/shard_map/ppermute | solution.py:317
  70.8 4.9 %collective-permute-done.7 = f32[224,256]{1,0:T(8,128)S(1)} collective-permute-done((f32[224,256]{1,0:T(8,128)S(1)}, f32[224,256]{1,0:T(8,128)S(1)}, u32[]{:S(2)}, u32[]{:S(2)}) %collective-permute-start.7) | collective-permute-done | bytes 229408 | tf_op jit(solution)/shard_map/ppermute | solution.py:325
  75.8 2.5 %collective-permute-start.8 = (f32[56,256]{1,0:T(8,128)S(1)}, f32[56,256]{1,0:T(8,128)S(1)}, u32[]{:S(2)}, u32[]{:S(2)}) collective-permute-start(f32[56,256]{1,0:T(8,128)S(1)} %get-tuple-element.59), channel_id=1, source_target_pairs={{0,64},{2,66},{4,68},{6,70},{8,10},{10,12},{12,14},{14,8},{16,80},... | collective-permute-start | bytes 172040 | tf_op jit(solution)/shard_map/ppermute | solution.py:335
  78.3 3.3 %collective-permute-start.9 = (f32[56,256]{1,0:T(8,128)S(1)}, f32[56,256]{1,0:T(8,128)S(1)}, u32[]{:S(2)}, u32[]{:S(2)}) collective-permute-start(f32[56,256]{1,0:T(8,128)S(1)} %get-tuple-element.60), channel_id=1, source_target_pairs={{0,128},{2,130},{4,132},{6,134},{8,12},{10,14},{12,8},{14,10},{16,... | collective-permute-start | bytes 172040 | tf_op jit(solution)/shard_map/ppermute | solution.py:335
  82.0 1.9 %collective-permute-done.9 = f32[56,256]{1,0:T(8,128)S(1)} collective-permute-done((f32[56,256]{1,0:T(8,128)S(1)}, f32[56,256]{1,0:T(8,128)S(1)}, u32[]{:S(2)}, u32[]{:S(2)}) %collective-permute-start.9) | collective-permute-done | bytes 57376 | tf_op jit(solution)/shard_map/ppermute | solution.py:335
  83.9 1.6 %collective-permute-done.10 = f32[56,256]{1,0:T(8,128)S(1)} collective-permute-done((f32[56,256]{1,0:T(8,128)S(1)}, f32[56,256]{1,0:T(8,128)S(1)}, u32[]{:S(2)}, u32[]{:S(2)}) %collective-permute-start.10) | collective-permute-done | bytes 57376 | tf_op jit(solution)/shard_map/ppermute | solution.py:335
  85.4 1.8 %collective-permute-start.13 = (f32[56,256]{1,0:T(8,128)S(1)}, f32[56,256]{1,0:T(8,128)S(1)}, u32[]{:S(2)}, u32[]{:S(2)}) collective-permute-start(f32[56,256]{1,0:T(8,128)S(1)} %fusion.6), channel_id=1, source_target_pairs={{0,48},{8,56},{16,0},{24,8},{32,16},{40,24},{48,32},{56,40},{1,49}... | collective-permute-start | bytes 172040 | tf_op jit(solution)/shard_map/ppermute | solution.py:317
  87.8 2.3 %collective-permute-start.11 = (f32[56,256]{1,0:T(8,128)S(1)}, f32[56,256]{1,0:T(8,128)S(1)}, u32[]{:S(2)}, u32[]{:S(2)}) collective-permute-start(f32[56,256]{1,0:T(8,128)S(1)} %fusion.6), channel_id=1, source_target_pairs={{0,16},{8,24},{16,32},{24,40},{32,48},{40,56},{48,0},{56,8},{1,17}... | collective-permute-start | bytes 172040 | tf_op jit(solution)/shard_map/ppermute | solution.py:317
  90.1 1.9 %input_grad.1 = bf16[4,512,256]{2,1,0:T(8,128)(2,1)} custom-call(bf16[2,256,256]{2,1,0:T(8,128)(2,1)S(1)} %copy-done.6, bf16[1,256,256]{2,1,0:T(8,128)(2,1)S(1)} %collective-permute-done.3.below_ref, bf16[3,3,256,256]{3,2,1,0:T(8,128)(2,1)S(1)} %copy-done.3), custom_call_target="tpu_custom_call" | custom-call | flops 604000000 | bytes 3000000 | tf_op jit(solution)/shard_map/input_grad/pallas_call | solution.py:285
  92.0 2.6 %collective-permute-done.12 = f32[56,256]{1,0:T(8,128)S(1)} collective-permute-done((f32[56,256]{1,0:T(8,128)S(1)}, f32[56,256]{1,0:T(8,128)S(1)}, u32[]{:S(2)}, u32[]{:S(2)}) %collective-permute-start.12) | collective-permute-done | bytes 57376 | tf_op jit(solution)/shard_map/ppermute | solution.py:317
  95.9 1.6 %collective-permute-start.16 = (f32[56,256]{1,0:T(8,128)S(1)}, f32[56,256]{1,0:T(8,128)S(1)}, u32[]{:S(2)}, u32[]{:S(2)}) collective-permute-start(f32[56,256]{1,0:T(8,128)S(1)} %get-tuple-element.76), channel_id=1, source_target_pairs={{0,192},{2,194},{4,196},{6,198},{8,14},{10,8},{12,10},{14,12},{16,... | collective-permute-start | bytes 172040 | tf_op jit(solution)/shard_map/ppermute | solution.py:335
  97.4 2.2 %collective-permute-done.14 = f32[56,256]{1,0:T(8,128)S(1)} collective-permute-done((f32[56,256]{1,0:T(8,128)S(1)}, f32[56,256]{1,0:T(8,128)S(1)}, u32[]{:S(2)}, u32[]{:S(2)}) %collective-permute-start.14) | collective-permute-done | bytes 57376 | tf_op jit(solution)/shard_map/ppermute | solution.py:335
  100.2 4.9 %collective-permute-done.17 = f32[224,256]{1,0:T(8,128)S(1)} collective-permute-done((f32[224,256]{1,0:T(8,128)S(1)}, f32[224,256]{1,0:T(8,128)S(1)}, u32[]{:S(2)}, u32[]{:S(2)}) %collective-permute-start.17) | collective-permute-done | bytes 229408 | tf_op jit(solution)/shard_map/ppermute | solution.py:325
  106.1 3.5 %all-to-all-start.2 = ((f32[4,192,256]{2,1,0:T(8,128)}), f32[4,192,256]{2,1,0:T(8,128)S(1)}, u32[]{:S(2)}, u32[]{:S(2)}) async-start(f32[4,192,256]{2,1,0:T(8,128)} %broadcast_in_dim.27), calls=%async_computation.2 | async-start | bytes 1572864 | tf_op jit(solution)/shard_map/all_to_all | solution.py:298
  109.6 2.6 %collective-permute-start.20 = (f32[224,256]{1,0:T(8,128)S(1)}, f32[224,256]{1,0:T(8,128)S(1)}, u32[]{:S(2)}, u32[]{:S(2)}) collective-permute-start(f32[224,256]{1,0:T(8,128)S(1)} %broadcast_select_fusion.refs_2_), channel_id=1, source_target_pairs={{0,192},{64,0},{128,64},{192,128},{1,193},{65,1},{129,65},{193,129... | collective-permute-start | bytes 688136 | tf_op jit(solution)/shard_map/ppermute | solution.py:317
  112.8 4.8 %collective-permute-done.20.refs_5_ = f32[224,256]{1,0:T(8,128)S(1)} collective-permute-done((f32[224,256]{1,0:T(8,128)S(1)}, f32[224,256]{1,0:T(8,128)S(1)}, u32[]{:S(2)}, u32[]{:S(2)}) %collective-permute-start.20) | collective-permute-done | bytes 229408 | tf_op jit(solution)/shard_map/ppermute | solution.py:317
  118.7 2.3 %collective-permute-done.18.refs_3_ = f32[224,256]{1,0:T(8,128)S(1)} collective-permute-done((f32[224,256]{1,0:T(8,128)S(1)}, f32[224,256]{1,0:T(8,128)S(1)}, u32[]{:S(2)}, u32[]{:S(2)}) %collective-permute-start.18) | collective-permute-done | bytes 229408 | tf_op jit(solution)/shard_map/ppermute | solution.py:317
  121.0 8.2 %collective-permute-start.21 = (f32[768,256]{1,0:T(8,128)S(1)}, f32[768,256]{1,0:T(8,128)S(1)}, u32[]{:S(2)}, u32[]{:S(2)}) collective-permute-start(f32[768,256]{1,0:T(8,128)S(1)} %bitcast.44), channel_id=1, source_target_pairs={{0,1},{1,0},{2,3},{3,2},{4,5},{5,4},{6,7},{7,6},{8,9},{9,8},{10,11... | collective-permute-start | bytes 2359304 | tf_op jit(solution)/shard_map/ppermute | solution.py:325
  130.2 1.2 collective-permute-done.22.refs_6_
  132.4 2.6 %assemble.1 = (f32[9,256,256]{2,1,0:T(8,128)}, f32[256,1024]{1,0:T(8,128)}) custom-call(s32[2]{0:T(128)S(1)} %pad_add_fusion.where_ref, f32[768,256]{1,0:T(8,128)S(1)} %bitcast.45, f32[768,256]{1,0:T(8,128)S(1)} %collective-permute-done.21.refs_1_, f32[224,256]{1,0:T(8,128)S(1)} %broadcast_select_fusion.refs_2_, ...), custom_call_target="tpu_custom_call" | custom-call | bytes 7000000 | tf_op jit(solution)/shard_map/assemble/pallas_call | solution.py:406
  (66 shorter events, 16.9 us)
Async XLA Ops:
  0.6 15.6 %copy-start.1 = (bf16[1,4,512,256]{3,2,1,0:T(8,128)(2,1)S(1)}, bf16[1,4,512,256]{3,2,1,0:T(8,128)(2,1)}, u32[]{:S(2)}) copy-start(bf16[1,4,512,256]{3,2,1,0:T(8,128)(2,1)} %param.6) | copy-start | bytes 3145732
  4.3 28.9 %all-to-all-start = ((bf16[32,32,256]{2,1,0:T(8,128)(2,1)}), bf16[32,32,256]{2,1,0:T(8,128)(2,1)S(1)}, u32[]{:S(2)}, u32[]{:S(2)}) async-start(bf16[32,32,256]{2,1,0:T(8,128)(2,1)} %get-tuple-element.39), calls=%async_computation | async-start | bytes 1048576 | tf_op jit(solution)/shard_map/all_to_all | solution.py:298
  16.3 16.0 %collective-permute-start = (bf16[1,512,256]{2,1,0:T(8,128)(2,1)S(1)}, bf16[1,512,256]{2,1,0:T(8,128)(2,1)S(1)}, u32[]{:S(2)}, u32[]{:S(2)}) collective-permute-start(bf16[1,512,256]{2,1,0:T(8,128)(2,1)S(1)} %slice_bitcast_fusion), channel_id=1, source_target_pairs={{0,8},{8,16},{16,24},{24,32},{32,40},{40,48},{48,56},{56,64},{64,7... | collective-permute-start | bytes 786440 | tf_op jit(solution)/shard_map/ppermute | solution.py:41
  38.4 6.3 %collective-permute-start.2 = (f32[896,256]{1,0:T(8,128)}, f32[896,256]{1,0:T(8,128)S(1)}, u32[]{:S(2)}, u32[]{:S(2)}) collective-permute-start(f32[896,256]{1,0:T(8,128)} %get-tuple-element.44), channel_id=1, source_target_pairs={{0,1},{1,0},{2,3},{3,2},{4,5},{5,4},{6,7},{7,6},{8,9},{9,8},{10,11... | collective-permute-start | bytes 2752520 | tf_op jit(solution)/shard_map/ppermute | solution.py:325
  41.3 3.4 %collective-permute-start.1 = (f32[768,256]{1,0:T(8,128)}, f32[768,256]{1,0:T(8,128)S(1)}, u32[]{:S(2)}, u32[]{:S(2)}) collective-permute-start(f32[768,256]{1,0:T(8,128)} %get-tuple-element.42), channel_id=1, source_target_pairs={{0,1},{1,0},{2,3},{3,2},{4,5},{5,4},{6,7},{7,6},{8,9},{9,8},{10,11... | collective-permute-start | bytes 2359304 | tf_op jit(solution)/shard_map/ppermute | solution.py:325
  42.3 7.3 %collective-permute-start.3 = (bf16[1,256,256]{2,1,0:T(8,128)(2,1)S(1)}, bf16[1,256,256]{2,1,0:T(8,128)(2,1)S(1)}, u32[]{:S(2)}, u32[]{:S(2)}) collective-permute-start(bf16[1,256,256]{2,1,0:T(8,128)(2,1)S(1)} %slice.10), channel_id=1, source_target_pairs={{8,0},{16,8},{24,16},{32,24},{40,32},{48,40},{56,48},{64,56},{72,6... | collective-permute-start | bytes 393224 | tf_op jit(solution)/shard_map/ppermute | solution.py:41
  49.6 20.6 %all-to-all-start.1 = ((f32[4,192,256]{2,1,0:T(8,128)}), f32[4,192,256]{2,1,0:T(8,128)S(1)}, u32[]{:S(2)}, u32[]{:S(2)}) async-start(f32[4,192,256]{2,1,0:T(8,128)} %bitcast.6), calls=%async_computation.1 | async-start | bytes 1572864 | tf_op jit(solution)/shard_map/all_to_all | solution.py:298
  53.8 10.7 %collective-permute-start.4 = (f32[224,256]{1,0:T(8,128)S(1)}, f32[224,256]{1,0:T(8,128)S(1)}, u32[]{:S(2)}, u32[]{:S(2)}) collective-permute-start(f32[224,256]{1,0:T(8,128)S(1)} %get-tuple-element.51), channel_id=1, source_target_pairs={{0,64},{64,128},{128,192},{192,0},{1,65},{65,129},{129,193},{193,1... | collective-permute-start | bytes 688136 | tf_op jit(solution)/shard_map/ppermute | solution.py:317
  57.9 12.3 %collective-permute-start.5 = (f32[224,256]{1,0:T(8,128)S(1)}, f32[224,256]{1,0:T(8,128)S(1)}, u32[]{:S(2)}, u32[]{:S(2)}) collective-permute-start(f32[224,256]{1,0:T(8,128)S(1)} %get-tuple-element.52), channel_id=1, source_target_pairs={{0,128},{64,192},{128,0},{192,64},{1,129},{65,193},{129,1},{193,65... | collective-permute-start | bytes 688136 | tf_op jit(solution)/shard_map/ppermute | solution.py:317
  60.6 9.6 %collective-permute-start.6 = (f32[224,256]{1,0:T(8,128)S(1)}, f32[224,256]{1,0:T(8,128)S(1)}, u32[]{:S(2)}, u32[]{:S(2)}) collective-permute-start(f32[224,256]{1,0:T(8,128)S(1)} %get-tuple-element.53), channel_id=1, source_target_pairs={{0,192},{64,0},{128,64},{192,128},{1,193},{65,1},{129,65},{193,129... | collective-permute-start | bytes 688136 | tf_op jit(solution)/shard_map/ppermute | solution.py:317
  70.3 19.8 %copy-start.3 = (bf16[3,3,256,256]{3,2,1,0:T(8,128)(2,1)S(1)}, bf16[3,3,256,256]{3,2,1,0:T(8,128)(2,1)}, u32[]{:S(2)}) copy-start(bf16[3,3,256,256]{3,2,1,0:T(8,128)(2,1)} %weight_ref.1) | copy-start | bytes 3538948
  70.3 19.8 %copy-start.6 = (bf16[2,256,256]{2,1,0:T(8,128)(2,1)S(1)}, bf16[2,256,256]{2,1,0:T(8,128)(2,1)}, u32[]{:S(2)}) copy-start(bf16[2,256,256]{2,1,0:T(8,128)(2,1)} %get-tuple-element.49.grad_ref) | copy-start | bytes 786436
  70.4 5.3 %collective-permute-start.7 = (f32[224,256]{1,0:T(8,128)S(1)}, f32[224,256]{1,0:T(8,128)S(1)}, u32[]{:S(2)}, u32[]{:S(2)}) collective-permute-start(f32[224,256]{1,0:T(8,128)S(1)} %fusion.1), channel_id=1, source_target_pairs={{0,8},{8,0},{16,24},{24,16},{32,40},{40,32},{48,56},{56,48},{1,9},... | collective-permute-start | bytes 688136 | tf_op jit(solution)/shard_map/ppermute | solution.py:325
  75.8 6.2 %collective-permute-start.8 = (f32[56,256]{1,0:T(8,128)S(1)}, f32[56,256]{1,0:T(8,128)S(1)}, u32[]{:S(2)}, u32[]{:S(2)}) collective-permute-start(f32[56,256]{1,0:T(8,128)S(1)} %get-tuple-element.59), channel_id=1, source_target_pairs={{0,64},{2,66},{4,68},{6,70},{8,10},{10,12},{12,14},{14,8},{16,80},... | collective-permute-start | bytes 172040 | tf_op jit(solution)/shard_map/ppermute | solution.py:335
  78.3 5.6 %collective-permute-start.9 = (f32[56,256]{1,0:T(8,128)S(1)}, f32[56,256]{1,0:T(8,128)S(1)}, u32[]{:S(2)}, u32[]{:S(2)}) collective-permute-start(f32[56,256]{1,0:T(8,128)S(1)} %get-tuple-element.60), channel_id=1, source_target_pairs={{0,128},{2,130},{4,132},{6,134},{8,12},{10,14},{12,8},{14,10},{16,... | collective-permute-start | bytes 172040 | tf_op jit(solution)/shard_map/ppermute | solution.py:335
  81.6 3.8 %collective-permute-start.10 = (f32[56,256]{1,0:T(8,128)S(1)}, f32[56,256]{1,0:T(8,128)S(1)}, u32[]{:S(2)}, u32[]{:S(2)}) collective-permute-start(f32[56,256]{1,0:T(8,128)S(1)} %get-tuple-element.61), channel_id=1, source_target_pairs={{0,192},{2,194},{4,196},{6,198},{8,14},{10,8},{12,10},{14,12},{16,... | collective-permute-start | bytes 172040 | tf_op jit(solution)/shard_map/ppermute | solution.py:335
  85.4 6.6 %collective-permute-start.13 = (f32[56,256]{1,0:T(8,128)S(1)}, f32[56,256]{1,0:T(8,128)S(1)}, u32[]{:S(2)}, u32[]{:S(2)}) collective-permute-start(f32[56,256]{1,0:T(8,128)S(1)} %fusion.6), channel_id=1, source_target_pairs={{0,48},{8,56},{16,0},{24,8},{32,16},{40,24},{48,32},{56,40},{1,49}... | collective-permute-start | bytes 172040 | tf_op jit(solution)/shard_map/ppermute | solution.py:317
  87.2 7.4 %collective-permute-start.12 = (f32[56,256]{1,0:T(8,128)S(1)}, f32[56,256]{1,0:T(8,128)S(1)}, u32[]{:S(2)}, u32[]{:S(2)}) collective-permute-start(f32[56,256]{1,0:T(8,128)S(1)} %fusion.6), channel_id=1, source_target_pairs={{0,32},{8,40},{16,48},{24,56},{32,0},{40,8},{48,16},{56,24},{1,33}... | collective-permute-start | bytes 172040 | tf_op jit(solution)/shard_map/ppermute | solution.py:317
  87.8 6.8 %collective-permute-start.11 = (f32[56,256]{1,0:T(8,128)S(1)}, f32[56,256]{1,0:T(8,128)S(1)}, u32[]{:S(2)}, u32[]{:S(2)}) collective-permute-start(f32[56,256]{1,0:T(8,128)S(1)} %fusion.6), channel_id=1, source_target_pairs={{0,16},{8,24},{16,32},{24,40},{32,48},{40,56},{48,0},{56,8},{1,17}... | collective-permute-start | bytes 172040 | tf_op jit(solution)/shard_map/ppermute | solution.py:317
  94.7 4.9 %collective-permute-start.14 = (f32[56,256]{1,0:T(8,128)S(1)}, f32[56,256]{1,0:T(8,128)S(1)}, u32[]{:S(2)}, u32[]{:S(2)}) collective-permute-start(f32[56,256]{1,0:T(8,128)S(1)} %get-tuple-element.76), channel_id=1, source_target_pairs={{0,64},{2,66},{4,68},{6,70},{8,10},{10,12},{12,14},{14,8},{16,80},... | collective-permute-start | bytes 172040 | tf_op jit(solution)/shard_map/ppermute | solution.py:335
  94.8 4.8 %collective-permute-start.15 = (f32[56,256]{1,0:T(8,128)S(1)}, f32[56,256]{1,0:T(8,128)S(1)}, u32[]{:S(2)}, u32[]{:S(2)}) collective-permute-start(f32[56,256]{1,0:T(8,128)S(1)} %get-tuple-element.76), channel_id=1, source_target_pairs={{0,128},{2,130},{4,132},{6,134},{8,12},{10,14},{12,8},{14,10},{16,... | collective-permute-start | bytes 172040 | tf_op jit(solution)/shard_map/ppermute | solution.py:335
  95.9 4.3 %collective-permute-start.16 = (f32[56,256]{1,0:T(8,128)S(1)}, f32[56,256]{1,0:T(8,128)S(1)}, u32[]{:S(2)}, u32[]{:S(2)}) collective-permute-start(f32[56,256]{1,0:T(8,128)S(1)} %get-tuple-element.76), channel_id=1, source_target_pairs={{0,192},{2,194},{4,196},{6,198},{8,14},{10,8},{12,10},{14,12},{16,... | collective-permute-start | bytes 172040 | tf_op jit(solution)/shard_map/ppermute | solution.py:335
  100.2 4.9 %collective-permute-start.17 = (f32[224,256]{1,0:T(8,128)S(1)}, f32[224,256]{1,0:T(8,128)S(1)}, u32[]{:S(2)}, u32[]{:S(2)}) collective-permute-start(f32[224,256]{1,0:T(8,128)S(1)} %bitcast.47), channel_id=1, source_target_pairs={{0,8},{8,0},{16,24},{24,16},{32,40},{40,32},{48,56},{56,48},{1,9},... | collective-permute-start | bytes 688136 | tf_op jit(solution)/shard_map/ppermute | solution.py:325
  106.1 14.9 %all-to-all-start.2 = ((f32[4,192,256]{2,1,0:T(8,128)}), f32[4,192,256]{2,1,0:T(8,128)S(1)}, u32[]{:S(2)}, u32[]{:S(2)}) async-start(f32[4,192,256]{2,1,0:T(8,128)} %broadcast_in_dim.27), calls=%async_computation.2 | async-start | bytes 1572864 | tf_op jit(solution)/shard_map/all_to_all | solution.py:298
  109.6 8.1 %collective-permute-start.20 = (f32[224,256]{1,0:T(8,128)S(1)}, f32[224,256]{1,0:T(8,128)S(1)}, u32[]{:S(2)}, u32[]{:S(2)}) collective-permute-start(f32[224,256]{1,0:T(8,128)S(1)} %broadcast_select_fusion.refs_2_), channel_id=1, source_target_pairs={{0,192},{64,0},{128,64},{192,128},{1,193},{65,1},{129,65},{193,129... | collective-permute-start | bytes 688136 | tf_op jit(solution)/shard_map/ppermute | solution.py:317
  112.2 6.5 %collective-permute-start.19 = (f32[224,256]{1,0:T(8,128)S(1)}, f32[224,256]{1,0:T(8,128)S(1)}, u32[]{:S(2)}, u32[]{:S(2)}) collective-permute-start(f32[224,256]{1,0:T(8,128)S(1)} %broadcast_select_fusion.refs_2_), channel_id=1, source_target_pairs={{0,128},{64,192},{128,0},{192,64},{1,129},{65,193},{129,1},{193,65... | collective-permute-start | bytes 688136 | tf_op jit(solution)/shard_map/ppermute | solution.py:317
  112.5 8.5 %collective-permute-start.18 = (f32[224,256]{1,0:T(8,128)S(1)}, f32[224,256]{1,0:T(8,128)S(1)}, u32[]{:S(2)}, u32[]{:S(2)}) collective-permute-start(f32[224,256]{1,0:T(8,128)S(1)} %broadcast_select_fusion.refs_2_), channel_id=1, source_target_pairs={{0,64},{64,128},{128,192},{192,0},{1,65},{65,129},{129,193},{193,1... | collective-permute-start | bytes 688136 | tf_op jit(solution)/shard_map/ppermute | solution.py:317
  121.0 11.4 %collective-permute-start.21 = (f32[768,256]{1,0:T(8,128)S(1)}, f32[768,256]{1,0:T(8,128)S(1)}, u32[]{:S(2)}, u32[]{:S(2)}) collective-permute-start(f32[768,256]{1,0:T(8,128)S(1)} %bitcast.44), channel_id=1, source_target_pairs={{0,1},{1,0},{2,3},{3,2},{4,5},{5,4},{6,7},{7,6},{8,9},{9,8},{10,11... | collective-permute-start | bytes 2359304 | tf_op jit(solution)/shard_map/ppermute | solution.py:325
  129.2 2.2 %collective-permute-start.22 = (f32[224,256]{1,0:T(8,128)S(1)}, f32[224,256]{1,0:T(8,128)S(1)}, u32[]{:S(2)}, u32[]{:S(2)}) collective-permute-start(f32[224,256]{1,0:T(8,128)S(1)} %broadcast_select_fusion.refs_2_), channel_id=1, source_target_pairs={{0,1},{1,0},{2,3},{3,2},{4,5},{5,4},{6,7},{7,6},{8,9},{9,8},{10,11... | collective-permute-start | bytes 688136 | tf_op jit(solution)/shard_map/ppermute | solution.py:325
  129.2 2.6 %collective-permute-start.23 = (f32[224,256]{1,0:T(8,128)S(1)}, f32[224,256]{1,0:T(8,128)S(1)}, u32[]{:S(2)}, u32[]{:S(2)}) collective-permute-start(f32[224,256]{1,0:T(8,128)S(1)} %collective-permute-done.18.refs_3_), channel_id=1, source_target_pairs={{0,1},{1,0},{2,3},{3,2},{4,5},{5,4},{6,7},{7,6},{8,9},{9,8},{10,11... | collective-permute-start | bytes 688136 | tf_op jit(solution)/shard_map/ppermute | solution.py:325
  129.7 2.4 %collective-permute-start.24 = (f32[224,256]{1,0:T(8,128)S(1)}, f32[224,256]{1,0:T(8,128)S(1)}, u32[]{:S(2)}, u32[]{:S(2)}) collective-permute-start(f32[224,256]{1,0:T(8,128)S(1)} %collective-permute-done.19.refs_4_), channel_id=1, source_target_pairs={{0,1},{1,0},{2,3},{3,2},{4,5},{5,4},{6,7},{7,6},{8,9},{9,8},{10,11... | collective-permute-start | bytes 688136 | tf_op jit(solution)/shard_map/ppermute | solution.py:325
  129.7 2.7 %collective-permute-start.25 = (f32[224,256]{1,0:T(8,128)S(1)}, f32[224,256]{1,0:T(8,128)S(1)}, u32[]{:S(2)}, u32[]{:S(2)}) collective-permute-start(f32[224,256]{1,0:T(8,128)S(1)} %collective-permute-done.20.refs_5_), channel_id=1, source_target_pairs={{0,1},{1,0},{2,3},{3,2},{4,5},{5,4},{6,7},{7,6},{8,9},{9,8},{10,11... | collective-permute-start | bytes 688136 | tf_op jit(solution)/shard_map/ppermute | solution.py:325
  (5 other events, 5.0 us)

commit v5 on v4

--- a/solution.py
+++ b/solution.py
@@ -121,22 +121,59 @@
     )(x)
 
 
-def terms_kernel(
-    core_ref, arrived_hbm, preact_hbm, above_hbm, blocks_hbm, weighted_hbm,
-    own_inner, other_inner, own_outer, other_outer, grad_hbm,
-    arrived_ref, preact_ref, above_ref, blocks_ref, weighted_ref,
-    grad_ref, turned, inner_ref, outer_ref, sems,
-):
-    pairs = (
-        (arrived_hbm, arrived_ref),
-        (preact_hbm, preact_ref),
-        (blocks_hbm, blocks_ref),
-        (above_hbm, above_ref),
-        (weighted_hbm, weighted_ref),
-    )
+def fetch(pairs, sems):
     copies = [pltpu.make_async_copy(a, b, sems.at[n]) for n, (a, b) in enumerate(pairs)]
     for copy in copies:
         copy.start()
+    return copies
+
+
+def half_terms(start, grad_ref, turned, above_ref, blocks_ref, weighted_ref, inner_ref, outer_ref):
+    channels = grad_ref.shape[2]
+
+    def taps(row_tap, col_tap):
+        total = None
+        for i in range(grad_ref.shape[0]):
+            row = 2 * i + row_tap - 1
+            source, at = (above_ref, col_tap) if row < 0 else (blocks_ref, 3 * row + col_tap)
+            term = jnp.dot(
+                source[at, pl.ds(start, LANES), :], grad_ref[i], preferred_element_type=jnp.float32
+            )
+            total = term if total is None else total + term
+        return total
+
+    for col_tap in range(3):
+        for row_tap in (1, 2):
+            at = (3 * (row_tap - 1) + col_tap) * LANES
+            inner_ref[at : at + LANES, :] = taps(row_tap, col_tap)
+    for col_tap in range(3):
+        at = col_tap * LANES
+        outer_ref[at : at + LANES, :] = taps(0, col_tap)
+    for k in range(weighted_ref.shape[1] // channels):
+        at = (3 + k) * LANES
+        outer_ref[at : at + LANES, :] = jnp.dot(
+            turned[pl.ds(start, LANES), :],
+            weighted_ref[:, k * channels : (k + 1) * channels],
+            preferred_element_type=jnp.float32,
+        )
+
+
+def other_kernel(
+    where_ref, arrived_hbm, preact_hbm, above_hbm, blocks_hbm, weighted_hbm,
+    inner_hbm, outer_hbm, grad_hbm, first_hbm, turned_hbm,
+    arrived_ref, preact_ref, above_ref, blocks_ref, weighted_ref,
+    inner_ref, outer_ref, grad_ref, turned, sems,
+):
+    copies = fetch(
+        (
+            (arrived_hbm, arrived_ref),
+            (preact_hbm, preact_ref),
+            (blocks_hbm, blocks_ref),
+            (above_hbm, above_ref),
+            (weighted_hbm, weighted_ref),
+        ),
+        sems,
+    )
     devices, chunk, channels = arrived_ref.shape
     rows, cols = preact_ref.shape[:2]
     chunk, band = chunk // 2, cols // devices
@@ -146,107 +183,110 @@
         hidden = arrived_ref[:, i * band : (i + 1) * band, :].astype(jnp.float32).reshape(cols, channels)
         kept = jnp.where(preact_ref[i].astype(jnp.float32) > 0.0, hidden, 0.0)
         grad_ref[i] = kept.astype(jnp.bfloat16)
-    back = [pltpu.make_async_copy(grad_ref, grad_hbm, sems.at[5])]
-    back[0].start()
     active = arrived_ref[:, chunk:, :].astype(jnp.float32).reshape(devices * chunk, channels)
     turned[...] = active.T.astype(jnp.bfloat16)
-
-    def half_taps(row_tap, col_tap, start):
-        total = None
-        for i in range(rows):
-            row = 2 * i + row_tap - 1
-            source, at = (above_ref, col_tap) if row < 0 else (blocks_ref, 3 * row + col_tap)
-            term = jnp.dot(
-                source[at, pl.ds(start, LANES), :], grad_ref[i], preferred_element_type=jnp.float32
-            )
-            total = term if total is None else total + term
-        return total
-
     for copy in copies[2:]:
         copy.wait()
-    for n, (inner_hbm, outer_hbm) in enumerate(((other_inner, other_outer), (own_inner, own_outer))):
-        owner = core_ref[0] if n else 1 - core_ref[0]
-        start = pl.multiple_of(owner * LANES, LANES)
-        for col_tap in range(3):
-            for row_tap in (1, 2):
-                at = (3 * (row_tap - 1) + col_tap) * LANES
-                inner_ref[n, at : at + LANES, :] = half_taps(row_tap, col_tap, start)
-        back.append(pltpu.make_async_copy(inner_ref.at[n], inner_hbm, sems.at[6 + 2 * n]))
-        back[-1].start()
-        for col_tap in range(3):
-            at = col_tap * LANES
-            outer_ref[n, at : at + LANES, :] = half_taps(0, col_tap, start)
-        for k in range(weighted_ref.shape[1] // channels):
-            at = (3 + k) * LANES
-            outer_ref[n, at : at + LANES, :] = jnp.dot(
-                turned[pl.ds(start, LANES), :],
-                weighted_ref[:, k * channels : (k + 1) * channels],
-                preferred_element_type=jnp.float32,
-            )
-        back.append(pltpu.make_async_copy(outer_ref.at[n], outer_hbm, sems.at[7 + 2 * n]))
-        back[-1].start()
+    start = pl.multiple_of((1 - where_ref[0]) * LANES, LANES)
+    half_terms(start, grad_ref, turned, above_ref, blocks_ref, weighted_ref, inner_ref, outer_ref)
+    back = fetch(
+        (
+            (inner_ref, inner_hbm),
+            (outer_ref, outer_hbm),
+            (grad_ref, grad_hbm),
+            (grad_ref.at[0:1], first_hbm),
+            (turned, turned_hbm),
+        ),
+        sems,
+    )
     for copy in back:
         copy.wait()
 
 
-def terms(core, arrived, preact, above, blocks, weighted):
+def other_terms(where, arrived, preact, above, blocks, weighted):
     rows, cols, channels = preact.shape
+    arrays = (arrived, preact, above, blocks, weighted)
     inner = jax.ShapeDtypeStruct((6 * LANES, channels), jnp.float32)
     outer = jax.ShapeDtypeStruct((3 * LANES + weighted.shape[1] // 2, channels), jnp.float32)
-    return pl.pallas_call(
-        terms_kernel,
-        out_shape=(inner, inner, outer, outer, jax.ShapeDtypeStruct(preact.shape, jnp.bfloat16)),
+    grad = jax.ShapeDtypeStruct(preact.shape, jnp.bfloat16)
+    first = jax.ShapeDtypeStruct((1, cols, channels), jnp.bfloat16)
+    turned = jax.ShapeDtypeStruct((channels, weighted.shape[0]), jnp.bfloat16)
+    return pl.pallas_call(
+        other_kernel,
+        out_shape=(inner, outer, grad, first, turned),
         in_specs=[scalars()] + [far()] * 5,
         out_specs=(far(),) * 5,
-        scratch_shapes=[room(x) for x in (arrived, preact, above, blocks, weighted, preact)]
-        + [
-            pltpu.VMEM((channels, weighted.shape[0]), jnp.bfloat16),
-            pltpu.VMEM((2,) + inner.shape, jnp.float32),
-            pltpu.VMEM((2,) + outer.shape, jnp.float32),
-            pltpu.SemaphoreType.DMA((10,)),
-        ],
+        scratch_shapes=[room(x) for x in arrays + (inner, outer, grad, turned)]
+        + [pltpu.SemaphoreType.DMA((5,))],
         compiler_params=params(54),
-        cost_estimate=pl.CostEstimate(flops=870 * 10**6, bytes_accessed=8 * 10**6, transcendentals=0),
-        name="terms",
-    )(core, arrived, preact, above, blocks, weighted)
-
-
-def combine_kernel(where_ref, *refs):
-    hbm, (inner_hbm, *outer_hbm), room_refs, sems = refs[:4], refs[4:9], refs[9:13], refs[13]
-    copies = [pltpu.make_async_copy(a, b, sems.at[n]) for n, (a, b) in enumerate(zip(hbm, room_refs))]
-    for copy in copies:
-        copy.start()
-    own_inner, got_inner, own_outer, got_outer = room_refs
-    rows = own_outer.shape[0] // 4
-    copies[0].wait()
-    copies[1].wait()
-    own_inner[...] += got_inner[...]
-    back = [pltpu.make_async_copy(own_inner, inner_hbm, sems.at[4])]
-    back[0].start()
-    copies[2].wait()
-    copies[3].wait()
-    own_outer[...] += got_outer[...]
-    for by, out in enumerate(outer_hbm):
-        at = pl.ds(pl.multiple_of(((where_ref[1] + by) & 3) * rows, 8), rows)
-        back.append(pltpu.make_async_copy(own_outer.at[at, :], out, sems.at[5 + by]))
-        back[-1].start()
-    for copy in back:
+        cost_estimate=pl.CostEstimate(flops=435 * 10**6, bytes_accessed=6 * 10**6, transcendentals=0),
+        name="other_terms",
+    )(where, *arrays)
+
+
+def own_kernel(
+    where_ref, grad_ref, turned, above_ref, blocks_ref, weighted_ref, got_inner, got_outer, *refs
+):
+    outs, (inner_ref, outer_ref, sems) = refs[:10], refs[10:]
+    start = pl.multiple_of(where_ref[0] * LANES, LANES)
+    half_terms(start, grad_ref, turned, above_ref, blocks_ref, weighted_ref, inner_ref, outer_ref)
+    inner_ref[...] += got_inner[...]
+    outer_ref[...] += got_outer[...]
+    pairs = []
+    for n, source in enumerate((inner_ref, outer_ref)):
+        rows = source.shape[0] // 4
+
+        def cut(by, offset, count):
+            at = ((where_ref[2 - n] + by) & 3) * rows + offset
+            return source.at[pl.ds(pl.multiple_of(at, 8), count), :]
+
+        half = rows // 2
+        cuts = (cut(0, 0, rows), cut(1, 0, rows), cut(3, 0, rows), cut(2, 0, half), cut(2, half, half))
+        pairs += zip(cuts, outs[5 * n : 5 * n + 5])
+    for copy in fetch(pairs, sems):
         copy.wait()
 
 
-def combine(where, *arrays):
-    inner, outer = arrays[0], arrays[2]
-    chunk = jax.ShapeDtypeStruct((outer.shape[0] // 4, outer.shape[1]), jnp.float32)
-    return pl.pallas_call(
-        combine_kernel,
-        out_shape=(jax.ShapeDtypeStruct(inner.shape, jnp.float32),) + (chunk,) * 4,
-        in_specs=[scalars()] + [far()] * 4,
-        out_specs=(far(),) * 5,
-        scratch_shapes=[room(x) for x in arrays] + [pltpu.SemaphoreType.DMA((9,))],
-        compiler_params=params(24),
-        cost_estimate=pl.CostEstimate(flops=10**6, bytes_accessed=5 * 10**6, transcendentals=0),
-        name="combine",
+def own_sums(where, grad, turned, above, blocks, weighted, got_inner, got_outer):
+    outs = []
+    for got in (got_inner, got_outer):
+        rows = got.shape[0] // 4
+        outs += [jax.ShapeDtypeStruct((n, got.shape[1]), jnp.float32) for n in (rows,) * 3 + (rows // 2,) * 2]
+    arrays = (grad, turned, above, blocks, weighted, got_inner, got_outer)
+    return pl.pallas_call(
+        own_kernel,
+        out_shape=tuple(outs),
+        in_specs=[scalars()] + [whole()] * len(arrays),
+        out_specs=(far(),) * 10,
+        scratch_shapes=[room(got_inner), room(got_outer), pltpu.SemaphoreType.DMA((10,))],
+        compiler_params=params(),
+        cost_estimate=pl.CostEstimate(flops=435 * 10**6, bytes_accessed=8 * 10**6, transcendentals=0),
+        name="own_sums",
     )(where, *arrays)
+
+
+def relay_kernel(*refs):
+    for n in range(2):
+        above, below, upper, lower = refs[4 * n : 4 * n + 4]
+        out_above, out_below = refs[8 + 2 * n : 10 + 2 * n]
+        half = upper.shape[0]
+        out_above[:half, :] = above[:half, :] + upper[...]
+        out_above[half:, :] = above[half:, :]
+        out_below[:half, :] = below[:half, :]
+        out_below[half:, :] = below[half:, :] + lower[...]
+
+
+def relay(*arrays):
+    outs = [jax.ShapeDtypeStruct(arrays[n].shape, jnp.float32) for n in (0, 1, 4, 5)]
+    return pl.pallas_call(
+        relay_kernel,
+        out_shape=tuple(outs),
+        in_specs=[whole()] * 8,
+        out_specs=(whole(),) * 4,
+        compiler_params=params(),
+        cost_estimate=pl.CostEstimate(flops=10**5, bytes_accessed=3 * 10**6, transcendentals=0),
+        name="relay",
+    )(*arrays)
 
 
 def input_kernel(grad_ref, below_ref, weight_ref, out_ref, wide):
@@ -344,13 +384,20 @@
 STEPS = (1, 2, 3)
 
 
-def total_sums(inner, outer, parts, scale, below, beside):
-    inner, parts, below = barrier((split(inner), parts, below))
-    inner = exchange(inner, "y")
-    moved = [rotated(p, "x", by) for p, by in zip(parts, STEPS)]
-    inner, moved = barrier((inner, moved))
-    inner = jnp.sum(inner, axis=0)
-    outer = sum(moved, outer)
+def total_sums(cuts, scale, below, beside):
+    cuts, below = barrier((cuts, below))
+    axes = ("y", "x")
+    passed = []
+    for n, axis in enumerate(axes):
+        passed += [rotated(cuts[5 * n + 3], axis, 1), rotated(cuts[5 * n + 4], axis, 3)]
+    passed = barrier(passed)
+    sums = relay(*cuts[1:3], *passed[:2], *cuts[6:8], *passed[2:])
+    moved = []
+    for n, axis in enumerate(axes):
+        moved += [rotated(sums[2 * n], axis, 1), rotated(sums[2 * n + 1], axis, 3)]
+    moved = barrier(moved)
+    inner = cuts[0] + moved[0] + moved[1]
+    outer = cuts[5] + moved[2] + moved[3]
 
     rows = outer.shape[0] - inner.shape[0]
     both = jnp.stack([jnp.pad(inner, ((0, rows), (0, 0))), outer])
@@ -374,31 +421,46 @@
     inner = jnp.where(bit == 0, part, got)[: part.shape[0] - rows]
     outer = jnp.where(bit == 0, got, part)
     inner, outer = barrier((inner, outer))
-    copies = barrier(jnp.broadcast_to(inner, (4,) + inner.shape))
-    copies, moved = barrier((exchange(copies, "y"), [rotated(outer, "x", by) for by in STEPS]))
-    return [copies.reshape(-1, part.shape[1])], [outer] + moved, beside
+    near = []
+    for value, axis in ((inner, "y"), (outer, "x")):
+        near += [rotated(value, axis, 1), rotated(value, axis, 3)]
+    near = barrier(near)
+    halves = []
+    for n in range(2):
+        half = near[2 * n].shape[0] // 2
+        halves += [near[2 * n][:half], near[2 * n + 1][half:]]
+    halves = barrier(halves)
+    for n, axis in enumerate(axes):
+        halves[2 * n] = rotated(halves[2 * n], axis, 1)
+        halves[2 * n + 1] = rotated(halves[2 * n + 1], axis, 3)
+    near, halves = barrier((near, halves))
+    inner = jnp.concatenate([inner, near[0], *halves[:2], near[1]])
+    outer = jnp.concatenate([outer, near[2], *halves[2:], near[3]])
+    return inner, outer, beside
 
 
 def assemble_kernel(where_ref, *refs):
-    inner, pieces, (conv_ref, expand_ref, joined) = refs[:2], refs[2:10], refs[10:]
+    conv_ref, expand_ref = refs[4:6]
+    scratch = refs[6:]
     channels = conv_ref.shape[2]
     core = where_ref[0]
-    for by in range(4):
-        rows = pieces[by].shape[0]
-        at = pl.multiple_of(((where_ref[1] + 4 - by) & 3) * rows, 8)
-        joined[core, pl.ds(at, rows), :] = pieces[by][...]
-        joined[1 - core, pl.ds(at, rows), :] = pieces[4 + by][...]
-    for tap in range(6):
-        rows = slice(tap * LANES, (tap + 1) * LANES)
-        conv_ref[3 + tap, pl.ds(pl.multiple_of(core * LANES, LANES), LANES), :] = inner[0][rows, :]
-        conv_ref[3 + tap, pl.ds(pl.multiple_of((1 - core) * LANES, LANES), LANES), :] = inner[1][rows, :]
+    for n, whole_ref in enumerate(scratch):
+        own, got = refs[2 * n : 2 * n + 2]
+        rows = own.shape[0] // 4
+        for by in range(4):
+            piece = slice(by * rows, (by + 1) * rows)
+            at = pl.multiple_of(((where_ref[2 - n] + 4 - by) & 3) * rows, 8)
+            whole_ref[core, pl.ds(at, rows), :] = own[piece, :]
+            whole_ref[1 - core, pl.ds(at, rows), :] = got[piece, :]
     for half in range(2):
         lanes = slice(half * LANES, (half + 1) * LANES)
+        for tap in range(6):
+            conv_ref[3 + tap, lanes, :] = scratch[0][half, tap * LANES : (tap + 1) * LANES, :]
         for tap in range(3):
-            conv_ref[tap, lanes, :] = joined[half, tap * LANES : (tap + 1) * LANES, :]
+            conv_ref[tap, lanes, :] = scratch[1][half, tap * LANES : (tap + 1) * LANES, :]
         for n in range(expand_ref.shape[1] // channels):
             at = (3 + n) * LANES
-            expand_ref[lanes, n * channels : (n + 1) * channels] = joined[half, at : at + LANES, :]
+            expand_ref[lanes, n * channels : (n + 1) * channels] = scratch[1][half, at : at + LANES, :]
 
 
 def assemble(where, groups, channels, deep):
@@ -411,7 +473,7 @@
         ),
         in_specs=[scalars()] + [whole()] * len(refs),
         out_specs=(whole(), whole()),
-        scratch_shapes=[pltpu.VMEM((2, 4 * groups[1][0].shape[0], channels), jnp.float32)],
+        scratch_shapes=[pltpu.VMEM((2,) + group[0].shape, jnp.float32) for group in groups],
         compiler_params=params(),
         cost_estimate=pl.CostEstimate(flops=0, bytes_accessed=7 * 10**6, transcendentals=0),
         name="assemble",
@@ -426,25 +488,25 @@
     cotangent = deep_cotangent[0].reshape(all_rows * band, deep)
     share = tissue_tiles.astype(jnp.float32) / TILES
     core = lax.axis_index("core").astype(jnp.int32)
-    where = jnp.stack([core, lax.axis_index("x")]).astype(jnp.int32)
+    where = jnp.stack([core, lax.axis_index("x"), lax.axis_index("y")]).astype(jnp.int32)
 
     sent, weighted = build_sent(share, cotangent, expand_weight, preact, devices)
     blocks = prepare(stem_input[0])
     above = prepare(shifted(stem_input[0, -1:], 1))
     arrived = exchange(sent, SPACE)
-    own_inner, other_inner, own_outer, other_outer, grad = terms(
-        where[:1], arrived, preact, above, blocks, weighted
-    )
-    below = shifted(grad[:1], -1)
+    other_inner, other_outer, grad, first, turned_active = other_terms(
+        where, arrived, preact, above, blocks, weighted
+    )
+    below = shifted(first, -1)
 
     samples_all = stem_input.shape[0] * SIZES["y"] * SIZES["core"]
     scale = float(samples_all * all_rows * out_cols) ** (-0.5)
     got_inner, got_outer = swapped(other_inner, "core", 1), swapped(other_outer, "core", 1)
-    inner, outer, *parts = combine(where, own_inner, got_inner, own_outer, got_outer)
+    cuts = own_sums(where, grad, turned_active, above, blocks, weighted, got_inner, got_outer)
     inner, outer, grad_input = total_sums(
-        inner, outer, parts, scale, below, lambda b: input_grad(grad, b, conv_weight)
-    )
-    groups = [pieces + [swapped(piece, "core", 1) for piece in pieces] for pieces in (inner, outer)]
+        cuts, scale, below, lambda b: input_grad(grad, b, conv_weight)
+    )
+    groups = [(x, swapped(x, "core", 1)) for x in (inner, outer)]
     grad_conv, grad_expand = assemble(where, groups, channels, deep)
     return (grad_input[None], grad_conv.reshape(3, 3, channels, channels), grad_expand)
 

time: 136 us -> 140 us (1.029)
  starting transfers between devices: 60.6 us -> 69 us
  waiting for transfers between devices: 50.3 us -> 46.5 us
  local copies, waits for them, and re-layouts: 6.94 us -> 4.85 us
  Pallas kernels: 15.1 us -> 16.8 us
    ppermute x9 -> x19, starting transfers between devices: 15.6 us -> 27.2 us  [rotated(): return lax.ppermute(x, axis, [(i, (i + by) % size) for i in range(size)])]
    all_to_all x3 -> x1, starting transfers between devices: 19.6 us -> 11.9 us  [exchange(): return lax.all_to_all(x, axis, split_axis=0, concat_axis=0, tiled=True)]
    ppermute x9 -> x6, starting transfers between devices: 12.6 us -> 19.1 us  [swapped(): return lax.ppermute(x, axis, [(i, i ^ bit) for i in range(SIZES[axis])])]
    ppermute x9 -> x19, waiting for transfers between devices: 19.5 us -> 16.5 us  [rotated(): return lax.ppermute(x, axis, [(i, (i + by) % size) for i in range(size)])]
    ppermute x6, starting transfers between devices: 8.52 us -> 6.37 us  [turned(): return lax.ppermute(x, ('x', 'z', 'y'), pairs)]
    pallas_call x2 -> x3, Pallas kernels: 6.85 us -> 8.4 us  [the longest x1 4.81 us: other_terms(): pl.pallas_call(other_kernel, out_shape=(inner, outer, grad, first, turned...]
    ppermute x9 -> x6, waiting for transfers between devices: 13 us -> 13.5 us  [swapped(): return lax.ppermute(x, axis, [(i, i ^ bit) for i in range(SIZES[axis])])]
    unnamed x16 -> x32, local copies, waits for them, and re-layouts: 5.01 us -> 4.7 us
  transfers between devices with their start and end apart: 29 -> 34, of which waited for: 19 -> 17; matrix products, arithmetic and copies ran while one was open for 1% -> 1% of each run, Pallas kernels for 4% -> 4%
where the time goes in v5:
time: 140 us
  starting transfers between devices  69 us (49%)
  waiting for transfers between devices  46.5 us (33%)
  Pallas kernels  16.8 us (12%)
  local copies, waits for them, and re-layouts  4.85 us (3%)
  between operations  1.75 us (1%)
    ppermute x19, starting transfers between devices, rotated(): return lax.ppermute(x, axis, [(i, (i + by) % size) for i in range(size)])  27.2 us
    ppermute x6, starting transfers between devices, swapped(): return lax.ppermute(x, axis, [(i, i ^ bit) for i in range(SIZES[axis])])  19.1 us
    ppermute x19, waiting for transfers between devices, rotated(): return lax.ppermute(x, axis, [(i, (i + by) % size) for i in range(size)])  16.5 us
    ppermute x6, waiting for transfers between devices, swapped(): return lax.ppermute(x, axis, [(i, i ^ bit) for i in range(SIZES[axis])])  13.5 us
    all_to_all x1, starting transfers between devices, exchange(): return lax.all_to_all(x, axis, split_axis=0, concat_axis=0, tiled=True)  11.9 us
    ppermute x2, waiting for transfers between devices, shifted(): return lax.ppermute(x, SPACE, pairs)  10.5 us
    ppermute x6, starting transfers between devices, turned(): return lax.ppermute(x, ('x', 'z', 'y'), pairs)  6.37 us
    ppermute x6, waiting for transfers between devices, turned(): return lax.ppermute(x, ('x', 'z', 'y'), pairs)  6.05 us
  transfers between devices with their start and end apart: 34, of which 17 were waited for; matrix products, arithmetic and copies ran while one was open for 1% of the time, Pallas kernels for 4%

profile of v5, /device:TPU:1, one launch (start us, length us, event | category | flops | bytes accessed | tf_op | source)
XLA Modules:
  0.0 139.8 jit_solution(7034954803693271466)
XLA Ops:
  1.4 2.9 %build_sent.1 = (bf16[32,32,256]{2,1,0:T(8,128)(2,1)}, bf16[512,1024]{1,0:T(8,128)(2,1)}) custom-call(f32[1]{0:T(128)S(6)} %div.3.share_ref, bf16[512,1024]{1,0:T(8,128)(2,1)} %bitcast.46, bf16[256,1024]{1,0:T(8,128)(2,1)} %weight_hbm.1, bf16[2,256,256]{2,1,0:T(8,128)(2,1)} %bitcast.48), custom_call_target="tpu_custom_call" | custom-call | flops 268000000 | bytes 4000000 | tf_op jit(solution)/shard_map/build_sent/pallas_call | solution.py:79
  4.3 11.9 %all-to-all-start = ((bf16[32,32,256]{2,1,0:T(8,128)(2,1)}), bf16[32,32,256]{2,1,0:T(8,128)(2,1)S(1)}, u32[]{:S(2)}, u32[]{:S(2)}) async-start(bf16[32,32,256]{2,1,0:T(8,128)(2,1)} %get-tuple-element.70), calls=%async_computation | async-start | bytes 1048576 | tf_op jit(solution)/shard_map/all_to_all | solution.py:338
  16.3 3.1 %collective-permute-start = (bf16[1,512,256]{2,1,0:T(8,128)(2,1)S(1)}, bf16[1,512,256]{2,1,0:T(8,128)(2,1)S(1)}, u32[]{:S(2)}, u32[]{:S(2)}) collective-permute-start(bf16[1,512,256]{2,1,0:T(8,128)(2,1)S(1)} %slice_bitcast_fusion), channel_id=1, source_target_pairs={{0,8},{8,16},{16,24},{24,32},{32,40},{40,48},{48,56},{56,64},{64,7... | collective-permute-start | bytes 786440 | tf_op jit(solution)/shard_map/ppermute | solution.py:41
  21.8 10.5 %collective-permute-done.x_ref = bf16[1,512,256]{2,1,0:T(8,128)(2,1)S(1)} collective-permute-done((bf16[1,512,256]{2,1,0:T(8,128)(2,1)S(1)}, bf16[1,512,256]{2,1,0:T(8,128)(2,1)S(1)}, u32[]{:S(2)}, u32[]{:S(2)}) %collective-permute-start) | collective-permute-done | bytes 262176 | tf_op jit(solution)/shard_map/ppermute | solution.py:41
  34.1 4.8 %other_terms.1 = (f32[768,256]{1,0:T(8,128)}, f32[896,256]{1,0:T(8,128)}, bf16[2,256,256]{2,1,0:T(8,128)(2,1)}, bf16[1,256,256]{2,1,0:T(8,128)(2,1)}, bf16[256,512]{1,0:T(8,128)(2,1)}) custom-call(s32[3]{0:T(128)} %pad_add_fusion.where_ref, bf16[32,32,256]{2,1,0:T(8,128)(2,1)} %copy-done.11, bf16[2,256,256]{2,1,0:T(8,128)(2,1)} %bitcast.49, ...), custom_call_target="tpu_custom_call" | custom-call | flops 435000000 | bytes 6000000 | tf_op jit(solution)/shard_map/other_terms/pallas_call | solution.py:214
  38.9 2.9 %collective-permute-start.2 = (f32[896,256]{1,0:T(8,128)}, f32[896,256]{1,0:T(8,128)S(1)}, u32[]{:S(2)}, u32[]{:S(2)}) collective-permute-start(f32[896,256]{1,0:T(8,128)} %get-tuple-element.75), channel_id=1, source_target_pairs={{0,1},{1,0},{2,3},{3,2},{4,5},{5,4},{6,7},{7,6},{8,9},{9,8},{10,11... | collective-permute-start | bytes 2752520 | tf_op jit(solution)/shard_map/ppermute | solution.py:365
  43.2 2.0 %collective-permute-done.1.got_inner = f32[768,256]{1,0:T(8,128)S(1)} collective-permute-done((f32[768,256]{1,0:T(8,128)}, f32[768,256]{1,0:T(8,128)S(1)}, u32[]{:S(2)}, u32[]{:S(2)}) %collective-permute-start.1) | collective-permute-done | bytes 786464 | tf_op jit(solution)/shard_map/ppermute | solution.py:365
  47.2 3.5 %own_sums.1 = (f32[192,256]{1,0:T(8,128)S(1)}, f32[192,256]{1,0:T(8,128)S(1)}, f32[192,256]{1,0:T(8,128)S(1)}, f32[96,256]{1,0:T(8,128)S(1)}, f32[96,256]{1,0:T(...) custom-call(s32[3]{0:T(128)S(1)} %copy-done.10, ...), custom_call_target="tpu_custom_call" | custom-call | flops 435000000 | bytes 8000000 | tf_op jit(solution)/shard_map/own_sums/pallas_call | solution.py:256
  50.7 3.4 %collective-permute-start.6 = (f32[112,256]{1,0:T(8,128)S(1)}, f32[112,256]{1,0:T(8,128)S(1)}, u32[]{:S(2)}, u32[]{:S(2)}) collective-permute-start(f32[112,256]{1,0:T(8,128)S(1)} %get-tuple-element.92), channel_id=1, source_target_pairs={{0,64},{64,128},{128,192},{192,0},{1,65},{65,129},{129,193},{193,1... | collective-permute-start | bytes 344072 | tf_op jit(solution)/shard_map/ppermute | solution.py:357
  54.1 1.6 %collective-permute-start.7 = (f32[112,256]{1,0:T(8,128)S(1)}, f32[112,256]{1,0:T(8,128)S(1)}, u32[]{:S(2)}, u32[]{:S(2)}) collective-permute-start(f32[112,256]{1,0:T(8,128)S(1)} %get-tuple-element.93), channel_id=1, source_target_pairs={{0,192},{64,0},{128,64},{192,128},{1,193},{65,1},{129,65},{193,129... | collective-permute-start | bytes 344072 | tf_op jit(solution)/shard_map/ppermute | solution.py:357
  58.5 2.0 %collective-permute-done.4.refs_2_ = f32[96,256]{1,0:T(8,128)S(1)} collective-permute-done((f32[96,256]{1,0:T(8,128)S(1)}, f32[96,256]{1,0:T(8,128)S(1)}, u32[]{:S(2)}, u32[]{:S(2)}) %collective-permute-start.4) | collective-permute-done | bytes 98336 | tf_op jit(solution)/shard_map/ppermute | solution.py:357
  60.7 2.7 %collective-permute-start.11 = (f32[224,256]{1,0:T(8,128)S(1)}, f32[224,256]{1,0:T(8,128)S(1)}, u32[]{:S(2)}, u32[]{:S(2)}) collective-permute-start(f32[224,256]{1,0:T(8,128)S(1)} %get-tuple-element.103), channel_id=1, source_target_pairs={{0,192},{64,0},{128,64},{192,128},{1,193},{65,1},{129,65},{193,129... | collective-permute-start | bytes 688136 | tf_op jit(solution)/shard_map/ppermute | solution.py:357
  63.4 1.5 %collective-permute-start.8 = (f32[192,256]{1,0:T(8,128)S(1)}, f32[192,256]{1,0:T(8,128)S(1)}, u32[]{:S(2)}, u32[]{:S(2)}) collective-permute-start(f32[192,256]{1,0:T(8,128)S(1)} %get-tuple-element.100), channel_id=1, source_target_pairs={{0,2},{2,4},{4,6},{6,0},{1,3},{3,5},{5,7},{7,1},{8,10},{10,12},{12... | collective-permute-start | bytes 589832 | tf_op jit(solution)/shard_map/ppermute | solution.py:357
  66.0 3.3 %collective-permute-done.8 = f32[192,256]{1,0:T(8,128)S(1)} collective-permute-done((f32[192,256]{1,0:T(8,128)S(1)}, f32[192,256]{1,0:T(8,128)S(1)}, u32[]{:S(2)}, u32[]{:S(2)}) %collective-permute-start.8) | collective-permute-done | bytes 196640 | tf_op jit(solution)/shard_map/ppermute | solution.py:357
  70.1 4.7 %collective-permute-done.12 = f32[224,256]{1,0:T(8,128)S(1)} collective-permute-done((f32[224,256]{1,0:T(8,128)S(1)}, f32[224,256]{1,0:T(8,128)S(1)}, u32[]{:S(2)}, u32[]{:S(2)}) %collective-permute-start.12) | collective-permute-done | bytes 229408 | tf_op jit(solution)/shard_map/ppermute | solution.py:365
  77.9 2.2 %collective-permute-done.13 = f32[56,256]{1,0:T(8,128)S(1)} collective-permute-done((f32[56,256]{1,0:T(8,128)S(1)}, f32[56,256]{1,0:T(8,128)S(1)}, u32[]{:S(2)}, u32[]{:S(2)}) %collective-permute-start.13) | collective-permute-done | bytes 57376 | tf_op jit(solution)/shard_map/ppermute | solution.py:375
  80.6 2.1 %collective-permute-start.18 = (f32[56,256]{1,0:T(8,128)S(1)}, f32[56,256]{1,0:T(8,128)S(1)}, u32[]{:S(2)}, u32[]{:S(2)}) collective-permute-start(f32[56,256]{1,0:T(8,128)S(1)} %fusion.6), channel_id=1, source_target_pairs={{0,48},{8,56},{16,0},{24,8},{32,16},{40,24},{48,32},{56,40},{1,49}... | collective-permute-start | bytes 172040 | tf_op jit(solution)/shard_map/ppermute | solution.py:357
  83.8 2.2 %collective-permute-start.16 = (f32[56,256]{1,0:T(8,128)S(1)}, f32[56,256]{1,0:T(8,128)S(1)}, u32[]{:S(2)}, u32[]{:S(2)}) collective-permute-start(f32[56,256]{1,0:T(8,128)S(1)} %fusion.6), channel_id=1, source_target_pairs={{0,16},{8,24},{16,32},{24,40},{32,48},{40,56},{48,0},{56,8},{1,17}... | collective-permute-start | bytes 172040 | tf_op jit(solution)/shard_map/ppermute | solution.py:357
  86.0 1.9 %input_grad.1 = bf16[4,512,256]{2,1,0:T(8,128)(2,1)} custom-call(bf16[2,256,256]{2,1,0:T(8,128)(2,1)S(1)} %copy-done.8, bf16[1,256,256]{2,1,0:T(8,128)(2,1)S(1)} %collective-permute-done.3.below_ref, bf16[3,3,256,256]{3,2,1,0:T(8,128)(2,1)S(1)} %copy-done.6), custom_call_target="tpu_custom_call" | custom-call | flops 604000000 | bytes 3000000 | tf_op jit(solution)/shard_map/input_grad/pallas_call | solution.py:325
  87.9 1.8 %collective-permute-done.17 = f32[56,256]{1,0:T(8,128)S(1)} collective-permute-done((f32[56,256]{1,0:T(8,128)S(1)}, f32[56,256]{1,0:T(8,128)S(1)}, u32[]{:S(2)}, u32[]{:S(2)}) %collective-permute-start.17) | collective-permute-done | bytes 57376 | tf_op jit(solution)/shard_map/ppermute | solution.py:357
  90.7 2.5 %collective-permute-start.20 = (f32[56,256]{1,0:T(8,128)S(1)}, f32[56,256]{1,0:T(8,128)S(1)}, u32[]{:S(2)}, u32[]{:S(2)}) collective-permute-start(f32[56,256]{1,0:T(8,128)S(1)} %get-tuple-element.138), channel_id=1, source_target_pairs={{0,128},{2,130},{4,132},{6,134},{8,12},{10,14},{12,8},{14,10},{16,... | collective-permute-start | bytes 172040 | tf_op jit(solution)/shard_map/ppermute | solution.py:375
  96.5 1.9 %collective-permute-start.22 = (f32[224,256]{1,0:T(8,128)S(1)}, f32[224,256]{1,0:T(8,128)S(1)}, u32[]{:S(2)}, u32[]{:S(2)}) collective-permute-start(f32[224,256]{1,0:T(8,128)S(1)} %bitcast.44), channel_id=1, source_target_pairs={{0,8},{8,0},{16,24},{24,16},{32,40},{40,32},{48,56},{56,48},{1,9},... | collective-permute-start | bytes 688136 | tf_op jit(solution)/shard_map/ppermute | solution.py:365
  98.4 3.7 %collective-permute-done.22 = f32[224,256]{1,0:T(8,128)S(1)} collective-permute-done((f32[224,256]{1,0:T(8,128)S(1)}, f32[224,256]{1,0:T(8,128)S(1)}, u32[]{:S(2)}, u32[]{:S(2)}) %collective-permute-start.22) | collective-permute-done | bytes 229408 | tf_op jit(solution)/shard_map/ppermute | solution.py:365
  103.7 1.7 %collective-permute-start.24 = (f32[192,256]{1,0:T(8,128)S(1)}, f32[192,256]{1,0:T(8,128)S(1)}, u32[]{:S(2)}, u32[]{:S(2)}) collective-permute-start(f32[192,256]{1,0:T(8,128)S(1)} %slice_select_fusion), channel_id=1, source_target_pairs={{0,6},{2,0},{4,2},{6,4},{1,7},{3,1},{5,3},{7,5},{8,14},{10,8},{12,... | collective-permute-start | bytes 589832 | tf_op jit(solution)/shard_map/ppermute | solution.py:357
  105.4 2.8 %collective-permute-done.24 = f32[192,256]{1,0:T(8,128)S(1)} collective-permute-done((f32[192,256]{1,0:T(8,128)S(1)}, f32[192,256]{1,0:T(8,128)S(1)}, u32[]{:S(2)}, u32[]{:S(2)}) %collective-permute-start.24) | collective-permute-done | bytes 196640 | tf_op jit(solution)/shard_map/ppermute | solution.py:357
  108.2 2.9 %collective-permute-done.23 = f32[192,256]{1,0:T(8,128)S(1)} collective-permute-done((f32[192,256]{1,0:T(8,128)S(1)}, f32[192,256]{1,0:T(8,128)S(1)}, u32[]{:S(2)}, u32[]{:S(2)}) %collective-permute-start.23) | collective-permute-done | bytes 196640 | tf_op jit(solution)/shard_map/ppermute | solution.py:357
  111.3 2.7 %collective-permute-start.28 = (f32[96,256]{1,0:T(8,128)S(1)}, f32[96,256]{1,0:T(8,128)S(1)}, u32[]{:S(2)}, u32[]{:S(2)}) collective-permute-start(f32[96,256]{1,0:T(8,128)S(1)} %slice.21), channel_id=1, source_target_pairs={{0,6},{2,0},{4,2},{6,4},{1,7},{3,1},{5,3},{7,5},{8,14},{10,8},{12,... | collective-permute-start | bytes 294920 | tf_op jit(solution)/shard_map/ppermute | solution.py:357
  113.9 2.7 %collective-permute-start.30 = (f32[112,256]{1,0:T(8,128)S(1)}, f32[112,256]{1,0:T(8,128)S(1)}, u32[]{:S(2)}, u32[]{:S(2)}) collective-permute-start(f32[112,256]{1,0:T(8,128)S(1)} %slice.23), channel_id=1, source_target_pairs={{0,192},{64,0},{128,64},{192,128},{1,193},{65,1},{129,65},{193,129... | collective-permute-start | bytes 344072 | tf_op jit(solution)/shard_map/ppermute | solution.py:357
  116.6 3.3 %collective-permute-done.29 = f32[112,256]{1,0:T(8,128)S(1)} collective-permute-done((f32[112,256]{1,0:T(8,128)S(1)}, f32[112,256]{1,0:T(8,128)S(1)}, u32[]{:S(2)}, u32[]{:S(2)}) %collective-permute-start.29) | collective-permute-done | bytes 114720 | tf_op jit(solution)/shard_map/ppermute | solution.py:357
  120.0 13.9 %collective-permute-start.32 = (f32[896,256]{1,0:T(8,128)S(1)}, f32[896,256]{1,0:T(8,128)S(1)}, u32[]{:S(2)}, u32[]{:S(2)}) collective-permute-start(f32[896,256]{1,0:T(8,128)S(1)} %constant_dynamic-update-slice_fusion.5.refs_2_), channel_id=1, source_target_pairs={{0,1},{1,0},{2,3},{3,2},{4,5},{5,4},{6,7},{7,6},{8,9},{9,8},{10,11... | collective-permute-start | bytes 2752520 | tf_op jit(solution)/shard_map/ppermute | solution.py:365
  134.1 3.0 %collective-permute-done.31.refs_1_ = f32[768,256]{1,0:T(8,128)S(1)} collective-permute-done((f32[768,256]{1,0:T(8,128)S(1)}, f32[768,256]{1,0:T(8,128)S(1)}, u32[]{:S(2)}, u32[]{:S(2)}) %collective-permute-start.31) | collective-permute-done | bytes 786464 | tf_op jit(solution)/shard_map/ppermute | solution.py:365
  137.2 2.7 %assemble.1 = (f32[9,256,256]{2,1,0:T(8,128)}, f32[256,1024]{1,0:T(8,128)}) custom-call(s32[3]{0:T(128)S(1)} %copy-done.10, f32[768,256]{1,0:T(8,128)S(1)} %constant_dynamic-update-slice_fusion.refs_0_, f32[768,256]{1,0:T(8,128)S(1)} %collective-permute-done.31.refs_1_, f32[896,256]{1,0:T(8,128)S(1)} %constant_dynamic-update-slice_fusion.5.refs_2_, ...), custom_call_target="tpu_custom_call" | custom-call | bytes 7000000 | tf_op jit(solution)/shard_map/assemble/pallas_call | solution.py:468
  (97 shorter events, 23.1 us)
Async XLA Ops:
  4.3 28.9 %all-to-all-start = ((bf16[32,32,256]{2,1,0:T(8,128)(2,1)}), bf16[32,32,256]{2,1,0:T(8,128)(2,1)S(1)}, u32[]{:S(2)}, u32[]{:S(2)}) async-start(bf16[32,32,256]{2,1,0:T(8,128)(2,1)} %get-tuple-element.70), calls=%async_computation | async-start | bytes 1048576 | tf_op jit(solution)/shard_map/all_to_all | solution.py:338
  16.3 16.0 %collective-permute-start = (bf16[1,512,256]{2,1,0:T(8,128)(2,1)S(1)}, bf16[1,512,256]{2,1,0:T(8,128)(2,1)S(1)}, u32[]{:S(2)}, u32[]{:S(2)}) collective-permute-start(bf16[1,512,256]{2,1,0:T(8,128)(2,1)S(1)} %slice_bitcast_fusion), channel_id=1, source_target_pairs={{0,8},{8,16},{16,24},{24,32},{32,40},{40,48},{48,56},{56,64},{64,7... | collective-permute-start | bytes 786440 | tf_op jit(solution)/shard_map/ppermute | solution.py:41
  38.9 6.3 %collective-permute-start.2 = (f32[896,256]{1,0:T(8,128)}, f32[896,256]{1,0:T(8,128)S(1)}, u32[]{:S(2)}, u32[]{:S(2)}) collective-permute-start(f32[896,256]{1,0:T(8,128)} %get-tuple-element.75), channel_id=1, source_target_pairs={{0,1},{1,0},{2,3},{3,2},{4,5},{5,4},{6,7},{7,6},{8,9},{9,8},{10,11... | collective-permute-start | bytes 2752520 | tf_op jit(solution)/shard_map/ppermute | solution.py:365
  41.8 3.4 %collective-permute-start.1 = (f32[768,256]{1,0:T(8,128)}, f32[768,256]{1,0:T(8,128)S(1)}, u32[]{:S(2)}, u32[]{:S(2)}) collective-permute-start(f32[768,256]{1,0:T(8,128)} %get-tuple-element.74), channel_id=1, source_target_pairs={{0,1},{1,0},{2,3},{3,2},{4,5},{5,4},{6,7},{7,6},{8,9},{9,8},{10,11... | collective-permute-start | bytes 2359304 | tf_op jit(solution)/shard_map/ppermute | solution.py:365
  41.9 8.8 %collective-permute-start.3 = (bf16[1,256,256]{2,1,0:T(8,128)(2,1)}, bf16[1,256,256]{2,1,0:T(8,128)(2,1)S(1)}, u32[]{:S(2)}, u32[]{:S(2)}) collective-permute-start(bf16[1,256,256]{2,1,0:T(8,128)(2,1)} %get-tuple-element.86), channel_id=1, source_target_pairs={{8,0},{16,8},{24,16},{32,24},{40,32},{48,40},{56,48},{64,56},{72,6... | collective-permute-start | bytes 393224 | tf_op jit(solution)/shard_map/ppermute | solution.py:41
  50.7 9.8 %collective-permute-start.6 = (f32[112,256]{1,0:T(8,128)S(1)}, f32[112,256]{1,0:T(8,128)S(1)}, u32[]{:S(2)}, u32[]{:S(2)}) collective-permute-start(f32[112,256]{1,0:T(8,128)S(1)} %get-tuple-element.92), channel_id=1, source_target_pairs={{0,64},{64,128},{128,192},{192,0},{1,65},{65,129},{129,193},{193,1... | collective-permute-start | bytes 344072 | tf_op jit(solution)/shard_map/ppermute | solution.py:357
  54.1 6.4 %collective-permute-start.7 = (f32[112,256]{1,0:T(8,128)S(1)}, f32[112,256]{1,0:T(8,128)S(1)}, u32[]{:S(2)}, u32[]{:S(2)}) collective-permute-start(f32[112,256]{1,0:T(8,128)S(1)} %get-tuple-element.93), channel_id=1, source_target_pairs={{0,192},{64,0},{128,64},{192,128},{1,193},{65,1},{129,65},{193,129... | collective-permute-start | bytes 344072 | tf_op jit(solution)/shard_map/ppermute | solution.py:357
  55.8 4.7 %collective-permute-start.4 = (f32[96,256]{1,0:T(8,128)S(1)}, f32[96,256]{1,0:T(8,128)S(1)}, u32[]{:S(2)}, u32[]{:S(2)}) collective-permute-start(f32[96,256]{1,0:T(8,128)S(1)} %get-tuple-element.90), channel_id=1, source_target_pairs={{0,2},{2,4},{4,6},{6,0},{1,3},{3,5},{5,7},{7,1},{8,10},{10,12},{12... | collective-permute-start | bytes 294920 | tf_op jit(solution)/shard_map/ppermute | solution.py:357
  57.1 3.5 %collective-permute-start.5 = (f32[96,256]{1,0:T(8,128)S(1)}, f32[96,256]{1,0:T(8,128)S(1)}, u32[]{:S(2)}, u32[]{:S(2)}) collective-permute-start(f32[96,256]{1,0:T(8,128)S(1)} %get-tuple-element.91), channel_id=1, source_target_pairs={{0,6},{2,0},{4,2},{6,4},{1,7},{3,1},{5,3},{7,5},{8,14},{10,8},{12,... | collective-permute-start | bytes 294920 | tf_op jit(solution)/shard_map/ppermute | solution.py:357
  60.6 9.1 %collective-permute-start.10 = (f32[224,256]{1,0:T(8,128)S(1)}, f32[224,256]{1,0:T(8,128)S(1)}, u32[]{:S(2)}, u32[]{:S(2)}) collective-permute-start(f32[224,256]{1,0:T(8,128)S(1)} %get-tuple-element.102), channel_id=1, source_target_pairs={{0,64},{64,128},{128,192},{192,0},{1,65},{65,129},{129,193},{193,1... | collective-permute-start | bytes 688136 | tf_op jit(solution)/shard_map/ppermute | solution.py:357
  60.7 9.0 %collective-permute-start.11 = (f32[224,256]{1,0:T(8,128)S(1)}, f32[224,256]{1,0:T(8,128)S(1)}, u32[]{:S(2)}, u32[]{:S(2)}) collective-permute-start(f32[224,256]{1,0:T(8,128)S(1)} %get-tuple-element.103), channel_id=1, source_target_pairs={{0,192},{64,0},{128,64},{192,128},{1,193},{65,1},{129,65},{193,129... | collective-permute-start | bytes 688136 | tf_op jit(solution)/shard_map/ppermute | solution.py:357
  63.4 6.0 %collective-permute-start.8 = (f32[192,256]{1,0:T(8,128)S(1)}, f32[192,256]{1,0:T(8,128)S(1)}, u32[]{:S(2)}, u32[]{:S(2)}) collective-permute-start(f32[192,256]{1,0:T(8,128)S(1)} %get-tuple-element.100), channel_id=1, source_target_pairs={{0,2},{2,4},{4,6},{6,0},{1,3},{3,5},{5,7},{7,1},{8,10},{10,12},{12... | collective-permute-start | bytes 589832 | tf_op jit(solution)/shard_map/ppermute | solution.py:357
  64.9 4.8 %collective-permute-start.9 = (f32[192,256]{1,0:T(8,128)S(1)}, f32[192,256]{1,0:T(8,128)S(1)}, u32[]{:S(2)}, u32[]{:S(2)}) collective-permute-start(f32[192,256]{1,0:T(8,128)S(1)} %get-tuple-element.101), channel_id=1, source_target_pairs={{0,6},{2,0},{4,2},{6,4},{1,7},{3,1},{5,3},{7,5},{8,14},{10,8},{12,... | collective-permute-start | bytes 589832 | tf_op jit(solution)/shard_map/ppermute | solution.py:357
  69.9 5.0 %collective-permute-start.12 = (f32[224,256]{1,0:T(8,128)S(1)}, f32[224,256]{1,0:T(8,128)S(1)}, u32[]{:S(2)}, u32[]{:S(2)}) collective-permute-start(f32[224,256]{1,0:T(8,128)S(1)} %fusion.1), channel_id=1, source_target_pairs={{0,8},{8,0},{16,24},{24,16},{32,40},{40,32},{48,56},{56,48},{1,9},... | collective-permute-start | bytes 688136 | tf_op jit(solution)/shard_map/ppermute | solution.py:365
  74.9 5.1 %collective-permute-start.13 = (f32[56,256]{1,0:T(8,128)S(1)}, f32[56,256]{1,0:T(8,128)S(1)}, u32[]{:S(2)}, u32[]{:S(2)}) collective-permute-start(f32[56,256]{1,0:T(8,128)S(1)} %get-tuple-element.109), channel_id=1, source_target_pairs={{0,64},{2,66},{4,68},{6,70},{8,10},{10,12},{12,14},{14,8},{16,80},... | collective-permute-start | bytes 172040 | tf_op jit(solution)/shard_map/ppermute | solution.py:375
  75.2 4.8 %collective-permute-start.14 = (f32[56,256]{1,0:T(8,128)S(1)}, f32[56,256]{1,0:T(8,128)S(1)}, u32[]{:S(2)}, u32[]{:S(2)}) collective-permute-start(f32[56,256]{1,0:T(8,128)S(1)} %get-tuple-element.110), channel_id=1, source_target_pairs={{0,128},{2,130},{4,132},{6,134},{8,12},{10,14},{12,8},{14,10},{16,... | collective-permute-start | bytes 172040 | tf_op jit(solution)/shard_map/ppermute | solution.py:375
  76.6 4.0 %collective-permute-start.15 = (f32[56,256]{1,0:T(8,128)S(1)}, f32[56,256]{1,0:T(8,128)S(1)}, u32[]{:S(2)}, u32[]{:S(2)}) collective-permute-start(f32[56,256]{1,0:T(8,128)S(1)} %get-tuple-element.111), channel_id=1, source_target_pairs={{0,192},{2,194},{4,196},{6,198},{8,14},{10,8},{12,10},{14,12},{16,... | collective-permute-start | bytes 172040 | tf_op jit(solution)/shard_map/ppermute | solution.py:375
  80.6 7.3 %collective-permute-start.18 = (f32[56,256]{1,0:T(8,128)S(1)}, f32[56,256]{1,0:T(8,128)S(1)}, u32[]{:S(2)}, u32[]{:S(2)}) collective-permute-start(f32[56,256]{1,0:T(8,128)S(1)} %fusion.6), channel_id=1, source_target_pairs={{0,48},{8,56},{16,0},{24,8},{32,16},{40,24},{48,32},{56,40},{1,49}... | collective-permute-start | bytes 172040 | tf_op jit(solution)/shard_map/ppermute | solution.py:357
  82.7 7.0 %collective-permute-start.17 = (f32[56,256]{1,0:T(8,128)S(1)}, f32[56,256]{1,0:T(8,128)S(1)}, u32[]{:S(2)}, u32[]{:S(2)}) collective-permute-start(f32[56,256]{1,0:T(8,128)S(1)} %fusion.6), channel_id=1, source_target_pairs={{0,32},{8,40},{16,48},{24,56},{32,0},{40,8},{48,16},{56,24},{1,33}... | collective-permute-start | bytes 172040 | tf_op jit(solution)/shard_map/ppermute | solution.py:357
  83.8 5.9 %collective-permute-start.16 = (f32[56,256]{1,0:T(8,128)S(1)}, f32[56,256]{1,0:T(8,128)S(1)}, u32[]{:S(2)}, u32[]{:S(2)}) collective-permute-start(f32[56,256]{1,0:T(8,128)S(1)} %fusion.6), channel_id=1, source_target_pairs={{0,16},{8,24},{16,32},{24,40},{32,48},{40,56},{48,0},{56,8},{1,17}... | collective-permute-start | bytes 172040 | tf_op jit(solution)/shard_map/ppermute | solution.py:357
  89.7 4.3 %collective-permute-start.19 = (f32[56,256]{1,0:T(8,128)S(1)}, f32[56,256]{1,0:T(8,128)S(1)}, u32[]{:S(2)}, u32[]{:S(2)}) collective-permute-start(f32[56,256]{1,0:T(8,128)S(1)} %get-tuple-element.138), channel_id=1, source_target_pairs={{0,64},{2,66},{4,68},{6,70},{8,10},{10,12},{12,14},{14,8},{16,80},... | collective-permute-start | bytes 172040 | tf_op jit(solution)/shard_map/ppermute | solution.py:375
  90.7 4.7 %collective-permute-start.20 = (f32[56,256]{1,0:T(8,128)S(1)}, f32[56,256]{1,0:T(8,128)S(1)}, u32[]{:S(2)}, u32[]{:S(2)}) collective-permute-start(f32[56,256]{1,0:T(8,128)S(1)} %get-tuple-element.138), channel_id=1, source_target_pairs={{0,128},{2,130},{4,132},{6,134},{8,12},{10,14},{12,8},{14,10},{16,... | collective-permute-start | bytes 172040 | tf_op jit(solution)/shard_map/ppermute | solution.py:375
  96.5 5.6 %collective-permute-start.22 = (f32[224,256]{1,0:T(8,128)S(1)}, f32[224,256]{1,0:T(8,128)S(1)}, u32[]{:S(2)}, u32[]{:S(2)}) collective-permute-start(f32[224,256]{1,0:T(8,128)S(1)} %bitcast.44), channel_id=1, source_target_pairs={{0,8},{8,0},{16,24},{24,16},{32,40},{40,32},{48,56},{56,48},{1,9},... | collective-permute-start | bytes 688136 | tf_op jit(solution)/shard_map/ppermute | solution.py:365
  102.2 8.9 %collective-permute-start.26 = (f32[224,256]{1,0:T(8,128)S(1)}, f32[224,256]{1,0:T(8,128)S(1)}, u32[]{:S(2)}, u32[]{:S(2)}) collective-permute-start(f32[224,256]{1,0:T(8,128)S(1)} %broadcast_select_fusion), channel_id=1, source_target_pairs={{0,192},{64,0},{128,64},{192,128},{1,193},{65,1},{129,65},{193,129... | collective-permute-start | bytes 688136 | tf_op jit(solution)/shard_map/ppermute | solution.py:357
  103.0 8.1 %collective-permute-start.25 = (f32[224,256]{1,0:T(8,128)S(1)}, f32[224,256]{1,0:T(8,128)S(1)}, u32[]{:S(2)}, u32[]{:S(2)}) collective-permute-start(f32[224,256]{1,0:T(8,128)S(1)} %broadcast_select_fusion), channel_id=1, source_target_pairs={{0,64},{64,128},{128,192},{192,0},{1,65},{65,129},{129,193},{193,1... | collective-permute-start | bytes 688136 | tf_op jit(solution)/shard_map/ppermute | solution.py:357
  103.7 4.5 %collective-permute-start.24 = (f32[192,256]{1,0:T(8,128)S(1)}, f32[192,256]{1,0:T(8,128)S(1)}, u32[]{:S(2)}, u32[]{:S(2)}) collective-permute-start(f32[192,256]{1,0:T(8,128)S(1)} %slice_select_fusion), channel_id=1, source_target_pairs={{0,6},{2,0},{4,2},{6,4},{1,7},{3,1},{5,3},{7,5},{8,14},{10,8},{12,... | collective-permute-start | bytes 589832 | tf_op jit(solution)/shard_map/ppermute | solution.py:357
  105.4 5.7 %collective-permute-start.23 = (f32[192,256]{1,0:T(8,128)S(1)}, f32[192,256]{1,0:T(8,128)S(1)}, u32[]{:S(2)}, u32[]{:S(2)}) collective-permute-start(f32[192,256]{1,0:T(8,128)S(1)} %slice_select_fusion), channel_id=1, source_target_pairs={{0,2},{2,4},{4,6},{6,0},{1,3},{3,5},{5,7},{7,1},{8,10},{10,12},{12... | collective-permute-start | bytes 589832 | tf_op jit(solution)/shard_map/ppermute | solution.py:357
  111.2 5.5 %collective-permute-start.27 = (f32[96,256]{1,0:T(8,128)S(1)}, f32[96,256]{1,0:T(8,128)S(1)}, u32[]{:S(2)}, u32[]{:S(2)}) collective-permute-start(f32[96,256]{1,0:T(8,128)S(1)} %slice.20), channel_id=1, source_target_pairs={{0,2},{2,4},{4,6},{6,0},{1,3},{3,5},{5,7},{7,1},{8,10},{10,12},{12... | collective-permute-start | bytes 294920 | tf_op jit(solution)/shard_map/ppermute | solution.py:357
  111.3 5.4 %collective-permute-start.28 = (f32[96,256]{1,0:T(8,128)S(1)}, f32[96,256]{1,0:T(8,128)S(1)}, u32[]{:S(2)}, u32[]{:S(2)}) collective-permute-start(f32[96,256]{1,0:T(8,128)S(1)} %slice.21), channel_id=1, source_target_pairs={{0,6},{2,0},{4,2},{6,4},{1,7},{3,1},{5,3},{7,5},{8,14},{10,8},{12,... | collective-permute-start | bytes 294920 | tf_op jit(solution)/shard_map/ppermute | solution.py:357
  113.9 6.0 %collective-permute-start.29 = (f32[112,256]{1,0:T(8,128)S(1)}, f32[112,256]{1,0:T(8,128)S(1)}, u32[]{:S(2)}, u32[]{:S(2)}) collective-permute-start(f32[112,256]{1,0:T(8,128)S(1)} %slice.22), channel_id=1, source_target_pairs={{0,64},{64,128},{128,192},{192,0},{1,65},{65,129},{129,193},{193,1... | collective-permute-start | bytes 344072 | tf_op jit(solution)/shard_map/ppermute | solution.py:357
  113.9 6.0 %collective-permute-start.30 = (f32[112,256]{1,0:T(8,128)S(1)}, f32[112,256]{1,0:T(8,128)S(1)}, u32[]{:S(2)}, u32[]{:S(2)}) collective-permute-start(f32[112,256]{1,0:T(8,128)S(1)} %slice.23), channel_id=1, source_target_pairs={{0,192},{64,0},{128,64},{192,128},{1,193},{65,1},{129,65},{193,129... | collective-permute-start | bytes 344072 | tf_op jit(solution)/shard_map/ppermute | solution.py:357
  120.0 17.1 %collective-permute-start.32 = (f32[896,256]{1,0:T(8,128)S(1)}, f32[896,256]{1,0:T(8,128)S(1)}, u32[]{:S(2)}, u32[]{:S(2)}) collective-permute-start(f32[896,256]{1,0:T(8,128)S(1)} %constant_dynamic-update-slice_fusion.5.refs_2_), channel_id=1, source_target_pairs={{0,1},{1,0},{2,3},{3,2},{4,5},{5,4},{6,7},{7,6},{8,9},{9,8},{10,11... | collective-permute-start | bytes 2752520 | tf_op jit(solution)/shard_map/ppermute | solution.py:365
  (14 other events, 103.9 us)

commit v6 on v4

--- a/solution.py
+++ b/solution.py
@@ -123,7 +123,7 @@
 
 def terms_kernel(
     core_ref, arrived_hbm, preact_hbm, above_hbm, blocks_hbm, weighted_hbm,
-    own_inner, other_inner, own_outer, other_outer, grad_hbm,
+    inner_hbm, own_outer, other_outer, grad_hbm, first_hbm,
     arrived_ref, preact_ref, above_ref, blocks_ref, weighted_ref,
     grad_ref, turned, inner_ref, outer_ref, sems,
 ):
@@ -146,8 +146,10 @@
         hidden = arrived_ref[:, i * band : (i + 1) * band, :].astype(jnp.float32).reshape(cols, channels)
         kept = jnp.where(preact_ref[i].astype(jnp.float32) > 0.0, hidden, 0.0)
         grad_ref[i] = kept.astype(jnp.bfloat16)
-    back = [pltpu.make_async_copy(grad_ref, grad_hbm, sems.at[5])]
-    back[0].start()
+    back = [
+        pltpu.make_async_copy(grad_ref, grad_hbm, sems.at[5]),
+        pltpu.make_async_copy(grad_ref.at[0:1], first_hbm, sems.at[6]),
+    ]
     active = arrived_ref[:, chunk:, :].astype(jnp.float32).reshape(devices * chunk, channels)
     turned[...] = active.T.astype(jnp.bfloat16)
 
@@ -164,15 +166,22 @@
 
     for copy in copies[2:]:
         copy.wait()
-    for n, (inner_hbm, outer_hbm) in enumerate(((other_inner, other_outer), (own_inner, own_outer))):
-        owner = core_ref[0] if n else 1 - core_ref[0]
-        start = pl.multiple_of(owner * LANES, LANES)
+    back[0].start()
+    back[1].start()
+    pieces = inner_hbm.shape[0] // 2
+    rows_each = inner_ref.shape[1] // pieces
+    for half in range(2):
         for col_tap in range(3):
             for row_tap in (1, 2):
                 at = (3 * (row_tap - 1) + col_tap) * LANES
-                inner_ref[n, at : at + LANES, :] = half_taps(row_tap, col_tap, start)
-        back.append(pltpu.make_async_copy(inner_ref.at[n], inner_hbm, sems.at[6 + 2 * n]))
-        back[-1].start()
+                inner_ref[half, at : at + LANES, :] = half_taps(row_tap, col_tap, half * LANES)
+        for n in range(pieces):
+            piece = inner_ref.at[half, n * rows_each : (n + 1) * rows_each, :]
+            back.append(pltpu.make_async_copy(piece, inner_hbm.at[2 * n + half], sems.at[9 + 2 * n + half]))
+            back[-1].start()
+    for n, outer_hbm in enumerate((other_outer, own_outer)):
+        owner = core_ref[0] if n else 1 - core_ref[0]
+        start = pl.multiple_of(owner * LANES, LANES)
         for col_tap in range(3):
             at = col_tap * LANES
             outer_ref[n, at : at + LANES, :] = half_taps(0, col_tap, start)
@@ -183,7 +192,7 @@
                 weighted_ref[:, k * channels : (k + 1) * channels],
                 preferred_element_type=jnp.float32,
             )
-        back.append(pltpu.make_async_copy(outer_ref.at[n], outer_hbm, sems.at[7 + 2 * n]))
+        back.append(pltpu.make_async_copy(outer_ref.at[n], outer_hbm, sems.at[7 + n]))
         back[-1].start()
     for copy in back:
         copy.wait()
@@ -191,19 +200,25 @@
 
 def terms(core, arrived, preact, above, blocks, weighted):
     rows, cols, channels = preact.shape
-    inner = jax.ShapeDtypeStruct((6 * LANES, channels), jnp.float32)
+    inner = jax.ShapeDtypeStruct((8, 6 * LANES // 4, channels), jnp.float32)
     outer = jax.ShapeDtypeStruct((3 * LANES + weighted.shape[1] // 2, channels), jnp.float32)
     return pl.pallas_call(
         terms_kernel,
-        out_shape=(inner, inner, outer, outer, jax.ShapeDtypeStruct(preact.shape, jnp.bfloat16)),
+        out_shape=(
+            inner,
+            outer,
+            outer,
+            jax.ShapeDtypeStruct(preact.shape, jnp.bfloat16),
+            jax.ShapeDtypeStruct((1, cols, channels), jnp.bfloat16),
+        ),
         in_specs=[scalars()] + [far()] * 5,
         out_specs=(far(),) * 5,
         scratch_shapes=[room(x) for x in (arrived, preact, above, blocks, weighted, preact)]
         + [
             pltpu.VMEM((channels, weighted.shape[0]), jnp.bfloat16),
-            pltpu.VMEM((2,) + inner.shape, jnp.float32),
+            pltpu.VMEM((2, 6 * LANES, channels), jnp.float32),
             pltpu.VMEM((2,) + outer.shape, jnp.float32),
-            pltpu.SemaphoreType.DMA((10,)),
+            pltpu.SemaphoreType.DMA((17,)),
         ],
         compiler_params=params(54),
         cost_estimate=pl.CostEstimate(flops=870 * 10**6, bytes_accessed=8 * 10**6, transcendentals=0),
@@ -211,42 +226,24 @@
     )(core, arrived, preact, above, blocks, weighted)
 
 
-def combine_kernel(where_ref, *refs):
-    hbm, (inner_hbm, *outer_hbm), room_refs, sems = refs[:4], refs[4:9], refs[9:13], refs[13]
-    copies = [pltpu.make_async_copy(a, b, sems.at[n]) for n, (a, b) in enumerate(zip(hbm, room_refs))]
-    for copy in copies:
-        copy.start()
-    own_inner, got_inner, own_outer, got_outer = room_refs
-    rows = own_outer.shape[0] // 4
-    copies[0].wait()
-    copies[1].wait()
-    own_inner[...] += got_inner[...]
-    back = [pltpu.make_async_copy(own_inner, inner_hbm, sems.at[4])]
-    back[0].start()
-    copies[2].wait()
-    copies[3].wait()
-    own_outer[...] += got_outer[...]
-    for by, out in enumerate(outer_hbm):
+def combine_kernel(where_ref, own, got, *out_refs):
+    rows = out_refs[0].shape[0]
+    for by, out_ref in enumerate(out_refs):
         at = pl.ds(pl.multiple_of(((where_ref[1] + by) & 3) * rows, 8), rows)
-        back.append(pltpu.make_async_copy(own_outer.at[at, :], out, sems.at[5 + by]))
-        back[-1].start()
-    for copy in back:
-        copy.wait()
-
-
-def combine(where, *arrays):
-    inner, outer = arrays[0], arrays[2]
-    chunk = jax.ShapeDtypeStruct((outer.shape[0] // 4, outer.shape[1]), jnp.float32)
+        out_ref[...] = own[at, :] + got[at, :]
+
+
+def combine(where, own, got):
+    chunk = jax.ShapeDtypeStruct((own.shape[0] // 4, own.shape[1]), jnp.float32)
     return pl.pallas_call(
         combine_kernel,
-        out_shape=(jax.ShapeDtypeStruct(inner.shape, jnp.float32),) + (chunk,) * 4,
-        in_specs=[scalars()] + [far()] * 4,
-        out_specs=(far(),) * 5,
-        scratch_shapes=[room(x) for x in arrays] + [pltpu.SemaphoreType.DMA((9,))],
+        out_shape=(chunk,) * 4,
+        in_specs=[scalars()] + [whole()] * 2,
+        out_specs=(whole(),) * 4,
         compiler_params=params(24),
-        cost_estimate=pl.CostEstimate(flops=10**6, bytes_accessed=5 * 10**6, transcendentals=0),
+        cost_estimate=pl.CostEstimate(flops=10**6, bytes_accessed=3 * 10**6, transcendentals=0),
         name="combine",
-    )(where, *arrays)
+    )(where, own, got)
 
 
 def input_kernel(grad_ref, below_ref, weight_ref, out_ref, wide):
@@ -344,18 +341,16 @@
 STEPS = (1, 2, 3)
 
 
-def total_sums(inner, outer, parts, scale, below, beside):
-    inner, parts, below = barrier((split(inner), parts, below))
-    inner = exchange(inner, "y")
-    moved = [rotated(p, "x", by) for p, by in zip(parts, STEPS)]
-    inner, moved = barrier((inner, moved))
-    inner = jnp.sum(inner, axis=0)
+def total_sums(inner, outer, parts, scale, first, beside):
+    moved = barrier([rotated(p, "x", by) for p, by in zip(parts, STEPS)])
     outer = sum(moved, outer)
 
     rows = outer.shape[0] - inner.shape[0]
     both = jnp.stack([jnp.pad(inner, ((0, rows), (0, 0))), outer])
     bit = place("z") & jnp.uint32(1)
-    part = pick(both, bit) + swapped(pick(both, jnp.uint32(1) - bit), "z", 1)
+    own, other, first = barrier((pick(both, bit), pick(both, jnp.uint32(1) - bit), first))
+    part = own + swapped(other, "z", 1)
+    below = shifted(first, -1)
 
     parts = split(part)
     moved = barrier([pick(parts, turned_place(by)) for by in STEPS])
@@ -374,13 +369,12 @@
     inner = jnp.where(bit == 0, part, got)[: part.shape[0] - rows]
     outer = jnp.where(bit == 0, got, part)
     inner, outer = barrier((inner, outer))
-    copies = barrier(jnp.broadcast_to(inner, (4,) + inner.shape))
-    copies, moved = barrier((exchange(copies, "y"), [rotated(outer, "x", by) for by in STEPS]))
-    return [copies.reshape(-1, part.shape[1])], [outer] + moved, beside
+    inner = lax.all_gather(inner, REP, axis=0, tiled=True)
+    return inner, [outer] + [rotated(outer, "x", by) for by in STEPS], beside
 
 
 def assemble_kernel(where_ref, *refs):
-    inner, pieces, (conv_ref, expand_ref, joined) = refs[:2], refs[2:10], refs[10:]
+    inner, pieces, (conv_ref, expand_ref, joined) = refs[0], refs[1:9], refs[9:]
     channels = conv_ref.shape[2]
     core = where_ref[0]
     for by in range(4):
@@ -388,10 +382,13 @@
         at = pl.multiple_of(((where_ref[1] + 4 - by) & 3) * rows, 8)
         joined[core, pl.ds(at, rows), :] = pieces[by][...]
         joined[1 - core, pl.ds(at, rows), :] = pieces[4 + by][...]
-    for tap in range(6):
-        rows = slice(tap * LANES, (tap + 1) * LANES)
-        conv_ref[3 + tap, pl.ds(pl.multiple_of(core * LANES, LANES), LANES), :] = inner[0][rows, :]
-        conv_ref[3 + tap, pl.ds(pl.multiple_of((1 - core) * LANES, LANES), LANES), :] = inner[1][rows, :]
+    rows = inner.shape[0] // 8
+    step = LANES // 2
+    for half in range(2):
+        for at in range(0, 4 * rows, step):
+            source = (2 * (at // rows) + half) * rows + at % rows
+            target = half * LANES + at % LANES
+            conv_ref[3 + at // LANES, target : target + step, :] = inner[source : source + step, :]
     for half in range(2):
         lanes = slice(half * LANES, (half + 1) * LANES)
         for tap in range(3):
@@ -401,8 +398,8 @@
             expand_ref[lanes, n * channels : (n + 1) * channels] = joined[half, at : at + LANES, :]
 
 
-def assemble(where, groups, channels, deep):
-    refs = [piece for group in groups for piece in group]
+def assemble(where, inner, pieces, channels, deep):
+    refs = [inner] + pieces
     return pl.pallas_call(
         assemble_kernel,
         out_shape=(
@@ -411,7 +408,7 @@
         ),
         in_specs=[scalars()] + [whole()] * len(refs),
         out_specs=(whole(), whole()),
-        scratch_shapes=[pltpu.VMEM((2, 4 * groups[1][0].shape[0], channels), jnp.float32)],
+        scratch_shapes=[pltpu.VMEM((2, 4 * pieces[0].shape[0], channels), jnp.float32)],
         compiler_params=params(),
         cost_estimate=pl.CostEstimate(flops=0, bytes_accessed=7 * 10**6, transcendentals=0),
         name="assemble",
@@ -432,20 +429,17 @@
     blocks = prepare(stem_input[0])
     above = prepare(shifted(stem_input[0, -1:], 1))
     arrived = exchange(sent, SPACE)
-    own_inner, other_inner, own_outer, other_outer, grad = terms(
-        where[:1], arrived, preact, above, blocks, weighted
-    )
-    below = shifted(grad[:1], -1)
+    inner, own, other, grad, first = terms(where[:1], arrived, preact, above, blocks, weighted)
+    inner = lax.psum_scatter(inner.reshape(-1, channels), REP, scatter_dimension=0, tiled=True)
 
     samples_all = stem_input.shape[0] * SIZES["y"] * SIZES["core"]
     scale = float(samples_all * all_rows * out_cols) ** (-0.5)
-    got_inner, got_outer = swapped(other_inner, "core", 1), swapped(other_outer, "core", 1)
-    inner, outer, *parts = combine(where, own_inner, got_inner, own_outer, got_outer)
-    inner, outer, grad_input = total_sums(
-        inner, outer, parts, scale, below, lambda b: input_grad(grad, b, conv_weight)
+    outer, *parts = combine(where, own, swapped(other, "core", 1))
+    inner, pieces, grad_input = total_sums(
+        inner, outer, parts, scale, first, lambda b: input_grad(grad, b, conv_weight)
     )
-    groups = [pieces + [swapped(piece, "core", 1) for piece in pieces] for pieces in (inner, outer)]
-    grad_conv, grad_expand = assemble(where, groups, channels, deep)
+    pieces = pieces + [swapped(piece, "core", 1) for piece in pieces]
+    grad_conv, grad_expand = assemble(where, inner, pieces, channels, deep)
     return (grad_input[None], grad_conv.reshape(3, 3, channels, channels), grad_expand)
 
 

time: 136 us -> 163 us (1.20)
  between operations: 1.63 us -> 15 us
  waiting for transfers between devices: 50.3 us -> 62 us
  starting transfers between devices: 60.6 us -> 66.5 us
  Pallas kernels: 15.1 us -> 13.2 us
  local copies, waits for them, and re-layouts: 6.94 us -> 5.14 us
    reduce_scatter x0 -> x1, waiting for transfers between devices: none -> 14.1 us  [body(): lax.psum_scatter(inner.reshape(-1, channels), REP, scatter_dimension=0, t...]
    all_gather x0 -> x1, waiting for transfers between devices: none -> 10.9 us  [total_sums(): inner = lax.all_gather(inner, REP, axis=0, tiled=True)]
    ppermute x9 -> x7, starting transfers between devices: 12.6 us -> 21.5 us  [swapped(): return lax.ppermute(x, axis, [(i, i ^ bit) for i in range(SIZES[axis])])]
    all_to_all x3 -> x1, starting transfers between devices: 19.6 us -> 11.9 us  [exchange(): return lax.all_to_all(x, axis, split_axis=0, concat_axis=0, tiled=True)]
    ppermute x9, waiting for transfers between devices: 19.5 us -> 12.2 us  [rotated(): return lax.ppermute(x, axis, [(i, (i + by) % size) for i in range(size)])]
    ppermute x9, starting transfers between devices: 15.6 us -> 20.1 us  [rotated(): return lax.ppermute(x, axis, [(i, (i + by) % size) for i in range(size)])]
    ppermute x6, waiting for transfers between devices: 6.56 us -> 2.91 us  [turned(): return lax.ppermute(x, ('x', 'z', 'y'), pairs)]
    ppermute x9 -> x7, waiting for transfers between devices: 13 us -> 10.8 us  [swapped(): return lax.ppermute(x, axis, [(i, i ^ bit) for i in range(SIZES[axis])])]
  transfers between devices with their start and end apart: 29 -> 27, of which waited for: 19 -> 14; matrix products, arithmetic and copies ran while one was open for 1% -> 0% of each run, Pallas kernels for 4% -> 2%
where the time goes in v6:
time: 163 us
  starting transfers between devices  66.5 us (41%)
  waiting for transfers between devices  62 us (38%)
  between operations  15 us (9%)
  Pallas kernels  13.2 us (8%)
  local copies, waits for them, and re-layouts  5.14 us (3%)
    ppermute x7, starting transfers between devices, swapped(): return lax.ppermute(x, axis, [(i, i ^ bit) for i in range(SIZES[axis])])  21.5 us
    ppermute x9, starting transfers between devices, rotated(): return lax.ppermute(x, axis, [(i, (i + by) % size) for i in range(size)])  20.1 us
    reduce_scatter x1, waiting for transfers between devices, body(): lax.psum_scatter(inner.reshape(-1, channels), REP, scatter_dimension=0, t...  14.1 us
    ppermute x9, waiting for transfers between devices, rotated(): return lax.ppermute(x, axis, [(i, (i + by) % size) for i in range(size)])  12.2 us
    all_to_all x1, starting transfers between devices, exchange(): return lax.all_to_all(x, axis, split_axis=0, concat_axis=0, tiled=True)  11.9 us
    ppermute x2, waiting for transfers between devices, shifted(): return lax.ppermute(x, SPACE, pairs)  11.1 us
    all_gather x1, waiting for transfers between devices, total_sums(): inner = lax.all_gather(inner, REP, axis=0, tiled=True)  10.9 us
    ppermute x7, waiting for transfers between devices, swapped(): return lax.ppermute(x, axis, [(i, i ^ bit) for i in range(SIZES[axis])])  10.8 us
  transfers between devices with their start and end apart: 27, of which 14 were waited for; matrix products, arithmetic and copies ran while one was open for 0% of the time, Pallas kernels for 2%

profile of v6, /device:TPU:1, one launch (start us, length us, event | category | flops | bytes accessed | tf_op | source)
XLA Modules:
  0.0 162.9 jit_solution(1043527912443219556)
XLA Ops:
  7.9 2.9 %build_sent.1 = (bf16[32,32,256]{2,1,0:T(8,128)(2,1)}, bf16[512,1024]{1,0:T(8,128)(2,1)}) custom-call(f32[1]{0:T(128)S(6)} %div.3.share_ref, bf16[512,1024]{1,0:T(8,128)(2,1)} %bitcast.45, bf16[256,1024]{1,0:T(8,128)(2,1)} %weight_hbm.1, bf16[2,256,256]{2,1,0:T(8,128)(2,1)} %bitcast.47), custom_call_target="tpu_custom_call" | custom-call | flops 268000000 | bytes 4000000 | tf_op jit(solution)/shard_map/build_sent/pallas_call | solution.py:79
  10.9 11.9 %all-to-all-start = ((bf16[32,32,256]{2,1,0:T(8,128)(2,1)}), bf16[32,32,256]{2,1,0:T(8,128)(2,1)S(1)}, u32[]{:S(2)}, u32[]{:S(2)}) async-start(bf16[32,32,256]{2,1,0:T(8,128)(2,1)} %get-tuple-element.31), calls=%async_computation | async-start | bytes 1048576 | tf_op jit(solution)/shard_map/all_to_all | solution.py:295
  22.8 3.1 %collective-permute-start = (bf16[1,512,256]{2,1,0:T(8,128)(2,1)S(1)}, bf16[1,512,256]{2,1,0:T(8,128)(2,1)S(1)}, u32[]{:S(2)}, u32[]{:S(2)}) collective-permute-start(bf16[1,512,256]{2,1,0:T(8,128)(2,1)S(1)} %slice_bitcast_fusion), channel_id=1, source_target_pairs={{0,8},{8,16},{16,24},{24,32},{32,40},{40,48},{48,56},{56,64},{64,7... | collective-permute-start | bytes 786440 | tf_op jit(solution)/shard_map/ppermute | solution.py:41
  26.6 1.1 copy-done
  27.7 11.1 %collective-permute-done.x_ref = bf16[1,512,256]{2,1,0:T(8,128)(2,1)S(1)} collective-permute-done((bf16[1,512,256]{2,1,0:T(8,128)(2,1)S(1)}, bf16[1,512,256]{2,1,0:T(8,128)(2,1)S(1)}, u32[]{:S(2)}, u32[]{:S(2)}) %collective-permute-start) | collective-permute-done | bytes 262176 | tf_op jit(solution)/shard_map/ppermute | solution.py:41
  40.6 4.3 %terms.1 = (f32[8,192,256]{2,1,0:T(8,128)}, f32[896,256]{1,0:T(8,128)}, f32[896,256]{1,0:T(8,128)}, bf16[2,256,256]{2,1,0:T(8,128)(2,1)}, bf16[1,256,256]{2,1,0:T(8,128)(2,1)}) custom-call(s32[1]{0:T(128)} %bitcast.core_ref, bf16[32,32,256]{2,1,0:T(8,128)(2,1)} %copy-done.7, bf16[2,256,256]{2,1,0:T(8,128)(2,1)} %bitcast.48, bf16[3,256,256]{2,1,0:T(8,128)(2,1)} %copy-done.3, ...), custom_call_target="tpu_custom_call" | custom-call | flops 870000000 | bytes 8000000 | tf_op jit(solution)/shard_map/terms/pallas_call | solution.py:205
  45.0 2.9 %collective-permute-start.1 = (f32[896,256]{1,0:T(8,128)}, f32[896,256]{1,0:T(8,128)S(1)}, u32[]{:S(2)}, u32[]{:S(2)}) collective-permute-start(f32[896,256]{1,0:T(8,128)} %get-tuple-element.35), channel_id=1, source_target_pairs={{0,1},{1,0},{2,3},{3,2},{4,5},{5,4},{6,7},{7,6},{8,9},{9,8},{10,11... | collective-permute-start | bytes 2752520 | tf_op jit(solution)/shard_map/ppermute | solution.py:322
  48.0 2.2 %collective-permute-done.1.got = f32[896,256]{1,0:T(8,128)S(1)} collective-permute-done((f32[896,256]{1,0:T(8,128)}, f32[896,256]{1,0:T(8,128)S(1)}, u32[]{:S(2)}, u32[]{:S(2)}) %collective-permute-start.1) | collective-permute-done | bytes 917536 | tf_op jit(solution)/shard_map/ppermute | solution.py:322
  50.9 3.4 %collective-permute-start.2 = (f32[224,256]{1,0:T(8,128)S(1)}, f32[224,256]{1,0:T(8,128)S(1)}, u32[]{:S(2)}, u32[]{:S(2)}) collective-permute-start(f32[224,256]{1,0:T(8,128)S(1)} %get-tuple-element.37), channel_id=1, source_target_pairs={{0,64},{64,128},{128,192},{192,0},{1,65},{65,129},{129,193},{193,1... | collective-permute-start | bytes 688136 | tf_op jit(solution)/shard_map/ppermute | solution.py:314
  54.3 2.7 %collective-permute-start.3 = (f32[224,256]{1,0:T(8,128)S(1)}, f32[224,256]{1,0:T(8,128)S(1)}, u32[]{:S(2)}, u32[]{:S(2)}) collective-permute-start(f32[224,256]{1,0:T(8,128)S(1)} %get-tuple-element.38), channel_id=1, source_target_pairs={{0,128},{64,192},{128,0},{192,64},{1,129},{65,193},{129,1},{193,65... | collective-permute-start | bytes 688136 | tf_op jit(solution)/shard_map/ppermute | solution.py:314
  57.9 3.6 %collective-permute-done.2 = f32[224,256]{1,0:T(8,128)S(1)} collective-permute-done((f32[224,256]{1,0:T(8,128)S(1)}, f32[224,256]{1,0:T(8,128)S(1)}, u32[]{:S(2)}, u32[]{:S(2)}) %collective-permute-start.2) | collective-permute-done | bytes 229408 | tf_op jit(solution)/shard_map/ppermute | solution.py:314
  61.5 5.8 %collective-permute-done.3 = f32[224,256]{1,0:T(8,128)S(1)} collective-permute-done((f32[224,256]{1,0:T(8,128)S(1)}, f32[224,256]{1,0:T(8,128)S(1)}, u32[]{:S(2)}, u32[]{:S(2)}) %collective-permute-start.3) | collective-permute-done | bytes 229408 | tf_op jit(solution)/shard_map/ppermute | solution.py:314
  67.4 14.1 %reduce-scatter.2.cloned.1.call-done = f32[192,256]{1,0:T(8,128)} async-done(((f32[1536,256]{1,0:T(8,128)}), f32[192,256]{1,0:T(8,128)}) %reduce-scatter.2.cloned.1.call-update) | async-done | bytes 196624 | tf_op jit(solution)/shard_map/reduce_scatter | solution.py:433
  83.5 4.0 %collective-permute-done.5 = f32[224,256]{1,0:T(8,128)S(1)} collective-permute-done((f32[224,256]{1,0:T(8,128)S(1)}, f32[224,256]{1,0:T(8,128)S(1)}, u32[]{:S(2)}, u32[]{:S(2)}) %collective-permute-start.5) | collective-permute-done | bytes 229408 | tf_op jit(solution)/shard_map/ppermute | solution.py:322
  88.2 2.7 %collective-permute-start.7 = (f32[56,256]{1,0:T(8,128)S(1)}, f32[56,256]{1,0:T(8,128)S(1)}, u32[]{:S(2)}, u32[]{:S(2)}) collective-permute-start(f32[56,256]{1,0:T(8,128)S(1)} %get-tuple-element.47), channel_id=1, source_target_pairs={{0,128},{2,130},{4,132},{6,134},{8,12},{10,14},{12,8},{14,10},{16,... | collective-permute-start | bytes 172040 | tf_op jit(solution)/shard_map/ppermute | solution.py:332
  91.8 1.3 collective-permute-start.12
  94.0 7.2 %collective-permute-start.11 = (f32[56,256]{1,0:T(8,128)S(1)}, f32[56,256]{1,0:T(8,128)S(1)}, u32[]{:S(2)}, u32[]{:S(2)}) collective-permute-start(f32[56,256]{1,0:T(8,128)S(1)} %fusion.5), channel_id=1, source_target_pairs={{0,48},{8,56},{16,0},{24,8},{32,16},{40,24},{48,32},{56,40},{1,49}... | collective-permute-start | bytes 172040 | tf_op jit(solution)/shard_map/ppermute | solution.py:314
  101.9 2.2 %collective-permute-start.9 = (f32[56,256]{1,0:T(8,128)S(1)}, f32[56,256]{1,0:T(8,128)S(1)}, u32[]{:S(2)}, u32[]{:S(2)}) collective-permute-start(f32[56,256]{1,0:T(8,128)S(1)} %fusion.5), channel_id=1, source_target_pairs={{0,16},{8,24},{16,32},{24,40},{32,48},{40,56},{48,0},{56,8},{1,17}... | collective-permute-start | bytes 172040 | tf_op jit(solution)/shard_map/ppermute | solution.py:314
  104.1 1.9 %input_grad.1 = bf16[4,512,256]{2,1,0:T(8,128)(2,1)} custom-call(bf16[2,256,256]{2,1,0:T(8,128)(2,1)S(1)} %copy-done.6, bf16[1,256,256]{2,1,0:T(8,128)(2,1)S(1)} %collective-permute-done.12.below_ref, bf16[3,3,256,256]{3,2,1,0:T(8,128)(2,1)S(1)} %copy-done.4), custom_call_target="tpu_custom_call" | custom-call | flops 604000000 | bytes 3000000 | tf_op jit(solution)/shard_map/input_grad/pallas_call | solution.py:282
  106.0 2.7 %collective-permute-done.10 = f32[56,256]{1,0:T(8,128)S(1)} collective-permute-done((f32[56,256]{1,0:T(8,128)S(1)}, f32[56,256]{1,0:T(8,128)S(1)}, u32[]{:S(2)}, u32[]{:S(2)}) %collective-permute-start.10) | collective-permute-done | bytes 57376 | tf_op jit(solution)/shard_map/ppermute | solution.py:314
  109.6 2.5 %collective-permute-start.14 = (f32[56,256]{1,0:T(8,128)S(1)}, f32[56,256]{1,0:T(8,128)S(1)}, u32[]{:S(2)}, u32[]{:S(2)}) collective-permute-start(f32[56,256]{1,0:T(8,128)S(1)} %get-tuple-element.60), channel_id=1, source_target_pairs={{0,128},{2,130},{4,132},{6,134},{8,12},{10,14},{12,8},{14,10},{16,... | collective-permute-start | bytes 172040 | tf_op jit(solution)/shard_map/ppermute | solution.py:332
  115.1 2.8 %collective-permute-start.16 = (f32[224,256]{1,0:T(8,128)S(1)}, f32[224,256]{1,0:T(8,128)S(1)}, u32[]{:S(2)}, u32[]{:S(2)}) collective-permute-start(f32[224,256]{1,0:T(8,128)S(1)} %bitcast.42), channel_id=1, source_target_pairs={{0,8},{8,0},{16,24},{24,16},{32,40},{40,32},{48,56},{56,48},{1,9},... | collective-permute-start | bytes 688136 | tf_op jit(solution)/shard_map/ppermute | solution.py:322
  117.9 3.4 %collective-permute-done.16 = f32[224,256]{1,0:T(8,128)S(1)} collective-permute-done((f32[224,256]{1,0:T(8,128)S(1)}, f32[224,256]{1,0:T(8,128)S(1)}, u32[]{:S(2)}, u32[]{:S(2)}) %collective-permute-start.16) | collective-permute-done | bytes 229408 | tf_op jit(solution)/shard_map/ppermute | solution.py:322
  122.1 1.8 %collective-permute-start.19 = (f32[224,256]{1,0:T(8,128)S(1)}, f32[224,256]{1,0:T(8,128)S(1)}, u32[]{:S(2)}, u32[]{:S(2)}) collective-permute-start(f32[224,256]{1,0:T(8,128)S(1)} %broadcast_select_fusion.refs_1_), channel_id=1, source_target_pairs={{0,192},{64,0},{128,64},{192,128},{1,193},{65,1},{129,65},{193,129... | collective-permute-start | bytes 688136 | tf_op jit(solution)/shard_map/ppermute | solution.py:314
  125.1 6.3 %collective-permute-start.20 = (f32[224,256]{1,0:T(8,128)S(1)}, f32[224,256]{1,0:T(8,128)S(1)}, u32[]{:S(2)}, u32[]{:S(2)}) collective-permute-start(f32[224,256]{1,0:T(8,128)S(1)} %broadcast_select_fusion.refs_1_), channel_id=1, source_target_pairs={{0,1},{1,0},{2,3},{3,2},{4,5},{5,4},{6,7},{7,6},{8,9},{9,8},{10,11... | collective-permute-start | bytes 688136 | tf_op jit(solution)/shard_map/ppermute | solution.py:322
  131.4 3.0 %collective-permute-start.23 = (f32[224,256]{1,0:T(8,128)S(1)}, f32[224,256]{1,0:T(8,128)S(1)}, u32[]{:S(2)}, u32[]{:S(2)}) collective-permute-start(f32[224,256]{1,0:T(8,128)S(1)} %collective-permute-done.19.refs_4_), channel_id=1, source_target_pairs={{0,1},{1,0},{2,3},{3,2},{4,5},{5,4},{6,7},{7,6},{8,9},{9,8},{10,11... | collective-permute-start | bytes 688136 | tf_op jit(solution)/shard_map/ppermute | solution.py:322
  134.4 3.2 %collective-permute-start.22 = (f32[224,256]{1,0:T(8,128)S(1)}, f32[224,256]{1,0:T(8,128)S(1)}, u32[]{:S(2)}, u32[]{:S(2)}) collective-permute-start(f32[224,256]{1,0:T(8,128)S(1)} %collective-permute-done.18.refs_3_), channel_id=1, source_target_pairs={{0,1},{1,0},{2,3},{3,2},{4,5},{5,4},{6,7},{7,6},{8,9},{9,8},{10,11... | collective-permute-start | bytes 688136 | tf_op jit(solution)/shard_map/ppermute | solution.py:322
  137.7 2.4 %collective-permute-start.21 = (f32[224,256]{1,0:T(8,128)S(1)}, f32[224,256]{1,0:T(8,128)S(1)}, u32[]{:S(2)}, u32[]{:S(2)}) collective-permute-start(f32[224,256]{1,0:T(8,128)S(1)} %collective-permute-done.17.refs_2_), channel_id=1, source_target_pairs={{0,1},{1,0},{2,3},{3,2},{4,5},{5,4},{6,7},{7,6},{8,9},{9,8},{10,11... | collective-permute-start | bytes 688136 | tf_op jit(solution)/shard_map/ppermute | solution.py:322
  140.0 1.1 collective-permute-done.21.refs_6_
  141.1 10.9 %all-gather.2.cloned.1.call-done.refs_0_ = f32[1536,256]{1,0:T(8,128)} async-done(((f32[192,256]{1,0:T(8,128)}), f32[1536,256]{1,0:T(8,128)}) %all-gather.2.cloned.1.call-update) | async-done | bytes 1572880 | tf_op jit(solution)/shard_map/all_gather | solution.py:372
  152.1 1.4 copy-done.2
  153.5 2.6 %assemble.1 = (f32[9,256,256]{2,1,0:T(8,128)}, f32[256,1024]{1,0:T(8,128)}) custom-call(s32[2]{0:T(128)S(1)} %pad_add_fusion.where_ref, f32[1536,256]{1,0:T(8,128)S(1)} %copy-done.2, f32[224,256]{1,0:T(8,128)S(1)} %broadcast_select_fusion.refs_1_, f32[224,256]{1,0:T(8,128)S(1)} %collective-permute-done.17.refs_2_, ...), custom_call_target="tpu_custom_call" | custom-call | bytes 7000000 | tf_op jit(solution)/shard_map/assemble/pallas_call | solution.py:403
  (64 shorter events, 15.2 us)
Async XLA Ops:
  7.2 15.6 %copy-start.1 = (bf16[1,4,512,256]{3,2,1,0:T(8,128)(2,1)S(1)}, bf16[1,4,512,256]{3,2,1,0:T(8,128)(2,1)}, u32[]{:S(2)}) copy-start(bf16[1,4,512,256]{3,2,1,0:T(8,128)(2,1)} %param.6) | copy-start | bytes 3145732
  10.9 28.9 %all-to-all-start = ((bf16[32,32,256]{2,1,0:T(8,128)(2,1)}), bf16[32,32,256]{2,1,0:T(8,128)(2,1)S(1)}, u32[]{:S(2)}, u32[]{:S(2)}) async-start(bf16[32,32,256]{2,1,0:T(8,128)(2,1)} %get-tuple-element.31), calls=%async_computation | async-start | bytes 1048576 | tf_op jit(solution)/shard_map/all_to_all | solution.py:295
  22.7 58.8 %reduce-scatter.2.cloned.1.call-start = ((), (), s32[]{:S(2)}) async-start(), calls=%async_computation.2 | async-start | bytes 1769472 | tf_op jit(solution)/shard_map/reduce_scatter | solution.py:433
  22.8 16.0 %collective-permute-start = (bf16[1,512,256]{2,1,0:T(8,128)(2,1)S(1)}, bf16[1,512,256]{2,1,0:T(8,128)(2,1)S(1)}, u32[]{:S(2)}, u32[]{:S(2)}) collective-permute-start(bf16[1,512,256]{2,1,0:T(8,128)(2,1)S(1)} %slice_bitcast_fusion), channel_id=1, source_target_pairs={{0,8},{8,16},{16,24},{24,32},{32,40},{40,48},{48,56},{56,64},{64,7... | collective-permute-start | bytes 786440 | tf_op jit(solution)/shard_map/ppermute | solution.py:41
  44.9 5.3 %copy-start.5 = (f32[896,256]{1,0:T(8,128)S(1)}, f32[896,256]{1,0:T(8,128)}, u32[]{:S(2)}) copy-start(f32[896,256]{1,0:T(8,128)} %get-tuple-element.34.own) | copy-start | bytes 2752516
  45.0 107.1 %all-gather.2.cloned.1.call-start = ((), (), s32[]{:S(2)}) async-start(), calls=%async_computation.3 | async-start | bytes 1769472 | tf_op jit(solution)/shard_map/all_gather | solution.py:372
  45.0 5.2 %collective-permute-start.1 = (f32[896,256]{1,0:T(8,128)}, f32[896,256]{1,0:T(8,128)S(1)}, u32[]{:S(2)}, u32[]{:S(2)}) collective-permute-start(f32[896,256]{1,0:T(8,128)} %get-tuple-element.35), channel_id=1, source_target_pairs={{0,1},{1,0},{2,3},{3,2},{4,5},{5,4},{6,7},{7,6},{8,9},{9,8},{10,11... | collective-permute-start | bytes 2752520 | tf_op jit(solution)/shard_map/ppermute | solution.py:322
  50.9 10.6 %collective-permute-start.2 = (f32[224,256]{1,0:T(8,128)S(1)}, f32[224,256]{1,0:T(8,128)S(1)}, u32[]{:S(2)}, u32[]{:S(2)}) collective-permute-start(f32[224,256]{1,0:T(8,128)S(1)} %get-tuple-element.37), channel_id=1, source_target_pairs={{0,64},{64,128},{128,192},{192,0},{1,65},{65,129},{129,193},{193,1... | collective-permute-start | bytes 688136 | tf_op jit(solution)/shard_map/ppermute | solution.py:314
  54.3 13.0 %collective-permute-start.3 = (f32[224,256]{1,0:T(8,128)S(1)}, f32[224,256]{1,0:T(8,128)S(1)}, u32[]{:S(2)}, u32[]{:S(2)}) collective-permute-start(f32[224,256]{1,0:T(8,128)S(1)} %get-tuple-element.38), channel_id=1, source_target_pairs={{0,128},{64,192},{128,0},{192,64},{1,129},{65,193},{129,1},{193,65... | collective-permute-start | bytes 688136 | tf_op jit(solution)/shard_map/ppermute | solution.py:314
  57.0 10.3 %collective-permute-start.4 = (f32[224,256]{1,0:T(8,128)S(1)}, f32[224,256]{1,0:T(8,128)S(1)}, u32[]{:S(2)}, u32[]{:S(2)}) collective-permute-start(f32[224,256]{1,0:T(8,128)S(1)} %get-tuple-element.39), channel_id=1, source_target_pairs={{0,192},{64,0},{128,64},{192,128},{1,193},{65,1},{129,65},{193,129... | collective-permute-start | bytes 688136 | tf_op jit(solution)/shard_map/ppermute | solution.py:314
  67.3 24.5 %copy-start.8 = (bf16[1,256,256]{2,1,0:T(8,128)(2,1)S(1)}, bf16[1,256,256]{2,1,0:T(8,128)(2,1)}, u32[]{:S(2)}) copy-start(bf16[1,256,256]{2,1,0:T(8,128)(2,1)} %get-tuple-element.50) | copy-start | bytes 393220
  67.4 36.7 %copy-start.4 = (bf16[3,3,256,256]{3,2,1,0:T(8,128)(2,1)S(1)}, bf16[3,3,256,256]{3,2,1,0:T(8,128)(2,1)}, u32[]{:S(2)}) copy-start(bf16[3,3,256,256]{3,2,1,0:T(8,128)(2,1)} %weight_ref.1) | copy-start | bytes 3538948
  67.4 36.7 %copy-start.6 = (bf16[2,256,256]{2,1,0:T(8,128)(2,1)S(1)}, bf16[2,256,256]{2,1,0:T(8,128)(2,1)}, u32[]{:S(2)}) copy-start(bf16[2,256,256]{2,1,0:T(8,128)(2,1)} %get-tuple-element.49.grad_ref) | copy-start | bytes 786436
  82.6 5.0 %collective-permute-start.5 = (f32[224,256]{1,0:T(8,128)S(1)}, f32[224,256]{1,0:T(8,128)S(1)}, u32[]{:S(2)}, u32[]{:S(2)}) collective-permute-start(f32[224,256]{1,0:T(8,128)S(1)} %get-tuple-element.45), channel_id=1, source_target_pairs={{0,8},{8,0},{16,24},{24,16},{32,40},{40,32},{48,56},{56,48},{1,9},... | collective-permute-start | bytes 688136 | tf_op jit(solution)/shard_map/ppermute | solution.py:322
  87.6 5.5 %collective-permute-start.6 = (f32[56,256]{1,0:T(8,128)S(1)}, f32[56,256]{1,0:T(8,128)S(1)}, u32[]{:S(2)}, u32[]{:S(2)}) collective-permute-start(f32[56,256]{1,0:T(8,128)S(1)} %get-tuple-element.46), channel_id=1, source_target_pairs={{0,64},{2,66},{4,68},{6,70},{8,10},{10,12},{12,14},{14,8},{16,80},... | collective-permute-start | bytes 172040 | tf_op jit(solution)/shard_map/ppermute | solution.py:332
  88.2 4.9 %collective-permute-start.7 = (f32[56,256]{1,0:T(8,128)S(1)}, f32[56,256]{1,0:T(8,128)S(1)}, u32[]{:S(2)}, u32[]{:S(2)}) collective-permute-start(f32[56,256]{1,0:T(8,128)S(1)} %get-tuple-element.47), channel_id=1, source_target_pairs={{0,128},{2,130},{4,132},{6,134},{8,12},{10,14},{12,8},{14,10},{16,... | collective-permute-start | bytes 172040 | tf_op jit(solution)/shard_map/ppermute | solution.py:332
  91.0 3.0 %collective-permute-start.8 = (f32[56,256]{1,0:T(8,128)S(1)}, f32[56,256]{1,0:T(8,128)S(1)}, u32[]{:S(2)}, u32[]{:S(2)}) collective-permute-start(f32[56,256]{1,0:T(8,128)S(1)} %get-tuple-element.48), channel_id=1, source_target_pairs={{0,192},{2,194},{4,196},{6,198},{8,14},{10,8},{12,10},{14,12},{16,... | collective-permute-start | bytes 172040 | tf_op jit(solution)/shard_map/ppermute | solution.py:332
  91.8 12.2 %collective-permute-start.12 = (bf16[1,256,256]{2,1,0:T(8,128)(2,1)S(1)}, bf16[1,256,256]{2,1,0:T(8,128)(2,1)S(1)}, u32[]{:S(2)}, u32[]{:S(2)}) collective-permute-start(bf16[1,256,256]{2,1,0:T(8,128)(2,1)S(1)} %copy-done.8), channel_id=1, source_target_pairs={{8,0},{16,8},{24,16},{32,24},{40,32},{48,40},{56,48},{64,56},{72,6... | collective-permute-start | bytes 393224 | tf_op jit(solution)/shard_map/ppermute | solution.py:41
  94.0 12.0 %collective-permute-start.11 = (f32[56,256]{1,0:T(8,128)S(1)}, f32[56,256]{1,0:T(8,128)S(1)}, u32[]{:S(2)}, u32[]{:S(2)}) collective-permute-start(f32[56,256]{1,0:T(8,128)S(1)} %fusion.5), channel_id=1, source_target_pairs={{0,48},{8,56},{16,0},{24,8},{32,16},{40,24},{48,32},{56,40},{1,49}... | collective-permute-start | bytes 172040 | tf_op jit(solution)/shard_map/ppermute | solution.py:314
  101.2 7.6 %collective-permute-start.10 = (f32[56,256]{1,0:T(8,128)S(1)}, f32[56,256]{1,0:T(8,128)S(1)}, u32[]{:S(2)}, u32[]{:S(2)}) collective-permute-start(f32[56,256]{1,0:T(8,128)S(1)} %fusion.5), channel_id=1, source_target_pairs={{0,32},{8,40},{16,48},{24,56},{32,0},{40,8},{48,16},{56,24},{1,33}... | collective-permute-start | bytes 172040 | tf_op jit(solution)/shard_map/ppermute | solution.py:314
  101.9 6.9 %collective-permute-start.9 = (f32[56,256]{1,0:T(8,128)S(1)}, f32[56,256]{1,0:T(8,128)S(1)}, u32[]{:S(2)}, u32[]{:S(2)}) collective-permute-start(f32[56,256]{1,0:T(8,128)S(1)} %fusion.5), channel_id=1, source_target_pairs={{0,16},{8,24},{16,32},{24,40},{32,48},{40,56},{48,0},{56,8},{1,17}... | collective-permute-start | bytes 172040 | tf_op jit(solution)/shard_map/ppermute | solution.py:314
  108.8 4.5 %collective-permute-start.13 = (f32[56,256]{1,0:T(8,128)S(1)}, f32[56,256]{1,0:T(8,128)S(1)}, u32[]{:S(2)}, u32[]{:S(2)}) collective-permute-start(f32[56,256]{1,0:T(8,128)S(1)} %get-tuple-element.60), channel_id=1, source_target_pairs={{0,64},{2,66},{4,68},{6,70},{8,10},{10,12},{12,14},{14,8},{16,80},... | collective-permute-start | bytes 172040 | tf_op jit(solution)/shard_map/ppermute | solution.py:332
  109.6 4.6 %collective-permute-start.14 = (f32[56,256]{1,0:T(8,128)S(1)}, f32[56,256]{1,0:T(8,128)S(1)}, u32[]{:S(2)}, u32[]{:S(2)}) collective-permute-start(f32[56,256]{1,0:T(8,128)S(1)} %get-tuple-element.60), channel_id=1, source_target_pairs={{0,128},{2,130},{4,132},{6,134},{8,12},{10,14},{12,8},{14,10},{16,... | collective-permute-start | bytes 172040 | tf_op jit(solution)/shard_map/ppermute | solution.py:332
  112.1 3.0 %collective-permute-start.15 = (f32[56,256]{1,0:T(8,128)S(1)}, f32[56,256]{1,0:T(8,128)S(1)}, u32[]{:S(2)}, u32[]{:S(2)}) collective-permute-start(f32[56,256]{1,0:T(8,128)S(1)} %get-tuple-element.60), channel_id=1, source_target_pairs={{0,192},{2,194},{4,196},{6,198},{8,14},{10,8},{12,10},{14,12},{16,... | collective-permute-start | bytes 172040 | tf_op jit(solution)/shard_map/ppermute | solution.py:332
  115.1 6.2 %collective-permute-start.16 = (f32[224,256]{1,0:T(8,128)S(1)}, f32[224,256]{1,0:T(8,128)S(1)}, u32[]{:S(2)}, u32[]{:S(2)}) collective-permute-start(f32[224,256]{1,0:T(8,128)S(1)} %bitcast.42), channel_id=1, source_target_pairs={{0,8},{8,0},{16,24},{24,16},{32,40},{40,32},{48,56},{56,48},{1,9},... | collective-permute-start | bytes 688136 | tf_op jit(solution)/shard_map/ppermute | solution.py:322
  122.1 9.4 %collective-permute-start.19 = (f32[224,256]{1,0:T(8,128)S(1)}, f32[224,256]{1,0:T(8,128)S(1)}, u32[]{:S(2)}, u32[]{:S(2)}) collective-permute-start(f32[224,256]{1,0:T(8,128)S(1)} %broadcast_select_fusion.refs_1_), channel_id=1, source_target_pairs={{0,192},{64,0},{128,64},{192,128},{1,193},{65,1},{129,65},{193,129... | collective-permute-start | bytes 688136 | tf_op jit(solution)/shard_map/ppermute | solution.py:314
  123.9 10.5 %collective-permute-start.18 = (f32[224,256]{1,0:T(8,128)S(1)}, f32[224,256]{1,0:T(8,128)S(1)}, u32[]{:S(2)}, u32[]{:S(2)}) collective-permute-start(f32[224,256]{1,0:T(8,128)S(1)} %broadcast_select_fusion.refs_1_), channel_id=1, source_target_pairs={{0,128},{64,192},{128,0},{192,64},{1,129},{65,193},{129,1},{193,65... | collective-permute-start | bytes 688136 | tf_op jit(solution)/shard_map/ppermute | solution.py:314
  124.6 13.1 %collective-permute-start.17 = (f32[224,256]{1,0:T(8,128)S(1)}, f32[224,256]{1,0:T(8,128)S(1)}, u32[]{:S(2)}, u32[]{:S(2)}) collective-permute-start(f32[224,256]{1,0:T(8,128)S(1)} %broadcast_select_fusion.refs_1_), channel_id=1, source_target_pairs={{0,64},{64,128},{128,192},{192,0},{1,65},{65,129},{129,193},{193,1... | collective-permute-start | bytes 688136 | tf_op jit(solution)/shard_map/ppermute | solution.py:314
  125.1 14.9 %collective-permute-start.20 = (f32[224,256]{1,0:T(8,128)S(1)}, f32[224,256]{1,0:T(8,128)S(1)}, u32[]{:S(2)}, u32[]{:S(2)}) collective-permute-start(f32[224,256]{1,0:T(8,128)S(1)} %broadcast_select_fusion.refs_1_), channel_id=1, source_target_pairs={{0,1},{1,0},{2,3},{3,2},{4,5},{5,4},{6,7},{7,6},{8,9},{9,8},{10,11... | collective-permute-start | bytes 688136 | tf_op jit(solution)/shard_map/ppermute | solution.py:322
  131.4 8.6 %collective-permute-start.23 = (f32[224,256]{1,0:T(8,128)S(1)}, f32[224,256]{1,0:T(8,128)S(1)}, u32[]{:S(2)}, u32[]{:S(2)}) collective-permute-start(f32[224,256]{1,0:T(8,128)S(1)} %collective-permute-done.19.refs_4_), channel_id=1, source_target_pairs={{0,1},{1,0},{2,3},{3,2},{4,5},{5,4},{6,7},{7,6},{8,9},{9,8},{10,11... | collective-permute-start | bytes 688136 | tf_op jit(solution)/shard_map/ppermute | solution.py:322
  134.4 5.6 %collective-permute-start.22 = (f32[224,256]{1,0:T(8,128)S(1)}, f32[224,256]{1,0:T(8,128)S(1)}, u32[]{:S(2)}, u32[]{:S(2)}) collective-permute-start(f32[224,256]{1,0:T(8,128)S(1)} %collective-permute-done.18.refs_3_), channel_id=1, source_target_pairs={{0,1},{1,0},{2,3},{3,2},{4,5},{5,4},{6,7},{7,6},{8,9},{9,8},{10,11... | collective-permute-start | bytes 688136 | tf_op jit(solution)/shard_map/ppermute | solution.py:322
  137.7 3.5 %collective-permute-start.21 = (f32[224,256]{1,0:T(8,128)S(1)}, f32[224,256]{1,0:T(8,128)S(1)}, u32[]{:S(2)}, u32[]{:S(2)}) collective-permute-start(f32[224,256]{1,0:T(8,128)S(1)} %collective-permute-done.17.refs_2_), channel_id=1, source_target_pairs={{0,1},{1,0},{2,3},{3,2},{4,5},{5,4},{6,7},{7,6},{8,9},{9,8},{10,11... | collective-permute-start | bytes 688136 | tf_op jit(solution)/shard_map/ppermute | solution.py:322
  (4 other events, 4.1 us)
Sparse Core Ops, SparseCore 0:
  45.1 36.3 reduce-scatter.1
  122.2 29.8 all-gather.1

commit v7 on v6

--- a/solution.py
+++ b/solution.py
@@ -123,7 +123,7 @@
 
 def terms_kernel(
     core_ref, arrived_hbm, preact_hbm, above_hbm, blocks_hbm, weighted_hbm,
-    inner_hbm, own_outer, other_outer, grad_hbm, first_hbm,
+    own_inner, other_inner, own_outer, other_outer, grad_hbm, first_hbm,
     arrived_ref, preact_ref, above_ref, blocks_ref, weighted_ref,
     grad_ref, turned, inner_ref, outer_ref, sems,
 ):
@@ -148,7 +148,7 @@
         grad_ref[i] = kept.astype(jnp.bfloat16)
     back = [
         pltpu.make_async_copy(grad_ref, grad_hbm, sems.at[5]),
-        pltpu.make_async_copy(grad_ref.at[0:1], first_hbm, sems.at[6]),
+        pltpu.make_async_copy(grad_ref.at[0:1], first_hbm, sems.at[10]),
     ]
     active = arrived_ref[:, chunk:, :].astype(jnp.float32).reshape(devices * chunk, channels)
     turned[...] = active.T.astype(jnp.bfloat16)
@@ -168,20 +168,15 @@
         copy.wait()
     back[0].start()
     back[1].start()
-    pieces = inner_hbm.shape[0] // 2
-    rows_each = inner_ref.shape[1] // pieces
-    for half in range(2):
+    for n, (inner_hbm, outer_hbm) in enumerate(((other_inner, other_outer), (own_inner, own_outer))):
+        owner = core_ref[0] if n else 1 - core_ref[0]
+        start = pl.multiple_of(owner * LANES, LANES)
         for col_tap in range(3):
             for row_tap in (1, 2):
                 at = (3 * (row_tap - 1) + col_tap) * LANES
-                inner_ref[half, at : at + LANES, :] = half_taps(row_tap, col_tap, half * LANES)
-        for n in range(pieces):
-            piece = inner_ref.at[half, n * rows_each : (n + 1) * rows_each, :]
-            back.append(pltpu.make_async_copy(piece, inner_hbm.at[2 * n + half], sems.at[9 + 2 * n + half]))
-            back[-1].start()
-    for n, outer_hbm in enumerate((other_outer, own_outer)):
-        owner = core_ref[0] if n else 1 - core_ref[0]
-        start = pl.multiple_of(owner * LANES, LANES)
+                inner_ref[n, at : at + LANES, :] = half_taps(row_tap, col_tap, start)
+        back.append(pltpu.make_async_copy(inner_ref.at[n], inner_hbm, sems.at[6 + 2 * n]))
+        back[-1].start()
         for col_tap in range(3):
             at = col_tap * LANES
             outer_ref[n, at : at + LANES, :] = half_taps(0, col_tap, start)
@@ -192,7 +187,7 @@
                 weighted_ref[:, k * channels : (k + 1) * channels],
                 preferred_element_type=jnp.float32,
             )
-        back.append(pltpu.make_async_copy(outer_ref.at[n], outer_hbm, sems.at[7 + n]))
+        back.append(pltpu.make_async_copy(outer_ref.at[n], outer_hbm, sems.at[7 + 2 * n]))
         back[-1].start()
     for copy in back:
         copy.wait()
@@ -200,11 +195,12 @@
 
 def terms(core, arrived, preact, above, blocks, weighted):
     rows, cols, channels = preact.shape
-    inner = jax.ShapeDtypeStruct((8, 6 * LANES // 4, channels), jnp.float32)
+    inner = jax.ShapeDtypeStruct((6 * LANES, channels), jnp.float32)
     outer = jax.ShapeDtypeStruct((3 * LANES + weighted.shape[1] // 2, channels), jnp.float32)
     return pl.pallas_call(
         terms_kernel,
         out_shape=(
+            inner,
             inner,
             outer,
             outer,
@@ -212,13 +208,13 @@
             jax.ShapeDtypeStruct((1, cols, channels), jnp.bfloat16),
         ),
         in_specs=[scalars()] + [far()] * 5,
-        out_specs=(far(),) * 5,
+        out_specs=(far(),) * 6,
         scratch_shapes=[room(x) for x in (arrived, preact, above, blocks, weighted, preact)]
         + [
             pltpu.VMEM((channels, weighted.shape[0]), jnp.bfloat16),
-            pltpu.VMEM((2, 6 * LANES, channels), jnp.float32),
+            pltpu.VMEM((2,) + inner.shape, jnp.float32),
             pltpu.VMEM((2,) + outer.shape, jnp.float32),
-            pltpu.SemaphoreType.DMA((17,)),
+            pltpu.SemaphoreType.DMA((11,)),
         ],
         compiler_params=params(54),
         cost_estimate=pl.CostEstimate(flops=870 * 10**6, bytes_accessed=8 * 10**6, transcendentals=0),
@@ -342,15 +338,18 @@
 
 
 def total_sums(inner, outer, parts, scale, first, beside):
-    moved = barrier([rotated(p, "x", by) for p, by in zip(parts, STEPS)])
+    inner, parts = exchange(split(inner), "y"), barrier(parts)
+    moved = [rotated(p, "x", by) for p, by in zip(parts, STEPS)]
+    inner, moved = barrier((inner, moved))
+    inner = jnp.sum(inner, axis=0)
     outer = sum(moved, outer)
 
     rows = outer.shape[0] - inner.shape[0]
     both = jnp.stack([jnp.pad(inner, ((0, rows), (0, 0))), outer])
     bit = place("z") & jnp.uint32(1)
-    own, other, first = barrier((pick(both, bit), pick(both, jnp.uint32(1) - bit), first))
-    part = own + swapped(other, "z", 1)
-    below = shifted(first, -1)
+    other, first = barrier((pick(both, jnp.uint32(1) - bit), first))
+    got, below = barrier((swapped(other, "z", 1), shifted(first, -1)))
+    part = pick(both, bit) + got
 
     parts = split(part)
     moved = barrier([pick(parts, turned_place(by)) for by in STEPS])
@@ -369,12 +368,13 @@
     inner = jnp.where(bit == 0, part, got)[: part.shape[0] - rows]
     outer = jnp.where(bit == 0, got, part)
     inner, outer = barrier((inner, outer))
-    inner = lax.all_gather(inner, REP, axis=0, tiled=True)
-    return inner, [outer] + [rotated(outer, "x", by) for by in STEPS], beside
+    copies = barrier(jnp.broadcast_to(inner, (4,) + inner.shape))
+    copies, moved = barrier((exchange(copies, "y"), [rotated(outer, "x", by) for by in STEPS]))
+    return [copies.reshape(-1, part.shape[1])], [outer] + moved, beside
 
 
 def assemble_kernel(where_ref, *refs):
-    inner, pieces, (conv_ref, expand_ref, joined) = refs[0], refs[1:9], refs[9:]
+    inner, pieces, (conv_ref, expand_ref, joined) = refs[:2], refs[2:10], refs[10:]
     channels = conv_ref.shape[2]
     core = where_ref[0]
     for by in range(4):
@@ -382,13 +382,10 @@
         at = pl.multiple_of(((where_ref[1] + 4 - by) & 3) * rows, 8)
         joined[core, pl.ds(at, rows), :] = pieces[by][...]
         joined[1 - core, pl.ds(at, rows), :] = pieces[4 + by][...]
-    rows = inner.shape[0] // 8
-    step = LANES // 2
-    for half in range(2):
-        for at in range(0, 4 * rows, step):
-            source = (2 * (at // rows) + half) * rows + at % rows
-            target = half * LANES + at % LANES
-            conv_ref[3 + at // LANES, target : target + step, :] = inner[source : source + step, :]
+    for tap in range(6):
+        rows = slice(tap * LANES, (tap + 1) * LANES)
+        conv_ref[3 + tap, pl.ds(pl.multiple_of(core * LANES, LANES), LANES), :] = inner[0][rows, :]
+        conv_ref[3 + tap, pl.ds(pl.multiple_of((1 - core) * LANES, LANES), LANES), :] = inner[1][rows, :]
     for half in range(2):
         lanes = slice(half * LANES, (half + 1) * LANES)
         for tap in range(3):
@@ -398,8 +395,8 @@
             expand_ref[lanes, n * channels : (n + 1) * channels] = joined[half, at : at + LANES, :]
 
 
-def assemble(where, inner, pieces, channels, deep):
-    refs = [inner] + pieces
+def assemble(where, groups, channels, deep):
+    refs = [piece for group in groups for piece in group]
     return pl.pallas_call(
         assemble_kernel,
         out_shape=(
@@ -408,7 +405,7 @@
         ),
         in_specs=[scalars()] + [whole()] * len(refs),
         out_specs=(whole(), whole()),
-        scratch_shapes=[pltpu.VMEM((2, 4 * pieces[0].shape[0], channels), jnp.float32)],
+        scratch_shapes=[pltpu.VMEM((2, 4 * groups[1][0].shape[0], channels), jnp.float32)],
         compiler_params=params(),
         cost_estimate=pl.CostEstimate(flops=0, bytes_accessed=7 * 10**6, transcendentals=0),
         name="assemble",
@@ -429,17 +426,19 @@
     blocks = prepare(stem_input[0])
     above = prepare(shifted(stem_input[0, -1:], 1))
     arrived = exchange(sent, SPACE)
-    inner, own, other, grad, first = terms(where[:1], arrived, preact, above, blocks, weighted)
-    inner = lax.psum_scatter(inner.reshape(-1, channels), REP, scatter_dimension=0, tiled=True)
+    own_inner, other_inner, own_outer, other_outer, grad, first = terms(
+        where[:1], arrived, preact, above, blocks, weighted
+    )
 
     samples_all = stem_input.shape[0] * SIZES["y"] * SIZES["core"]
     scale = float(samples_all * all_rows * out_cols) ** (-0.5)
-    outer, *parts = combine(where, own, swapped(other, "core", 1))
-    inner, pieces, grad_input = total_sums(
+    inner = own_inner + swapped(other_inner, "core", 1)
+    outer, *parts = combine(where, own_outer, swapped(other_outer, "core", 1))
+    inner, outer, grad_input = total_sums(
         inner, outer, parts, scale, first, lambda b: input_grad(grad, b, conv_weight)
     )
-    pieces = pieces + [swapped(piece, "core", 1) for piece in pieces]
-    grad_conv, grad_expand = assemble(where, inner, pieces, channels, deep)
+    groups = [pieces + [swapped(piece, "core", 1) for piece in pieces] for pieces in (inner, outer)]
+    grad_conv, grad_expand = assemble(where, groups, channels, deep)
     return (grad_input[None], grad_conv.reshape(3, 3, channels, channels), grad_expand)
 
 

time: 163 us -> 137 us (0.84)
  between operations: 15 us -> 1.64 us
  waiting for transfers between devices: 62 us -> 52.8 us
  starting transfers between devices: 66.5 us -> 60.6 us
  other arithmetic: 1.04 us -> 3.86 us
    reduce_scatter x1 -> x0, waiting for transfers between devices: 14.1 us -> none  [body(): lax.psum_scatter(inner.reshape(-1, channels), REP, scatter_dimension=0, t...]
    all_gather x1 -> x0, waiting for transfers between devices: 10.9 us -> none  [total_sums(): inner = lax.all_gather(inner, REP, axis=0, tiled=True)]
    ppermute x7 -> x9, starting transfers between devices: 21.5 us -> 12.8 us  [swapped(): return lax.ppermute(x, axis, [(i, i ^ bit) for i in range(SIZES[axis])])]
    all_to_all x1 -> x3, starting transfers between devices: 11.9 us -> 20 us  [exchange(): return lax.all_to_all(x, axis, split_axis=0, concat_axis=0, tiled=True)]
    ppermute x2, waiting for transfers between devices: 11.1 us -> 18.2 us  [shifted(): return lax.ppermute(x, SPACE, pairs)]
    ppermute x9, waiting for transfers between devices: 12.2 us -> 19.1 us  [rotated(): return lax.ppermute(x, axis, [(i, (i + by) % size) for i in range(size)])]
    ppermute x9, starting transfers between devices: 20.1 us -> 15 us  [rotated(): return lax.ppermute(x, axis, [(i, (i + by) % size) for i in range(size)])]
    ppermute x6, waiting for transfers between devices: 2.91 us -> 6.16 us  [turned(): return lax.ppermute(x, ('x', 'z', 'y'), pairs)]
  transfers between devices with their start and end apart: 27 -> 29, of which waited for: 14 -> 19; matrix products, arithmetic and copies ran while one was open for 0% -> 2% of each run, Pallas kernels for 2% -> 2%
where the time goes in v7:
time: 137 us
  starting transfers between devices  60.6 us (44%)
  waiting for transfers between devices  52.8 us (39%)
  Pallas kernels  13.2 us (10%)
  local copies, waits for them, and re-layouts  4.41 us (3%)
  other arithmetic  3.86 us (3%)
  between operations  1.64 us (1%)
    all_to_all x3, starting transfers between devices, exchange(): return lax.all_to_all(x, axis, split_axis=0, concat_axis=0, tiled=True)  20 us
    ppermute x9, waiting for transfers between devices, rotated(): return lax.ppermute(x, axis, [(i, (i + by) % size) for i in range(size)])  19.1 us
    ppermute x2, waiting for transfers between devices, shifted(): return lax.ppermute(x, SPACE, pairs)  18.2 us
    ppermute x9, starting transfers between devices, rotated(): return lax.ppermute(x, axis, [(i, (i + by) % size) for i in range(size)])  15 us
    ppermute x9, starting transfers between devices, swapped(): return lax.ppermute(x, axis, [(i, i ^ bit) for i in range(SIZES[axis])])  12.8 us
    ppermute x9, waiting for transfers between devices, swapped(): return lax.ppermute(x, axis, [(i, i ^ bit) for i in range(SIZES[axis])])  9.38 us
    ppermute x6, starting transfers between devices, turned(): return lax.ppermute(x, ('x', 'z', 'y'), pairs)  8.3 us
    ppermute x6, waiting for transfers between devices, turned(): return lax.ppermute(x, ('x', 'z', 'y'), pairs)  6.16 us
  transfers between devices with their start and end apart: 29, of which 19 were waited for; matrix products, arithmetic and copies ran while one was open for 2% of the time, Pallas kernels for 2%

profile of v7, /device:TPU:1, one launch (start us, length us, event | category | flops | bytes accessed | tf_op | source)
XLA Modules:
  0.0 136.5 jit_solution(11849060915046642278)
XLA Ops:
  1.4 2.9 %build_sent.1 = (bf16[32,32,256]{2,1,0:T(8,128)(2,1)}, bf16[512,1024]{1,0:T(8,128)(2,1)}) custom-call(f32[1]{0:T(128)S(6)} %div.3.share_ref, bf16[512,1024]{1,0:T(8,128)(2,1)} %bitcast.49, bf16[256,1024]{1,0:T(8,128)(2,1)} %weight_hbm.1, bf16[2,256,256]{2,1,0:T(8,128)(2,1)} %bitcast.51), custom_call_target="tpu_custom_call" | custom-call | flops 268000000 | bytes 4000000 | tf_op jit(solution)/shard_map/build_sent/pallas_call | solution.py:79
  4.3 11.9 %all-to-all-start = ((bf16[32,32,256]{2,1,0:T(8,128)(2,1)}), bf16[32,32,256]{2,1,0:T(8,128)(2,1)S(1)}, u32[]{:S(2)}, u32[]{:S(2)}) async-start(bf16[32,32,256]{2,1,0:T(8,128)(2,1)} %get-tuple-element.41), calls=%async_computation | async-start | bytes 1048576 | tf_op jit(solution)/shard_map/all_to_all | solution.py:291
  16.3 3.1 %collective-permute-start = (bf16[1,512,256]{2,1,0:T(8,128)(2,1)S(1)}, bf16[1,512,256]{2,1,0:T(8,128)(2,1)S(1)}, u32[]{:S(2)}, u32[]{:S(2)}) collective-permute-start(bf16[1,512,256]{2,1,0:T(8,128)(2,1)S(1)} %slice_bitcast_fusion), channel_id=1, source_target_pairs={{0,8},{8,16},{16,24},{24,32},{32,40},{40,48},{48,56},{56,64},{64,7... | collective-permute-start | bytes 786440 | tf_op jit(solution)/shard_map/ppermute | solution.py:41
  21.1 11.1 %collective-permute-done.x_ref = bf16[1,512,256]{2,1,0:T(8,128)(2,1)S(1)} collective-permute-done((bf16[1,512,256]{2,1,0:T(8,128)(2,1)S(1)}, bf16[1,512,256]{2,1,0:T(8,128)(2,1)S(1)}, u32[]{:S(2)}, u32[]{:S(2)}) %collective-permute-start) | collective-permute-done | bytes 262176 | tf_op jit(solution)/shard_map/ppermute | solution.py:41
  34.1 4.3 %terms.1 = (f32[768,256]{1,0:T(8,128)}, f32[768,256]{1,0:T(8,128)}, f32[896,256]{1,0:T(8,128)}, f32[896,256]{1,0:T(8,128)}, bf16[2,256,256]{2,1,0:T(8,128)(2,1)}, /*index=5*/bf16[1,256,256]{2,1,0:T(8,128)(2,1)}) custom-call(s32[1]{0:T(128)} %bitcast.core_ref, bf16[32,32,256]{2,1,0:T(8,128)(2,1)} %copy-done.6, bf16[2,256,256]{2,1,0:T(8,128)(2,1)} %bitcast.52, ...), custom_call_target="tpu_custom_call" | custom-call | flops 870000000 | bytes 8000000 | tf_op jit(solution)/shard_map/terms/pallas_call | solution.py:200
  38.4 2.9 %collective-permute-start.1 = (f32[768,256]{1,0:T(8,128)}, f32[768,256]{1,0:T(8,128)S(1)}, u32[]{:S(2)}, u32[]{:S(2)}) collective-permute-start(f32[768,256]{1,0:T(8,128)} %get-tuple-element.44), channel_id=1, source_target_pairs={{0,1},{1,0},{2,3},{3,2},{4,5},{5,4},{6,7},{7,6},{8,9},{9,8},{10,11... | collective-permute-start | bytes 2359304 | tf_op jit(solution)/shard_map/ppermute | solution.py:318
  41.3 2.0 %collective-permute-done.1 = f32[768,256]{1,0:T(8,128)S(1)} collective-permute-done((f32[768,256]{1,0:T(8,128)}, f32[768,256]{1,0:T(8,128)S(1)}, u32[]{:S(2)}, u32[]{:S(2)}) %collective-permute-start.1) | collective-permute-done | bytes 786464 | tf_op jit(solution)/shard_map/ppermute | solution.py:318
  43.4 2.2 %add.59 = f32[768,256]{1,0:T(8,128)} add(f32[768,256]{1,0:T(8,128)} %get-tuple-element.43, f32[768,256]{1,0:T(8,128)S(1)} %collective-permute-done.1) | non-fusion elementwise | flops 196608 | bytes 2359296 | tf_op jit(solution)/shard_map/add | solution.py:435
  45.6 4.2 %all-to-all-start.1 = ((f32[4,192,256]{2,1,0:T(8,128)}), f32[4,192,256]{2,1,0:T(8,128)S(1)}, u32[]{:S(2)}, u32[]{:S(2)}) async-start(f32[4,192,256]{2,1,0:T(8,128)} %bitcast.5), calls=%async_computation.1 | async-start | bytes 1572864 | tf_op jit(solution)/shard_map/all_to_all | solution.py:291
  50.5 3.4 %collective-permute-start.3 = (f32[224,256]{1,0:T(8,128)S(1)}, f32[224,256]{1,0:T(8,128)S(1)}, u32[]{:S(2)}, u32[]{:S(2)}) collective-permute-start(f32[224,256]{1,0:T(8,128)S(1)} %get-tuple-element.50), channel_id=1, source_target_pairs={{0,64},{64,128},{128,192},{192,0},{1,65},{65,129},{129,193},{193,1... | collective-permute-start | bytes 688136 | tf_op jit(solution)/shard_map/ppermute | solution.py:310
  53.9 2.7 %collective-permute-start.4 = (f32[224,256]{1,0:T(8,128)S(1)}, f32[224,256]{1,0:T(8,128)S(1)}, u32[]{:S(2)}, u32[]{:S(2)}) collective-permute-start(f32[224,256]{1,0:T(8,128)S(1)} %get-tuple-element.51), channel_id=1, source_target_pairs={{0,128},{64,192},{128,0},{192,64},{1,129},{65,193},{129,1},{193,65... | collective-permute-start | bytes 688136 | tf_op jit(solution)/shard_map/ppermute | solution.py:310
  57.5 3.3 %collective-permute-done.3 = f32[224,256]{1,0:T(8,128)S(1)} collective-permute-done((f32[224,256]{1,0:T(8,128)S(1)}, f32[224,256]{1,0:T(8,128)S(1)}, u32[]{:S(2)}, u32[]{:S(2)}) %collective-permute-start.3) | collective-permute-done | bytes 229408 | tf_op jit(solution)/shard_map/ppermute | solution.py:310
  60.8 5.8 %collective-permute-done.4 = f32[224,256]{1,0:T(8,128)S(1)} collective-permute-done((f32[224,256]{1,0:T(8,128)S(1)}, f32[224,256]{1,0:T(8,128)S(1)}, u32[]{:S(2)}, u32[]{:S(2)}) %collective-permute-start.4) | collective-permute-done | bytes 229408 | tf_op jit(solution)/shard_map/ppermute | solution.py:310
  70.2 7.0 %collective-permute-done.7.below_ref = bf16[1,256,256]{2,1,0:T(8,128)(2,1)S(1)} collective-permute-done((bf16[1,256,256]{2,1,0:T(8,128)(2,1)S(1)}, bf16[1,256,256]{2,1,0:T(8,128)(2,1)S(1)}, u32[]{:S(2)}, u32[]{:S(2)}) %collective-permute-start.7) | collective-permute-done | bytes 131104 | tf_op jit(solution)/shard_map/ppermute | solution.py:41
  77.3 2.0 %collective-permute-start.8 = (f32[56,256]{1,0:T(8,128)S(1)}, f32[56,256]{1,0:T(8,128)S(1)}, u32[]{:S(2)}, u32[]{:S(2)}) collective-permute-start(f32[56,256]{1,0:T(8,128)S(1)} %get-tuple-element.62), channel_id=1, source_target_pairs={{0,64},{2,66},{4,68},{6,70},{8,10},{10,12},{12,14},{14,8},{16,80},... | collective-permute-start | bytes 172040 | tf_op jit(solution)/shard_map/ppermute | solution.py:328
  79.3 3.2 %collective-permute-start.9 = (f32[56,256]{1,0:T(8,128)S(1)}, f32[56,256]{1,0:T(8,128)S(1)}, u32[]{:S(2)}, u32[]{:S(2)}) collective-permute-start(f32[56,256]{1,0:T(8,128)S(1)} %get-tuple-element.63), channel_id=1, source_target_pairs={{0,128},{2,130},{4,132},{6,134},{8,12},{10,14},{12,8},{14,10},{16,... | collective-permute-start | bytes 172040 | tf_op jit(solution)/shard_map/ppermute | solution.py:328
  82.9 1.9 %collective-permute-done.9 = f32[56,256]{1,0:T(8,128)S(1)} collective-permute-done((f32[56,256]{1,0:T(8,128)S(1)}, f32[56,256]{1,0:T(8,128)S(1)}, u32[]{:S(2)}, u32[]{:S(2)}) %collective-permute-start.9) | collective-permute-done | bytes 57376 | tf_op jit(solution)/shard_map/ppermute | solution.py:328
  84.8 1.5 %collective-permute-done.10 = f32[56,256]{1,0:T(8,128)S(1)} collective-permute-done((f32[56,256]{1,0:T(8,128)S(1)}, f32[56,256]{1,0:T(8,128)S(1)}, u32[]{:S(2)}, u32[]{:S(2)}) %collective-permute-start.10) | collective-permute-done | bytes 57376 | tf_op jit(solution)/shard_map/ppermute | solution.py:328
  86.3 2.0 %collective-permute-start.13 = (f32[56,256]{1,0:T(8,128)S(1)}, f32[56,256]{1,0:T(8,128)S(1)}, u32[]{:S(2)}, u32[]{:S(2)}) collective-permute-start(f32[56,256]{1,0:T(8,128)S(1)} %fusion.6), channel_id=1, source_target_pairs={{0,48},{8,56},{16,0},{24,8},{32,16},{40,24},{48,32},{56,40},{1,49}... | collective-permute-start | bytes 172040 | tf_op jit(solution)/shard_map/ppermute | solution.py:310
  89.4 2.2 %collective-permute-start.11 = (f32[56,256]{1,0:T(8,128)S(1)}, f32[56,256]{1,0:T(8,128)S(1)}, u32[]{:S(2)}, u32[]{:S(2)}) collective-permute-start(f32[56,256]{1,0:T(8,128)S(1)} %fusion.6), channel_id=1, source_target_pairs={{0,16},{8,24},{16,32},{24,40},{32,48},{40,56},{48,0},{56,8},{1,17}... | collective-permute-start | bytes 172040 | tf_op jit(solution)/shard_map/ppermute | solution.py:310
  91.6 1.9 %input_grad.1 = bf16[4,512,256]{2,1,0:T(8,128)(2,1)} custom-call(bf16[2,256,256]{2,1,0:T(8,128)(2,1)S(1)} %copy-done.5, bf16[1,256,256]{2,1,0:T(8,128)(2,1)S(1)} %collective-permute-done.7.below_ref, bf16[3,3,256,256]{3,2,1,0:T(8,128)(2,1)S(1)} %copy-done.3), custom_call_target="tpu_custom_call" | custom-call | flops 604000000 | bytes 3000000 | tf_op jit(solution)/shard_map/input_grad/pallas_call | solution.py:278
  93.5 1.8 %collective-permute-done.12 = f32[56,256]{1,0:T(8,128)S(1)} collective-permute-done((f32[56,256]{1,0:T(8,128)S(1)}, f32[56,256]{1,0:T(8,128)S(1)}, u32[]{:S(2)}, u32[]{:S(2)}) %collective-permute-start.12) | collective-permute-done | bytes 57376 | tf_op jit(solution)/shard_map/ppermute | solution.py:310
  95.4 1.6 %collective-permute-start.15 = (f32[56,256]{1,0:T(8,128)S(1)}, f32[56,256]{1,0:T(8,128)S(1)}, u32[]{:S(2)}, u32[]{:S(2)}) collective-permute-start(f32[56,256]{1,0:T(8,128)S(1)} %get-tuple-element.80), channel_id=1, source_target_pairs={{0,128},{2,130},{4,132},{6,134},{8,12},{10,14},{12,8},{14,10},{16,... | collective-permute-start | bytes 172040 | tf_op jit(solution)/shard_map/ppermute | solution.py:328
  97.1 1.4 collective-permute-start.16
  98.4 1.8 %collective-permute-done.14 = f32[56,256]{1,0:T(8,128)S(1)} collective-permute-done((f32[56,256]{1,0:T(8,128)S(1)}, f32[56,256]{1,0:T(8,128)S(1)}, u32[]{:S(2)}, u32[]{:S(2)}) %collective-permute-start.14) | collective-permute-done | bytes 57376 | tf_op jit(solution)/shard_map/ppermute | solution.py:328
  100.9 5.2 %collective-permute-done.17 = f32[224,256]{1,0:T(8,128)S(1)} collective-permute-done((f32[224,256]{1,0:T(8,128)S(1)}, f32[224,256]{1,0:T(8,128)S(1)}, u32[]{:S(2)}, u32[]{:S(2)}) %collective-permute-start.17) | collective-permute-done | bytes 229408 | tf_op jit(solution)/shard_map/ppermute | solution.py:318
  107.0 3.9 %all-to-all-start.2 = ((f32[4,192,256]{2,1,0:T(8,128)}), f32[4,192,256]{2,1,0:T(8,128)S(1)}, u32[]{:S(2)}, u32[]{:S(2)}) async-start(f32[4,192,256]{2,1,0:T(8,128)} %broadcast_in_dim.27), calls=%async_computation.2 | async-start | bytes 1572864 | tf_op jit(solution)/shard_map/all_to_all | solution.py:291
  111.0 2.2 %collective-permute-start.20 = (f32[224,256]{1,0:T(8,128)S(1)}, f32[224,256]{1,0:T(8,128)S(1)}, u32[]{:S(2)}, u32[]{:S(2)}) collective-permute-start(f32[224,256]{1,0:T(8,128)S(1)} %broadcast_select_fusion.refs_2_), channel_id=1, source_target_pairs={{0,192},{64,0},{128,64},{192,128},{1,193},{65,1},{129,65},{193,129... | collective-permute-start | bytes 688136 | tf_op jit(solution)/shard_map/ppermute | solution.py:310
  113.7 4.8 %collective-permute-done.20.refs_5_ = f32[224,256]{1,0:T(8,128)S(1)} collective-permute-done((f32[224,256]{1,0:T(8,128)S(1)}, f32[224,256]{1,0:T(8,128)S(1)}, u32[]{:S(2)}, u32[]{:S(2)}) %collective-permute-start.20) | collective-permute-done | bytes 229408 | tf_op jit(solution)/shard_map/ppermute | solution.py:310
  119.6 2.4 %collective-permute-done.18.refs_3_ = f32[224,256]{1,0:T(8,128)S(1)} collective-permute-done((f32[224,256]{1,0:T(8,128)S(1)}, f32[224,256]{1,0:T(8,128)S(1)}, u32[]{:S(2)}, u32[]{:S(2)}) %collective-permute-start.18) | collective-permute-done | bytes 229408 | tf_op jit(solution)/shard_map/ppermute | solution.py:310
  122.0 8.7 %collective-permute-start.21 = (f32[768,256]{1,0:T(8,128)S(1)}, f32[768,256]{1,0:T(8,128)S(1)}, u32[]{:S(2)}, u32[]{:S(2)}) collective-permute-start(f32[768,256]{1,0:T(8,128)S(1)} %bitcast.44), channel_id=1, source_target_pairs={{0,1},{1,0},{2,3},{3,2},{4,5},{5,4},{6,7},{7,6},{8,9},{9,8},{10,11... | collective-permute-start | bytes 2359304 | tf_op jit(solution)/shard_map/ppermute | solution.py:318
  133.9 2.6 %assemble.1 = (f32[9,256,256]{2,1,0:T(8,128)}, f32[256,1024]{1,0:T(8,128)}) custom-call(s32[2]{0:T(128)S(1)} %pad_add_fusion.where_ref, f32[768,256]{1,0:T(8,128)S(1)} %bitcast.45, f32[768,256]{1,0:T(8,128)S(1)} %collective-permute-done.21.refs_1_, f32[224,256]{1,0:T(8,128)S(1)} %broadcast_select_fusion.refs_2_, ...), custom_call_target="tpu_custom_call" | custom-call | bytes 7000000 | tf_op jit(solution)/shard_map/assemble/pallas_call | solution.py:400
  (72 shorter events, 16.8 us)
Async XLA Ops:
  0.6 15.6 %copy-start.1 = (bf16[1,4,512,256]{3,2,1,0:T(8,128)(2,1)S(1)}, bf16[1,4,512,256]{3,2,1,0:T(8,128)(2,1)}, u32[]{:S(2)}) copy-start(bf16[1,4,512,256]{3,2,1,0:T(8,128)(2,1)} %param.6) | copy-start | bytes 3145732
  4.3 28.9 %all-to-all-start = ((bf16[32,32,256]{2,1,0:T(8,128)(2,1)}), bf16[32,32,256]{2,1,0:T(8,128)(2,1)S(1)}, u32[]{:S(2)}, u32[]{:S(2)}) async-start(bf16[32,32,256]{2,1,0:T(8,128)(2,1)} %get-tuple-element.41), calls=%async_computation | async-start | bytes 1048576 | tf_op jit(solution)/shard_map/all_to_all | solution.py:291
  16.3 16.0 %collective-permute-start = (bf16[1,512,256]{2,1,0:T(8,128)(2,1)S(1)}, bf16[1,512,256]{2,1,0:T(8,128)(2,1)S(1)}, u32[]{:S(2)}, u32[]{:S(2)}) collective-permute-start(bf16[1,512,256]{2,1,0:T(8,128)(2,1)S(1)} %slice_bitcast_fusion), channel_id=1, source_target_pairs={{0,8},{8,16},{16,24},{24,32},{32,40},{40,48},{48,56},{56,64},{64,7... | collective-permute-start | bytes 786440 | tf_op jit(solution)/shard_map/ppermute | solution.py:41
  38.4 5.0 %collective-permute-start.1 = (f32[768,256]{1,0:T(8,128)}, f32[768,256]{1,0:T(8,128)S(1)}, u32[]{:S(2)}, u32[]{:S(2)}) collective-permute-start(f32[768,256]{1,0:T(8,128)} %get-tuple-element.44), channel_id=1, source_target_pairs={{0,1},{1,0},{2,3},{3,2},{4,5},{5,4},{6,7},{7,6},{8,9},{9,8},{10,11... | collective-permute-start | bytes 2359304 | tf_op jit(solution)/shard_map/ppermute | solution.py:318
  41.2 8.6 %collective-permute-start.2 = (f32[896,256]{1,0:T(8,128)}, f32[896,256]{1,0:T(8,128)S(1)}, u32[]{:S(2)}, u32[]{:S(2)}) collective-permute-start(f32[896,256]{1,0:T(8,128)} %get-tuple-element.46), channel_id=1, source_target_pairs={{0,1},{1,0},{2,3},{3,2},{4,5},{5,4},{6,7},{7,6},{8,9},{9,8},{10,11... | collective-permute-start | bytes 2752520 | tf_op jit(solution)/shard_map/ppermute | solution.py:318
  45.6 21.0 %all-to-all-start.1 = ((f32[4,192,256]{2,1,0:T(8,128)}), f32[4,192,256]{2,1,0:T(8,128)S(1)}, u32[]{:S(2)}, u32[]{:S(2)}) async-start(f32[4,192,256]{2,1,0:T(8,128)} %bitcast.5), calls=%async_computation.1 | async-start | bytes 1572864 | tf_op jit(solution)/shard_map/all_to_all | solution.py:291
  50.5 10.3 %collective-permute-start.3 = (f32[224,256]{1,0:T(8,128)S(1)}, f32[224,256]{1,0:T(8,128)S(1)}, u32[]{:S(2)}, u32[]{:S(2)}) collective-permute-start(f32[224,256]{1,0:T(8,128)S(1)} %get-tuple-element.50), channel_id=1, source_target_pairs={{0,64},{64,128},{128,192},{192,0},{1,65},{65,129},{129,193},{193,1... | collective-permute-start | bytes 688136 | tf_op jit(solution)/shard_map/ppermute | solution.py:310
  53.9 12.7 %collective-permute-start.4 = (f32[224,256]{1,0:T(8,128)S(1)}, f32[224,256]{1,0:T(8,128)S(1)}, u32[]{:S(2)}, u32[]{:S(2)}) collective-permute-start(f32[224,256]{1,0:T(8,128)S(1)} %get-tuple-element.51), channel_id=1, source_target_pairs={{0,128},{64,192},{128,0},{192,64},{1,129},{65,193},{129,1},{193,65... | collective-permute-start | bytes 688136 | tf_op jit(solution)/shard_map/ppermute | solution.py:310
  56.6 9.9 %collective-permute-start.5 = (f32[224,256]{1,0:T(8,128)S(1)}, f32[224,256]{1,0:T(8,128)S(1)}, u32[]{:S(2)}, u32[]{:S(2)}) collective-permute-start(f32[224,256]{1,0:T(8,128)S(1)} %get-tuple-element.52), channel_id=1, source_target_pairs={{0,192},{64,0},{128,64},{192,128},{1,193},{65,1},{129,65},{193,129... | collective-permute-start | bytes 688136 | tf_op jit(solution)/shard_map/ppermute | solution.py:310
  67.3 24.2 %copy-start.3 = (bf16[3,3,256,256]{3,2,1,0:T(8,128)(2,1)S(1)}, bf16[3,3,256,256]{3,2,1,0:T(8,128)(2,1)}, u32[]{:S(2)}) copy-start(bf16[3,3,256,256]{3,2,1,0:T(8,128)(2,1)} %weight_ref.1) | copy-start | bytes 3538948
  67.3 24.2 %copy-start.5 = (bf16[2,256,256]{2,1,0:T(8,128)(2,1)S(1)}, bf16[2,256,256]{2,1,0:T(8,128)(2,1)}, u32[]{:S(2)}) copy-start(bf16[2,256,256]{2,1,0:T(8,128)(2,1)} %get-tuple-element.65.grad_ref) | copy-start | bytes 786436
  68.8 8.5 %collective-permute-start.6 = (f32[224,256]{1,0:T(8,128)S(1)}, f32[224,256]{1,0:T(8,128)S(1)}, u32[]{:S(2)}, u32[]{:S(2)}) collective-permute-start(f32[224,256]{1,0:T(8,128)S(1)} %fusion.1), channel_id=1, source_target_pairs={{0,8},{8,0},{16,24},{24,16},{32,40},{40,32},{48,56},{56,48},{1,9},... | collective-permute-start | bytes 688136 | tf_op jit(solution)/shard_map/ppermute | solution.py:318
  68.9 8.4 %collective-permute-start.7 = (bf16[1,256,256]{2,1,0:T(8,128)(2,1)S(1)}, bf16[1,256,256]{2,1,0:T(8,128)(2,1)S(1)}, u32[]{:S(2)}, u32[]{:S(2)}) collective-permute-start(bf16[1,256,256]{2,1,0:T(8,128)(2,1)S(1)} %copy-done.10), channel_id=1, source_target_pairs={{8,0},{16,8},{24,16},{32,24},{40,32},{48,40},{56,48},{64,56},{72,6... | collective-permute-start | bytes 393224 | tf_op jit(solution)/shard_map/ppermute | solution.py:41
  77.3 5.6 %collective-permute-start.8 = (f32[56,256]{1,0:T(8,128)S(1)}, f32[56,256]{1,0:T(8,128)S(1)}, u32[]{:S(2)}, u32[]{:S(2)}) collective-permute-start(f32[56,256]{1,0:T(8,128)S(1)} %get-tuple-element.62), channel_id=1, source_target_pairs={{0,64},{2,66},{4,68},{6,70},{8,10},{10,12},{12,14},{14,8},{16,80},... | collective-permute-start | bytes 172040 | tf_op jit(solution)/shard_map/ppermute | solution.py:328
  79.3 5.5 %collective-permute-start.9 = (f32[56,256]{1,0:T(8,128)S(1)}, f32[56,256]{1,0:T(8,128)S(1)}, u32[]{:S(2)}, u32[]{:S(2)}) collective-permute-start(f32[56,256]{1,0:T(8,128)S(1)} %get-tuple-element.63), channel_id=1, source_target_pairs={{0,128},{2,130},{4,132},{6,134},{8,12},{10,14},{12,8},{14,10},{16,... | collective-permute-start | bytes 172040 | tf_op jit(solution)/shard_map/ppermute | solution.py:328
  82.5 3.8 %collective-permute-start.10 = (f32[56,256]{1,0:T(8,128)S(1)}, f32[56,256]{1,0:T(8,128)S(1)}, u32[]{:S(2)}, u32[]{:S(2)}) collective-permute-start(f32[56,256]{1,0:T(8,128)S(1)} %get-tuple-element.64), channel_id=1, source_target_pairs={{0,192},{2,194},{4,196},{6,198},{8,14},{10,8},{12,10},{14,12},{16,... | collective-permute-start | bytes 172040 | tf_op jit(solution)/shard_map/ppermute | solution.py:328
  86.3 7.2 %collective-permute-start.13 = (f32[56,256]{1,0:T(8,128)S(1)}, f32[56,256]{1,0:T(8,128)S(1)}, u32[]{:S(2)}, u32[]{:S(2)}) collective-permute-start(f32[56,256]{1,0:T(8,128)S(1)} %fusion.6), channel_id=1, source_target_pairs={{0,48},{8,56},{16,0},{24,8},{32,16},{40,24},{48,32},{56,40},{1,49}... | collective-permute-start | bytes 172040 | tf_op jit(solution)/shard_map/ppermute | solution.py:310
  88.3 6.9 %collective-permute-start.12 = (f32[56,256]{1,0:T(8,128)S(1)}, f32[56,256]{1,0:T(8,128)S(1)}, u32[]{:S(2)}, u32[]{:S(2)}) collective-permute-start(f32[56,256]{1,0:T(8,128)S(1)} %fusion.6), channel_id=1, source_target_pairs={{0,32},{8,40},{16,48},{24,56},{32,0},{40,8},{48,16},{56,24},{1,33}... | collective-permute-start | bytes 172040 | tf_op jit(solution)/shard_map/ppermute | solution.py:310
  89.4 5.9 %collective-permute-start.11 = (f32[56,256]{1,0:T(8,128)S(1)}, f32[56,256]{1,0:T(8,128)S(1)}, u32[]{:S(2)}, u32[]{:S(2)}) collective-permute-start(f32[56,256]{1,0:T(8,128)S(1)} %fusion.6), channel_id=1, source_target_pairs={{0,16},{8,24},{16,32},{24,40},{32,48},{40,56},{48,0},{56,8},{1,17}... | collective-permute-start | bytes 172040 | tf_op jit(solution)/shard_map/ppermute | solution.py:310
  95.3 4.9 %collective-permute-start.14 = (f32[56,256]{1,0:T(8,128)S(1)}, f32[56,256]{1,0:T(8,128)S(1)}, u32[]{:S(2)}, u32[]{:S(2)}) collective-permute-start(f32[56,256]{1,0:T(8,128)S(1)} %get-tuple-element.80), channel_id=1, source_target_pairs={{0,64},{2,66},{4,68},{6,70},{8,10},{10,12},{12,14},{14,8},{16,80},... | collective-permute-start | bytes 172040 | tf_op jit(solution)/shard_map/ppermute | solution.py:328
  95.4 4.8 %collective-permute-start.15 = (f32[56,256]{1,0:T(8,128)S(1)}, f32[56,256]{1,0:T(8,128)S(1)}, u32[]{:S(2)}, u32[]{:S(2)}) collective-permute-start(f32[56,256]{1,0:T(8,128)S(1)} %get-tuple-element.80), channel_id=1, source_target_pairs={{0,128},{2,130},{4,132},{6,134},{8,12},{10,14},{12,8},{14,10},{16,... | collective-permute-start | bytes 172040 | tf_op jit(solution)/shard_map/ppermute | solution.py:328
  97.1 3.8 %collective-permute-start.16 = (f32[56,256]{1,0:T(8,128)S(1)}, f32[56,256]{1,0:T(8,128)S(1)}, u32[]{:S(2)}, u32[]{:S(2)}) collective-permute-start(f32[56,256]{1,0:T(8,128)S(1)} %get-tuple-element.80), channel_id=1, source_target_pairs={{0,192},{2,194},{4,196},{6,198},{8,14},{10,8},{12,10},{14,12},{16,... | collective-permute-start | bytes 172040 | tf_op jit(solution)/shard_map/ppermute | solution.py:328
  100.8 5.2 %collective-permute-start.17 = (f32[224,256]{1,0:T(8,128)S(1)}, f32[224,256]{1,0:T(8,128)S(1)}, u32[]{:S(2)}, u32[]{:S(2)}) collective-permute-start(f32[224,256]{1,0:T(8,128)S(1)} %bitcast.47), channel_id=1, source_target_pairs={{0,8},{8,0},{16,24},{24,16},{32,40},{40,32},{48,56},{56,48},{1,9},... | collective-permute-start | bytes 688136 | tf_op jit(solution)/shard_map/ppermute | solution.py:318
  107.0 15.0 %all-to-all-start.2 = ((f32[4,192,256]{2,1,0:T(8,128)}), f32[4,192,256]{2,1,0:T(8,128)S(1)}, u32[]{:S(2)}, u32[]{:S(2)}) async-start(f32[4,192,256]{2,1,0:T(8,128)} %broadcast_in_dim.27), calls=%async_computation.2 | async-start | bytes 1572864 | tf_op jit(solution)/shard_map/all_to_all | solution.py:291
  111.0 7.6 %collective-permute-start.20 = (f32[224,256]{1,0:T(8,128)S(1)}, f32[224,256]{1,0:T(8,128)S(1)}, u32[]{:S(2)}, u32[]{:S(2)}) collective-permute-start(f32[224,256]{1,0:T(8,128)S(1)} %broadcast_select_fusion.refs_2_), channel_id=1, source_target_pairs={{0,192},{64,0},{128,64},{192,128},{1,193},{65,1},{129,65},{193,129... | collective-permute-start | bytes 688136 | tf_op jit(solution)/shard_map/ppermute | solution.py:310
  113.1 6.5 %collective-permute-start.19 = (f32[224,256]{1,0:T(8,128)S(1)}, f32[224,256]{1,0:T(8,128)S(1)}, u32[]{:S(2)}, u32[]{:S(2)}) collective-permute-start(f32[224,256]{1,0:T(8,128)S(1)} %broadcast_select_fusion.refs_2_), channel_id=1, source_target_pairs={{0,128},{64,192},{128,0},{192,64},{1,129},{65,193},{129,1},{193,65... | collective-permute-start | bytes 688136 | tf_op jit(solution)/shard_map/ppermute | solution.py:310
  113.6 8.4 %collective-permute-start.18 = (f32[224,256]{1,0:T(8,128)S(1)}, f32[224,256]{1,0:T(8,128)S(1)}, u32[]{:S(2)}, u32[]{:S(2)}) collective-permute-start(f32[224,256]{1,0:T(8,128)S(1)} %broadcast_select_fusion.refs_2_), channel_id=1, source_target_pairs={{0,64},{64,128},{128,192},{192,0},{1,65},{65,129},{129,193},{193,1... | collective-permute-start | bytes 688136 | tf_op jit(solution)/shard_map/ppermute | solution.py:310
  122.0 12.0 %collective-permute-start.21 = (f32[768,256]{1,0:T(8,128)S(1)}, f32[768,256]{1,0:T(8,128)S(1)}, u32[]{:S(2)}, u32[]{:S(2)}) collective-permute-start(f32[768,256]{1,0:T(8,128)S(1)} %bitcast.44), channel_id=1, source_target_pairs={{0,1},{1,0},{2,3},{3,2},{4,5},{5,4},{6,7},{7,6},{8,9},{9,8},{10,11... | collective-permute-start | bytes 2359304 | tf_op jit(solution)/shard_map/ppermute | solution.py:318
  130.7 2.2 %collective-permute-start.22 = (f32[224,256]{1,0:T(8,128)S(1)}, f32[224,256]{1,0:T(8,128)S(1)}, u32[]{:S(2)}, u32[]{:S(2)}) collective-permute-start(f32[224,256]{1,0:T(8,128)S(1)} %broadcast_select_fusion.refs_2_), channel_id=1, source_target_pairs={{0,1},{1,0},{2,3},{3,2},{4,5},{5,4},{6,7},{7,6},{8,9},{9,8},{10,11... | collective-permute-start | bytes 688136 | tf_op jit(solution)/shard_map/ppermute | solution.py:318
  130.7 2.6 %collective-permute-start.23 = (f32[224,256]{1,0:T(8,128)S(1)}, f32[224,256]{1,0:T(8,128)S(1)}, u32[]{:S(2)}, u32[]{:S(2)}) collective-permute-start(f32[224,256]{1,0:T(8,128)S(1)} %collective-permute-done.18.refs_3_), channel_id=1, source_target_pairs={{0,1},{1,0},{2,3},{3,2},{4,5},{5,4},{6,7},{7,6},{8,9},{9,8},{10,11... | collective-permute-start | bytes 688136 | tf_op jit(solution)/shard_map/ppermute | solution.py:318
  131.2 2.4 %collective-permute-start.24 = (f32[224,256]{1,0:T(8,128)S(1)}, f32[224,256]{1,0:T(8,128)S(1)}, u32[]{:S(2)}, u32[]{:S(2)}) collective-permute-start(f32[224,256]{1,0:T(8,128)S(1)} %collective-permute-done.19.refs_4_), channel_id=1, source_target_pairs={{0,1},{1,0},{2,3},{3,2},{4,5},{5,4},{6,7},{7,6},{8,9},{9,8},{10,11... | collective-permute-start | bytes 688136 | tf_op jit(solution)/shard_map/ppermute | solution.py:318
  131.2 2.7 %collective-permute-start.25 = (f32[224,256]{1,0:T(8,128)S(1)}, f32[224,256]{1,0:T(8,128)S(1)}, u32[]{:S(2)}, u32[]{:S(2)}) collective-permute-start(f32[224,256]{1,0:T(8,128)S(1)} %collective-permute-done.20.refs_5_), channel_id=1, source_target_pairs={{0,1},{1,0},{2,3},{3,2},{4,5},{5,4},{6,7},{7,6},{8,9},{9,8},{10,11... | collective-permute-start | bytes 688136 | tf_op jit(solution)/shard_map/ppermute | solution.py:318
  (8 other events, 24.5 us)

commit v8 on v7

--- a/solution.py
+++ b/solution.py
@@ -222,6 +222,22 @@
     )(core, arrived, preact, above, blocks, weighted)
 
 
+def add_kernel(own, got, out_ref):
+    out_ref[...] = own[...] + got[...]
+
+
+def add(own, got):
+    return pl.pallas_call(
+        add_kernel,
+        out_shape=jax.ShapeDtypeStruct(own.shape, own.dtype),
+        in_specs=[whole()] * 2,
+        out_specs=whole(),
+        compiler_params=params(24),
+        cost_estimate=pl.CostEstimate(flops=10**5, bytes_accessed=2 * 10**6, transcendentals=0),
+        name="add",
+    )(own, got)
+
+
 def combine_kernel(where_ref, own, got, *out_refs):
     rows = out_refs[0].shape[0]
     for by, out_ref in enumerate(out_refs):
@@ -347,13 +363,12 @@
     rows = outer.shape[0] - inner.shape[0]
     both = jnp.stack([jnp.pad(inner, ((0, rows), (0, 0))), outer])
     bit = place("z") & jnp.uint32(1)
-    other, first = barrier((pick(both, jnp.uint32(1) - bit), first))
-    got, below = barrier((swapped(other, "z", 1), shifted(first, -1)))
-    part = pick(both, bit) + got
+    part = pick(both, bit) + swapped(pick(both, jnp.uint32(1) - bit), "z", 1)
 
     parts = split(part)
-    moved = barrier([pick(parts, turned_place(by)) for by in STEPS])
+    moved, first = barrier(([pick(parts, turned_place(by)) for by in STEPS], first))
     moved = [turned(p, by) for p, by in zip(moved, STEPS)]
+    below = shifted(first, -1)
     part = sum(moved, pick(parts, turned_place()))
 
     moved = [rotated(part, "z", by) for by in (2, 4, 6)]
@@ -432,7 +447,7 @@
 
     samples_all = stem_input.shape[0] * SIZES["y"] * SIZES["core"]
     scale = float(samples_all * all_rows * out_cols) ** (-0.5)
-    inner = own_inner + swapped(other_inner, "core", 1)
+    inner = add(own_inner, swapped(other_inner, "core", 1))
     outer, *parts = combine(where, own_outer, swapped(other_outer, "core", 1))
     inner, outer, grad_input = total_sums(
         inner, outer, parts, scale, first, lambda b: input_grad(grad, b, conv_weight)

time: 137 us -> 134 us (0.978)
  waiting for transfers between devices: 52.8 us -> 49.8 us
  other arithmetic: 3.86 us -> 1.68 us
    ppermute x2, waiting for transfers between devices: 18.2 us -> 11.1 us  [shifted(): return lax.ppermute(x, SPACE, pairs)]
    ppermute x9, waiting for transfers between devices: 9.38 us -> 14.6 us  [swapped(): return lax.ppermute(x, axis, [(i, i ^ bit) for i in range(SIZES[axis])])]
    add x2 -> x1, other arithmetic: 2.24 us -> 0.05 us  [total_sums(): part = pick(both, bit) + swapped(pick(both, jnp.uint32(1) - bit), 'z', 1)]
    ppermute x6, starting transfers between devices: 8.3 us -> 10.3 us  [turned(): return lax.ppermute(x, ('x', 'z', 'y'), pairs)]
    unnamed x22 -> x24, local copies, waits for them, and re-layouts: 3.38 us -> 4.53 us
  transfers between devices with their start and end apart: 29 -> 29, of which waited for: 19 -> 20; matrix products, arithmetic and copies ran while one was open for 2% -> 0% of each run, Pallas kernels for 2% -> 3%
where the time goes in v8:
time: 134 us
  starting transfers between devices  61 us (46%)
  waiting for transfers between devices  49.8 us (37%)
  Pallas kernels  14.2 us (11%)
  local copies, waits for them, and re-layouts  5.55 us (4%)
  other arithmetic  1.68 us (1%)
  between operations  1.63 us (1%)
    all_to_all x3, starting transfers between devices, exchange(): return lax.all_to_all(x, axis, split_axis=0, concat_axis=0, tiled=True)  19.5 us
    ppermute x9, waiting for transfers between devices, rotated(): return lax.ppermute(x, axis, [(i, (i + by) % size) for i in range(size)])  18.6 us
    ppermute x9, starting transfers between devices, rotated(): return lax.ppermute(x, axis, [(i, (i + by) % size) for i in range(size)])  14.9 us
    ppermute x9, waiting for transfers between devices, swapped(): return lax.ppermute(x, axis, [(i, i ^ bit) for i in range(SIZES[axis])])  14.6 us
    ppermute x9, starting transfers between devices, swapped(): return lax.ppermute(x, axis, [(i, i ^ bit) for i in range(SIZES[axis])])  11.9 us
    ppermute x2, waiting for transfers between devices, shifted(): return lax.ppermute(x, SPACE, pairs)  11.1 us
    ppermute x6, starting transfers between devices, turned(): return lax.ppermute(x, ('x', 'z', 'y'), pairs)  10.3 us
    ppermute x6, waiting for transfers between devices, turned(): return lax.ppermute(x, ('x', 'z', 'y'), pairs)  5.48 us
  transfers between devices with their start and end apart: 29, of which 20 were waited for; matrix products, arithmetic and copies ran while one was open for 0% of the time, Pallas kernels for 3%

profile of v8, /device:TPU:1, one launch (start us, length us, event | category | flops | bytes accessed | tf_op | source)
XLA Modules:
  0.0 133.8 jit_solution(3911025998857768883)
XLA Ops:
  1.4 2.9 %build_sent.1 = (bf16[32,32,256]{2,1,0:T(8,128)(2,1)}, bf16[512,1024]{1,0:T(8,128)(2,1)}) custom-call(f32[1]{0:T(128)S(6)} %div.3.share_ref, bf16[512,1024]{1,0:T(8,128)(2,1)} %bitcast.49, bf16[256,1024]{1,0:T(8,128)(2,1)} %weight_hbm.1, bf16[2,256,256]{2,1,0:T(8,128)(2,1)} %bitcast.51), custom_call_target="tpu_custom_call" | custom-call | flops 268000000 | bytes 4000000 | tf_op jit(solution)/shard_map/build_sent/pallas_call | solution.py:79
  4.3 11.9 %all-to-all-start = ((bf16[32,32,256]{2,1,0:T(8,128)(2,1)}), bf16[32,32,256]{2,1,0:T(8,128)(2,1)S(1)}, u32[]{:S(2)}, u32[]{:S(2)}) async-start(bf16[32,32,256]{2,1,0:T(8,128)(2,1)} %get-tuple-element.38), calls=%async_computation | async-start | bytes 1048576 | tf_op jit(solution)/shard_map/all_to_all | solution.py:307
  16.3 3.1 %collective-permute-start = (bf16[1,512,256]{2,1,0:T(8,128)(2,1)S(1)}, bf16[1,512,256]{2,1,0:T(8,128)(2,1)S(1)}, u32[]{:S(2)}, u32[]{:S(2)}) collective-permute-start(bf16[1,512,256]{2,1,0:T(8,128)(2,1)S(1)} %slice_bitcast_fusion), channel_id=1, source_target_pairs={{0,8},{8,16},{16,24},{24,32},{32,40},{40,48},{48,56},{56,64},{64,7... | collective-permute-start | bytes 786440 | tf_op jit(solution)/shard_map/ppermute | solution.py:41
  21.1 11.1 %collective-permute-done.x_ref = bf16[1,512,256]{2,1,0:T(8,128)(2,1)S(1)} collective-permute-done((bf16[1,512,256]{2,1,0:T(8,128)(2,1)S(1)}, bf16[1,512,256]{2,1,0:T(8,128)(2,1)S(1)}, u32[]{:S(2)}, u32[]{:S(2)}) %collective-permute-start) | collective-permute-done | bytes 262176 | tf_op jit(solution)/shard_map/ppermute | solution.py:41
  34.1 4.3 %terms.1 = (f32[768,256]{1,0:T(8,128)}, f32[768,256]{1,0:T(8,128)}, f32[896,256]{1,0:T(8,128)}, f32[896,256]{1,0:T(8,128)}, bf16[2,256,256]{2,1,0:T(8,128)(2,1)}, /*index=5*/bf16[1,256,256]{2,1,0:T(8,128)(2,1)}) custom-call(s32[1]{0:T(128)} %bitcast.core_ref, bf16[32,32,256]{2,1,0:T(8,128)(2,1)} %copy-done.7, bf16[2,256,256]{2,1,0:T(8,128)(2,1)} %bitcast.52, ...), custom_call_target="tpu_custom_call" | custom-call | flops 870000000 | bytes 8000000 | tf_op jit(solution)/shard_map/terms/pallas_call | solution.py:200
  38.4 2.9 %collective-permute-start.1 = (f32[768,256]{1,0:T(8,128)}, f32[768,256]{1,0:T(8,128)S(1)}, u32[]{:S(2)}, u32[]{:S(2)}) collective-permute-start(f32[768,256]{1,0:T(8,128)} %get-tuple-element.41), channel_id=1, source_target_pairs={{0,1},{1,0},{2,3},{3,2},{4,5},{5,4},{6,7},{7,6},{8,9},{9,8},{10,11... | collective-permute-start | bytes 2359304 | tf_op jit(solution)/shard_map/ppermute | solution.py:334
  41.4 2.0 %collective-permute-done.1.got = f32[768,256]{1,0:T(8,128)S(1)} collective-permute-done((f32[768,256]{1,0:T(8,128)}, f32[768,256]{1,0:T(8,128)S(1)}, u32[]{:S(2)}, u32[]{:S(2)}) %collective-permute-start.1) | collective-permute-done | bytes 786464 | tf_op jit(solution)/shard_map/ppermute | solution.py:334
  45.5 4.2 %all-to-all-start.1 = ((f32[4,192,256]{2,1,0:T(8,128)}), f32[4,192,256]{2,1,0:T(8,128)S(1)}, u32[]{:S(2)}, u32[]{:S(2)}) async-start(f32[4,192,256]{2,1,0:T(8,128)} %bitcast.5), calls=%async_computation.1 | async-start | bytes 1572864 | tf_op jit(solution)/shard_map/all_to_all | solution.py:307
  50.4 3.4 %collective-permute-start.3 = (f32[224,256]{1,0:T(8,128)S(1)}, f32[224,256]{1,0:T(8,128)S(1)}, u32[]{:S(2)}, u32[]{:S(2)}) collective-permute-start(f32[224,256]{1,0:T(8,128)S(1)} %get-tuple-element.47), channel_id=1, source_target_pairs={{0,64},{64,128},{128,192},{192,0},{1,65},{65,129},{129,193},{193,1... | collective-permute-start | bytes 688136 | tf_op jit(solution)/shard_map/ppermute | solution.py:326
  53.8 2.7 %collective-permute-start.4 = (f32[224,256]{1,0:T(8,128)S(1)}, f32[224,256]{1,0:T(8,128)S(1)}, u32[]{:S(2)}, u32[]{:S(2)}) collective-permute-start(f32[224,256]{1,0:T(8,128)S(1)} %get-tuple-element.48), channel_id=1, source_target_pairs={{0,128},{64,192},{128,0},{192,64},{1,129},{65,193},{129,1},{193,65... | collective-permute-start | bytes 688136 | tf_op jit(solution)/shard_map/ppermute | solution.py:326
  57.4 3.3 %collective-permute-done.3 = f32[224,256]{1,0:T(8,128)S(1)} collective-permute-done((f32[224,256]{1,0:T(8,128)S(1)}, f32[224,256]{1,0:T(8,128)S(1)}, u32[]{:S(2)}, u32[]{:S(2)}) %collective-permute-start.3) | collective-permute-done | bytes 229408 | tf_op jit(solution)/shard_map/ppermute | solution.py:326
  60.7 5.8 %collective-permute-done.4 = f32[224,256]{1,0:T(8,128)S(1)} collective-permute-done((f32[224,256]{1,0:T(8,128)S(1)}, f32[224,256]{1,0:T(8,128)S(1)}, u32[]{:S(2)}, u32[]{:S(2)}) %collective-permute-start.4) | collective-permute-done | bytes 229408 | tf_op jit(solution)/shard_map/ppermute | solution.py:326
  67.3 1.4 %add_bitcast_fusion = (f32[1,224,256]{2,1,0:T(8,128)S(1)}, f32[1,224,256]{2,1,0:T(8,128)S(1)}) fusion(f32[224,256]{1,0:T(8,128)} %copy-done.10, f32[224,256]{1,0:T(8,128)} %copy-done.9, f32[224,256]{1,0:T(8,128)S(1)} %get-tuple-element.51, f32[224,256]{1,0:T(8,128)} %copy-done.8, f32[192,256]{1,0:T(8,128)S(1)} %reduce_sum.9), kind=kLoop, calls=%fused_computation.10 | loop fusion | flops 172032 | bytes 1572864 | tf_op jit(solution)/shard_map/stack | solution.py:364
  68.8 5.5 %collective-permute-done.6 = f32[224,256]{1,0:T(8,128)S(1)} collective-permute-done((f32[224,256]{1,0:T(8,128)S(1)}, f32[224,256]{1,0:T(8,128)S(1)}, u32[]{:S(2)}, u32[]{:S(2)}) %collective-permute-start.6) | collective-permute-done | bytes 229408 | tf_op jit(solution)/shard_map/ppermute | solution.py:334
  74.4 2.0 %collective-permute-start.7 = (f32[56,256]{1,0:T(8,128)S(1)}, f32[56,256]{1,0:T(8,128)S(1)}, u32[]{:S(2)}, u32[]{:S(2)}) collective-permute-start(f32[56,256]{1,0:T(8,128)S(1)} %get-tuple-element.56), channel_id=1, source_target_pairs={{0,64},{2,66},{4,68},{6,70},{8,10},{10,12},{12,14},{14,8},{16,80},... | collective-permute-start | bytes 172040 | tf_op jit(solution)/shard_map/ppermute | solution.py:344
  76.4 3.2 %collective-permute-start.8 = (f32[56,256]{1,0:T(8,128)S(1)}, f32[56,256]{1,0:T(8,128)S(1)}, u32[]{:S(2)}, u32[]{:S(2)}) collective-permute-start(f32[56,256]{1,0:T(8,128)S(1)} %get-tuple-element.57), channel_id=1, source_target_pairs={{0,128},{2,130},{4,132},{6,134},{8,12},{10,14},{12,8},{14,10},{16,... | collective-permute-start | bytes 172040 | tf_op jit(solution)/shard_map/ppermute | solution.py:344
  81.9 1.5 %collective-permute-done.9 = f32[56,256]{1,0:T(8,128)S(1)} collective-permute-done((f32[56,256]{1,0:T(8,128)S(1)}, f32[56,256]{1,0:T(8,128)S(1)}, u32[]{:S(2)}, u32[]{:S(2)}) %collective-permute-start.9) | collective-permute-done | bytes 57376 | tf_op jit(solution)/shard_map/ppermute | solution.py:344
  83.4 2.0 %collective-permute-start.12 = (f32[56,256]{1,0:T(8,128)S(1)}, f32[56,256]{1,0:T(8,128)S(1)}, u32[]{:S(2)}, u32[]{:S(2)}) collective-permute-start(f32[56,256]{1,0:T(8,128)S(1)} %fusion.6), channel_id=1, source_target_pairs={{0,48},{8,56},{16,0},{24,8},{32,16},{40,24},{48,32},{56,40},{1,49}... | collective-permute-start | bytes 172040 | tf_op jit(solution)/shard_map/ppermute | solution.py:326
  86.5 2.2 %collective-permute-start.10 = (f32[56,256]{1,0:T(8,128)S(1)}, f32[56,256]{1,0:T(8,128)S(1)}, u32[]{:S(2)}, u32[]{:S(2)}) collective-permute-start(f32[56,256]{1,0:T(8,128)S(1)} %fusion.6), channel_id=1, source_target_pairs={{0,16},{8,24},{16,32},{24,40},{32,48},{40,56},{48,0},{56,8},{1,17}... | collective-permute-start | bytes 172040 | tf_op jit(solution)/shard_map/ppermute | solution.py:326
  88.7 1.9 %input_grad.1 = bf16[4,512,256]{2,1,0:T(8,128)(2,1)} custom-call(bf16[2,256,256]{2,1,0:T(8,128)(2,1)S(1)} %copy-done.6, bf16[1,256,256]{2,1,0:T(8,128)(2,1)S(1)} %collective-permute-done.13.below_ref, bf16[3,3,256,256]{3,2,1,0:T(8,128)(2,1)S(1)} %copy-done.3), custom_call_target="tpu_custom_call" | custom-call | flops 604000000 | bytes 3000000 | tf_op jit(solution)/shard_map/input_grad/pallas_call | solution.py:294
  90.6 1.7 %collective-permute-done.11 = f32[56,256]{1,0:T(8,128)S(1)} collective-permute-done((f32[56,256]{1,0:T(8,128)S(1)}, f32[56,256]{1,0:T(8,128)S(1)}, u32[]{:S(2)}, u32[]{:S(2)}) %collective-permute-start.11) | collective-permute-done | bytes 57376 | tf_op jit(solution)/shard_map/ppermute | solution.py:326
  92.6 1.5 %collective-permute-start.14 = (f32[56,256]{1,0:T(8,128)S(1)}, f32[56,256]{1,0:T(8,128)S(1)}, u32[]{:S(2)}, u32[]{:S(2)}) collective-permute-start(f32[56,256]{1,0:T(8,128)S(1)} %get-tuple-element.74), channel_id=1, source_target_pairs={{0,64},{2,66},{4,68},{6,70},{8,10},{10,12},{12,14},{14,8},{16,80},... | collective-permute-start | bytes 172040 | tf_op jit(solution)/shard_map/ppermute | solution.py:344
  94.1 3.6 %collective-permute-start.15 = (f32[56,256]{1,0:T(8,128)S(1)}, f32[56,256]{1,0:T(8,128)S(1)}, u32[]{:S(2)}, u32[]{:S(2)}) collective-permute-start(f32[56,256]{1,0:T(8,128)S(1)} %get-tuple-element.74), channel_id=1, source_target_pairs={{0,128},{2,130},{4,132},{6,134},{8,12},{10,14},{12,8},{14,10},{16,... | collective-permute-start | bytes 172040 | tf_op jit(solution)/shard_map/ppermute | solution.py:344
  98.1 1.8 %collective-permute-done.15 = f32[56,256]{1,0:T(8,128)S(1)} collective-permute-done((f32[56,256]{1,0:T(8,128)S(1)}, f32[56,256]{1,0:T(8,128)S(1)}, u32[]{:S(2)}, u32[]{:S(2)}) %collective-permute-start.15) | collective-permute-done | bytes 57376 | tf_op jit(solution)/shard_map/ppermute | solution.py:344
  100.8 4.9 %collective-permute-done.17 = f32[224,256]{1,0:T(8,128)S(1)} collective-permute-done((f32[224,256]{1,0:T(8,128)S(1)}, f32[224,256]{1,0:T(8,128)S(1)}, u32[]{:S(2)}, u32[]{:S(2)}) %collective-permute-start.17) | collective-permute-done | bytes 229408 | tf_op jit(solution)/shard_map/ppermute | solution.py:334
  106.6 3.5 %all-to-all-start.2 = ((f32[4,192,256]{2,1,0:T(8,128)}), f32[4,192,256]{2,1,0:T(8,128)S(1)}, u32[]{:S(2)}, u32[]{:S(2)}) async-start(f32[4,192,256]{2,1,0:T(8,128)} %broadcast_in_dim.27), calls=%async_computation.2 | async-start | bytes 1572864 | tf_op jit(solution)/shard_map/all_to_all | solution.py:307
  110.1 1.3 collective-permute-start.20
  112.7 2.4 %collective-permute-done.20.refs_5_ = f32[224,256]{1,0:T(8,128)S(1)} collective-permute-done((f32[224,256]{1,0:T(8,128)S(1)}, f32[224,256]{1,0:T(8,128)S(1)}, u32[]{:S(2)}, u32[]{:S(2)}) %collective-permute-start.20) | collective-permute-done | bytes 229408 | tf_op jit(solution)/shard_map/ppermute | solution.py:326
  115.1 2.8 %collective-permute-done.19.refs_4_ = f32[224,256]{1,0:T(8,128)S(1)} collective-permute-done((f32[224,256]{1,0:T(8,128)S(1)}, f32[224,256]{1,0:T(8,128)S(1)}, u32[]{:S(2)}, u32[]{:S(2)}) %collective-permute-start.19) | collective-permute-done | bytes 229408 | tf_op jit(solution)/shard_map/ppermute | solution.py:326
  117.9 2.4 %collective-permute-done.18.refs_3_ = f32[224,256]{1,0:T(8,128)S(1)} collective-permute-done((f32[224,256]{1,0:T(8,128)S(1)}, f32[224,256]{1,0:T(8,128)S(1)}, u32[]{:S(2)}, u32[]{:S(2)}) %collective-permute-start.18) | collective-permute-done | bytes 229408 | tf_op jit(solution)/shard_map/ppermute | solution.py:326
  120.2 7.8 %collective-permute-start.21 = (f32[768,256]{1,0:T(8,128)S(1)}, f32[768,256]{1,0:T(8,128)S(1)}, u32[]{:S(2)}, u32[]{:S(2)}) collective-permute-start(f32[768,256]{1,0:T(8,128)S(1)} %bitcast.44), channel_id=1, source_target_pairs={{0,1},{1,0},{2,3},{3,2},{4,5},{5,4},{6,7},{7,6},{8,9},{9,8},{10,11... | collective-permute-start | bytes 2359304 | tf_op jit(solution)/shard_map/ppermute | solution.py:334
  131.2 2.6 %assemble.1 = (f32[9,256,256]{2,1,0:T(8,128)}, f32[256,1024]{1,0:T(8,128)}) custom-call(s32[2]{0:T(128)S(1)} %pad_add_fusion.where_ref, f32[768,256]{1,0:T(8,128)S(1)} %bitcast.45, f32[768,256]{1,0:T(8,128)S(1)} %collective-permute-done.21.refs_1_, f32[224,256]{1,0:T(8,128)S(1)} %broadcast_select_fusion.refs_2_, ...), custom_call_target="tpu_custom_call" | custom-call | bytes 7000000 | tf_op jit(solution)/shard_map/assemble/pallas_call | solution.py:415
  (74 shorter events, 18.6 us)
Async XLA Ops:
  0.6 15.6 %copy-start.1 = (bf16[1,4,512,256]{3,2,1,0:T(8,128)(2,1)S(1)}, bf16[1,4,512,256]{3,2,1,0:T(8,128)(2,1)}, u32[]{:S(2)}) copy-start(bf16[1,4,512,256]{3,2,1,0:T(8,128)(2,1)} %param.6) | copy-start | bytes 3145732
  4.3 28.9 %all-to-all-start = ((bf16[32,32,256]{2,1,0:T(8,128)(2,1)}), bf16[32,32,256]{2,1,0:T(8,128)(2,1)S(1)}, u32[]{:S(2)}, u32[]{:S(2)}) async-start(bf16[32,32,256]{2,1,0:T(8,128)(2,1)} %get-tuple-element.38), calls=%async_computation | async-start | bytes 1048576 | tf_op jit(solution)/shard_map/all_to_all | solution.py:307
  16.3 16.0 %collective-permute-start = (bf16[1,512,256]{2,1,0:T(8,128)(2,1)S(1)}, bf16[1,512,256]{2,1,0:T(8,128)(2,1)S(1)}, u32[]{:S(2)}, u32[]{:S(2)}) collective-permute-start(bf16[1,512,256]{2,1,0:T(8,128)(2,1)S(1)} %slice_bitcast_fusion), channel_id=1, source_target_pairs={{0,8},{8,16},{16,24},{24,32},{32,40},{40,48},{48,56},{56,64},{64,7... | collective-permute-start | bytes 786440 | tf_op jit(solution)/shard_map/ppermute | solution.py:41
  38.4 5.0 %collective-permute-start.1 = (f32[768,256]{1,0:T(8,128)}, f32[768,256]{1,0:T(8,128)S(1)}, u32[]{:S(2)}, u32[]{:S(2)}) collective-permute-start(f32[768,256]{1,0:T(8,128)} %get-tuple-element.41), channel_id=1, source_target_pairs={{0,1},{1,0},{2,3},{3,2},{4,5},{5,4},{6,7},{7,6},{8,9},{9,8},{10,11... | collective-permute-start | bytes 2359304 | tf_op jit(solution)/shard_map/ppermute | solution.py:334
  41.3 8.5 %collective-permute-start.2 = (f32[896,256]{1,0:T(8,128)}, f32[896,256]{1,0:T(8,128)S(1)}, u32[]{:S(2)}, u32[]{:S(2)}) collective-permute-start(f32[896,256]{1,0:T(8,128)} %get-tuple-element.43), channel_id=1, source_target_pairs={{0,1},{1,0},{2,3},{3,2},{4,5},{5,4},{6,7},{7,6},{8,9},{9,8},{10,11... | collective-permute-start | bytes 2752520 | tf_op jit(solution)/shard_map/ppermute | solution.py:334
  45.5 21.0 %all-to-all-start.1 = ((f32[4,192,256]{2,1,0:T(8,128)}), f32[4,192,256]{2,1,0:T(8,128)S(1)}, u32[]{:S(2)}, u32[]{:S(2)}) async-start(f32[4,192,256]{2,1,0:T(8,128)} %bitcast.5), calls=%async_computation.1 | async-start | bytes 1572864 | tf_op jit(solution)/shard_map/all_to_all | solution.py:307
  50.4 10.3 %collective-permute-start.3 = (f32[224,256]{1,0:T(8,128)S(1)}, f32[224,256]{1,0:T(8,128)S(1)}, u32[]{:S(2)}, u32[]{:S(2)}) collective-permute-start(f32[224,256]{1,0:T(8,128)S(1)} %get-tuple-element.47), channel_id=1, source_target_pairs={{0,64},{64,128},{128,192},{192,0},{1,65},{65,129},{129,193},{193,1... | collective-permute-start | bytes 688136 | tf_op jit(solution)/shard_map/ppermute | solution.py:326
  53.8 12.7 %collective-permute-start.4 = (f32[224,256]{1,0:T(8,128)S(1)}, f32[224,256]{1,0:T(8,128)S(1)}, u32[]{:S(2)}, u32[]{:S(2)}) collective-permute-start(f32[224,256]{1,0:T(8,128)S(1)} %get-tuple-element.48), channel_id=1, source_target_pairs={{0,128},{64,192},{128,0},{192,64},{1,129},{65,193},{129,1},{193,65... | collective-permute-start | bytes 688136 | tf_op jit(solution)/shard_map/ppermute | solution.py:326
  56.5 9.9 %collective-permute-start.5 = (f32[224,256]{1,0:T(8,128)S(1)}, f32[224,256]{1,0:T(8,128)S(1)}, u32[]{:S(2)}, u32[]{:S(2)}) collective-permute-start(f32[224,256]{1,0:T(8,128)S(1)} %get-tuple-element.49), channel_id=1, source_target_pairs={{0,192},{64,0},{128,64},{192,128},{1,193},{65,1},{129,65},{193,129... | collective-permute-start | bytes 688136 | tf_op jit(solution)/shard_map/ppermute | solution.py:326
  67.3 21.5 %copy-start.3 = (bf16[3,3,256,256]{3,2,1,0:T(8,128)(2,1)S(1)}, bf16[3,3,256,256]{3,2,1,0:T(8,128)(2,1)}, u32[]{:S(2)}) copy-start(bf16[3,3,256,256]{3,2,1,0:T(8,128)(2,1)} %weight_ref.1) | copy-start | bytes 3538948
  67.3 21.5 %copy-start.6 = (bf16[2,256,256]{2,1,0:T(8,128)(2,1)S(1)}, bf16[2,256,256]{2,1,0:T(8,128)(2,1)}, u32[]{:S(2)}) copy-start(bf16[2,256,256]{2,1,0:T(8,128)(2,1)} %get-tuple-element.59.grad_ref) | copy-start | bytes 786436
  68.7 5.7 %collective-permute-start.6 = (f32[224,256]{1,0:T(8,128)S(1)}, f32[224,256]{1,0:T(8,128)S(1)}, u32[]{:S(2)}, u32[]{:S(2)}) collective-permute-start(f32[224,256]{1,0:T(8,128)S(1)} %fusion.1), channel_id=1, source_target_pairs={{0,8},{8,0},{16,24},{24,16},{32,40},{40,32},{48,56},{56,48},{1,9},... | collective-permute-start | bytes 688136 | tf_op jit(solution)/shard_map/ppermute | solution.py:334
  74.4 6.5 %collective-permute-start.7 = (f32[56,256]{1,0:T(8,128)S(1)}, f32[56,256]{1,0:T(8,128)S(1)}, u32[]{:S(2)}, u32[]{:S(2)}) collective-permute-start(f32[56,256]{1,0:T(8,128)S(1)} %get-tuple-element.56), channel_id=1, source_target_pairs={{0,64},{2,66},{4,68},{6,70},{8,10},{10,12},{12,14},{14,8},{16,80},... | collective-permute-start | bytes 172040 | tf_op jit(solution)/shard_map/ppermute | solution.py:344
  76.4 5.5 %collective-permute-start.8 = (f32[56,256]{1,0:T(8,128)S(1)}, f32[56,256]{1,0:T(8,128)S(1)}, u32[]{:S(2)}, u32[]{:S(2)}) collective-permute-start(f32[56,256]{1,0:T(8,128)S(1)} %get-tuple-element.57), channel_id=1, source_target_pairs={{0,128},{2,130},{4,132},{6,134},{8,12},{10,14},{12,8},{14,10},{16,... | collective-permute-start | bytes 172040 | tf_op jit(solution)/shard_map/ppermute | solution.py:344
  79.6 3.8 %collective-permute-start.9 = (f32[56,256]{1,0:T(8,128)S(1)}, f32[56,256]{1,0:T(8,128)S(1)}, u32[]{:S(2)}, u32[]{:S(2)}) collective-permute-start(f32[56,256]{1,0:T(8,128)S(1)} %get-tuple-element.58), channel_id=1, source_target_pairs={{0,192},{2,194},{4,196},{6,198},{8,14},{10,8},{12,10},{14,12},{16,... | collective-permute-start | bytes 172040 | tf_op jit(solution)/shard_map/ppermute | solution.py:344
  79.6 9.1 %collective-permute-start.13 = (bf16[1,256,256]{2,1,0:T(8,128)(2,1)S(1)}, bf16[1,256,256]{2,1,0:T(8,128)(2,1)S(1)}, u32[]{:S(2)}, u32[]{:S(2)}) collective-permute-start(bf16[1,256,256]{2,1,0:T(8,128)(2,1)S(1)} %copy-done.11), channel_id=1, source_target_pairs={{8,0},{16,8},{24,16},{32,24},{40,32},{48,40},{56,48},{64,56},{72,6... | collective-permute-start | bytes 393224 | tf_op jit(solution)/shard_map/ppermute | solution.py:41
  83.4 7.2 %collective-permute-start.12 = (f32[56,256]{1,0:T(8,128)S(1)}, f32[56,256]{1,0:T(8,128)S(1)}, u32[]{:S(2)}, u32[]{:S(2)}) collective-permute-start(f32[56,256]{1,0:T(8,128)S(1)} %fusion.6), channel_id=1, source_target_pairs={{0,48},{8,56},{16,0},{24,8},{32,16},{40,24},{48,32},{56,40},{1,49}... | collective-permute-start | bytes 172040 | tf_op jit(solution)/shard_map/ppermute | solution.py:326
  85.4 6.9 %collective-permute-start.11 = (f32[56,256]{1,0:T(8,128)S(1)}, f32[56,256]{1,0:T(8,128)S(1)}, u32[]{:S(2)}, u32[]{:S(2)}) collective-permute-start(f32[56,256]{1,0:T(8,128)S(1)} %fusion.6), channel_id=1, source_target_pairs={{0,32},{8,40},{16,48},{24,56},{32,0},{40,8},{48,16},{56,24},{1,33}... | collective-permute-start | bytes 172040 | tf_op jit(solution)/shard_map/ppermute | solution.py:326
  86.5 6.1 %collective-permute-start.10 = (f32[56,256]{1,0:T(8,128)S(1)}, f32[56,256]{1,0:T(8,128)S(1)}, u32[]{:S(2)}, u32[]{:S(2)}) collective-permute-start(f32[56,256]{1,0:T(8,128)S(1)} %fusion.6), channel_id=1, source_target_pairs={{0,16},{8,24},{16,32},{24,40},{32,48},{40,56},{48,0},{56,8},{1,17}... | collective-permute-start | bytes 172040 | tf_op jit(solution)/shard_map/ppermute | solution.py:326
  92.6 5.5 %collective-permute-start.14 = (f32[56,256]{1,0:T(8,128)S(1)}, f32[56,256]{1,0:T(8,128)S(1)}, u32[]{:S(2)}, u32[]{:S(2)}) collective-permute-start(f32[56,256]{1,0:T(8,128)S(1)} %get-tuple-element.74), channel_id=1, source_target_pairs={{0,64},{2,66},{4,68},{6,70},{8,10},{10,12},{12,14},{14,8},{16,80},... | collective-permute-start | bytes 172040 | tf_op jit(solution)/shard_map/ppermute | solution.py:344
  94.1 5.8 %collective-permute-start.15 = (f32[56,256]{1,0:T(8,128)S(1)}, f32[56,256]{1,0:T(8,128)S(1)}, u32[]{:S(2)}, u32[]{:S(2)}) collective-permute-start(f32[56,256]{1,0:T(8,128)S(1)} %get-tuple-element.74), channel_id=1, source_target_pairs={{0,128},{2,130},{4,132},{6,134},{8,12},{10,14},{12,8},{14,10},{16,... | collective-permute-start | bytes 172040 | tf_op jit(solution)/shard_map/ppermute | solution.py:344
  97.7 3.0 %collective-permute-start.16 = (f32[56,256]{1,0:T(8,128)S(1)}, f32[56,256]{1,0:T(8,128)S(1)}, u32[]{:S(2)}, u32[]{:S(2)}) collective-permute-start(f32[56,256]{1,0:T(8,128)S(1)} %get-tuple-element.74), channel_id=1, source_target_pairs={{0,192},{2,194},{4,196},{6,198},{8,14},{10,8},{12,10},{14,12},{16,... | collective-permute-start | bytes 172040 | tf_op jit(solution)/shard_map/ppermute | solution.py:344
  100.7 4.9 %collective-permute-start.17 = (f32[224,256]{1,0:T(8,128)S(1)}, f32[224,256]{1,0:T(8,128)S(1)}, u32[]{:S(2)}, u32[]{:S(2)}) collective-permute-start(f32[224,256]{1,0:T(8,128)S(1)} %bitcast.47), channel_id=1, source_target_pairs={{0,8},{8,0},{16,24},{24,16},{32,40},{40,32},{48,56},{56,48},{1,9},... | collective-permute-start | bytes 688136 | tf_op jit(solution)/shard_map/ppermute | solution.py:334
  106.6 13.6 %all-to-all-start.2 = ((f32[4,192,256]{2,1,0:T(8,128)}), f32[4,192,256]{2,1,0:T(8,128)S(1)}, u32[]{:S(2)}, u32[]{:S(2)}) async-start(f32[4,192,256]{2,1,0:T(8,128)} %broadcast_in_dim.27), calls=%async_computation.2 | async-start | bytes 1572864 | tf_op jit(solution)/shard_map/all_to_all | solution.py:307
  110.1 4.9 %collective-permute-start.20 = (f32[224,256]{1,0:T(8,128)S(1)}, f32[224,256]{1,0:T(8,128)S(1)}, u32[]{:S(2)}, u32[]{:S(2)}) collective-permute-start(f32[224,256]{1,0:T(8,128)S(1)} %broadcast_select_fusion.refs_2_), channel_id=1, source_target_pairs={{0,192},{64,0},{128,64},{192,128},{1,193},{65,1},{129,65},{193,129... | collective-permute-start | bytes 688136 | tf_op jit(solution)/shard_map/ppermute | solution.py:326
  111.4 6.5 %collective-permute-start.19 = (f32[224,256]{1,0:T(8,128)S(1)}, f32[224,256]{1,0:T(8,128)S(1)}, u32[]{:S(2)}, u32[]{:S(2)}) collective-permute-start(f32[224,256]{1,0:T(8,128)S(1)} %broadcast_select_fusion.refs_2_), channel_id=1, source_target_pairs={{0,128},{64,192},{128,0},{192,64},{1,129},{65,193},{129,1},{193,65... | collective-permute-start | bytes 688136 | tf_op jit(solution)/shard_map/ppermute | solution.py:326
  111.9 8.3 %collective-permute-start.18 = (f32[224,256]{1,0:T(8,128)S(1)}, f32[224,256]{1,0:T(8,128)S(1)}, u32[]{:S(2)}, u32[]{:S(2)}) collective-permute-start(f32[224,256]{1,0:T(8,128)S(1)} %broadcast_select_fusion.refs_2_), channel_id=1, source_target_pairs={{0,64},{64,128},{128,192},{192,0},{1,65},{65,129},{129,193},{193,1... | collective-permute-start | bytes 688136 | tf_op jit(solution)/shard_map/ppermute | solution.py:326
  120.2 11.0 %collective-permute-start.21 = (f32[768,256]{1,0:T(8,128)S(1)}, f32[768,256]{1,0:T(8,128)S(1)}, u32[]{:S(2)}, u32[]{:S(2)}) collective-permute-start(f32[768,256]{1,0:T(8,128)S(1)} %bitcast.44), channel_id=1, source_target_pairs={{0,1},{1,0},{2,3},{3,2},{4,5},{5,4},{6,7},{7,6},{8,9},{9,8},{10,11... | collective-permute-start | bytes 2359304 | tf_op jit(solution)/shard_map/ppermute | solution.py:334
  128.0 2.2 %collective-permute-start.22 = (f32[224,256]{1,0:T(8,128)S(1)}, f32[224,256]{1,0:T(8,128)S(1)}, u32[]{:S(2)}, u32[]{:S(2)}) collective-permute-start(f32[224,256]{1,0:T(8,128)S(1)} %broadcast_select_fusion.refs_2_), channel_id=1, source_target_pairs={{0,1},{1,0},{2,3},{3,2},{4,5},{5,4},{6,7},{7,6},{8,9},{9,8},{10,11... | collective-permute-start | bytes 688136 | tf_op jit(solution)/shard_map/ppermute | solution.py:334
  128.0 2.6 %collective-permute-start.23 = (f32[224,256]{1,0:T(8,128)S(1)}, f32[224,256]{1,0:T(8,128)S(1)}, u32[]{:S(2)}, u32[]{:S(2)}) collective-permute-start(f32[224,256]{1,0:T(8,128)S(1)} %collective-permute-done.18.refs_3_), channel_id=1, source_target_pairs={{0,1},{1,0},{2,3},{3,2},{4,5},{5,4},{6,7},{7,6},{8,9},{9,8},{10,11... | collective-permute-start | bytes 688136 | tf_op jit(solution)/shard_map/ppermute | solution.py:334
  128.5 2.4 %collective-permute-start.24 = (f32[224,256]{1,0:T(8,128)S(1)}, f32[224,256]{1,0:T(8,128)S(1)}, u32[]{:S(2)}, u32[]{:S(2)}) collective-permute-start(f32[224,256]{1,0:T(8,128)S(1)} %collective-permute-done.19.refs_4_), channel_id=1, source_target_pairs={{0,1},{1,0},{2,3},{3,2},{4,5},{5,4},{6,7},{7,6},{8,9},{9,8},{10,11... | collective-permute-start | bytes 688136 | tf_op jit(solution)/shard_map/ppermute | solution.py:334
  128.5 2.7 %collective-permute-start.25 = (f32[224,256]{1,0:T(8,128)S(1)}, f32[224,256]{1,0:T(8,128)S(1)}, u32[]{:S(2)}, u32[]{:S(2)}) collective-permute-start(f32[224,256]{1,0:T(8,128)S(1)} %collective-permute-done.20.refs_5_), channel_id=1, source_target_pairs={{0,1},{1,0},{2,3},{3,2},{4,5},{5,4},{6,7},{7,6},{8,9},{9,8},{10,11... | collective-permute-start | bytes 688136 | tf_op jit(solution)/shard_map/ppermute | solution.py:334
  (9 other events, 28.7 us)

commit v9 on v8

--- a/solution.py
+++ b/solution.py
@@ -10,6 +10,8 @@
 
 TILES = 64
 LANES = 128
+INNER_TAPS = ((1, 0), (1, 1), (1, 2), (2, 0), (2, 1), (2, 2), (0, 0))
+OUTER_TAPS = ((0, 1), (0, 2))
 SIZES = {"x": 4, "z": 8, "y": 4, "core": 2}
 SPACE = ("x", "z")
 REP = ("y", "core")
@@ -171,17 +173,14 @@
     for n, (inner_hbm, outer_hbm) in enumerate(((other_inner, other_outer), (own_inner, own_outer))):
         owner = core_ref[0] if n else 1 - core_ref[0]
         start = pl.multiple_of(owner * LANES, LANES)
-        for col_tap in range(3):
-            for row_tap in (1, 2):
-                at = (3 * (row_tap - 1) + col_tap) * LANES
-                inner_ref[n, at : at + LANES, :] = half_taps(row_tap, col_tap, start)
+        for at, (row_tap, col_tap) in enumerate(INNER_TAPS):
+            inner_ref[n, at * LANES : (at + 1) * LANES, :] = half_taps(row_tap, col_tap, start)
         back.append(pltpu.make_async_copy(inner_ref.at[n], inner_hbm, sems.at[6 + 2 * n]))
         back[-1].start()
-        for col_tap in range(3):
-            at = col_tap * LANES
-            outer_ref[n, at : at + LANES, :] = half_taps(0, col_tap, start)
+        for at, (row_tap, col_tap) in enumerate(OUTER_TAPS):
+            outer_ref[n, at * LANES : (at + 1) * LANES, :] = half_taps(row_tap, col_tap, start)
         for k in range(weighted_ref.shape[1] // channels):
-            at = (3 + k) * LANES
+            at = (len(OUTER_TAPS) + k) * LANES
             outer_ref[n, at : at + LANES, :] = jnp.dot(
                 turned[pl.ds(start, LANES), :],
                 weighted_ref[:, k * channels : (k + 1) * channels],
@@ -195,8 +194,8 @@
 
 def terms(core, arrived, preact, above, blocks, weighted):
     rows, cols, channels = preact.shape
-    inner = jax.ShapeDtypeStruct((6 * LANES, channels), jnp.float32)
-    outer = jax.ShapeDtypeStruct((3 * LANES + weighted.shape[1] // 2, channels), jnp.float32)
+    inner = jax.ShapeDtypeStruct((len(INNER_TAPS) * LANES, channels), jnp.float32)
+    outer = jax.ShapeDtypeStruct((len(OUTER_TAPS) * LANES + weighted.shape[1] // 2, channels), jnp.float32)
     return pl.pallas_call(
         terms_kernel,
         out_shape=(
@@ -360,8 +359,8 @@
     inner = jnp.sum(inner, axis=0)
     outer = sum(moved, outer)
 
-    rows = outer.shape[0] - inner.shape[0]
-    both = jnp.stack([jnp.pad(inner, ((0, rows), (0, 0))), outer])
+    rows = inner.shape[0] - outer.shape[0]
+    both = jnp.stack([inner, jnp.pad(outer, ((0, rows), (0, 0)))])
     bit = place("z") & jnp.uint32(1)
     part = pick(both, bit) + swapped(pick(both, jnp.uint32(1) - bit), "z", 1)
 
@@ -380,9 +379,8 @@
         whole_part = put(whole_part, turned(part, by) if by else part, turned_place(-by))
     part = whole_part.reshape(-1, part.shape[1])
     got = swapped(part, "z", 1)
-    inner = jnp.where(bit == 0, part, got)[: part.shape[0] - rows]
-    outer = jnp.where(bit == 0, got, part)
-    inner, outer = barrier((inner, outer))
+    inner = jnp.where(bit == 0, part, got)
+    outer = jnp.where(bit == 0, got, part)[: part.shape[0] - rows]
     copies = barrier(jnp.broadcast_to(inner, (4,) + inner.shape))
     copies, moved = barrier((exchange(copies, "y"), [rotated(outer, "x", by) for by in STEPS]))
     return [copies.reshape(-1, part.shape[1])], [outer] + moved, beside
@@ -397,16 +395,16 @@
         at = pl.multiple_of(((where_ref[1] + 4 - by) & 3) * rows, 8)
         joined[core, pl.ds(at, rows), :] = pieces[by][...]
         joined[1 - core, pl.ds(at, rows), :] = pieces[4 + by][...]
-    for tap in range(6):
-        rows = slice(tap * LANES, (tap + 1) * LANES)
-        conv_ref[3 + tap, pl.ds(pl.multiple_of(core * LANES, LANES), LANES), :] = inner[0][rows, :]
-        conv_ref[3 + tap, pl.ds(pl.multiple_of((1 - core) * LANES, LANES), LANES), :] = inner[1][rows, :]
+    for at, (row_tap, col_tap) in enumerate(INNER_TAPS):
+        rows, tap = slice(at * LANES, (at + 1) * LANES), 3 * row_tap + col_tap
+        conv_ref[tap, pl.ds(pl.multiple_of(core * LANES, LANES), LANES), :] = inner[0][rows, :]
+        conv_ref[tap, pl.ds(pl.multiple_of((1 - core) * LANES, LANES), LANES), :] = inner[1][rows, :]
     for half in range(2):
         lanes = slice(half * LANES, (half + 1) * LANES)
-        for tap in range(3):
-            conv_ref[tap, lanes, :] = joined[half, tap * LANES : (tap + 1) * LANES, :]
+        for at, (row_tap, col_tap) in enumerate(OUTER_TAPS):
+            conv_ref[3 * row_tap + col_tap, lanes, :] = joined[half, at * LANES : (at + 1) * LANES, :]
         for n in range(expand_ref.shape[1] // channels):
-            at = (3 + n) * LANES
+            at = (len(OUTER_TAPS) + n) * LANES
             expand_ref[lanes, n * channels : (n + 1) * channels] = joined[half, at : at + LANES, :]
 
 

time: 134 us -> 131 us (0.978)
  waiting for transfers between devices: 49.8 us -> 47.7 us
    ppermute x9, waiting for transfers between devices: 18.6 us -> 16.9 us  [rotated(): return lax.ppermute(x, axis, [(i, (i + by) % size) for i in range(size)])]
    another operation x1 -> x0, other arithmetic: 1.35 us -> none  [total_sums(): both = jnp.stack([jnp.pad(inner, ((0, rows), (0, 0))), outer])]
    unnamed x24 -> x18, local copies, waits for them, and re-layouts: 4.53 us -> 3.88 us
where the time goes in v9:
time: 131 us; the launch traced here: 130 us
  starting transfers between devices  61.4 us (47%)
  waiting for transfers between devices  47.7 us (36%)
  Pallas kernels  14.3 us (11%)
  local copies, waits for them, and re-layouts  4.97 us (4%)
  between operations  1.65 us (1%)
    all_to_all x3, starting transfers between devices, exchange(): return lax.all_to_all(x, axis, split_axis=0, concat_axis=0, tiled=True)  19.7 us
    ppermute x9, waiting for transfers between devices, rotated(): return lax.ppermute(x, axis, [(i, (i + by) % size) for i in range(size)])  16.9 us
    ppermute x9, waiting for transfers between devices, swapped(): return lax.ppermute(x, axis, [(i, i ^ bit) for i in range(SIZES[axis])])  15.1 us
    ppermute x9, starting transfers between devices, rotated(): return lax.ppermute(x, axis, [(i, (i + by) % size) for i in range(size)])  14.6 us
    ppermute x9, starting transfers between devices, swapped(): return lax.ppermute(x, axis, [(i, i ^ bit) for i in range(SIZES[axis])])  12.9 us
    ppermute x2, waiting for transfers between devices, shifted(): return lax.ppermute(x, SPACE, pairs)  11.1 us
    ppermute x6, starting transfers between devices, turned(): return lax.ppermute(x, ('x', 'z', 'y'), pairs)  9.76 us
    ppermute x6, waiting for transfers between devices, turned(): return lax.ppermute(x, ('x', 'z', 'y'), pairs)  4.48 us
  transfers between devices with their start and end apart: 29, of which 20 were waited for; matrix products, arithmetic and copies ran while one was open for 0% of the time, Pallas kernels for 3%

profile of v9, /device:TPU:1, one launch (start us, length us, event | category | flops | bytes accessed | tf_op | source)
XLA Modules:
  0.0 130.3 jit_solution(8928447422153095667)
XLA Ops:
  1.4 2.9 %build_sent.1 = (bf16[32,32,256]{2,1,0:T(8,128)(2,1)}, bf16[512,1024]{1,0:T(8,128)(2,1)}) custom-call(f32[1]{0:T(128)S(6)} %div.3.share_ref, bf16[512,1024]{1,0:T(8,128)(2,1)} %bitcast.50, bf16[256,1024]{1,0:T(8,128)(2,1)} %weight_hbm.1, bf16[2,256,256]{2,1,0:T(8,128)(2,1)} %bitcast.52), custom_call_target="tpu_custom_call" | custom-call | flops 268000000 | bytes 4000000 | tf_op jit(solution)/shard_map/build_sent/pallas_call | solution.py:81
  4.3 11.9 %all-to-all-start = ((bf16[32,32,256]{2,1,0:T(8,128)(2,1)}), bf16[32,32,256]{2,1,0:T(8,128)(2,1)S(1)}, u32[]{:S(2)}, u32[]{:S(2)}) async-start(bf16[32,32,256]{2,1,0:T(8,128)(2,1)} %get-tuple-element.36), calls=%async_computation | async-start | bytes 1048576 | tf_op jit(solution)/shard_map/all_to_all | solution.py:306
  16.3 3.1 %collective-permute-start = (bf16[1,512,256]{2,1,0:T(8,128)(2,1)S(1)}, bf16[1,512,256]{2,1,0:T(8,128)(2,1)S(1)}, u32[]{:S(2)}, u32[]{:S(2)}) collective-permute-start(bf16[1,512,256]{2,1,0:T(8,128)(2,1)S(1)} %slice_bitcast_fusion), channel_id=1, source_target_pairs={{0,8},{8,16},{16,24},{24,32},{32,40},{40,48},{48,56},{56,64},{64,7... | collective-permute-start | bytes 786440 | tf_op jit(solution)/shard_map/ppermute | solution.py:43
  21.1 11.1 %collective-permute-done.x_ref = bf16[1,512,256]{2,1,0:T(8,128)(2,1)S(1)} collective-permute-done((bf16[1,512,256]{2,1,0:T(8,128)(2,1)S(1)}, bf16[1,512,256]{2,1,0:T(8,128)(2,1)S(1)}, u32[]{:S(2)}, u32[]{:S(2)}) %collective-permute-start) | collective-permute-done | bytes 262176 | tf_op jit(solution)/shard_map/ppermute | solution.py:43
  34.1 4.4 %terms.1 = (f32[896,256]{1,0:T(8,128)}, f32[896,256]{1,0:T(8,128)}, f32[768,256]{1,0:T(8,128)}, f32[768,256]{1,0:T(8,128)}, bf16[2,256,256]{2,1,0:T(8,128)(2,1)}, /*index=5*/bf16[1,256,256]{2,1,0:T(8,128)(2,1)}) custom-call(s32[1]{0:T(128)} %bitcast.core_ref, bf16[32,32,256]{2,1,0:T(8,128)(2,1)} %copy-done.7, bf16[2,256,256]{2,1,0:T(8,128)(2,1)} %bitcast.53, ...), custom_call_target="tpu_custom_call" | custom-call | flops 870000000 | bytes 8000000 | tf_op jit(solution)/shard_map/terms/pallas_call | solution.py:199
  38.4 2.9 %collective-permute-start.1 = (f32[896,256]{1,0:T(8,128)}, f32[896,256]{1,0:T(8,128)S(1)}, u32[]{:S(2)}, u32[]{:S(2)}) collective-permute-start(f32[896,256]{1,0:T(8,128)} %get-tuple-element.39), channel_id=1, source_target_pairs={{0,1},{1,0},{2,3},{3,2},{4,5},{5,4},{6,7},{7,6},{8,9},{9,8},{10,11... | collective-permute-start | bytes 2752520 | tf_op jit(solution)/shard_map/ppermute | solution.py:333
  41.4 2.2 %collective-permute-done.1.got = f32[896,256]{1,0:T(8,128)S(1)} collective-permute-done((f32[896,256]{1,0:T(8,128)}, f32[896,256]{1,0:T(8,128)S(1)}, u32[]{:S(2)}, u32[]{:S(2)}) %collective-permute-start.1) | collective-permute-done | bytes 917536 | tf_op jit(solution)/shard_map/ppermute | solution.py:333
  45.8 4.3 %all-to-all-start.1 = ((f32[4,224,256]{2,1,0:T(8,128)}), f32[4,224,256]{2,1,0:T(8,128)S(1)}, u32[]{:S(2)}, u32[]{:S(2)}) async-start(f32[4,224,256]{2,1,0:T(8,128)} %bitcast.5), calls=%async_computation.1 | async-start | bytes 1835008 | tf_op jit(solution)/shard_map/all_to_all | solution.py:306
  50.9 3.4 %collective-permute-start.3 = (f32[192,256]{1,0:T(8,128)S(1)}, f32[192,256]{1,0:T(8,128)S(1)}, u32[]{:S(2)}, u32[]{:S(2)}) collective-permute-start(f32[192,256]{1,0:T(8,128)S(1)} %get-tuple-element.45), channel_id=1, source_target_pairs={{0,64},{64,128},{128,192},{192,0},{1,65},{65,129},{129,193},{193,1... | collective-permute-start | bytes 589832 | tf_op jit(solution)/shard_map/ppermute | solution.py:325
  54.3 2.7 %collective-permute-start.4 = (f32[192,256]{1,0:T(8,128)S(1)}, f32[192,256]{1,0:T(8,128)S(1)}, u32[]{:S(2)}, u32[]{:S(2)}) collective-permute-start(f32[192,256]{1,0:T(8,128)S(1)} %get-tuple-element.46), channel_id=1, source_target_pairs={{0,128},{64,192},{128,0},{192,64},{1,129},{65,193},{129,1},{193,65... | collective-permute-start | bytes 589832 | tf_op jit(solution)/shard_map/ppermute | solution.py:325
  57.9 2.6 %collective-permute-done.3 = f32[192,256]{1,0:T(8,128)S(1)} collective-permute-done((f32[192,256]{1,0:T(8,128)S(1)}, f32[192,256]{1,0:T(8,128)S(1)}, u32[]{:S(2)}, u32[]{:S(2)}) %collective-permute-start.3) | collective-permute-done | bytes 196640 | tf_op jit(solution)/shard_map/ppermute | solution.py:325
  60.5 5.1 %collective-permute-done.4 = f32[192,256]{1,0:T(8,128)S(1)} collective-permute-done((f32[192,256]{1,0:T(8,128)S(1)}, f32[192,256]{1,0:T(8,128)S(1)}, u32[]{:S(2)}, u32[]{:S(2)}) %collective-permute-start.4) | collective-permute-done | bytes 196640 | tf_op jit(solution)/shard_map/ppermute | solution.py:325
  66.0 5.5 %collective-permute-done.6 = f32[224,256]{1,0:T(8,128)S(1)} collective-permute-done((f32[224,256]{1,0:T(8,128)S(1)}, f32[224,256]{1,0:T(8,128)S(1)}, u32[]{:S(2)}, u32[]{:S(2)}) %collective-permute-start.6) | collective-permute-done | bytes 229408 | tf_op jit(solution)/shard_map/ppermute | solution.py:333
  71.6 1.9 %collective-permute-start.7 = (f32[56,256]{1,0:T(8,128)S(1)}, f32[56,256]{1,0:T(8,128)S(1)}, u32[]{:S(2)}, u32[]{:S(2)}) collective-permute-start(f32[56,256]{1,0:T(8,128)S(1)} %get-tuple-element.54), channel_id=1, source_target_pairs={{0,64},{2,66},{4,68},{6,70},{8,10},{10,12},{12,14},{14,8},{16,80},... | collective-permute-start | bytes 172040 | tf_op jit(solution)/shard_map/ppermute | solution.py:343
  73.5 2.5 %collective-permute-start.8 = (f32[56,256]{1,0:T(8,128)S(1)}, f32[56,256]{1,0:T(8,128)S(1)}, u32[]{:S(2)}, u32[]{:S(2)}) collective-permute-start(f32[56,256]{1,0:T(8,128)S(1)} %get-tuple-element.55), channel_id=1, source_target_pairs={{0,128},{2,130},{4,132},{6,134},{8,12},{10,14},{12,8},{14,10},{16,... | collective-permute-start | bytes 172040 | tf_op jit(solution)/shard_map/ppermute | solution.py:343
  76.3 1.3 collective-permute-start.13
  79.1 1.9 %collective-permute-start.12 = (f32[56,256]{1,0:T(8,128)S(1)}, f32[56,256]{1,0:T(8,128)S(1)}, u32[]{:S(2)}, u32[]{:S(2)}) collective-permute-start(f32[56,256]{1,0:T(8,128)S(1)} %fusion.6), channel_id=1, source_target_pairs={{0,48},{8,56},{16,0},{24,8},{32,16},{40,24},{48,32},{56,40},{1,49}... | collective-permute-start | bytes 172040 | tf_op jit(solution)/shard_map/ppermute | solution.py:325
  81.1 1.8 %collective-permute-start.11 = (f32[56,256]{1,0:T(8,128)S(1)}, f32[56,256]{1,0:T(8,128)S(1)}, u32[]{:S(2)}, u32[]{:S(2)}) collective-permute-start(f32[56,256]{1,0:T(8,128)S(1)} %fusion.6), channel_id=1, source_target_pairs={{0,32},{8,40},{16,48},{24,56},{32,0},{40,8},{48,16},{56,24},{1,33}... | collective-permute-start | bytes 172040 | tf_op jit(solution)/shard_map/ppermute | solution.py:325
  82.8 1.3 %collective-permute-start.10 = (f32[56,256]{1,0:T(8,128)S(1)}, f32[56,256]{1,0:T(8,128)S(1)}, u32[]{:S(2)}, u32[]{:S(2)}) collective-permute-start(f32[56,256]{1,0:T(8,128)S(1)} %fusion.6), channel_id=1, source_target_pairs={{0,16},{8,24},{16,32},{24,40},{32,48},{40,56},{48,0},{56,8},{1,17}... | collective-permute-start | bytes 172040 | tf_op jit(solution)/shard_map/ppermute | solution.py:325
  84.2 1.9 %input_grad.1 = bf16[4,512,256]{2,1,0:T(8,128)(2,1)} custom-call(bf16[2,256,256]{2,1,0:T(8,128)(2,1)S(1)} %copy-done.6, bf16[1,256,256]{2,1,0:T(8,128)(2,1)S(1)} %collective-permute-done.13.below_ref, bf16[3,3,256,256]{3,2,1,0:T(8,128)(2,1)S(1)} %copy-done.3), custom_call_target="tpu_custom_call" | custom-call | flops 604000000 | bytes 3000000 | tf_op jit(solution)/shard_map/input_grad/pallas_call | solution.py:293
  86.1 2.1 %collective-permute-done.11 = f32[56,256]{1,0:T(8,128)S(1)} collective-permute-done((f32[56,256]{1,0:T(8,128)S(1)}, f32[56,256]{1,0:T(8,128)S(1)}, u32[]{:S(2)}, u32[]{:S(2)}) %collective-permute-start.11) | collective-permute-done | bytes 57376 | tf_op jit(solution)/shard_map/ppermute | solution.py:325
  88.8 2.6 %collective-permute-start.14 = (f32[56,256]{1,0:T(8,128)S(1)}, f32[56,256]{1,0:T(8,128)S(1)}, u32[]{:S(2)}, u32[]{:S(2)}) collective-permute-start(f32[56,256]{1,0:T(8,128)S(1)} %get-tuple-element.70), channel_id=1, source_target_pairs={{0,64},{2,66},{4,68},{6,70},{8,10},{10,12},{12,14},{14,8},{16,80},... | collective-permute-start | bytes 172040 | tf_op jit(solution)/shard_map/ppermute | solution.py:343
  91.3 2.4 %collective-permute-start.15 = (f32[56,256]{1,0:T(8,128)S(1)}, f32[56,256]{1,0:T(8,128)S(1)}, u32[]{:S(2)}, u32[]{:S(2)}) collective-permute-start(f32[56,256]{1,0:T(8,128)S(1)} %get-tuple-element.70), channel_id=1, source_target_pairs={{0,128},{2,130},{4,132},{6,134},{8,12},{10,14},{12,8},{14,10},{16,... | collective-permute-start | bytes 172040 | tf_op jit(solution)/shard_map/ppermute | solution.py:343
  94.1 1.8 %collective-permute-done.15 = f32[56,256]{1,0:T(8,128)S(1)} collective-permute-done((f32[56,256]{1,0:T(8,128)S(1)}, f32[56,256]{1,0:T(8,128)S(1)}, u32[]{:S(2)}, u32[]{:S(2)}) %collective-permute-start.15) | collective-permute-done | bytes 57376 | tf_op jit(solution)/shard_map/ppermute | solution.py:343
  96.8 5.2 %collective-permute-done.17 = f32[224,256]{1,0:T(8,128)S(1)} collective-permute-done((f32[224,256]{1,0:T(8,128)S(1)}, f32[224,256]{1,0:T(8,128)S(1)}, u32[]{:S(2)}, u32[]{:S(2)}) %collective-permute-start.17) | collective-permute-done | bytes 229408 | tf_op jit(solution)/shard_map/ppermute | solution.py:333
  103.0 3.5 %all-to-all-start.2 = ((f32[4,224,256]{2,1,0:T(8,128)}), f32[4,224,256]{2,1,0:T(8,128)S(1)}, u32[]{:S(2)}, u32[]{:S(2)}) async-start(f32[4,224,256]{2,1,0:T(8,128)} %broadcast_in_dim.27), calls=%async_computation.2 | async-start | bytes 1835008 | tf_op jit(solution)/shard_map/all_to_all | solution.py:306
  109.1 2.0 %collective-permute-done.20.refs_5_ = f32[192,256]{1,0:T(8,128)S(1)} collective-permute-done((f32[192,256]{1,0:T(8,128)S(1)}, f32[192,256]{1,0:T(8,128)S(1)}, u32[]{:S(2)}, u32[]{:S(2)}) %collective-permute-start.20) | collective-permute-done | bytes 196640 | tf_op jit(solution)/shard_map/ppermute | solution.py:325
  111.1 2.6 %collective-permute-done.19.refs_4_ = f32[192,256]{1,0:T(8,128)S(1)} collective-permute-done((f32[192,256]{1,0:T(8,128)S(1)}, f32[192,256]{1,0:T(8,128)S(1)}, u32[]{:S(2)}, u32[]{:S(2)}) %collective-permute-start.19) | collective-permute-done | bytes 196640 | tf_op jit(solution)/shard_map/ppermute | solution.py:325
  113.7 2.0 %collective-permute-done.18.refs_3_ = f32[192,256]{1,0:T(8,128)S(1)} collective-permute-done((f32[192,256]{1,0:T(8,128)S(1)}, f32[192,256]{1,0:T(8,128)S(1)}, u32[]{:S(2)}, u32[]{:S(2)}) %collective-permute-start.18) | collective-permute-done | bytes 196640 | tf_op jit(solution)/shard_map/ppermute | solution.py:325
  115.7 8.8 %collective-permute-start.21 = (f32[896,256]{1,0:T(8,128)S(1)}, f32[896,256]{1,0:T(8,128)S(1)}, u32[]{:S(2)}, u32[]{:S(2)}) collective-permute-start(f32[896,256]{1,0:T(8,128)S(1)} %bitcast.43), channel_id=1, source_target_pairs={{0,1},{1,0},{2,3},{3,2},{4,5},{5,4},{6,7},{7,6},{8,9},{9,8},{10,11... | collective-permute-start | bytes 2752520 | tf_op jit(solution)/shard_map/ppermute | solution.py:333
  125.6 1.4 %collective-permute-done.22.refs_6_ = f32[192,256]{1,0:T(8,128)S(1)} collective-permute-done((f32[192,256]{1,0:T(8,128)S(1)}, f32[192,256]{1,0:T(8,128)S(1)}, u32[]{:S(2)}, u32[]{:S(2)}) %collective-permute-start.22) | collective-permute-done | bytes 196640 | tf_op jit(solution)/shard_map/ppermute | solution.py:333
  127.8 2.6 %assemble.1 = (f32[9,256,256]{2,1,0:T(8,128)}, f32[256,1024]{1,0:T(8,128)}) custom-call(s32[2]{0:T(128)S(1)} %pad_add_fusion.where_ref, f32[896,256]{1,0:T(8,128)S(1)} %bitcast.44, f32[896,256]{1,0:T(8,128)S(1)} %collective-permute-done.21.refs_1_, f32[192,256]{1,0:T(8,128)S(1)} %slice_select_fusion.refs_2_, f32[192,256]{1,0:T(8,128)S(1)} %collective-permute-done.18.refs_3_, ...), custom_call_target="tpu_custom_call" | custom-call | bytes 7000000 | tf_op jit(solution)/shard_map/assemble/pallas_call | solution.py:413
  (69 shorter events, 16.8 us)
Async XLA Ops:
  0.6 15.6 %copy-start.1 = (bf16[1,4,512,256]{3,2,1,0:T(8,128)(2,1)S(1)}, bf16[1,4,512,256]{3,2,1,0:T(8,128)(2,1)}, u32[]{:S(2)}) copy-start(bf16[1,4,512,256]{3,2,1,0:T(8,128)(2,1)} %param.6) | copy-start | bytes 3145732
  4.3 28.9 %all-to-all-start = ((bf16[32,32,256]{2,1,0:T(8,128)(2,1)}), bf16[32,32,256]{2,1,0:T(8,128)(2,1)S(1)}, u32[]{:S(2)}, u32[]{:S(2)}) async-start(bf16[32,32,256]{2,1,0:T(8,128)(2,1)} %get-tuple-element.36), calls=%async_computation | async-start | bytes 1048576 | tf_op jit(solution)/shard_map/all_to_all | solution.py:306
  16.3 16.0 %collective-permute-start = (bf16[1,512,256]{2,1,0:T(8,128)(2,1)S(1)}, bf16[1,512,256]{2,1,0:T(8,128)(2,1)S(1)}, u32[]{:S(2)}, u32[]{:S(2)}) collective-permute-start(bf16[1,512,256]{2,1,0:T(8,128)(2,1)S(1)} %slice_bitcast_fusion), channel_id=1, source_target_pairs={{0,8},{8,16},{16,24},{24,32},{32,40},{40,48},{48,56},{56,64},{64,7... | collective-permute-start | bytes 786440 | tf_op jit(solution)/shard_map/ppermute | solution.py:43
  38.4 5.2 %collective-permute-start.1 = (f32[896,256]{1,0:T(8,128)}, f32[896,256]{1,0:T(8,128)S(1)}, u32[]{:S(2)}, u32[]{:S(2)}) collective-permute-start(f32[896,256]{1,0:T(8,128)} %get-tuple-element.39), channel_id=1, source_target_pairs={{0,1},{1,0},{2,3},{3,2},{4,5},{5,4},{6,7},{7,6},{8,9},{9,8},{10,11... | collective-permute-start | bytes 2752520 | tf_op jit(solution)/shard_map/ppermute | solution.py:333
  41.3 8.9 %collective-permute-start.2 = (f32[768,256]{1,0:T(8,128)}, f32[768,256]{1,0:T(8,128)S(1)}, u32[]{:S(2)}, u32[]{:S(2)}) collective-permute-start(f32[768,256]{1,0:T(8,128)} %get-tuple-element.41), channel_id=1, source_target_pairs={{0,1},{1,0},{2,3},{3,2},{4,5},{5,4},{6,7},{7,6},{8,9},{9,8},{10,11... | collective-permute-start | bytes 2359304 | tf_op jit(solution)/shard_map/ppermute | solution.py:333
  45.8 19.7 %all-to-all-start.1 = ((f32[4,224,256]{2,1,0:T(8,128)}), f32[4,224,256]{2,1,0:T(8,128)S(1)}, u32[]{:S(2)}, u32[]{:S(2)}) async-start(f32[4,224,256]{2,1,0:T(8,128)} %bitcast.5), calls=%async_computation.1 | async-start | bytes 1835008 | tf_op jit(solution)/shard_map/all_to_all | solution.py:306
  50.9 9.6 %collective-permute-start.3 = (f32[192,256]{1,0:T(8,128)S(1)}, f32[192,256]{1,0:T(8,128)S(1)}, u32[]{:S(2)}, u32[]{:S(2)}) collective-permute-start(f32[192,256]{1,0:T(8,128)S(1)} %get-tuple-element.45), channel_id=1, source_target_pairs={{0,64},{64,128},{128,192},{192,0},{1,65},{65,129},{129,193},{193,1... | collective-permute-start | bytes 589832 | tf_op jit(solution)/shard_map/ppermute | solution.py:325
  54.3 11.3 %collective-permute-start.4 = (f32[192,256]{1,0:T(8,128)S(1)}, f32[192,256]{1,0:T(8,128)S(1)}, u32[]{:S(2)}, u32[]{:S(2)}) collective-permute-start(f32[192,256]{1,0:T(8,128)S(1)} %get-tuple-element.46), channel_id=1, source_target_pairs={{0,128},{64,192},{128,0},{192,64},{1,129},{65,193},{129,1},{193,65... | collective-permute-start | bytes 589832 | tf_op jit(solution)/shard_map/ppermute | solution.py:325
  57.0 8.5 %collective-permute-start.5 = (f32[192,256]{1,0:T(8,128)S(1)}, f32[192,256]{1,0:T(8,128)S(1)}, u32[]{:S(2)}, u32[]{:S(2)}) collective-permute-start(f32[192,256]{1,0:T(8,128)S(1)} %get-tuple-element.47), channel_id=1, source_target_pairs={{0,192},{64,0},{128,64},{192,128},{1,193},{65,1},{129,65},{193,129... | collective-permute-start | bytes 589832 | tf_op jit(solution)/shard_map/ppermute | solution.py:325
  65.7 18.5 %copy-start.3 = (bf16[3,3,256,256]{3,2,1,0:T(8,128)(2,1)S(1)}, bf16[3,3,256,256]{3,2,1,0:T(8,128)(2,1)}, u32[]{:S(2)}) copy-start(bf16[3,3,256,256]{3,2,1,0:T(8,128)(2,1)} %weight_ref.1) | copy-start | bytes 3538948
  65.7 18.5 %copy-start.6 = (bf16[2,256,256]{2,1,0:T(8,128)(2,1)S(1)}, bf16[2,256,256]{2,1,0:T(8,128)(2,1)}, u32[]{:S(2)}) copy-start(bf16[2,256,256]{2,1,0:T(8,128)(2,1)} %get-tuple-element.57.grad_ref) | copy-start | bytes 786436
  65.8 5.7 %collective-permute-start.6 = (f32[224,256]{1,0:T(8,128)S(1)}, f32[224,256]{1,0:T(8,128)S(1)}, u32[]{:S(2)}, u32[]{:S(2)}) collective-permute-start(f32[224,256]{1,0:T(8,128)S(1)} %fusion.1), channel_id=1, source_target_pairs={{0,8},{8,0},{16,24},{24,16},{32,40},{40,32},{48,56},{56,48},{1,9},... | collective-permute-start | bytes 688136 | tf_op jit(solution)/shard_map/ppermute | solution.py:333
  71.6 6.0 %collective-permute-start.7 = (f32[56,256]{1,0:T(8,128)S(1)}, f32[56,256]{1,0:T(8,128)S(1)}, u32[]{:S(2)}, u32[]{:S(2)}) collective-permute-start(f32[56,256]{1,0:T(8,128)S(1)} %get-tuple-element.54), channel_id=1, source_target_pairs={{0,64},{2,66},{4,68},{6,70},{8,10},{10,12},{12,14},{14,8},{16,80},... | collective-permute-start | bytes 172040 | tf_op jit(solution)/shard_map/ppermute | solution.py:343
  73.5 4.7 %collective-permute-start.8 = (f32[56,256]{1,0:T(8,128)S(1)}, f32[56,256]{1,0:T(8,128)S(1)}, u32[]{:S(2)}, u32[]{:S(2)}) collective-permute-start(f32[56,256]{1,0:T(8,128)S(1)} %get-tuple-element.55), channel_id=1, source_target_pairs={{0,128},{2,130},{4,132},{6,134},{8,12},{10,14},{12,8},{14,10},{16,... | collective-permute-start | bytes 172040 | tf_op jit(solution)/shard_map/ppermute | solution.py:343
  76.0 3.1 %collective-permute-start.9 = (f32[56,256]{1,0:T(8,128)S(1)}, f32[56,256]{1,0:T(8,128)S(1)}, u32[]{:S(2)}, u32[]{:S(2)}) collective-permute-start(f32[56,256]{1,0:T(8,128)S(1)} %get-tuple-element.56), channel_id=1, source_target_pairs={{0,192},{2,194},{4,196},{6,198},{8,14},{10,8},{12,10},{14,12},{16,... | collective-permute-start | bytes 172040 | tf_op jit(solution)/shard_map/ppermute | solution.py:343
  76.3 7.9 %collective-permute-start.13 = (bf16[1,256,256]{2,1,0:T(8,128)(2,1)S(1)}, bf16[1,256,256]{2,1,0:T(8,128)(2,1)S(1)}, u32[]{:S(2)}, u32[]{:S(2)}) collective-permute-start(bf16[1,256,256]{2,1,0:T(8,128)(2,1)S(1)} %copy-done.8), channel_id=1, source_target_pairs={{8,0},{16,8},{24,16},{32,24},{40,32},{48,40},{56,48},{64,56},{72,6... | collective-permute-start | bytes 393224 | tf_op jit(solution)/shard_map/ppermute | solution.py:43
  79.1 7.0 %collective-permute-start.12 = (f32[56,256]{1,0:T(8,128)S(1)}, f32[56,256]{1,0:T(8,128)S(1)}, u32[]{:S(2)}, u32[]{:S(2)}) collective-permute-start(f32[56,256]{1,0:T(8,128)S(1)} %fusion.6), channel_id=1, source_target_pairs={{0,48},{8,56},{16,0},{24,8},{32,16},{40,24},{48,32},{56,40},{1,49}... | collective-permute-start | bytes 172040 | tf_op jit(solution)/shard_map/ppermute | solution.py:325
  81.1 7.1 %collective-permute-start.11 = (f32[56,256]{1,0:T(8,128)S(1)}, f32[56,256]{1,0:T(8,128)S(1)}, u32[]{:S(2)}, u32[]{:S(2)}) collective-permute-start(f32[56,256]{1,0:T(8,128)S(1)} %fusion.6), channel_id=1, source_target_pairs={{0,32},{8,40},{16,48},{24,56},{32,0},{40,8},{48,16},{56,24},{1,33}... | collective-permute-start | bytes 172040 | tf_op jit(solution)/shard_map/ppermute | solution.py:325
  82.8 5.9 %collective-permute-start.10 = (f32[56,256]{1,0:T(8,128)S(1)}, f32[56,256]{1,0:T(8,128)S(1)}, u32[]{:S(2)}, u32[]{:S(2)}) collective-permute-start(f32[56,256]{1,0:T(8,128)S(1)} %fusion.6), channel_id=1, source_target_pairs={{0,16},{8,24},{16,32},{24,40},{32,48},{40,56},{48,0},{56,8},{1,17}... | collective-permute-start | bytes 172040 | tf_op jit(solution)/shard_map/ppermute | solution.py:325
  88.8 5.4 %collective-permute-start.14 = (f32[56,256]{1,0:T(8,128)S(1)}, f32[56,256]{1,0:T(8,128)S(1)}, u32[]{:S(2)}, u32[]{:S(2)}) collective-permute-start(f32[56,256]{1,0:T(8,128)S(1)} %get-tuple-element.70), channel_id=1, source_target_pairs={{0,64},{2,66},{4,68},{6,70},{8,10},{10,12},{12,14},{14,8},{16,80},... | collective-permute-start | bytes 172040 | tf_op jit(solution)/shard_map/ppermute | solution.py:343
  91.3 4.6 %collective-permute-start.15 = (f32[56,256]{1,0:T(8,128)S(1)}, f32[56,256]{1,0:T(8,128)S(1)}, u32[]{:S(2)}, u32[]{:S(2)}) collective-permute-start(f32[56,256]{1,0:T(8,128)S(1)} %get-tuple-element.70), channel_id=1, source_target_pairs={{0,128},{2,130},{4,132},{6,134},{8,12},{10,14},{12,8},{14,10},{16,... | collective-permute-start | bytes 172040 | tf_op jit(solution)/shard_map/ppermute | solution.py:343
  93.8 3.0 %collective-permute-start.16 = (f32[56,256]{1,0:T(8,128)S(1)}, f32[56,256]{1,0:T(8,128)S(1)}, u32[]{:S(2)}, u32[]{:S(2)}) collective-permute-start(f32[56,256]{1,0:T(8,128)S(1)} %get-tuple-element.70), channel_id=1, source_target_pairs={{0,192},{2,194},{4,196},{6,198},{8,14},{10,8},{12,10},{14,12},{16,... | collective-permute-start | bytes 172040 | tf_op jit(solution)/shard_map/ppermute | solution.py:343
  96.8 5.2 %collective-permute-start.17 = (f32[224,256]{1,0:T(8,128)S(1)}, f32[224,256]{1,0:T(8,128)S(1)}, u32[]{:S(2)}, u32[]{:S(2)}) collective-permute-start(f32[224,256]{1,0:T(8,128)S(1)} %bitcast.48), channel_id=1, source_target_pairs={{0,8},{8,0},{16,24},{24,16},{32,40},{40,32},{48,56},{56,48},{1,9},... | collective-permute-start | bytes 688136 | tf_op jit(solution)/shard_map/ppermute | solution.py:333
  103.0 12.7 %all-to-all-start.2 = ((f32[4,224,256]{2,1,0:T(8,128)}), f32[4,224,256]{2,1,0:T(8,128)S(1)}, u32[]{:S(2)}, u32[]{:S(2)}) async-start(f32[4,224,256]{2,1,0:T(8,128)} %broadcast_in_dim.27), calls=%async_computation.2 | async-start | bytes 1835008 | tf_op jit(solution)/shard_map/all_to_all | solution.py:306
  106.5 4.6 %collective-permute-start.20 = (f32[192,256]{1,0:T(8,128)S(1)}, f32[192,256]{1,0:T(8,128)S(1)}, u32[]{:S(2)}, u32[]{:S(2)}) collective-permute-start(f32[192,256]{1,0:T(8,128)S(1)} %slice_select_fusion.refs_2_), channel_id=1, source_target_pairs={{0,192},{64,0},{128,64},{192,128},{1,193},{65,1},{129,65},{193,129... | collective-permute-start | bytes 589832 | tf_op jit(solution)/shard_map/ppermute | solution.py:325
  107.6 6.1 %collective-permute-start.19 = (f32[192,256]{1,0:T(8,128)S(1)}, f32[192,256]{1,0:T(8,128)S(1)}, u32[]{:S(2)}, u32[]{:S(2)}) collective-permute-start(f32[192,256]{1,0:T(8,128)S(1)} %slice_select_fusion.refs_2_), channel_id=1, source_target_pairs={{0,128},{64,192},{128,0},{192,64},{1,129},{65,193},{129,1},{193,65... | collective-permute-start | bytes 589832 | tf_op jit(solution)/shard_map/ppermute | solution.py:325
  108.4 7.4 %collective-permute-start.18 = (f32[192,256]{1,0:T(8,128)S(1)}, f32[192,256]{1,0:T(8,128)S(1)}, u32[]{:S(2)}, u32[]{:S(2)}) collective-permute-start(f32[192,256]{1,0:T(8,128)S(1)} %slice_select_fusion.refs_2_), channel_id=1, source_target_pairs={{0,64},{64,128},{128,192},{192,0},{1,65},{65,129},{129,193},{193,1... | collective-permute-start | bytes 589832 | tf_op jit(solution)/shard_map/ppermute | solution.py:325
  115.7 12.0 %collective-permute-start.21 = (f32[896,256]{1,0:T(8,128)S(1)}, f32[896,256]{1,0:T(8,128)S(1)}, u32[]{:S(2)}, u32[]{:S(2)}) collective-permute-start(f32[896,256]{1,0:T(8,128)S(1)} %bitcast.43), channel_id=1, source_target_pairs={{0,1},{1,0},{2,3},{3,2},{4,5},{5,4},{6,7},{7,6},{8,9},{9,8},{10,11... | collective-permute-start | bytes 2752520 | tf_op jit(solution)/shard_map/ppermute | solution.py:333
  124.5 2.4 %collective-permute-start.22 = (f32[192,256]{1,0:T(8,128)S(1)}, f32[192,256]{1,0:T(8,128)S(1)}, u32[]{:S(2)}, u32[]{:S(2)}) collective-permute-start(f32[192,256]{1,0:T(8,128)S(1)} %slice_select_fusion.refs_2_), channel_id=1, source_target_pairs={{0,1},{1,0},{2,3},{3,2},{4,5},{5,4},{6,7},{7,6},{8,9},{9,8},{10,11... | collective-permute-start | bytes 589832 | tf_op jit(solution)/shard_map/ppermute | solution.py:333
  124.5 2.7 %collective-permute-start.23 = (f32[192,256]{1,0:T(8,128)S(1)}, f32[192,256]{1,0:T(8,128)S(1)}, u32[]{:S(2)}, u32[]{:S(2)}) collective-permute-start(f32[192,256]{1,0:T(8,128)S(1)} %collective-permute-done.18.refs_3_), channel_id=1, source_target_pairs={{0,1},{1,0},{2,3},{3,2},{4,5},{5,4},{6,7},{7,6},{8,9},{9,8},{10,11... | collective-permute-start | bytes 589832 | tf_op jit(solution)/shard_map/ppermute | solution.py:333
  125.0 2.4 %collective-permute-start.24 = (f32[192,256]{1,0:T(8,128)S(1)}, f32[192,256]{1,0:T(8,128)S(1)}, u32[]{:S(2)}, u32[]{:S(2)}) collective-permute-start(f32[192,256]{1,0:T(8,128)S(1)} %collective-permute-done.19.refs_4_), channel_id=1, source_target_pairs={{0,1},{1,0},{2,3},{3,2},{4,5},{5,4},{6,7},{7,6},{8,9},{9,8},{10,11... | collective-permute-start | bytes 589832 | tf_op jit(solution)/shard_map/ppermute | solution.py:333
  125.1 2.7 %collective-permute-start.25 = (f32[192,256]{1,0:T(8,128)S(1)}, f32[192,256]{1,0:T(8,128)S(1)}, u32[]{:S(2)}, u32[]{:S(2)}) collective-permute-start(f32[192,256]{1,0:T(8,128)S(1)} %collective-permute-done.20.refs_5_), channel_id=1, source_target_pairs={{0,1},{1,0},{2,3},{3,2},{4,5},{5,4},{6,7},{7,6},{8,9},{9,8},{10,11... | collective-permute-start | bytes 589832 | tf_op jit(solution)/shard_map/ppermute | solution.py:333
  (6 other events, 18.9 us)

commit v10 on v9

--- a/solution.py
+++ b/solution.py
@@ -215,7 +215,7 @@
             pltpu.VMEM((2,) + outer.shape, jnp.float32),
             pltpu.SemaphoreType.DMA((11,)),
         ],
-        compiler_params=params(54),
+        compiler_params=params(50),
         cost_estimate=pl.CostEstimate(flops=870 * 10**6, bytes_accessed=8 * 10**6, transcendentals=0),
         name="terms",
     )(core, arrived, preact, above, blocks, weighted)

time: 131 us -> 129 us (0.985)
  local copies, waits for them, and re-layouts: 4.97 us -> 2.24 us
  other arithmetic: 0.38 us -> 1.69 us
    unnamed x18 -> x8, local copies, waits for them, and re-layouts: 3.88 us -> 1.15 us
where the time goes in v10:
time: 129 us
  starting transfers between devices  61.3 us (48%)
  waiting for transfers between devices  48.1 us (37%)
  Pallas kernels  13.8 us (11%)
  local copies, waits for them, and re-layouts  2.24 us (2%)
  other arithmetic  1.69 us (1%)
  between operations  1.65 us (1%)
    all_to_all x3, starting transfers between devices, exchange(): return lax.all_to_all(x, axis, split_axis=0, concat_axis=0, tiled=True)  19.6 us
    ppermute x9, waiting for transfers between devices, rotated(): return lax.ppermute(x, axis, [(i, (i + by) % size) for i in range(size)])  16.9 us
    ppermute x9, waiting for transfers between devices, swapped(): return lax.ppermute(x, axis, [(i, i ^ bit) for i in range(SIZES[axis])])  15.5 us
    ppermute x9, starting transfers between devices, rotated(): return lax.ppermute(x, axis, [(i, (i + by) % size) for i in range(size)])  13.9 us
    ppermute x9, starting transfers between devices, swapped(): return lax.ppermute(x, axis, [(i, i ^ bit) for i in range(SIZES[axis])])  13.8 us
    ppermute x2, waiting for transfers between devices, shifted(): return lax.ppermute(x, SPACE, pairs)  11.1 us
    ppermute x6, starting transfers between devices, turned(): return lax.ppermute(x, ('x', 'z', 'y'), pairs)  9.62 us
    ppermute x6, waiting for transfers between devices, turned(): return lax.ppermute(x, ('x', 'z', 'y'), pairs)  4.67 us
  transfers between devices with their start and end apart: 29, of which 20 were waited for; matrix products, arithmetic and copies ran while one was open for 0% of the time, Pallas kernels for 3%

profile of v10, /device:TPU:1, one launch (start us, length us, event | category | flops | bytes accessed | tf_op | source)
XLA Modules:
  0.0 128.9 jit_solution(4037396222407253431)
XLA Ops:
  1.4 2.9 %build_sent.1 = (bf16[32,32,256]{2,1,0:T(8,128)(2,1)}, bf16[512,1024]{1,0:T(8,128)(2,1)}) custom-call(f32[1]{0:T(128)S(6)} %div.3.share_ref, bf16[512,1024]{1,0:T(8,128)(2,1)} %bitcast.52, bf16[256,1024]{1,0:T(8,128)(2,1)} %weight_hbm.1, bf16[2,256,256]{2,1,0:T(8,128)(2,1)} %bitcast.46), custom_call_target="tpu_custom_call" | custom-call | flops 268000000 | bytes 4000000 | tf_op jit(solution)/shard_map/build_sent/pallas_call | solution.py:81
  4.3 11.9 %all-to-all-start = ((bf16[32,32,256]{2,1,0:T(8,128)(2,1)}), bf16[32,32,256]{2,1,0:T(8,128)(2,1)S(1)}, u32[]{:S(2)}, u32[]{:S(2)}) async-start(bf16[32,32,256]{2,1,0:T(8,128)(2,1)} %get-tuple-element.36), calls=%async_computation | async-start | bytes 1048576 | tf_op jit(solution)/shard_map/all_to_all | solution.py:306
  16.3 3.1 %collective-permute-start = (bf16[1,512,256]{2,1,0:T(8,128)(2,1)S(1)}, bf16[1,512,256]{2,1,0:T(8,128)(2,1)S(1)}, u32[]{:S(2)}, u32[]{:S(2)}) collective-permute-start(bf16[1,512,256]{2,1,0:T(8,128)(2,1)S(1)} %slice_bitcast_fusion), channel_id=1, source_target_pairs={{0,8},{8,16},{16,24},{24,32},{32,40},{40,48},{48,56},{56,64},{64,7... | collective-permute-start | bytes 786440 | tf_op jit(solution)/shard_map/ppermute | solution.py:43
  21.2 11.1 %collective-permute-done.x_ref = bf16[1,512,256]{2,1,0:T(8,128)(2,1)S(1)} collective-permute-done((bf16[1,512,256]{2,1,0:T(8,128)(2,1)S(1)}, bf16[1,512,256]{2,1,0:T(8,128)(2,1)S(1)}, u32[]{:S(2)}, u32[]{:S(2)}) %collective-permute-start) | collective-permute-done | bytes 262176 | tf_op jit(solution)/shard_map/ppermute | solution.py:43
  32.5 3.9 %terms.1 = (f32[896,256]{1,0:T(8,128)S(1)}, f32[896,256]{1,0:T(8,128)}, f32[768,256]{1,0:T(8,128)S(1)}, f32[768,256]{1,0:T(8,128)S(1)}, bf16[2,256,256]{2,1,0:T(...) custom-call(s32[1]{0:T(128)} %bitcast.core_ref, bf16[32,32,256]{2,1,0:T(8,128)(2,1)S(1)} %all-to-all-done.arrived_hbm, ...), custom_call_target="tpu_custom_call" | custom-call | flops 870000000 | bytes 8000000 | tf_op jit(solution)/shard_map/terms/pallas_call | solution.py:199
  36.5 3.6 %collective-permute-start.1 = (f32[896,256]{1,0:T(8,128)}, f32[896,256]{1,0:T(8,128)S(1)}, u32[]{:S(2)}, u32[]{:S(2)}) collective-permute-start(f32[896,256]{1,0:T(8,128)} %get-tuple-element.39), channel_id=1, source_target_pairs={{0,1},{1,0},{2,3},{3,2},{4,5},{5,4},{6,7},{7,6},{8,9},{9,8},{10,11... | collective-permute-start | bytes 2752520 | tf_op jit(solution)/shard_map/ppermute | solution.py:333
  40.2 2.5 %collective-permute-done.1.got = f32[896,256]{1,0:T(8,128)S(1)} collective-permute-done((f32[896,256]{1,0:T(8,128)}, f32[896,256]{1,0:T(8,128)S(1)}, u32[]{:S(2)}, u32[]{:S(2)}) %collective-permute-start.1) | collective-permute-done | bytes 917536 | tf_op jit(solution)/shard_map/ppermute | solution.py:333
  43.7 4.2 %all-to-all-start.1 = ((f32[4,224,256]{2,1,0:T(8,128)}), f32[4,224,256]{2,1,0:T(8,128)}, u32[]{:S(2)}, u32[]{:S(2)}) async-start(f32[4,224,256]{2,1,0:T(8,128)} %bitcast.5), calls=%async_computation.1 | async-start | bytes 1835008 | tf_op jit(solution)/shard_map/all_to_all | solution.py:306
  48.7 2.7 %collective-permute-start.3 = (f32[192,256]{1,0:T(8,128)S(1)}, f32[192,256]{1,0:T(8,128)S(1)}, u32[]{:S(2)}, u32[]{:S(2)}) collective-permute-start(f32[192,256]{1,0:T(8,128)S(1)} %get-tuple-element.45), channel_id=1, source_target_pairs={{0,64},{64,128},{128,192},{192,0},{1,65},{65,129},{129,193},{193,1... | collective-permute-start | bytes 589832 | tf_op jit(solution)/shard_map/ppermute | solution.py:325
  51.4 2.7 %collective-permute-start.4 = (f32[192,256]{1,0:T(8,128)S(1)}, f32[192,256]{1,0:T(8,128)S(1)}, u32[]{:S(2)}, u32[]{:S(2)}) collective-permute-start(f32[192,256]{1,0:T(8,128)S(1)} %get-tuple-element.46), channel_id=1, source_target_pairs={{0,128},{64,192},{128,0},{192,64},{1,129},{65,193},{129,1},{193,65... | collective-permute-start | bytes 589832 | tf_op jit(solution)/shard_map/ppermute | solution.py:325
  54.9 2.8 %collective-permute-done.3 = f32[192,256]{1,0:T(8,128)S(1)} collective-permute-done((f32[192,256]{1,0:T(8,128)S(1)}, f32[192,256]{1,0:T(8,128)S(1)}, u32[]{:S(2)}, u32[]{:S(2)}) %collective-permute-start.3) | collective-permute-done | bytes 196640 | tf_op jit(solution)/shard_map/ppermute | solution.py:325
  57.7 5.0 %collective-permute-done.4 = f32[192,256]{1,0:T(8,128)S(1)} collective-permute-done((f32[192,256]{1,0:T(8,128)S(1)}, f32[192,256]{1,0:T(8,128)S(1)}, u32[]{:S(2)}, u32[]{:S(2)}) %collective-permute-start.4) | collective-permute-done | bytes 196640 | tf_op jit(solution)/shard_map/ppermute | solution.py:325
  62.8 1.4 %reduce_sum.9 = f32[224,256]{1,0:T(8,128)S(1)} reduce(f32[4,224,256]{2,1,0:T(8,128)} %all-to-all-done.1, f32[]{:T(128)} %constant.26.clone.1), dimensions={0}, to_apply=%region_0.0 | reduce | flops 172032 | bytes 1146884 | tf_op jit(solution)/shard_map/reduce_sum | solution.py:359
  64.3 5.6 %collective-permute-done.6 = f32[224,256]{1,0:T(8,128)S(1)} collective-permute-done((f32[224,256]{1,0:T(8,128)S(1)}, f32[224,256]{1,0:T(8,128)S(1)}, u32[]{:S(2)}, u32[]{:S(2)}) %collective-permute-start.6) | collective-permute-done | bytes 229408 | tf_op jit(solution)/shard_map/ppermute | solution.py:333
  70.0 2.0 %collective-permute-start.7 = (f32[56,256]{1,0:T(8,128)S(1)}, f32[56,256]{1,0:T(8,128)S(1)}, u32[]{:S(2)}, u32[]{:S(2)}) collective-permute-start(f32[56,256]{1,0:T(8,128)S(1)} %get-tuple-element.54), channel_id=1, source_target_pairs={{0,64},{2,66},{4,68},{6,70},{8,10},{10,12},{12,14},{14,8},{16,80},... | collective-permute-start | bytes 172040 | tf_op jit(solution)/shard_map/ppermute | solution.py:343
  72.0 2.5 %collective-permute-start.8 = (f32[56,256]{1,0:T(8,128)S(1)}, f32[56,256]{1,0:T(8,128)S(1)}, u32[]{:S(2)}, u32[]{:S(2)}) collective-permute-start(f32[56,256]{1,0:T(8,128)S(1)} %get-tuple-element.55), channel_id=1, source_target_pairs={{0,128},{2,130},{4,132},{6,134},{8,12},{10,14},{12,8},{14,10},{16,... | collective-permute-start | bytes 172040 | tf_op jit(solution)/shard_map/ppermute | solution.py:343
  77.6 1.9 %collective-permute-start.12 = (f32[56,256]{1,0:T(8,128)S(1)}, f32[56,256]{1,0:T(8,128)S(1)}, u32[]{:S(2)}, u32[]{:S(2)}) collective-permute-start(f32[56,256]{1,0:T(8,128)S(1)} %fusion.6), channel_id=1, source_target_pairs={{0,48},{8,56},{16,0},{24,8},{32,16},{40,24},{48,32},{56,40},{1,49}... | collective-permute-start | bytes 172040 | tf_op jit(solution)/shard_map/ppermute | solution.py:325
  79.5 1.6 %collective-permute-start.11 = (f32[56,256]{1,0:T(8,128)S(1)}, f32[56,256]{1,0:T(8,128)S(1)}, u32[]{:S(2)}, u32[]{:S(2)}) collective-permute-start(f32[56,256]{1,0:T(8,128)S(1)} %fusion.6), channel_id=1, source_target_pairs={{0,32},{8,40},{16,48},{24,56},{32,0},{40,8},{48,16},{56,24},{1,33}... | collective-permute-start | bytes 172040 | tf_op jit(solution)/shard_map/ppermute | solution.py:325
  81.1 1.7 %collective-permute-start.10 = (f32[56,256]{1,0:T(8,128)S(1)}, f32[56,256]{1,0:T(8,128)S(1)}, u32[]{:S(2)}, u32[]{:S(2)}) collective-permute-start(f32[56,256]{1,0:T(8,128)S(1)} %fusion.6), channel_id=1, source_target_pairs={{0,16},{8,24},{16,32},{24,40},{32,48},{40,56},{48,0},{56,8},{1,17}... | collective-permute-start | bytes 172040 | tf_op jit(solution)/shard_map/ppermute | solution.py:325
  82.8 1.9 %input_grad.1 = bf16[4,512,256]{2,1,0:T(8,128)(2,1)} custom-call(bf16[2,256,256]{2,1,0:T(8,128)(2,1)S(1)} %get-tuple-element.57.grad_ref, bf16[1,256,256]{2,1,0:T(8,128)(2,1)S(1)} %collective-permute-done.13.below_ref, bf16[3,3,256,256]{3,2,1,0:T(8,128)(2,1)S(1)} %copy-done.2), custom_call_target="tpu_custom_call" | custom-call | flops 604000000 | bytes 3000000 | tf_op jit(solution)/shard_map/input_grad/pallas_call | solution.py:293
  84.7 1.9 %collective-permute-done.11 = f32[56,256]{1,0:T(8,128)S(1)} collective-permute-done((f32[56,256]{1,0:T(8,128)S(1)}, f32[56,256]{1,0:T(8,128)S(1)}, u32[]{:S(2)}, u32[]{:S(2)}) %collective-permute-start.11) | collective-permute-done | bytes 57376 | tf_op jit(solution)/shard_map/ppermute | solution.py:325
  87.2 2.4 %collective-permute-start.14 = (f32[56,256]{1,0:T(8,128)S(1)}, f32[56,256]{1,0:T(8,128)S(1)}, u32[]{:S(2)}, u32[]{:S(2)}) collective-permute-start(f32[56,256]{1,0:T(8,128)S(1)} %get-tuple-element.70), channel_id=1, source_target_pairs={{0,64},{2,66},{4,68},{6,70},{8,10},{10,12},{12,14},{14,8},{16,80},... | collective-permute-start | bytes 172040 | tf_op jit(solution)/shard_map/ppermute | solution.py:343
  89.6 2.5 %collective-permute-start.15 = (f32[56,256]{1,0:T(8,128)S(1)}, f32[56,256]{1,0:T(8,128)S(1)}, u32[]{:S(2)}, u32[]{:S(2)}) collective-permute-start(f32[56,256]{1,0:T(8,128)S(1)} %get-tuple-element.70), channel_id=1, source_target_pairs={{0,128},{2,130},{4,132},{6,134},{8,12},{10,14},{12,8},{14,10},{16,... | collective-permute-start | bytes 172040 | tf_op jit(solution)/shard_map/ppermute | solution.py:343
  92.5 1.8 %collective-permute-done.15 = f32[56,256]{1,0:T(8,128)S(1)} collective-permute-done((f32[56,256]{1,0:T(8,128)S(1)}, f32[56,256]{1,0:T(8,128)S(1)}, u32[]{:S(2)}, u32[]{:S(2)}) %collective-permute-start.15) | collective-permute-done | bytes 57376 | tf_op jit(solution)/shard_map/ppermute | solution.py:343
  95.2 5.2 %collective-permute-done.17 = f32[224,256]{1,0:T(8,128)S(1)} collective-permute-done((f32[224,256]{1,0:T(8,128)S(1)}, f32[224,256]{1,0:T(8,128)S(1)}, u32[]{:S(2)}, u32[]{:S(2)}) %collective-permute-start.17) | collective-permute-done | bytes 229408 | tf_op jit(solution)/shard_map/ppermute | solution.py:333
  101.3 3.5 %all-to-all-start.2 = ((f32[4,224,256]{2,1,0:T(8,128)}), f32[4,224,256]{2,1,0:T(8,128)S(1)}, u32[]{:S(2)}, u32[]{:S(2)}) async-start(f32[4,224,256]{2,1,0:T(8,128)} %broadcast_in_dim.27), calls=%async_computation.2 | async-start | bytes 1835008 | tf_op jit(solution)/shard_map/all_to_all | solution.py:306
  107.4 2.1 %collective-permute-done.20.refs_5_ = f32[192,256]{1,0:T(8,128)S(1)} collective-permute-done((f32[192,256]{1,0:T(8,128)S(1)}, f32[192,256]{1,0:T(8,128)S(1)}, u32[]{:S(2)}, u32[]{:S(2)}) %collective-permute-start.20) | collective-permute-done | bytes 196640 | tf_op jit(solution)/shard_map/ppermute | solution.py:325
  109.5 2.6 %collective-permute-done.19.refs_4_ = f32[192,256]{1,0:T(8,128)S(1)} collective-permute-done((f32[192,256]{1,0:T(8,128)S(1)}, f32[192,256]{1,0:T(8,128)S(1)}, u32[]{:S(2)}, u32[]{:S(2)}) %collective-permute-start.19) | collective-permute-done | bytes 196640 | tf_op jit(solution)/shard_map/ppermute | solution.py:325
  112.1 2.0 %collective-permute-done.18.refs_3_ = f32[192,256]{1,0:T(8,128)S(1)} collective-permute-done((f32[192,256]{1,0:T(8,128)S(1)}, f32[192,256]{1,0:T(8,128)S(1)}, u32[]{:S(2)}, u32[]{:S(2)}) %collective-permute-start.18) | collective-permute-done | bytes 196640 | tf_op jit(solution)/shard_map/ppermute | solution.py:325
  114.1 9.0 %collective-permute-start.21 = (f32[896,256]{1,0:T(8,128)S(1)}, f32[896,256]{1,0:T(8,128)S(1)}, u32[]{:S(2)}, u32[]{:S(2)}) collective-permute-start(f32[896,256]{1,0:T(8,128)S(1)} %bitcast.43), channel_id=1, source_target_pairs={{0,1},{1,0},{2,3},{3,2},{4,5},{5,4},{6,7},{7,6},{8,9},{9,8},{10,11... | collective-permute-start | bytes 2752520 | tf_op jit(solution)/shard_map/ppermute | solution.py:333
  124.1 1.4 %collective-permute-done.22.refs_6_ = f32[192,256]{1,0:T(8,128)S(1)} collective-permute-done((f32[192,256]{1,0:T(8,128)S(1)}, f32[192,256]{1,0:T(8,128)S(1)}, u32[]{:S(2)}, u32[]{:S(2)}) %collective-permute-start.22) | collective-permute-done | bytes 196640 | tf_op jit(solution)/shard_map/ppermute | solution.py:333
  126.3 2.6 %assemble.1 = (f32[9,256,256]{2,1,0:T(8,128)}, f32[256,1024]{1,0:T(8,128)}) custom-call(s32[2]{0:T(128)S(1)} %pad_add_fusion.where_ref, f32[896,256]{1,0:T(8,128)S(1)} %bitcast.44, f32[896,256]{1,0:T(8,128)S(1)} %collective-permute-done.21.refs_1_, f32[192,256]{1,0:T(8,128)S(1)} %slice_select_fusion.refs_2_, f32[192,256]{1,0:T(8,128)S(1)} %collective-permute-done.18.refs_3_, ...), custom_call_target="tpu_custom_call" | custom-call | bytes 7000000 | tf_op jit(solution)/shard_map/assemble/pallas_call | solution.py:413
  (59 shorter events, 15.2 us)
Async XLA Ops:
  0.6 15.6 %copy-start.1 = (bf16[1,4,512,256]{3,2,1,0:T(8,128)(2,1)S(1)}, bf16[1,4,512,256]{3,2,1,0:T(8,128)(2,1)}, u32[]{:S(2)}) copy-start(bf16[1,4,512,256]{3,2,1,0:T(8,128)(2,1)} %param.6) | copy-start | bytes 3145732
  4.3 28.2 %all-to-all-start = ((bf16[32,32,256]{2,1,0:T(8,128)(2,1)}), bf16[32,32,256]{2,1,0:T(8,128)(2,1)S(1)}, u32[]{:S(2)}, u32[]{:S(2)}) async-start(bf16[32,32,256]{2,1,0:T(8,128)(2,1)} %get-tuple-element.36), calls=%async_computation | async-start | bytes 1048576 | tf_op jit(solution)/shard_map/all_to_all | solution.py:306
  16.3 16.0 %collective-permute-start = (bf16[1,512,256]{2,1,0:T(8,128)(2,1)S(1)}, bf16[1,512,256]{2,1,0:T(8,128)(2,1)S(1)}, u32[]{:S(2)}, u32[]{:S(2)}) collective-permute-start(bf16[1,512,256]{2,1,0:T(8,128)(2,1)S(1)} %slice_bitcast_fusion), channel_id=1, source_target_pairs={{0,8},{8,16},{16,24},{24,32},{32,40},{40,48},{48,56},{56,64},{64,7... | collective-permute-start | bytes 786440 | tf_op jit(solution)/shard_map/ppermute | solution.py:43
  19.4 13.1 %copy-start.3 = (bf16[1,2,256,256]{3,2,1,0:T(8,128)(2,1)S(1)}, bf16[1,2,256,256]{3,2,1,0:T(8,128)(2,1)}, u32[]{:S(2)}) copy-start(bf16[1,2,256,256]{3,2,1,0:T(8,128)(2,1)} %param.7) | copy-start | bytes 786436
  36.5 6.3 %collective-permute-start.1 = (f32[896,256]{1,0:T(8,128)}, f32[896,256]{1,0:T(8,128)S(1)}, u32[]{:S(2)}, u32[]{:S(2)}) collective-permute-start(f32[896,256]{1,0:T(8,128)} %get-tuple-element.39), channel_id=1, source_target_pairs={{0,1},{1,0},{2,3},{3,2},{4,5},{5,4},{6,7},{7,6},{8,9},{9,8},{10,11... | collective-permute-start | bytes 2752520 | tf_op jit(solution)/shard_map/ppermute | solution.py:333
  40.1 7.9 %collective-permute-start.2 = (f32[768,256]{1,0:T(8,128)S(1)}, f32[768,256]{1,0:T(8,128)S(1)}, u32[]{:S(2)}, u32[]{:S(2)}) collective-permute-start(f32[768,256]{1,0:T(8,128)S(1)} %get-tuple-element.41), channel_id=1, source_target_pairs={{0,1},{1,0},{2,3},{3,2},{4,5},{5,4},{6,7},{7,6},{8,9},{9,8},{10,11... | collective-permute-start | bytes 2359304 | tf_op jit(solution)/shard_map/ppermute | solution.py:333
  43.7 18.9 %all-to-all-start.1 = ((f32[4,224,256]{2,1,0:T(8,128)}), f32[4,224,256]{2,1,0:T(8,128)}, u32[]{:S(2)}, u32[]{:S(2)}) async-start(f32[4,224,256]{2,1,0:T(8,128)} %bitcast.5), calls=%async_computation.1 | async-start | bytes 1835008 | tf_op jit(solution)/shard_map/all_to_all | solution.py:306
  48.7 9.0 %collective-permute-start.3 = (f32[192,256]{1,0:T(8,128)S(1)}, f32[192,256]{1,0:T(8,128)S(1)}, u32[]{:S(2)}, u32[]{:S(2)}) collective-permute-start(f32[192,256]{1,0:T(8,128)S(1)} %get-tuple-element.45), channel_id=1, source_target_pairs={{0,64},{64,128},{128,192},{192,0},{1,65},{65,129},{129,193},{193,1... | collective-permute-start | bytes 589832 | tf_op jit(solution)/shard_map/ppermute | solution.py:325
  51.4 11.3 %collective-permute-start.4 = (f32[192,256]{1,0:T(8,128)S(1)}, f32[192,256]{1,0:T(8,128)S(1)}, u32[]{:S(2)}, u32[]{:S(2)}) collective-permute-start(f32[192,256]{1,0:T(8,128)S(1)} %get-tuple-element.46), channel_id=1, source_target_pairs={{0,128},{64,192},{128,0},{192,64},{1,129},{65,193},{129,1},{193,65... | collective-permute-start | bytes 589832 | tf_op jit(solution)/shard_map/ppermute | solution.py:325
  54.1 8.6 %collective-permute-start.5 = (f32[192,256]{1,0:T(8,128)S(1)}, f32[192,256]{1,0:T(8,128)S(1)}, u32[]{:S(2)}, u32[]{:S(2)}) collective-permute-start(f32[192,256]{1,0:T(8,128)S(1)} %get-tuple-element.47), channel_id=1, source_target_pairs={{0,192},{64,0},{128,64},{192,128},{1,193},{65,1},{129,65},{193,129... | collective-permute-start | bytes 589832 | tf_op jit(solution)/shard_map/ppermute | solution.py:325
  62.8 20.0 %copy-start.2 = (bf16[3,3,256,256]{3,2,1,0:T(8,128)(2,1)S(1)}, bf16[3,3,256,256]{3,2,1,0:T(8,128)(2,1)}, u32[]{:S(2)}) copy-start(bf16[3,3,256,256]{3,2,1,0:T(8,128)(2,1)} %weight_ref.1) | copy-start | bytes 3538948
  64.2 5.7 %collective-permute-start.6 = (f32[224,256]{1,0:T(8,128)S(1)}, f32[224,256]{1,0:T(8,128)S(1)}, u32[]{:S(2)}, u32[]{:S(2)}) collective-permute-start(f32[224,256]{1,0:T(8,128)S(1)} %fusion.1), channel_id=1, source_target_pairs={{0,8},{8,0},{16,24},{24,16},{32,40},{40,32},{48,56},{56,48},{1,9},... | collective-permute-start | bytes 688136 | tf_op jit(solution)/shard_map/ppermute | solution.py:333
  70.0 6.0 %collective-permute-start.7 = (f32[56,256]{1,0:T(8,128)S(1)}, f32[56,256]{1,0:T(8,128)S(1)}, u32[]{:S(2)}, u32[]{:S(2)}) collective-permute-start(f32[56,256]{1,0:T(8,128)S(1)} %get-tuple-element.54), channel_id=1, source_target_pairs={{0,64},{2,66},{4,68},{6,70},{8,10},{10,12},{12,14},{14,8},{16,80},... | collective-permute-start | bytes 172040 | tf_op jit(solution)/shard_map/ppermute | solution.py:343
  72.0 4.7 %collective-permute-start.8 = (f32[56,256]{1,0:T(8,128)S(1)}, f32[56,256]{1,0:T(8,128)S(1)}, u32[]{:S(2)}, u32[]{:S(2)}) collective-permute-start(f32[56,256]{1,0:T(8,128)S(1)} %get-tuple-element.55), channel_id=1, source_target_pairs={{0,128},{2,130},{4,132},{6,134},{8,12},{10,14},{12,8},{14,10},{16,... | collective-permute-start | bytes 172040 | tf_op jit(solution)/shard_map/ppermute | solution.py:343
  74.5 3.1 %collective-permute-start.9 = (f32[56,256]{1,0:T(8,128)S(1)}, f32[56,256]{1,0:T(8,128)S(1)}, u32[]{:S(2)}, u32[]{:S(2)}) collective-permute-start(f32[56,256]{1,0:T(8,128)S(1)} %get-tuple-element.56), channel_id=1, source_target_pairs={{0,192},{2,194},{4,196},{6,198},{8,14},{10,8},{12,10},{14,12},{16,... | collective-permute-start | bytes 172040 | tf_op jit(solution)/shard_map/ppermute | solution.py:343
  74.7 8.1 %collective-permute-start.13 = (bf16[1,256,256]{2,1,0:T(8,128)(2,1)S(1)}, bf16[1,256,256]{2,1,0:T(8,128)(2,1)S(1)}, u32[]{:S(2)}, u32[]{:S(2)}) collective-permute-start(bf16[1,256,256]{2,1,0:T(8,128)(2,1)S(1)} %get-tuple-element.58), channel_id=1, source_target_pairs={{8,0},{16,8},{24,16},{32,24},{40,32},{48,40},{56,48},{64,56},{72,6... | collective-permute-start | bytes 393224 | tf_op jit(solution)/shard_map/ppermute | solution.py:43
  77.6 7.1 %collective-permute-start.12 = (f32[56,256]{1,0:T(8,128)S(1)}, f32[56,256]{1,0:T(8,128)S(1)}, u32[]{:S(2)}, u32[]{:S(2)}) collective-permute-start(f32[56,256]{1,0:T(8,128)S(1)} %fusion.6), channel_id=1, source_target_pairs={{0,48},{8,56},{16,0},{24,8},{32,16},{40,24},{48,32},{56,40},{1,49}... | collective-permute-start | bytes 172040 | tf_op jit(solution)/shard_map/ppermute | solution.py:325
  79.5 7.1 %collective-permute-start.11 = (f32[56,256]{1,0:T(8,128)S(1)}, f32[56,256]{1,0:T(8,128)S(1)}, u32[]{:S(2)}, u32[]{:S(2)}) collective-permute-start(f32[56,256]{1,0:T(8,128)S(1)} %fusion.6), channel_id=1, source_target_pairs={{0,32},{8,40},{16,48},{24,56},{32,0},{40,8},{48,16},{56,24},{1,33}... | collective-permute-start | bytes 172040 | tf_op jit(solution)/shard_map/ppermute | solution.py:325
  81.1 6.0 %collective-permute-start.10 = (f32[56,256]{1,0:T(8,128)S(1)}, f32[56,256]{1,0:T(8,128)S(1)}, u32[]{:S(2)}, u32[]{:S(2)}) collective-permute-start(f32[56,256]{1,0:T(8,128)S(1)} %fusion.6), channel_id=1, source_target_pairs={{0,16},{8,24},{16,32},{24,40},{32,48},{40,56},{48,0},{56,8},{1,17}... | collective-permute-start | bytes 172040 | tf_op jit(solution)/shard_map/ppermute | solution.py:325
  87.2 5.3 %collective-permute-start.14 = (f32[56,256]{1,0:T(8,128)S(1)}, f32[56,256]{1,0:T(8,128)S(1)}, u32[]{:S(2)}, u32[]{:S(2)}) collective-permute-start(f32[56,256]{1,0:T(8,128)S(1)} %get-tuple-element.70), channel_id=1, source_target_pairs={{0,64},{2,66},{4,68},{6,70},{8,10},{10,12},{12,14},{14,8},{16,80},... | collective-permute-start | bytes 172040 | tf_op jit(solution)/shard_map/ppermute | solution.py:343
  89.6 4.7 %collective-permute-start.15 = (f32[56,256]{1,0:T(8,128)S(1)}, f32[56,256]{1,0:T(8,128)S(1)}, u32[]{:S(2)}, u32[]{:S(2)}) collective-permute-start(f32[56,256]{1,0:T(8,128)S(1)} %get-tuple-element.70), channel_id=1, source_target_pairs={{0,128},{2,130},{4,132},{6,134},{8,12},{10,14},{12,8},{14,10},{16,... | collective-permute-start | bytes 172040 | tf_op jit(solution)/shard_map/ppermute | solution.py:343
  92.1 3.0 %collective-permute-start.16 = (f32[56,256]{1,0:T(8,128)S(1)}, f32[56,256]{1,0:T(8,128)S(1)}, u32[]{:S(2)}, u32[]{:S(2)}) collective-permute-start(f32[56,256]{1,0:T(8,128)S(1)} %get-tuple-element.70), channel_id=1, source_target_pairs={{0,192},{2,194},{4,196},{6,198},{8,14},{10,8},{12,10},{14,12},{16,... | collective-permute-start | bytes 172040 | tf_op jit(solution)/shard_map/ppermute | solution.py:343
  95.2 5.2 %collective-permute-start.17 = (f32[224,256]{1,0:T(8,128)S(1)}, f32[224,256]{1,0:T(8,128)S(1)}, u32[]{:S(2)}, u32[]{:S(2)}) collective-permute-start(f32[224,256]{1,0:T(8,128)S(1)} %bitcast.50), channel_id=1, source_target_pairs={{0,8},{8,0},{16,24},{24,16},{32,40},{40,32},{48,56},{56,48},{1,9},... | collective-permute-start | bytes 688136 | tf_op jit(solution)/shard_map/ppermute | solution.py:333
  101.3 12.8 %all-to-all-start.2 = ((f32[4,224,256]{2,1,0:T(8,128)}), f32[4,224,256]{2,1,0:T(8,128)S(1)}, u32[]{:S(2)}, u32[]{:S(2)}) async-start(f32[4,224,256]{2,1,0:T(8,128)} %broadcast_in_dim.27), calls=%async_computation.2 | async-start | bytes 1835008 | tf_op jit(solution)/shard_map/all_to_all | solution.py:306
  104.9 4.6 %collective-permute-start.20 = (f32[192,256]{1,0:T(8,128)S(1)}, f32[192,256]{1,0:T(8,128)S(1)}, u32[]{:S(2)}, u32[]{:S(2)}) collective-permute-start(f32[192,256]{1,0:T(8,128)S(1)} %slice_select_fusion.refs_2_), channel_id=1, source_target_pairs={{0,192},{64,0},{128,64},{192,128},{1,193},{65,1},{129,65},{193,129... | collective-permute-start | bytes 589832 | tf_op jit(solution)/shard_map/ppermute | solution.py:325
  106.0 6.1 %collective-permute-start.19 = (f32[192,256]{1,0:T(8,128)S(1)}, f32[192,256]{1,0:T(8,128)S(1)}, u32[]{:S(2)}, u32[]{:S(2)}) collective-permute-start(f32[192,256]{1,0:T(8,128)S(1)} %slice_select_fusion.refs_2_), channel_id=1, source_target_pairs={{0,128},{64,192},{128,0},{192,64},{1,129},{65,193},{129,1},{193,65... | collective-permute-start | bytes 589832 | tf_op jit(solution)/shard_map/ppermute | solution.py:325
  107.0 7.1 %collective-permute-start.18 = (f32[192,256]{1,0:T(8,128)S(1)}, f32[192,256]{1,0:T(8,128)S(1)}, u32[]{:S(2)}, u32[]{:S(2)}) collective-permute-start(f32[192,256]{1,0:T(8,128)S(1)} %slice_select_fusion.refs_2_), channel_id=1, source_target_pairs={{0,64},{64,128},{128,192},{192,0},{1,65},{65,129},{129,193},{193,1... | collective-permute-start | bytes 589832 | tf_op jit(solution)/shard_map/ppermute | solution.py:325
  114.1 12.2 %collective-permute-start.21 = (f32[896,256]{1,0:T(8,128)S(1)}, f32[896,256]{1,0:T(8,128)S(1)}, u32[]{:S(2)}, u32[]{:S(2)}) collective-permute-start(f32[896,256]{1,0:T(8,128)S(1)} %bitcast.43), channel_id=1, source_target_pairs={{0,1},{1,0},{2,3},{3,2},{4,5},{5,4},{6,7},{7,6},{8,9},{9,8},{10,11... | collective-permute-start | bytes 2752520 | tf_op jit(solution)/shard_map/ppermute | solution.py:333
  123.1 2.4 %collective-permute-start.22 = (f32[192,256]{1,0:T(8,128)S(1)}, f32[192,256]{1,0:T(8,128)S(1)}, u32[]{:S(2)}, u32[]{:S(2)}) collective-permute-start(f32[192,256]{1,0:T(8,128)S(1)} %slice_select_fusion.refs_2_), channel_id=1, source_target_pairs={{0,1},{1,0},{2,3},{3,2},{4,5},{5,4},{6,7},{7,6},{8,9},{9,8},{10,11... | collective-permute-start | bytes 589832 | tf_op jit(solution)/shard_map/ppermute | solution.py:333
  123.1 2.7 %collective-permute-start.23 = (f32[192,256]{1,0:T(8,128)S(1)}, f32[192,256]{1,0:T(8,128)S(1)}, u32[]{:S(2)}, u32[]{:S(2)}) collective-permute-start(f32[192,256]{1,0:T(8,128)S(1)} %collective-permute-done.18.refs_3_), channel_id=1, source_target_pairs={{0,1},{1,0},{2,3},{3,2},{4,5},{5,4},{6,7},{7,6},{8,9},{9,8},{10,11... | collective-permute-start | bytes 589832 | tf_op jit(solution)/shard_map/ppermute | solution.py:333
  123.6 2.4 %collective-permute-start.24 = (f32[192,256]{1,0:T(8,128)S(1)}, f32[192,256]{1,0:T(8,128)S(1)}, u32[]{:S(2)}, u32[]{:S(2)}) collective-permute-start(f32[192,256]{1,0:T(8,128)S(1)} %collective-permute-done.19.refs_4_), channel_id=1, source_target_pairs={{0,1},{1,0},{2,3},{3,2},{4,5},{5,4},{6,7},{7,6},{8,9},{9,8},{10,11... | collective-permute-start | bytes 589832 | tf_op jit(solution)/shard_map/ppermute | solution.py:333
  123.6 2.7 %collective-permute-start.25 = (f32[192,256]{1,0:T(8,128)S(1)}, f32[192,256]{1,0:T(8,128)S(1)}, u32[]{:S(2)}, u32[]{:S(2)}) collective-permute-start(f32[192,256]{1,0:T(8,128)S(1)} %collective-permute-done.20.refs_5_), channel_id=1, source_target_pairs={{0,1},{1,0},{2,3},{3,2},{4,5},{5,4},{6,7},{7,6},{8,9},{9,8},{10,11... | collective-permute-start | bytes 589832 | tf_op jit(solution)/shard_map/ppermute | solution.py:333
  (1 other events, 1.1 us)

commit v11 on v10

--- a/solution.py
+++ b/solution.py
@@ -349,12 +349,12 @@
 
 
 barrier = lax.optimization_barrier
-STEPS = (1, 2, 3)
+STEPS = (2, 1, 3)
 
 
 def total_sums(inner, outer, parts, scale, first, beside):
     inner, parts = exchange(split(inner), "y"), barrier(parts)
-    moved = [rotated(p, "x", by) for p, by in zip(parts, STEPS)]
+    moved = [rotated(parts[by - 1], "x", by) for by in STEPS]
     inner, moved = barrier((inner, moved))
     inner = jnp.sum(inner, axis=0)
     outer = sum(moved, outer)
@@ -382,8 +382,8 @@
     inner = jnp.where(bit == 0, part, got)
     outer = jnp.where(bit == 0, got, part)[: part.shape[0] - rows]
     copies = barrier(jnp.broadcast_to(inner, (4,) + inner.shape))
-    copies, moved = barrier((exchange(copies, "y"), [rotated(outer, "x", by) for by in STEPS]))
-    return [copies.reshape(-1, part.shape[1])], [outer] + moved, beside
+    copies, moved = barrier((exchange(copies, "y"), {by: rotated(outer, "x", by) for by in STEPS}))
+    return [copies.reshape(-1, part.shape[1])], [outer] + [moved[by] for by in sorted(STEPS)], beside
 
 
 def assemble_kernel(where_ref, *refs):

time: 129 us -> 130 us (level)
  starting transfers between devices: 61.3 us -> 63.3 us
  waiting for transfers between devices: 48.1 us -> 46.5 us
    ppermute x6, waiting for transfers between devices: 4.67 us -> 2.92 us  [turned(): return lax.ppermute(x, ('x', 'z', 'y'), pairs)]
  transfers between devices with their start and end apart: 29 -> 29, of which waited for: 20 -> 16; matrix products, arithmetic and copies ran while one was open for 0% -> 0% of each run, Pallas kernels for 3% -> 3%
where the time goes in v11:
time: 130 us; the launch traced here: 129 us
  starting transfers between devices  63.3 us (49%)
  waiting for transfers between devices  46.5 us (36%)
  Pallas kernels  13.8 us (11%)
  local copies, waits for them, and re-layouts  2.25 us (2%)
  other arithmetic  1.69 us (1%)
  between operations  1.66 us (1%)
    all_to_all x3, starting transfers between devices, exchange(): return lax.all_to_all(x, axis, split_axis=0, concat_axis=0, tiled=True)  19.6 us
    ppermute x9, waiting for transfers between devices, rotated(): return lax.ppermute(x, axis, [(i, (i + by) % size) for i in range(size)])  17.2 us
    ppermute x9, waiting for transfers between devices, swapped(): return lax.ppermute(x, axis, [(i, i ^ bit) for i in range(SIZES[axis])])  15.3 us
    ppermute x9, starting transfers between devices, rotated(): return lax.ppermute(x, axis, [(i, (i + by) % size) for i in range(size)])  15.1 us
    ppermute x9, starting transfers between devices, swapped(): return lax.ppermute(x, axis, [(i, i ^ bit) for i in range(SIZES[axis])])  13.4 us
    ppermute x2, waiting for transfers between devices, shifted(): return lax.ppermute(x, SPACE, pairs)  11.1 us
    ppermute x6, starting transfers between devices, turned(): return lax.ppermute(x, ('x', 'z', 'y'), pairs)  10.7 us
    ppermute x2, starting transfers between devices, shifted(): return lax.ppermute(x, SPACE, pairs)  4.43 us
  transfers between devices with their start and end apart: 29, of which 16 were waited for; matrix products, arithmetic and copies ran while one was open for 0% of the time, Pallas kernels for 3%

profile of v11, /device:TPU:1, one launch (start us, length us, event | category | flops | bytes accessed | tf_op | source)
XLA Modules:
  0.0 129.2 jit_solution(11324070786988903666)
XLA Ops:
  1.4 2.9 %build_sent.1 = (bf16[32,32,256]{2,1,0:T(8,128)(2,1)}, bf16[512,1024]{1,0:T(8,128)(2,1)}) custom-call(f32[1]{0:T(128)S(6)} %div.3.share_ref, bf16[512,1024]{1,0:T(8,128)(2,1)} %bitcast.52, bf16[256,1024]{1,0:T(8,128)(2,1)} %weight_hbm.1, bf16[2,256,256]{2,1,0:T(8,128)(2,1)} %bitcast.46), custom_call_target="tpu_custom_call" | custom-call | flops 268000000 | bytes 4000000 | tf_op jit(solution)/shard_map/build_sent/pallas_call | solution.py:81
  4.3 11.9 %all-to-all-start = ((bf16[32,32,256]{2,1,0:T(8,128)(2,1)}), bf16[32,32,256]{2,1,0:T(8,128)(2,1)S(1)}, u32[]{:S(2)}, u32[]{:S(2)}) async-start(bf16[32,32,256]{2,1,0:T(8,128)(2,1)} %get-tuple-element.36), calls=%async_computation | async-start | bytes 1048576 | tf_op jit(solution)/shard_map/all_to_all | solution.py:306
  16.3 3.1 %collective-permute-start = (bf16[1,512,256]{2,1,0:T(8,128)(2,1)S(1)}, bf16[1,512,256]{2,1,0:T(8,128)(2,1)S(1)}, u32[]{:S(2)}, u32[]{:S(2)}) collective-permute-start(bf16[1,512,256]{2,1,0:T(8,128)(2,1)S(1)} %slice_bitcast_fusion), channel_id=1, source_target_pairs={{0,8},{8,16},{16,24},{24,32},{32,40},{40,48},{48,56},{56,64},{64,7... | collective-permute-start | bytes 786440 | tf_op jit(solution)/shard_map/ppermute | solution.py:43
  21.2 11.1 %collective-permute-done.x_ref = bf16[1,512,256]{2,1,0:T(8,128)(2,1)S(1)} collective-permute-done((bf16[1,512,256]{2,1,0:T(8,128)(2,1)S(1)}, bf16[1,512,256]{2,1,0:T(8,128)(2,1)S(1)}, u32[]{:S(2)}, u32[]{:S(2)}) %collective-permute-start) | collective-permute-done | bytes 262176 | tf_op jit(solution)/shard_map/ppermute | solution.py:43
  32.5 3.9 %terms.1 = (f32[896,256]{1,0:T(8,128)S(1)}, f32[896,256]{1,0:T(8,128)}, f32[768,256]{1,0:T(8,128)S(1)}, f32[768,256]{1,0:T(8,128)S(1)}, bf16[2,256,256]{2,1,0:T(...) custom-call(s32[1]{0:T(128)} %bitcast.core_ref, bf16[32,32,256]{2,1,0:T(8,128)(2,1)S(1)} %all-to-all-done.arrived_hbm, ...), custom_call_target="tpu_custom_call" | custom-call | flops 870000000 | bytes 8000000 | tf_op jit(solution)/shard_map/terms/pallas_call | solution.py:199
  36.5 3.6 %collective-permute-start.1 = (f32[896,256]{1,0:T(8,128)}, f32[896,256]{1,0:T(8,128)S(1)}, u32[]{:S(2)}, u32[]{:S(2)}) collective-permute-start(f32[896,256]{1,0:T(8,128)} %get-tuple-element.39), channel_id=1, source_target_pairs={{0,1},{1,0},{2,3},{3,2},{4,5},{5,4},{6,7},{7,6},{8,9},{9,8},{10,11... | collective-permute-start | bytes 2752520 | tf_op jit(solution)/shard_map/ppermute | solution.py:333
  40.2 2.5 %collective-permute-done.1.got = f32[896,256]{1,0:T(8,128)S(1)} collective-permute-done((f32[896,256]{1,0:T(8,128)}, f32[896,256]{1,0:T(8,128)S(1)}, u32[]{:S(2)}, u32[]{:S(2)}) %collective-permute-start.1) | collective-permute-done | bytes 917536 | tf_op jit(solution)/shard_map/ppermute | solution.py:333
  43.7 4.2 %all-to-all-start.1 = ((f32[4,224,256]{2,1,0:T(8,128)}), f32[4,224,256]{2,1,0:T(8,128)}, u32[]{:S(2)}, u32[]{:S(2)}) async-start(f32[4,224,256]{2,1,0:T(8,128)} %bitcast.5), calls=%async_computation.1 | async-start | bytes 1835008 | tf_op jit(solution)/shard_map/all_to_all | solution.py:306
  48.7 4.2 %collective-permute-start.3 = (f32[192,256]{1,0:T(8,128)S(1)}, f32[192,256]{1,0:T(8,128)S(1)}, u32[]{:S(2)}, u32[]{:S(2)}) collective-permute-start(f32[192,256]{1,0:T(8,128)S(1)} %get-tuple-element.45), channel_id=1, source_target_pairs={{0,128},{64,192},{128,0},{192,64},{1,129},{65,193},{129,1},{193,65... | collective-permute-start | bytes 589832 | tf_op jit(solution)/shard_map/ppermute | solution.py:325
  53.5 2.1 %collective-permute-start.5 = (f32[192,256]{1,0:T(8,128)S(1)}, f32[192,256]{1,0:T(8,128)S(1)}, u32[]{:S(2)}, u32[]{:S(2)}) collective-permute-start(f32[192,256]{1,0:T(8,128)S(1)} %get-tuple-element.47), channel_id=1, source_target_pairs={{0,192},{64,0},{128,64},{192,128},{1,193},{65,1},{129,65},{193,129... | collective-permute-start | bytes 589832 | tf_op jit(solution)/shard_map/ppermute | solution.py:325
  55.6 2.0 %collective-permute-done.3 = f32[192,256]{1,0:T(8,128)S(1)} collective-permute-done((f32[192,256]{1,0:T(8,128)S(1)}, f32[192,256]{1,0:T(8,128)S(1)}, u32[]{:S(2)}, u32[]{:S(2)}) %collective-permute-start.3) | collective-permute-done | bytes 196640 | tf_op jit(solution)/shard_map/ppermute | solution.py:325
  57.6 4.7 %collective-permute-done.4 = f32[192,256]{1,0:T(8,128)S(1)} collective-permute-done((f32[192,256]{1,0:T(8,128)S(1)}, f32[192,256]{1,0:T(8,128)S(1)}, u32[]{:S(2)}, u32[]{:S(2)}) %collective-permute-start.4) | collective-permute-done | bytes 196640 | tf_op jit(solution)/shard_map/ppermute | solution.py:325
  62.4 1.4 %reduce_sum.9 = f32[224,256]{1,0:T(8,128)S(1)} reduce(f32[4,224,256]{2,1,0:T(8,128)} %all-to-all-done.1, f32[]{:T(128)} %constant.26.clone.1), dimensions={0}, to_apply=%region_0.0 | reduce | flops 172032 | bytes 1146884 | tf_op jit(solution)/shard_map/reduce_sum | solution.py:359
  63.9 5.8 %collective-permute-done.6 = f32[224,256]{1,0:T(8,128)S(1)} collective-permute-done((f32[224,256]{1,0:T(8,128)S(1)}, f32[224,256]{1,0:T(8,128)S(1)}, u32[]{:S(2)}, u32[]{:S(2)}) %collective-permute-start.6) | collective-permute-done | bytes 229408 | tf_op jit(solution)/shard_map/ppermute | solution.py:333
  69.8 2.8 %collective-permute-start.7 = (f32[56,256]{1,0:T(8,128)S(1)}, f32[56,256]{1,0:T(8,128)S(1)}, u32[]{:S(2)}, u32[]{:S(2)}) collective-permute-start(f32[56,256]{1,0:T(8,128)S(1)} %get-tuple-element.54), channel_id=1, source_target_pairs={{0,128},{2,130},{4,132},{6,134},{8,12},{10,14},{12,8},{14,10},{16,... | collective-permute-start | bytes 172040 | tf_op jit(solution)/shard_map/ppermute | solution.py:343
  73.2 2.1 %collective-permute-start.9 = (f32[56,256]{1,0:T(8,128)S(1)}, f32[56,256]{1,0:T(8,128)S(1)}, u32[]{:S(2)}, u32[]{:S(2)}) collective-permute-start(f32[56,256]{1,0:T(8,128)S(1)} %get-tuple-element.56), channel_id=1, source_target_pairs={{0,192},{2,194},{4,196},{6,198},{8,14},{10,8},{12,10},{14,12},{16,... | collective-permute-start | bytes 172040 | tf_op jit(solution)/shard_map/ppermute | solution.py:343
  75.3 1.3 collective-permute-start.13
  77.5 3.2 %collective-permute-start.12 = (f32[56,256]{1,0:T(8,128)S(1)}, f32[56,256]{1,0:T(8,128)S(1)}, u32[]{:S(2)}, u32[]{:S(2)}) collective-permute-start(f32[56,256]{1,0:T(8,128)S(1)} %fusion.6), channel_id=1, source_target_pairs={{0,48},{8,56},{16,0},{24,8},{32,16},{40,24},{48,32},{56,40},{1,49}... | collective-permute-start | bytes 172040 | tf_op jit(solution)/shard_map/ppermute | solution.py:325
  81.4 1.4 %collective-permute-start.10 = (f32[56,256]{1,0:T(8,128)S(1)}, f32[56,256]{1,0:T(8,128)S(1)}, u32[]{:S(2)}, u32[]{:S(2)}) collective-permute-start(f32[56,256]{1,0:T(8,128)S(1)} %fusion.6), channel_id=1, source_target_pairs={{0,16},{8,24},{16,32},{24,40},{32,48},{40,56},{48,0},{56,8},{1,17}... | collective-permute-start | bytes 172040 | tf_op jit(solution)/shard_map/ppermute | solution.py:325
  82.9 1.9 %input_grad.1 = bf16[4,512,256]{2,1,0:T(8,128)(2,1)} custom-call(bf16[2,256,256]{2,1,0:T(8,128)(2,1)S(1)} %get-tuple-element.57.grad_ref, bf16[1,256,256]{2,1,0:T(8,128)(2,1)S(1)} %collective-permute-done.13.below_ref, bf16[3,3,256,256]{3,2,1,0:T(8,128)(2,1)S(1)} %copy-done.2), custom_call_target="tpu_custom_call" | custom-call | flops 604000000 | bytes 3000000 | tf_op jit(solution)/shard_map/input_grad/pallas_call | solution.py:293
  84.8 3.3 %collective-permute-done.11 = f32[56,256]{1,0:T(8,128)S(1)} collective-permute-done((f32[56,256]{1,0:T(8,128)S(1)}, f32[56,256]{1,0:T(8,128)S(1)}, u32[]{:S(2)}, u32[]{:S(2)}) %collective-permute-start.11) | collective-permute-done | bytes 57376 | tf_op jit(solution)/shard_map/ppermute | solution.py:325
  88.2 2.7 %collective-permute-start.14 = (f32[56,256]{1,0:T(8,128)S(1)}, f32[56,256]{1,0:T(8,128)S(1)}, u32[]{:S(2)}, u32[]{:S(2)}) collective-permute-start(f32[56,256]{1,0:T(8,128)S(1)} %get-tuple-element.70), channel_id=1, source_target_pairs={{0,64},{2,66},{4,68},{6,70},{8,10},{10,12},{12,14},{14,8},{16,80},... | collective-permute-start | bytes 172040 | tf_op jit(solution)/shard_map/ppermute | solution.py:343
  93.4 2.0 %collective-permute-done.15 = f32[56,256]{1,0:T(8,128)S(1)} collective-permute-done((f32[56,256]{1,0:T(8,128)S(1)}, f32[56,256]{1,0:T(8,128)S(1)}, u32[]{:S(2)}, u32[]{:S(2)}) %collective-permute-start.15) | collective-permute-done | bytes 57376 | tf_op jit(solution)/shard_map/ppermute | solution.py:343
  95.9 4.8 %collective-permute-done.17 = f32[224,256]{1,0:T(8,128)S(1)} collective-permute-done((f32[224,256]{1,0:T(8,128)S(1)}, f32[224,256]{1,0:T(8,128)S(1)}, u32[]{:S(2)}, u32[]{:S(2)}) %collective-permute-start.17) | collective-permute-done | bytes 229408 | tf_op jit(solution)/shard_map/ppermute | solution.py:333
  101.8 3.5 %all-to-all-start.2 = ((f32[4,224,256]{2,1,0:T(8,128)}), f32[4,224,256]{2,1,0:T(8,128)S(1)}, u32[]{:S(2)}, u32[]{:S(2)}) async-start(f32[4,224,256]{2,1,0:T(8,128)} %broadcast_in_dim.27), calls=%async_computation.2 | async-start | bytes 1835008 | tf_op jit(solution)/shard_map/all_to_all | solution.py:306
  105.3 2.1 %collective-permute-start.20 = (f32[192,256]{1,0:T(8,128)S(1)}, f32[192,256]{1,0:T(8,128)S(1)}, u32[]{:S(2)}, u32[]{:S(2)}) collective-permute-start(f32[192,256]{1,0:T(8,128)S(1)} %slice_select_fusion.refs_2_), channel_id=1, source_target_pairs={{0,192},{64,0},{128,64},{192,128},{1,193},{65,1},{129,65},{193,129... | collective-permute-start | bytes 589832 | tf_op jit(solution)/shard_map/ppermute | solution.py:325
  108.1 4.0 %collective-permute-done.20.refs_5_ = f32[192,256]{1,0:T(8,128)S(1)} collective-permute-done((f32[192,256]{1,0:T(8,128)S(1)}, f32[192,256]{1,0:T(8,128)S(1)}, u32[]{:S(2)}, u32[]{:S(2)}) %collective-permute-start.20) | collective-permute-done | bytes 196640 | tf_op jit(solution)/shard_map/ppermute | solution.py:325
  112.2 1.4 %collective-permute-done.19.refs_4_ = f32[192,256]{1,0:T(8,128)S(1)} collective-permute-done((f32[192,256]{1,0:T(8,128)S(1)}, f32[192,256]{1,0:T(8,128)S(1)}, u32[]{:S(2)}, u32[]{:S(2)}) %collective-permute-start.19) | collective-permute-done | bytes 196640 | tf_op jit(solution)/shard_map/ppermute | solution.py:325
  113.6 1.7 %collective-permute-done.18.refs_3_ = f32[192,256]{1,0:T(8,128)S(1)} collective-permute-done((f32[192,256]{1,0:T(8,128)S(1)}, f32[192,256]{1,0:T(8,128)S(1)}, u32[]{:S(2)}, u32[]{:S(2)}) %collective-permute-start.18) | collective-permute-done | bytes 196640 | tf_op jit(solution)/shard_map/ppermute | solution.py:325
  115.3 8.1 %collective-permute-start.21 = (f32[896,256]{1,0:T(8,128)S(1)}, f32[896,256]{1,0:T(8,128)S(1)}, u32[]{:S(2)}, u32[]{:S(2)}) collective-permute-start(f32[896,256]{1,0:T(8,128)S(1)} %bitcast.43), channel_id=1, source_target_pairs={{0,1},{1,0},{2,3},{3,2},{4,5},{5,4},{6,7},{7,6},{8,9},{9,8},{10,11... | collective-permute-start | bytes 2752520 | tf_op jit(solution)/shard_map/ppermute | solution.py:333
  124.5 1.4 %collective-permute-done.22.refs_6_ = f32[192,256]{1,0:T(8,128)S(1)} collective-permute-done((f32[192,256]{1,0:T(8,128)S(1)}, f32[192,256]{1,0:T(8,128)S(1)}, u32[]{:S(2)}, u32[]{:S(2)}) %collective-permute-start.22) | collective-permute-done | bytes 196640 | tf_op jit(solution)/shard_map/ppermute | solution.py:333
  126.7 2.6 %assemble.1 = (f32[9,256,256]{2,1,0:T(8,128)}, f32[256,1024]{1,0:T(8,128)}) custom-call(s32[2]{0:T(128)S(1)} %pad_add_fusion.where_ref, f32[896,256]{1,0:T(8,128)S(1)} %bitcast.44, f32[896,256]{1,0:T(8,128)S(1)} %collective-permute-done.21.refs_1_, f32[192,256]{1,0:T(8,128)S(1)} %slice_select_fusion.refs_2_, f32[192,256]{1,0:T(8,128)S(1)} %collective-permute-done.18.refs_3_, ...), custom_call_target="tpu_custom_call" | custom-call | bytes 7000000 | tf_op jit(solution)/shard_map/assemble/pallas_call | solution.py:413
  (59 shorter events, 13.6 us)
Async XLA Ops:
  0.6 15.6 %copy-start.1 = (bf16[1,4,512,256]{3,2,1,0:T(8,128)(2,1)S(1)}, bf16[1,4,512,256]{3,2,1,0:T(8,128)(2,1)}, u32[]{:S(2)}) copy-start(bf16[1,4,512,256]{3,2,1,0:T(8,128)(2,1)} %param.6) | copy-start | bytes 3145732
  4.3 28.2 %all-to-all-start = ((bf16[32,32,256]{2,1,0:T(8,128)(2,1)}), bf16[32,32,256]{2,1,0:T(8,128)(2,1)S(1)}, u32[]{:S(2)}, u32[]{:S(2)}) async-start(bf16[32,32,256]{2,1,0:T(8,128)(2,1)} %get-tuple-element.36), calls=%async_computation | async-start | bytes 1048576 | tf_op jit(solution)/shard_map/all_to_all | solution.py:306
  16.3 16.0 %collective-permute-start = (bf16[1,512,256]{2,1,0:T(8,128)(2,1)S(1)}, bf16[1,512,256]{2,1,0:T(8,128)(2,1)S(1)}, u32[]{:S(2)}, u32[]{:S(2)}) collective-permute-start(bf16[1,512,256]{2,1,0:T(8,128)(2,1)S(1)} %slice_bitcast_fusion), channel_id=1, source_target_pairs={{0,8},{8,16},{16,24},{24,32},{32,40},{40,48},{48,56},{56,64},{64,7... | collective-permute-start | bytes 786440 | tf_op jit(solution)/shard_map/ppermute | solution.py:43
  19.4 13.1 %copy-start.3 = (bf16[1,2,256,256]{3,2,1,0:T(8,128)(2,1)S(1)}, bf16[1,2,256,256]{3,2,1,0:T(8,128)(2,1)}, u32[]{:S(2)}) copy-start(bf16[1,2,256,256]{3,2,1,0:T(8,128)(2,1)} %param.7) | copy-start | bytes 786436
  36.5 6.3 %collective-permute-start.1 = (f32[896,256]{1,0:T(8,128)}, f32[896,256]{1,0:T(8,128)S(1)}, u32[]{:S(2)}, u32[]{:S(2)}) collective-permute-start(f32[896,256]{1,0:T(8,128)} %get-tuple-element.39), channel_id=1, source_target_pairs={{0,1},{1,0},{2,3},{3,2},{4,5},{5,4},{6,7},{7,6},{8,9},{9,8},{10,11... | collective-permute-start | bytes 2752520 | tf_op jit(solution)/shard_map/ppermute | solution.py:333
  40.1 7.9 %collective-permute-start.2 = (f32[768,256]{1,0:T(8,128)S(1)}, f32[768,256]{1,0:T(8,128)S(1)}, u32[]{:S(2)}, u32[]{:S(2)}) collective-permute-start(f32[768,256]{1,0:T(8,128)S(1)} %get-tuple-element.41), channel_id=1, source_target_pairs={{0,1},{1,0},{2,3},{3,2},{4,5},{5,4},{6,7},{7,6},{8,9},{9,8},{10,11... | collective-permute-start | bytes 2359304 | tf_op jit(solution)/shard_map/ppermute | solution.py:333
  43.7 18.5 %all-to-all-start.1 = ((f32[4,224,256]{2,1,0:T(8,128)}), f32[4,224,256]{2,1,0:T(8,128)}, u32[]{:S(2)}, u32[]{:S(2)}) async-start(f32[4,224,256]{2,1,0:T(8,128)} %bitcast.5), calls=%async_computation.1 | async-start | bytes 1835008 | tf_op jit(solution)/shard_map/all_to_all | solution.py:306
  48.7 8.9 %collective-permute-start.3 = (f32[192,256]{1,0:T(8,128)S(1)}, f32[192,256]{1,0:T(8,128)S(1)}, u32[]{:S(2)}, u32[]{:S(2)}) collective-permute-start(f32[192,256]{1,0:T(8,128)S(1)} %get-tuple-element.45), channel_id=1, source_target_pairs={{0,128},{64,192},{128,0},{192,64},{1,129},{65,193},{129,1},{193,65... | collective-permute-start | bytes 589832 | tf_op jit(solution)/shard_map/ppermute | solution.py:325
  52.9 9.4 %collective-permute-start.4 = (f32[192,256]{1,0:T(8,128)S(1)}, f32[192,256]{1,0:T(8,128)S(1)}, u32[]{:S(2)}, u32[]{:S(2)}) collective-permute-start(f32[192,256]{1,0:T(8,128)S(1)} %get-tuple-element.46), channel_id=1, source_target_pairs={{0,64},{64,128},{128,192},{192,0},{1,65},{65,129},{129,193},{193,1... | collective-permute-start | bytes 589832 | tf_op jit(solution)/shard_map/ppermute | solution.py:325
  53.5 8.8 %collective-permute-start.5 = (f32[192,256]{1,0:T(8,128)S(1)}, f32[192,256]{1,0:T(8,128)S(1)}, u32[]{:S(2)}, u32[]{:S(2)}) collective-permute-start(f32[192,256]{1,0:T(8,128)S(1)} %get-tuple-element.47), channel_id=1, source_target_pairs={{0,192},{64,0},{128,64},{192,128},{1,193},{65,1},{129,65},{193,129... | collective-permute-start | bytes 589832 | tf_op jit(solution)/shard_map/ppermute | solution.py:325
  62.4 20.5 %copy-start.2 = (bf16[3,3,256,256]{3,2,1,0:T(8,128)(2,1)S(1)}, bf16[3,3,256,256]{3,2,1,0:T(8,128)(2,1)}, u32[]{:S(2)}) copy-start(bf16[3,3,256,256]{3,2,1,0:T(8,128)(2,1)} %weight_ref.1) | copy-start | bytes 3538948
  63.8 5.9 %collective-permute-start.6 = (f32[224,256]{1,0:T(8,128)S(1)}, f32[224,256]{1,0:T(8,128)S(1)}, u32[]{:S(2)}, u32[]{:S(2)}) collective-permute-start(f32[224,256]{1,0:T(8,128)S(1)} %fusion.1), channel_id=1, source_target_pairs={{0,8},{8,0},{16,24},{24,16},{32,40},{40,32},{48,56},{56,48},{1,9},... | collective-permute-start | bytes 688136 | tf_op jit(solution)/shard_map/ppermute | solution.py:333
  69.8 6.8 %collective-permute-start.7 = (f32[56,256]{1,0:T(8,128)S(1)}, f32[56,256]{1,0:T(8,128)S(1)}, u32[]{:S(2)}, u32[]{:S(2)}) collective-permute-start(f32[56,256]{1,0:T(8,128)S(1)} %get-tuple-element.54), channel_id=1, source_target_pairs={{0,128},{2,130},{4,132},{6,134},{8,12},{10,14},{12,8},{14,10},{16,... | collective-permute-start | bytes 172040 | tf_op jit(solution)/shard_map/ppermute | solution.py:343
  72.6 4.9 %collective-permute-start.8 = (f32[56,256]{1,0:T(8,128)S(1)}, f32[56,256]{1,0:T(8,128)S(1)}, u32[]{:S(2)}, u32[]{:S(2)}) collective-permute-start(f32[56,256]{1,0:T(8,128)S(1)} %get-tuple-element.55), channel_id=1, source_target_pairs={{0,64},{2,66},{4,68},{6,70},{8,10},{10,12},{12,14},{14,8},{16,80},... | collective-permute-start | bytes 172040 | tf_op jit(solution)/shard_map/ppermute | solution.py:343
  73.2 4.3 %collective-permute-start.9 = (f32[56,256]{1,0:T(8,128)S(1)}, f32[56,256]{1,0:T(8,128)S(1)}, u32[]{:S(2)}, u32[]{:S(2)}) collective-permute-start(f32[56,256]{1,0:T(8,128)S(1)} %get-tuple-element.56), channel_id=1, source_target_pairs={{0,192},{2,194},{4,196},{6,198},{8,14},{10,8},{12,10},{14,12},{16,... | collective-permute-start | bytes 172040 | tf_op jit(solution)/shard_map/ppermute | solution.py:343
  75.3 7.6 %collective-permute-start.13 = (bf16[1,256,256]{2,1,0:T(8,128)(2,1)S(1)}, bf16[1,256,256]{2,1,0:T(8,128)(2,1)S(1)}, u32[]{:S(2)}, u32[]{:S(2)}) collective-permute-start(bf16[1,256,256]{2,1,0:T(8,128)(2,1)S(1)} %get-tuple-element.58), channel_id=1, source_target_pairs={{8,0},{16,8},{24,16},{32,24},{40,32},{48,40},{56,48},{64,56},{72,6... | collective-permute-start | bytes 393224 | tf_op jit(solution)/shard_map/ppermute | solution.py:43
  77.5 7.3 %collective-permute-start.12 = (f32[56,256]{1,0:T(8,128)S(1)}, f32[56,256]{1,0:T(8,128)S(1)}, u32[]{:S(2)}, u32[]{:S(2)}) collective-permute-start(f32[56,256]{1,0:T(8,128)S(1)} %fusion.6), channel_id=1, source_target_pairs={{0,48},{8,56},{16,0},{24,8},{32,16},{40,24},{48,32},{56,40},{1,49}... | collective-permute-start | bytes 172040 | tf_op jit(solution)/shard_map/ppermute | solution.py:325
  80.7 7.4 %collective-permute-start.11 = (f32[56,256]{1,0:T(8,128)S(1)}, f32[56,256]{1,0:T(8,128)S(1)}, u32[]{:S(2)}, u32[]{:S(2)}) collective-permute-start(f32[56,256]{1,0:T(8,128)S(1)} %fusion.6), channel_id=1, source_target_pairs={{0,32},{8,40},{16,48},{24,56},{32,0},{40,8},{48,16},{56,24},{1,33}... | collective-permute-start | bytes 172040 | tf_op jit(solution)/shard_map/ppermute | solution.py:325
  81.4 6.7 %collective-permute-start.10 = (f32[56,256]{1,0:T(8,128)S(1)}, f32[56,256]{1,0:T(8,128)S(1)}, u32[]{:S(2)}, u32[]{:S(2)}) collective-permute-start(f32[56,256]{1,0:T(8,128)S(1)} %fusion.6), channel_id=1, source_target_pairs={{0,16},{8,24},{16,32},{24,40},{32,48},{40,56},{48,0},{56,8},{1,17}... | collective-permute-start | bytes 172040 | tf_op jit(solution)/shard_map/ppermute | solution.py:325
  88.2 5.2 %collective-permute-start.14 = (f32[56,256]{1,0:T(8,128)S(1)}, f32[56,256]{1,0:T(8,128)S(1)}, u32[]{:S(2)}, u32[]{:S(2)}) collective-permute-start(f32[56,256]{1,0:T(8,128)S(1)} %get-tuple-element.70), channel_id=1, source_target_pairs={{0,64},{2,66},{4,68},{6,70},{8,10},{10,12},{12,14},{14,8},{16,80},... | collective-permute-start | bytes 172040 | tf_op jit(solution)/shard_map/ppermute | solution.py:343
  90.9 4.5 %collective-permute-start.15 = (f32[56,256]{1,0:T(8,128)S(1)}, f32[56,256]{1,0:T(8,128)S(1)}, u32[]{:S(2)}, u32[]{:S(2)}) collective-permute-start(f32[56,256]{1,0:T(8,128)S(1)} %get-tuple-element.70), channel_id=1, source_target_pairs={{0,128},{2,130},{4,132},{6,134},{8,12},{10,14},{12,8},{14,10},{16,... | collective-permute-start | bytes 172040 | tf_op jit(solution)/shard_map/ppermute | solution.py:343
  92.2 3.3 %collective-permute-start.16 = (f32[56,256]{1,0:T(8,128)S(1)}, f32[56,256]{1,0:T(8,128)S(1)}, u32[]{:S(2)}, u32[]{:S(2)}) collective-permute-start(f32[56,256]{1,0:T(8,128)S(1)} %get-tuple-element.70), channel_id=1, source_target_pairs={{0,192},{2,194},{4,196},{6,198},{8,14},{10,8},{12,10},{14,12},{16,... | collective-permute-start | bytes 172040 | tf_op jit(solution)/shard_map/ppermute | solution.py:343
  95.5 5.3 %collective-permute-start.17 = (f32[224,256]{1,0:T(8,128)S(1)}, f32[224,256]{1,0:T(8,128)S(1)}, u32[]{:S(2)}, u32[]{:S(2)}) collective-permute-start(f32[224,256]{1,0:T(8,128)S(1)} %bitcast.50), channel_id=1, source_target_pairs={{0,8},{8,0},{16,24},{24,16},{32,40},{40,32},{48,56},{56,48},{1,9},... | collective-permute-start | bytes 688136 | tf_op jit(solution)/shard_map/ppermute | solution.py:333
  101.8 13.5 %all-to-all-start.2 = ((f32[4,224,256]{2,1,0:T(8,128)}), f32[4,224,256]{2,1,0:T(8,128)S(1)}, u32[]{:S(2)}, u32[]{:S(2)}) async-start(f32[4,224,256]{2,1,0:T(8,128)} %broadcast_in_dim.27), calls=%async_computation.2 | async-start | bytes 1835008 | tf_op jit(solution)/shard_map/all_to_all | solution.py:306
  105.3 6.9 %collective-permute-start.20 = (f32[192,256]{1,0:T(8,128)S(1)}, f32[192,256]{1,0:T(8,128)S(1)}, u32[]{:S(2)}, u32[]{:S(2)}) collective-permute-start(f32[192,256]{1,0:T(8,128)S(1)} %slice_select_fusion.refs_2_), channel_id=1, source_target_pairs={{0,192},{64,0},{128,64},{192,128},{1,193},{65,1},{129,65},{193,129... | collective-permute-start | bytes 589832 | tf_op jit(solution)/shard_map/ppermute | solution.py:325
  107.4 6.1 %collective-permute-start.19 = (f32[192,256]{1,0:T(8,128)S(1)}, f32[192,256]{1,0:T(8,128)S(1)}, u32[]{:S(2)}, u32[]{:S(2)}) collective-permute-start(f32[192,256]{1,0:T(8,128)S(1)} %slice_select_fusion.refs_2_), channel_id=1, source_target_pairs={{0,128},{64,192},{128,0},{192,64},{1,129},{65,193},{129,1},{193,65... | collective-permute-start | bytes 589832 | tf_op jit(solution)/shard_map/ppermute | solution.py:325
  107.5 7.8 %collective-permute-start.18 = (f32[192,256]{1,0:T(8,128)S(1)}, f32[192,256]{1,0:T(8,128)S(1)}, u32[]{:S(2)}, u32[]{:S(2)}) collective-permute-start(f32[192,256]{1,0:T(8,128)S(1)} %slice_select_fusion.refs_2_), channel_id=1, source_target_pairs={{0,64},{64,128},{128,192},{192,0},{1,65},{65,129},{129,193},{193,1... | collective-permute-start | bytes 589832 | tf_op jit(solution)/shard_map/ppermute | solution.py:325
  115.3 11.4 %collective-permute-start.21 = (f32[896,256]{1,0:T(8,128)S(1)}, f32[896,256]{1,0:T(8,128)S(1)}, u32[]{:S(2)}, u32[]{:S(2)}) collective-permute-start(f32[896,256]{1,0:T(8,128)S(1)} %bitcast.43), channel_id=1, source_target_pairs={{0,1},{1,0},{2,3},{3,2},{4,5},{5,4},{6,7},{7,6},{8,9},{9,8},{10,11... | collective-permute-start | bytes 2752520 | tf_op jit(solution)/shard_map/ppermute | solution.py:333
  123.4 2.4 %collective-permute-start.22 = (f32[192,256]{1,0:T(8,128)S(1)}, f32[192,256]{1,0:T(8,128)S(1)}, u32[]{:S(2)}, u32[]{:S(2)}) collective-permute-start(f32[192,256]{1,0:T(8,128)S(1)} %slice_select_fusion.refs_2_), channel_id=1, source_target_pairs={{0,1},{1,0},{2,3},{3,2},{4,5},{5,4},{6,7},{7,6},{8,9},{9,8},{10,11... | collective-permute-start | bytes 589832 | tf_op jit(solution)/shard_map/ppermute | solution.py:333
  123.4 2.7 %collective-permute-start.23 = (f32[192,256]{1,0:T(8,128)S(1)}, f32[192,256]{1,0:T(8,128)S(1)}, u32[]{:S(2)}, u32[]{:S(2)}) collective-permute-start(f32[192,256]{1,0:T(8,128)S(1)} %collective-permute-done.18.refs_3_), channel_id=1, source_target_pairs={{0,1},{1,0},{2,3},{3,2},{4,5},{5,4},{6,7},{7,6},{8,9},{9,8},{10,11... | collective-permute-start | bytes 589832 | tf_op jit(solution)/shard_map/ppermute | solution.py:333
  123.9 2.4 %collective-permute-start.24 = (f32[192,256]{1,0:T(8,128)S(1)}, f32[192,256]{1,0:T(8,128)S(1)}, u32[]{:S(2)}, u32[]{:S(2)}) collective-permute-start(f32[192,256]{1,0:T(8,128)S(1)} %collective-permute-done.19.refs_4_), channel_id=1, source_target_pairs={{0,1},{1,0},{2,3},{3,2},{4,5},{5,4},{6,7},{7,6},{8,9},{9,8},{10,11... | collective-permute-start | bytes 589832 | tf_op jit(solution)/shard_map/ppermute | solution.py:333
  123.9 2.7 %collective-permute-start.25 = (f32[192,256]{1,0:T(8,128)S(1)}, f32[192,256]{1,0:T(8,128)S(1)}, u32[]{:S(2)}, u32[]{:S(2)}) collective-permute-start(f32[192,256]{1,0:T(8,128)S(1)} %collective-permute-done.20.refs_5_), channel_id=1, source_target_pairs={{0,1},{1,0},{2,3},{3,2},{4,5},{5,4},{6,7},{7,6},{8,9},{9,8},{10,11... | collective-permute-start | bytes 589832 | tf_op jit(solution)/shard_map/ppermute | solution.py:333
  (1 other events, 1.1 us)

commit v12 on v10

--- a/solution.py
+++ b/solution.py
@@ -348,6 +348,29 @@
     return jnp.where(odd, place("y", by), place("x", by))
 
 
+def spread_kernel(bit_ref, part, got, copies_ref, outer_ref):
+    even = bit_ref[0] == 0
+    first = jnp.where(even, part[...], got[...])
+    for n in range(copies_ref.shape[0]):
+        copies_ref[n] = first
+    outer_ref[...] = jnp.where(even, got[...], part[...])[: outer_ref.shape[0], :]
+
+
+def spread(bit, part, got, rows):
+    return pl.pallas_call(
+        spread_kernel,
+        out_shape=(
+            jax.ShapeDtypeStruct((4,) + part.shape, part.dtype),
+            jax.ShapeDtypeStruct((rows, part.shape[1]), part.dtype),
+        ),
+        in_specs=[scalars()] + [whole()] * 2,
+        out_specs=(whole(), whole()),
+        compiler_params=params(24),
+        cost_estimate=pl.CostEstimate(flops=0, bytes_accessed=2 * 10**6, transcendentals=0),
+        name="spread",
+    )(bit, part, got)
+
+
 barrier = lax.optimization_barrier
 STEPS = (1, 2, 3)
 
@@ -379,9 +402,7 @@
         whole_part = put(whole_part, turned(part, by) if by else part, turned_place(-by))
     part = whole_part.reshape(-1, part.shape[1])
     got = swapped(part, "z", 1)
-    inner = jnp.where(bit == 0, part, got)
-    outer = jnp.where(bit == 0, got, part)[: part.shape[0] - rows]
-    copies = barrier(jnp.broadcast_to(inner, (4,) + inner.shape))
+    copies, outer = spread(bit.astype(jnp.int32).reshape(1), part, got, part.shape[0] - rows)
     copies, moved = barrier((exchange(copies, "y"), [rotated(outer, "x", by) for by in STEPS]))
     return [copies.reshape(-1, part.shape[1])], [outer] + moved, beside
 

time: 129 us -> 129 us (level)
  no operation moved by 1% of the time
where the time goes in v12:
time: 129 us
  starting transfers between devices  61.4 us (48%)
  waiting for transfers between devices  48.1 us (37%)
  Pallas kernels  14.8 us (11%)
  between operations  1.64 us (1%)
  other arithmetic  1.63 us (1%)
    all_to_all x3, starting transfers between devices, exchange(): return lax.all_to_all(x, axis, split_axis=0, concat_axis=0, tiled=True)  19.6 us
    ppermute x9, waiting for transfers between devices, rotated(): return lax.ppermute(x, axis, [(i, (i + by) % size) for i in range(size)])  16.8 us
    ppermute x9, waiting for transfers between devices, swapped(): return lax.ppermute(x, axis, [(i, i ^ bit) for i in range(SIZES[axis])])  15.5 us
    ppermute x9, starting transfers between devices, swapped(): return lax.ppermute(x, axis, [(i, i ^ bit) for i in range(SIZES[axis])])  13.9 us
    ppermute x9, starting transfers between devices, rotated(): return lax.ppermute(x, axis, [(i, (i + by) % size) for i in range(size)])  13.8 us
    ppermute x2, waiting for transfers between devices, shifted(): return lax.ppermute(x, SPACE, pairs)  11.1 us
    ppermute x6, starting transfers between devices, turned(): return lax.ppermute(x, ('x', 'z', 'y'), pairs)  9.62 us
    ppermute x6, waiting for transfers between devices, turned(): return lax.ppermute(x, ('x', 'z', 'y'), pairs)  4.7 us
  transfers between devices with their start and end apart: 29, of which 20 were waited for; matrix products, arithmetic and copies ran while one was open for 0% of the time, Pallas kernels for 3%

profile of v12, /device:TPU:1, one launch (start us, length us, event | category | flops | bytes accessed | tf_op | source)
XLA Modules:
  0.0 128.8 jit_solution(2056096531738697562)
XLA Ops:
  1.4 2.9 %build_sent.1 = (bf16[32,32,256]{2,1,0:T(8,128)(2,1)}, bf16[512,1024]{1,0:T(8,128)(2,1)}) custom-call(f32[1]{0:T(128)S(6)} %div.3.share_ref, bf16[512,1024]{1,0:T(8,128)(2,1)} %bitcast.52, bf16[256,1024]{1,0:T(8,128)(2,1)} %weight_hbm.1, bf16[2,256,256]{2,1,0:T(8,128)(2,1)} %bitcast.46), custom_call_target="tpu_custom_call" | custom-call | flops 268000000 | bytes 4000000 | tf_op jit(solution)/shard_map/build_sent/pallas_call | solution.py:81
  4.3 11.9 %all-to-all-start = ((bf16[32,32,256]{2,1,0:T(8,128)(2,1)}), bf16[32,32,256]{2,1,0:T(8,128)(2,1)S(1)}, u32[]{:S(2)}, u32[]{:S(2)}) async-start(bf16[32,32,256]{2,1,0:T(8,128)(2,1)} %get-tuple-element.38), calls=%async_computation | async-start | bytes 1048576 | tf_op jit(solution)/shard_map/all_to_all | solution.py:306
  16.3 3.1 %collective-permute-start = (bf16[1,512,256]{2,1,0:T(8,128)(2,1)S(1)}, bf16[1,512,256]{2,1,0:T(8,128)(2,1)S(1)}, u32[]{:S(2)}, u32[]{:S(2)}) collective-permute-start(bf16[1,512,256]{2,1,0:T(8,128)(2,1)S(1)} %slice_bitcast_fusion), channel_id=1, source_target_pairs={{0,8},{8,16},{16,24},{24,32},{32,40},{40,48},{48,56},{56,64},{64,7... | collective-permute-start | bytes 786440 | tf_op jit(solution)/shard_map/ppermute | solution.py:43
  21.2 11.1 %collective-permute-done.x_ref = bf16[1,512,256]{2,1,0:T(8,128)(2,1)S(1)} collective-permute-done((bf16[1,512,256]{2,1,0:T(8,128)(2,1)S(1)}, bf16[1,512,256]{2,1,0:T(8,128)(2,1)S(1)}, u32[]{:S(2)}, u32[]{:S(2)}) %collective-permute-start) | collective-permute-done | bytes 262176 | tf_op jit(solution)/shard_map/ppermute | solution.py:43
  32.5 3.9 %terms.1 = (f32[896,256]{1,0:T(8,128)S(1)}, f32[896,256]{1,0:T(8,128)}, f32[768,256]{1,0:T(8,128)S(1)}, f32[768,256]{1,0:T(8,128)S(1)}, bf16[2,256,256]{2,1,0:T(...) custom-call(s32[1]{0:T(128)} %bitcast.core_ref, bf16[32,32,256]{2,1,0:T(8,128)(2,1)S(1)} %all-to-all-done.arrived_hbm, ...), custom_call_target="tpu_custom_call" | custom-call | flops 870000000 | bytes 8000000 | tf_op jit(solution)/shard_map/terms/pallas_call | solution.py:199
  36.5 3.6 %collective-permute-start.1 = (f32[896,256]{1,0:T(8,128)}, f32[896,256]{1,0:T(8,128)S(1)}, u32[]{:S(2)}, u32[]{:S(2)}) collective-permute-start(f32[896,256]{1,0:T(8,128)} %get-tuple-element.41), channel_id=1, source_target_pairs={{0,1},{1,0},{2,3},{3,2},{4,5},{5,4},{6,7},{7,6},{8,9},{9,8},{10,11... | collective-permute-start | bytes 2752520 | tf_op jit(solution)/shard_map/ppermute | solution.py:333
  40.2 2.5 %collective-permute-done.1.got = f32[896,256]{1,0:T(8,128)S(1)} collective-permute-done((f32[896,256]{1,0:T(8,128)}, f32[896,256]{1,0:T(8,128)S(1)}, u32[]{:S(2)}, u32[]{:S(2)}) %collective-permute-start.1) | collective-permute-done | bytes 917536 | tf_op jit(solution)/shard_map/ppermute | solution.py:333
  43.7 4.2 %all-to-all-start.1 = ((f32[4,224,256]{2,1,0:T(8,128)}), f32[4,224,256]{2,1,0:T(8,128)}, u32[]{:S(2)}, u32[]{:S(2)}) async-start(f32[4,224,256]{2,1,0:T(8,128)} %bitcast.5), calls=%async_computation.1 | async-start | bytes 1835008 | tf_op jit(solution)/shard_map/all_to_all | solution.py:306
  48.7 2.7 %collective-permute-start.3 = (f32[192,256]{1,0:T(8,128)S(1)}, f32[192,256]{1,0:T(8,128)S(1)}, u32[]{:S(2)}, u32[]{:S(2)}) collective-permute-start(f32[192,256]{1,0:T(8,128)S(1)} %get-tuple-element.47), channel_id=1, source_target_pairs={{0,64},{64,128},{128,192},{192,0},{1,65},{65,129},{129,193},{193,1... | collective-permute-start | bytes 589832 | tf_op jit(solution)/shard_map/ppermute | solution.py:325
  51.4 2.7 %collective-permute-start.4 = (f32[192,256]{1,0:T(8,128)S(1)}, f32[192,256]{1,0:T(8,128)S(1)}, u32[]{:S(2)}, u32[]{:S(2)}) collective-permute-start(f32[192,256]{1,0:T(8,128)S(1)} %get-tuple-element.48), channel_id=1, source_target_pairs={{0,128},{64,192},{128,0},{192,64},{1,129},{65,193},{129,1},{193,65... | collective-permute-start | bytes 589832 | tf_op jit(solution)/shard_map/ppermute | solution.py:325
  55.0 2.8 %collective-permute-done.3 = f32[192,256]{1,0:T(8,128)S(1)} collective-permute-done((f32[192,256]{1,0:T(8,128)S(1)}, f32[192,256]{1,0:T(8,128)S(1)}, u32[]{:S(2)}, u32[]{:S(2)}) %collective-permute-start.3) | collective-permute-done | bytes 196640 | tf_op jit(solution)/shard_map/ppermute | solution.py:325
  57.7 5.0 %collective-permute-done.4 = f32[192,256]{1,0:T(8,128)S(1)} collective-permute-done((f32[192,256]{1,0:T(8,128)S(1)}, f32[192,256]{1,0:T(8,128)S(1)}, u32[]{:S(2)}, u32[]{:S(2)}) %collective-permute-start.4) | collective-permute-done | bytes 196640 | tf_op jit(solution)/shard_map/ppermute | solution.py:325
  62.8 1.4 %reduce_sum.9 = f32[224,256]{1,0:T(8,128)S(1)} reduce(f32[4,224,256]{2,1,0:T(8,128)} %all-to-all-done.1, f32[]{:T(128)} %constant.26.clone.1), dimensions={0}, to_apply=%region_0.0 | reduce | flops 172032 | bytes 1146884 | tf_op jit(solution)/shard_map/reduce_sum | solution.py:382
  64.4 5.6 %collective-permute-done.6 = f32[224,256]{1,0:T(8,128)S(1)} collective-permute-done((f32[224,256]{1,0:T(8,128)S(1)}, f32[224,256]{1,0:T(8,128)S(1)}, u32[]{:S(2)}, u32[]{:S(2)}) %collective-permute-start.6) | collective-permute-done | bytes 229408 | tf_op jit(solution)/shard_map/ppermute | solution.py:333
  70.0 2.0 %collective-permute-start.7 = (f32[56,256]{1,0:T(8,128)S(1)}, f32[56,256]{1,0:T(8,128)S(1)}, u32[]{:S(2)}, u32[]{:S(2)}) collective-permute-start(f32[56,256]{1,0:T(8,128)S(1)} %get-tuple-element.56), channel_id=1, source_target_pairs={{0,64},{2,66},{4,68},{6,70},{8,10},{10,12},{12,14},{14,8},{16,80},... | collective-permute-start | bytes 172040 | tf_op jit(solution)/shard_map/ppermute | solution.py:343
  72.0 2.5 %collective-permute-start.8 = (f32[56,256]{1,0:T(8,128)S(1)}, f32[56,256]{1,0:T(8,128)S(1)}, u32[]{:S(2)}, u32[]{:S(2)}) collective-permute-start(f32[56,256]{1,0:T(8,128)S(1)} %get-tuple-element.57), channel_id=1, source_target_pairs={{0,128},{2,130},{4,132},{6,134},{8,12},{10,14},{12,8},{14,10},{16,... | collective-permute-start | bytes 172040 | tf_op jit(solution)/shard_map/ppermute | solution.py:343
  77.7 1.8 %collective-permute-start.12 = (f32[56,256]{1,0:T(8,128)S(1)}, f32[56,256]{1,0:T(8,128)S(1)}, u32[]{:S(2)}, u32[]{:S(2)}) collective-permute-start(f32[56,256]{1,0:T(8,128)S(1)} %fusion.6), channel_id=1, source_target_pairs={{0,48},{8,56},{16,0},{24,8},{32,16},{40,24},{48,32},{56,40},{1,49}... | collective-permute-start | bytes 172040 | tf_op jit(solution)/shard_map/ppermute | solution.py:325
  79.5 1.6 %collective-permute-start.11 = (f32[56,256]{1,0:T(8,128)S(1)}, f32[56,256]{1,0:T(8,128)S(1)}, u32[]{:S(2)}, u32[]{:S(2)}) collective-permute-start(f32[56,256]{1,0:T(8,128)S(1)} %fusion.6), channel_id=1, source_target_pairs={{0,32},{8,40},{16,48},{24,56},{32,0},{40,8},{48,16},{56,24},{1,33}... | collective-permute-start | bytes 172040 | tf_op jit(solution)/shard_map/ppermute | solution.py:325
  81.1 1.7 %collective-permute-start.10 = (f32[56,256]{1,0:T(8,128)S(1)}, f32[56,256]{1,0:T(8,128)S(1)}, u32[]{:S(2)}, u32[]{:S(2)}) collective-permute-start(f32[56,256]{1,0:T(8,128)S(1)} %fusion.6), channel_id=1, source_target_pairs={{0,16},{8,24},{16,32},{24,40},{32,48},{40,56},{48,0},{56,8},{1,17}... | collective-permute-start | bytes 172040 | tf_op jit(solution)/shard_map/ppermute | solution.py:325
  82.8 1.9 %input_grad.1 = bf16[4,512,256]{2,1,0:T(8,128)(2,1)} custom-call(bf16[2,256,256]{2,1,0:T(8,128)(2,1)S(1)} %get-tuple-element.59.grad_ref, bf16[1,256,256]{2,1,0:T(8,128)(2,1)S(1)} %collective-permute-done.13.below_ref, bf16[3,3,256,256]{3,2,1,0:T(8,128)(2,1)S(1)} %copy-done.2), custom_call_target="tpu_custom_call" | custom-call | flops 604000000 | bytes 3000000 | tf_op jit(solution)/shard_map/input_grad/pallas_call | solution.py:293
  84.7 1.9 %collective-permute-done.11 = f32[56,256]{1,0:T(8,128)S(1)} collective-permute-done((f32[56,256]{1,0:T(8,128)S(1)}, f32[56,256]{1,0:T(8,128)S(1)}, u32[]{:S(2)}, u32[]{:S(2)}) %collective-permute-start.11) | collective-permute-done | bytes 57376 | tf_op jit(solution)/shard_map/ppermute | solution.py:325
  87.2 2.4 %collective-permute-start.14 = (f32[56,256]{1,0:T(8,128)S(1)}, f32[56,256]{1,0:T(8,128)S(1)}, u32[]{:S(2)}, u32[]{:S(2)}) collective-permute-start(f32[56,256]{1,0:T(8,128)S(1)} %get-tuple-element.74), channel_id=1, source_target_pairs={{0,64},{2,66},{4,68},{6,70},{8,10},{10,12},{12,14},{14,8},{16,80},... | collective-permute-start | bytes 172040 | tf_op jit(solution)/shard_map/ppermute | solution.py:343
  89.6 2.5 %collective-permute-start.15 = (f32[56,256]{1,0:T(8,128)S(1)}, f32[56,256]{1,0:T(8,128)S(1)}, u32[]{:S(2)}, u32[]{:S(2)}) collective-permute-start(f32[56,256]{1,0:T(8,128)S(1)} %get-tuple-element.74), channel_id=1, source_target_pairs={{0,128},{2,130},{4,132},{6,134},{8,12},{10,14},{12,8},{14,10},{16,... | collective-permute-start | bytes 172040 | tf_op jit(solution)/shard_map/ppermute | solution.py:343
  92.5 1.8 %collective-permute-done.15 = f32[56,256]{1,0:T(8,128)S(1)} collective-permute-done((f32[56,256]{1,0:T(8,128)S(1)}, f32[56,256]{1,0:T(8,128)S(1)}, u32[]{:S(2)}, u32[]{:S(2)}) %collective-permute-start.15) | collective-permute-done | bytes 57376 | tf_op jit(solution)/shard_map/ppermute | solution.py:343
  95.2 5.2 %collective-permute-done.17.got = f32[224,256]{1,0:T(8,128)S(1)} collective-permute-done((f32[224,256]{1,0:T(8,128)S(1)}, f32[224,256]{1,0:T(8,128)S(1)}, u32[]{:S(2)}, u32[]{:S(2)}) %collective-permute-start.17) | collective-permute-done | bytes 229408 | tf_op jit(solution)/shard_map/ppermute | solution.py:333
  101.3 3.5 %all-to-all-start.2 = ((f32[4,224,256]{2,1,0:T(8,128)}), f32[4,224,256]{2,1,0:T(8,128)S(1)}, u32[]{:S(2)}, u32[]{:S(2)}) async-start(f32[4,224,256]{2,1,0:T(8,128)} %get-tuple-element.65), calls=%async_computation.2 | async-start | bytes 1835008 | tf_op jit(solution)/shard_map/all_to_all | solution.py:306
  107.3 2.1 %collective-permute-done.20.refs_5_ = f32[192,256]{1,0:T(8,128)S(1)} collective-permute-done((f32[192,256]{1,0:T(8,128)S(1)}, f32[192,256]{1,0:T(8,128)S(1)}, u32[]{:S(2)}, u32[]{:S(2)}) %collective-permute-start.20) | collective-permute-done | bytes 196640 | tf_op jit(solution)/shard_map/ppermute | solution.py:325
  109.5 2.5 %collective-permute-done.19.refs_4_ = f32[192,256]{1,0:T(8,128)S(1)} collective-permute-done((f32[192,256]{1,0:T(8,128)S(1)}, f32[192,256]{1,0:T(8,128)S(1)}, u32[]{:S(2)}, u32[]{:S(2)}) %collective-permute-start.19) | collective-permute-done | bytes 196640 | tf_op jit(solution)/shard_map/ppermute | solution.py:325
  112.0 2.0 %collective-permute-done.18.refs_3_ = f32[192,256]{1,0:T(8,128)S(1)} collective-permute-done((f32[192,256]{1,0:T(8,128)S(1)}, f32[192,256]{1,0:T(8,128)S(1)}, u32[]{:S(2)}, u32[]{:S(2)}) %collective-permute-start.18) | collective-permute-done | bytes 196640 | tf_op jit(solution)/shard_map/ppermute | solution.py:325
  114.0 9.0 %collective-permute-start.21 = (f32[896,256]{1,0:T(8,128)S(1)}, f32[896,256]{1,0:T(8,128)S(1)}, u32[]{:S(2)}, u32[]{:S(2)}) collective-permute-start(f32[896,256]{1,0:T(8,128)S(1)} %bitcast.43), channel_id=1, source_target_pairs={{0,1},{1,0},{2,3},{3,2},{4,5},{5,4},{6,7},{7,6},{8,9},{9,8},{10,11... | collective-permute-start | bytes 2752520 | tf_op jit(solution)/shard_map/ppermute | solution.py:333
  124.0 1.4 %collective-permute-done.22.refs_6_ = f32[192,256]{1,0:T(8,128)S(1)} collective-permute-done((f32[192,256]{1,0:T(8,128)S(1)}, f32[192,256]{1,0:T(8,128)S(1)}, u32[]{:S(2)}, u32[]{:S(2)}) %collective-permute-start.22) | collective-permute-done | bytes 196640 | tf_op jit(solution)/shard_map/ppermute | solution.py:333
  126.3 2.6 %assemble.1 = (f32[9,256,256]{2,1,0:T(8,128)}, f32[256,1024]{1,0:T(8,128)}) custom-call(s32[2]{0:T(128)S(1)} %pad_add_fusion.where_ref, f32[896,256]{1,0:T(8,128)S(1)} %bitcast.44, f32[896,256]{1,0:T(8,128)S(1)} %collective-permute-done.21.refs_1_, f32[192,256]{1,0:T(8,128)S(1)} %get-tuple-element.66.refs_2_, ...), custom_call_target="tpu_custom_call" | custom-call | bytes 7000000 | tf_op jit(solution)/shard_map/assemble/pallas_call | solution.py:434
  (57 shorter events, 15.2 us)
Async XLA Ops:
  0.6 15.6 %copy-start.1 = (bf16[1,4,512,256]{3,2,1,0:T(8,128)(2,1)S(1)}, bf16[1,4,512,256]{3,2,1,0:T(8,128)(2,1)}, u32[]{:S(2)}) copy-start(bf16[1,4,512,256]{3,2,1,0:T(8,128)(2,1)} %param.6) | copy-start | bytes 3145732
  4.3 28.2 %all-to-all-start = ((bf16[32,32,256]{2,1,0:T(8,128)(2,1)}), bf16[32,32,256]{2,1,0:T(8,128)(2,1)S(1)}, u32[]{:S(2)}, u32[]{:S(2)}) async-start(bf16[32,32,256]{2,1,0:T(8,128)(2,1)} %get-tuple-element.38), calls=%async_computation | async-start | bytes 1048576 | tf_op jit(solution)/shard_map/all_to_all | solution.py:306
  16.3 16.0 %collective-permute-start = (bf16[1,512,256]{2,1,0:T(8,128)(2,1)S(1)}, bf16[1,512,256]{2,1,0:T(8,128)(2,1)S(1)}, u32[]{:S(2)}, u32[]{:S(2)}) collective-permute-start(bf16[1,512,256]{2,1,0:T(8,128)(2,1)S(1)} %slice_bitcast_fusion), channel_id=1, source_target_pairs={{0,8},{8,16},{16,24},{24,32},{32,40},{40,48},{48,56},{56,64},{64,7... | collective-permute-start | bytes 786440 | tf_op jit(solution)/shard_map/ppermute | solution.py:43
  19.4 13.1 %copy-start.3 = (bf16[1,2,256,256]{3,2,1,0:T(8,128)(2,1)S(1)}, bf16[1,2,256,256]{3,2,1,0:T(8,128)(2,1)}, u32[]{:S(2)}) copy-start(bf16[1,2,256,256]{3,2,1,0:T(8,128)(2,1)} %param.7) | copy-start | bytes 786436
  36.5 6.3 %collective-permute-start.1 = (f32[896,256]{1,0:T(8,128)}, f32[896,256]{1,0:T(8,128)S(1)}, u32[]{:S(2)}, u32[]{:S(2)}) collective-permute-start(f32[896,256]{1,0:T(8,128)} %get-tuple-element.41), channel_id=1, source_target_pairs={{0,1},{1,0},{2,3},{3,2},{4,5},{5,4},{6,7},{7,6},{8,9},{9,8},{10,11... | collective-permute-start | bytes 2752520 | tf_op jit(solution)/shard_map/ppermute | solution.py:333
  40.1 8.0 %collective-permute-start.2 = (f32[768,256]{1,0:T(8,128)S(1)}, f32[768,256]{1,0:T(8,128)S(1)}, u32[]{:S(2)}, u32[]{:S(2)}) collective-permute-start(f32[768,256]{1,0:T(8,128)S(1)} %get-tuple-element.43), channel_id=1, source_target_pairs={{0,1},{1,0},{2,3},{3,2},{4,5},{5,4},{6,7},{7,6},{8,9},{9,8},{10,11... | collective-permute-start | bytes 2359304 | tf_op jit(solution)/shard_map/ppermute | solution.py:333
  43.7 19.0 %all-to-all-start.1 = ((f32[4,224,256]{2,1,0:T(8,128)}), f32[4,224,256]{2,1,0:T(8,128)}, u32[]{:S(2)}, u32[]{:S(2)}) async-start(f32[4,224,256]{2,1,0:T(8,128)} %bitcast.5), calls=%async_computation.1 | async-start | bytes 1835008 | tf_op jit(solution)/shard_map/all_to_all | solution.py:306
  48.7 9.0 %collective-permute-start.3 = (f32[192,256]{1,0:T(8,128)S(1)}, f32[192,256]{1,0:T(8,128)S(1)}, u32[]{:S(2)}, u32[]{:S(2)}) collective-permute-start(f32[192,256]{1,0:T(8,128)S(1)} %get-tuple-element.47), channel_id=1, source_target_pairs={{0,64},{64,128},{128,192},{192,0},{1,65},{65,129},{129,193},{193,1... | collective-permute-start | bytes 589832 | tf_op jit(solution)/shard_map/ppermute | solution.py:325
  51.4 11.3 %collective-permute-start.4 = (f32[192,256]{1,0:T(8,128)S(1)}, f32[192,256]{1,0:T(8,128)S(1)}, u32[]{:S(2)}, u32[]{:S(2)}) collective-permute-start(f32[192,256]{1,0:T(8,128)S(1)} %get-tuple-element.48), channel_id=1, source_target_pairs={{0,128},{64,192},{128,0},{192,64},{1,129},{65,193},{129,1},{193,65... | collective-permute-start | bytes 589832 | tf_op jit(solution)/shard_map/ppermute | solution.py:325
  54.1 8.6 %collective-permute-start.5 = (f32[192,256]{1,0:T(8,128)S(1)}, f32[192,256]{1,0:T(8,128)S(1)}, u32[]{:S(2)}, u32[]{:S(2)}) collective-permute-start(f32[192,256]{1,0:T(8,128)S(1)} %get-tuple-element.49), channel_id=1, source_target_pairs={{0,192},{64,0},{128,64},{192,128},{1,193},{65,1},{129,65},{193,129... | collective-permute-start | bytes 589832 | tf_op jit(solution)/shard_map/ppermute | solution.py:325
  62.8 20.0 %copy-start.2 = (bf16[3,3,256,256]{3,2,1,0:T(8,128)(2,1)S(1)}, bf16[3,3,256,256]{3,2,1,0:T(8,128)(2,1)}, u32[]{:S(2)}) copy-start(bf16[3,3,256,256]{3,2,1,0:T(8,128)(2,1)} %weight_ref.1) | copy-start | bytes 3538948
  64.2 5.7 %collective-permute-start.6 = (f32[224,256]{1,0:T(8,128)S(1)}, f32[224,256]{1,0:T(8,128)S(1)}, u32[]{:S(2)}, u32[]{:S(2)}) collective-permute-start(f32[224,256]{1,0:T(8,128)S(1)} %fusion.1), channel_id=1, source_target_pairs={{0,8},{8,0},{16,24},{24,16},{32,40},{40,32},{48,56},{56,48},{1,9},... | collective-permute-start | bytes 688136 | tf_op jit(solution)/shard_map/ppermute | solution.py:333
  70.0 6.0 %collective-permute-start.7 = (f32[56,256]{1,0:T(8,128)S(1)}, f32[56,256]{1,0:T(8,128)S(1)}, u32[]{:S(2)}, u32[]{:S(2)}) collective-permute-start(f32[56,256]{1,0:T(8,128)S(1)} %get-tuple-element.56), channel_id=1, source_target_pairs={{0,64},{2,66},{4,68},{6,70},{8,10},{10,12},{12,14},{14,8},{16,80},... | collective-permute-start | bytes 172040 | tf_op jit(solution)/shard_map/ppermute | solution.py:343
  72.0 4.7 %collective-permute-start.8 = (f32[56,256]{1,0:T(8,128)S(1)}, f32[56,256]{1,0:T(8,128)S(1)}, u32[]{:S(2)}, u32[]{:S(2)}) collective-permute-start(f32[56,256]{1,0:T(8,128)S(1)} %get-tuple-element.57), channel_id=1, source_target_pairs={{0,128},{2,130},{4,132},{6,134},{8,12},{10,14},{12,8},{14,10},{16,... | collective-permute-start | bytes 172040 | tf_op jit(solution)/shard_map/ppermute | solution.py:343
  74.5 3.1 %collective-permute-start.9 = (f32[56,256]{1,0:T(8,128)S(1)}, f32[56,256]{1,0:T(8,128)S(1)}, u32[]{:S(2)}, u32[]{:S(2)}) collective-permute-start(f32[56,256]{1,0:T(8,128)S(1)} %get-tuple-element.58), channel_id=1, source_target_pairs={{0,192},{2,194},{4,196},{6,198},{8,14},{10,8},{12,10},{14,12},{16,... | collective-permute-start | bytes 172040 | tf_op jit(solution)/shard_map/ppermute | solution.py:343
  74.7 8.1 %collective-permute-start.13 = (bf16[1,256,256]{2,1,0:T(8,128)(2,1)S(1)}, bf16[1,256,256]{2,1,0:T(8,128)(2,1)S(1)}, u32[]{:S(2)}, u32[]{:S(2)}) collective-permute-start(bf16[1,256,256]{2,1,0:T(8,128)(2,1)S(1)} %get-tuple-element.60), channel_id=1, source_target_pairs={{8,0},{16,8},{24,16},{32,24},{40,32},{48,40},{56,48},{64,56},{72,6... | collective-permute-start | bytes 393224 | tf_op jit(solution)/shard_map/ppermute | solution.py:43
  77.7 7.0 %collective-permute-start.12 = (f32[56,256]{1,0:T(8,128)S(1)}, f32[56,256]{1,0:T(8,128)S(1)}, u32[]{:S(2)}, u32[]{:S(2)}) collective-permute-start(f32[56,256]{1,0:T(8,128)S(1)} %fusion.6), channel_id=1, source_target_pairs={{0,48},{8,56},{16,0},{24,8},{32,16},{40,24},{48,32},{56,40},{1,49}... | collective-permute-start | bytes 172040 | tf_op jit(solution)/shard_map/ppermute | solution.py:325
  79.5 7.1 %collective-permute-start.11 = (f32[56,256]{1,0:T(8,128)S(1)}, f32[56,256]{1,0:T(8,128)S(1)}, u32[]{:S(2)}, u32[]{:S(2)}) collective-permute-start(f32[56,256]{1,0:T(8,128)S(1)} %fusion.6), channel_id=1, source_target_pairs={{0,32},{8,40},{16,48},{24,56},{32,0},{40,8},{48,16},{56,24},{1,33}... | collective-permute-start | bytes 172040 | tf_op jit(solution)/shard_map/ppermute | solution.py:325
  81.1 6.0 %collective-permute-start.10 = (f32[56,256]{1,0:T(8,128)S(1)}, f32[56,256]{1,0:T(8,128)S(1)}, u32[]{:S(2)}, u32[]{:S(2)}) collective-permute-start(f32[56,256]{1,0:T(8,128)S(1)} %fusion.6), channel_id=1, source_target_pairs={{0,16},{8,24},{16,32},{24,40},{32,48},{40,56},{48,0},{56,8},{1,17}... | collective-permute-start | bytes 172040 | tf_op jit(solution)/shard_map/ppermute | solution.py:325
  87.2 5.3 %collective-permute-start.14 = (f32[56,256]{1,0:T(8,128)S(1)}, f32[56,256]{1,0:T(8,128)S(1)}, u32[]{:S(2)}, u32[]{:S(2)}) collective-permute-start(f32[56,256]{1,0:T(8,128)S(1)} %get-tuple-element.74), channel_id=1, source_target_pairs={{0,64},{2,66},{4,68},{6,70},{8,10},{10,12},{12,14},{14,8},{16,80},... | collective-permute-start | bytes 172040 | tf_op jit(solution)/shard_map/ppermute | solution.py:343
  89.6 4.7 %collective-permute-start.15 = (f32[56,256]{1,0:T(8,128)S(1)}, f32[56,256]{1,0:T(8,128)S(1)}, u32[]{:S(2)}, u32[]{:S(2)}) collective-permute-start(f32[56,256]{1,0:T(8,128)S(1)} %get-tuple-element.74), channel_id=1, source_target_pairs={{0,128},{2,130},{4,132},{6,134},{8,12},{10,14},{12,8},{14,10},{16,... | collective-permute-start | bytes 172040 | tf_op jit(solution)/shard_map/ppermute | solution.py:343
  92.1 3.0 %collective-permute-start.16 = (f32[56,256]{1,0:T(8,128)S(1)}, f32[56,256]{1,0:T(8,128)S(1)}, u32[]{:S(2)}, u32[]{:S(2)}) collective-permute-start(f32[56,256]{1,0:T(8,128)S(1)} %get-tuple-element.74), channel_id=1, source_target_pairs={{0,192},{2,194},{4,196},{6,198},{8,14},{10,8},{12,10},{14,12},{16,... | collective-permute-start | bytes 172040 | tf_op jit(solution)/shard_map/ppermute | solution.py:343
  95.2 5.2 %collective-permute-start.17 = (f32[224,256]{1,0:T(8,128)S(1)}, f32[224,256]{1,0:T(8,128)S(1)}, u32[]{:S(2)}, u32[]{:S(2)}) collective-permute-start(f32[224,256]{1,0:T(8,128)S(1)} %bitcast.48), channel_id=1, source_target_pairs={{0,8},{8,0},{16,24},{24,16},{32,40},{40,32},{48,56},{56,48},{1,9},... | collective-permute-start | bytes 688136 | tf_op jit(solution)/shard_map/ppermute | solution.py:333
  101.3 12.6 %all-to-all-start.2 = ((f32[4,224,256]{2,1,0:T(8,128)}), f32[4,224,256]{2,1,0:T(8,128)S(1)}, u32[]{:S(2)}, u32[]{:S(2)}) async-start(f32[4,224,256]{2,1,0:T(8,128)} %get-tuple-element.65), calls=%async_computation.2 | async-start | bytes 1835008 | tf_op jit(solution)/shard_map/all_to_all | solution.py:306
  104.9 4.6 %collective-permute-start.20 = (f32[192,256]{1,0:T(8,128)S(1)}, f32[192,256]{1,0:T(8,128)S(1)}, u32[]{:S(2)}, u32[]{:S(2)}) collective-permute-start(f32[192,256]{1,0:T(8,128)S(1)} %get-tuple-element.66.refs_2_), channel_id=1, source_target_pairs={{0,192},{64,0},{128,64},{192,128},{1,193},{65,1},{129,65},{193,129... | collective-permute-start | bytes 589832 | tf_op jit(solution)/shard_map/ppermute | solution.py:325
  105.9 6.1 %collective-permute-start.19 = (f32[192,256]{1,0:T(8,128)S(1)}, f32[192,256]{1,0:T(8,128)S(1)}, u32[]{:S(2)}, u32[]{:S(2)}) collective-permute-start(f32[192,256]{1,0:T(8,128)S(1)} %get-tuple-element.66.refs_2_), channel_id=1, source_target_pairs={{0,128},{64,192},{128,0},{192,64},{1,129},{65,193},{129,1},{193,65... | collective-permute-start | bytes 589832 | tf_op jit(solution)/shard_map/ppermute | solution.py:325
  106.9 7.0 %collective-permute-start.18 = (f32[192,256]{1,0:T(8,128)S(1)}, f32[192,256]{1,0:T(8,128)S(1)}, u32[]{:S(2)}, u32[]{:S(2)}) collective-permute-start(f32[192,256]{1,0:T(8,128)S(1)} %get-tuple-element.66.refs_2_), channel_id=1, source_target_pairs={{0,64},{64,128},{128,192},{192,0},{1,65},{65,129},{129,193},{193,1... | collective-permute-start | bytes 589832 | tf_op jit(solution)/shard_map/ppermute | solution.py:325
  114.0 12.3 %collective-permute-start.21 = (f32[896,256]{1,0:T(8,128)S(1)}, f32[896,256]{1,0:T(8,128)S(1)}, u32[]{:S(2)}, u32[]{:S(2)}) collective-permute-start(f32[896,256]{1,0:T(8,128)S(1)} %bitcast.43), channel_id=1, source_target_pairs={{0,1},{1,0},{2,3},{3,2},{4,5},{5,4},{6,7},{7,6},{8,9},{9,8},{10,11... | collective-permute-start | bytes 2752520 | tf_op jit(solution)/shard_map/ppermute | solution.py:333
  123.0 2.4 %collective-permute-start.22 = (f32[192,256]{1,0:T(8,128)S(1)}, f32[192,256]{1,0:T(8,128)S(1)}, u32[]{:S(2)}, u32[]{:S(2)}) collective-permute-start(f32[192,256]{1,0:T(8,128)S(1)} %get-tuple-element.66.refs_2_), channel_id=1, source_target_pairs={{0,1},{1,0},{2,3},{3,2},{4,5},{5,4},{6,7},{7,6},{8,9},{9,8},{10,11... | collective-permute-start | bytes 589832 | tf_op jit(solution)/shard_map/ppermute | solution.py:333
  123.0 2.7 %collective-permute-start.23 = (f32[192,256]{1,0:T(8,128)S(1)}, f32[192,256]{1,0:T(8,128)S(1)}, u32[]{:S(2)}, u32[]{:S(2)}) collective-permute-start(f32[192,256]{1,0:T(8,128)S(1)} %collective-permute-done.18.refs_3_), channel_id=1, source_target_pairs={{0,1},{1,0},{2,3},{3,2},{4,5},{5,4},{6,7},{7,6},{8,9},{9,8},{10,11... | collective-permute-start | bytes 589832 | tf_op jit(solution)/shard_map/ppermute | solution.py:333
  123.5 2.4 %collective-permute-start.24 = (f32[192,256]{1,0:T(8,128)S(1)}, f32[192,256]{1,0:T(8,128)S(1)}, u32[]{:S(2)}, u32[]{:S(2)}) collective-permute-start(f32[192,256]{1,0:T(8,128)S(1)} %collective-permute-done.19.refs_4_), channel_id=1, source_target_pairs={{0,1},{1,0},{2,3},{3,2},{4,5},{5,4},{6,7},{7,6},{8,9},{9,8},{10,11... | collective-permute-start | bytes 589832 | tf_op jit(solution)/shard_map/ppermute | solution.py:333
  123.5 2.7 %collective-permute-start.25 = (f32[192,256]{1,0:T(8,128)S(1)}, f32[192,256]{1,0:T(8,128)S(1)}, u32[]{:S(2)}, u32[]{:S(2)}) collective-permute-start(f32[192,256]{1,0:T(8,128)S(1)} %collective-permute-done.20.refs_5_), channel_id=1, source_target_pairs={{0,1},{1,0},{2,3},{3,2},{4,5},{5,4},{6,7},{7,6},{8,9},{9,8},{10,11... | collective-permute-start | bytes 589832 | tf_op jit(solution)/shard_map/ppermute | solution.py:333
  (1 other events, 1.1 us)
